TPU v7x, 32 devices: a whole 2x2x4 slice. The times are simulated.
32 devices in a mesh: heads: 8 (over y, x, core), batch: 4 (over z).
Axes of the slice: x: 2, y: 2, z: 4, core: 2. Of those that a mesh axis runs over, the one named last changes fastest.
Arguments:
- tokens: bfloat16 [2, 4, 1024, 2048], P(None, 'batch', 'heads'), may hold values from -6 to 6
- cotangent: bfloat16 [2, 4, 1024, 2048], P(None, 'batch', 'heads'), may hold values from -6 to 6
- doc_lengths: int32 [2, 4, 4], P(None, 'batch'), may hold values from 1 to 768, 1024 in all within a row
- pad_mask: int32 [2, 4, 1024], P(None, 'batch'), may hold values 0 or 1
- w_query: bfloat16 [2048, 1024], P(None, 'heads'), may hold values from -0.1875 to 0.1875
- w_key: bfloat16 [2048, 1024], P(None, 'heads'), may hold values from -0.1875 to 0.1875
- w_value: bfloat16 [2048, 1024], P(None, 'heads'), may hold values from -0.125 to 0.125
- w_out: bfloat16 [1024, 2048], P('heads'), may hold values from -0.75 to 0.75
- w_gate: bfloat16 [2048, 8192], P(None, 'heads'), may hold values from -0.125 to 0.125
- w_up: bfloat16 [2048, 8192], P(None, 'heads'), may hold values from -0.125 to 0.125
- w_down: bfloat16 [8192, 2048], P('heads'), may hold values from -0.0625 to 0.0625
- norm_attn: float32 [2048], replicated, may hold values from 0.1 to 1.9
- norm_mlp: float32 [2048], replicated, may hold values from 0.1 to 1.9
- mix_gate: float32 [8], P('heads'), may hold values from -2 to 2
Outputs:
- layer_out: bfloat16 [2, 4, 1024, 2048], P(None, 'batch', 'heads')
- grad_tokens: float32 [2, 4, 1024, 2048], P(None, 'batch', 'heads')
- grad_w_query: float32 [2048, 1024], P(None, 'heads')
- grad_w_key: float32 [2048, 1024], P(None, 'heads')
- grad_w_value: float32 [2048, 1024], P(None, 'heads')
- grad_w_out: float32 [1024, 2048], P('heads')
- grad_w_gate: float32 [2048, 8192], P(None, 'heads')
- grad_w_up: float32 [2048, 8192], P(None, 'heads')
- grad_w_down: float32 [8192, 2048], P('heads')
- grad_norm_attn: float32 [2048], replicated
- grad_norm_mlp: float32 [2048], replicated
- grad_mix_gate: float32 [8], P('heads')
Inputs may be any that keep to these rules, and one draw needn't show every extreme that they name: `doc_lengths`: the 4 lengths of a sequence sum to 1024; the longest is 768.
All inputs are finite; a program needn't handle non-finite values. No bound on the sum of `pad_mask` on one device may be relied on, other than what follows from the above.
Results may differ from a plain program's by a relative error of at most 0.018.
Values may be sent and summed in bfloat16 or wider, within the bound.
No kernel may reach another device: no remote copies, remote signals or barrier semaphores. Data moves between devices by JAX's collectives and lax.ppermute only.
A program may use at most 256 MiB of HBM per device.

v0:
```python
import jax
import jax.numpy as jnp
from jax import lax
from jax.sharding import PartitionSpec as P

DH = 128
SEG = 512
SEGS = 2
LEN = 1024
MICRO = 2


epsilon = 1e-05
big_negative = -1e30


def dot_rows(left_mat, right_mat):
    return lax.dot_general(
        left_mat, right_mat, (((1,), (1,)), ((), ())), preferred_element_type=jnp.float32
    )


def dot_cols(left_mat, right_mat):
    return lax.dot_general(
        left_mat, right_mat, (((0,), (0,)), ((), ())), preferred_element_type=jnp.float32
    )


def norm_rows(row_block, gain_vec):
    row_scale = lax.rsqrt(jnp.mean(row_block * row_block, axis=-1, keepdims=True) + epsilon)
    return (row_block * row_scale * gain_vec, row_scale)


def norm_back(row_block, row_scale, gain_vec, upstream):
    shaped = upstream * gain_vec
    inner = jnp.mean(shaped * row_block, axis=-1, keepdims=True)
    d_rows = row_scale * shaped - row_block * row_scale * row_scale * row_scale * inner
    d_gain = jnp.sum(upstream * row_block * row_scale, axis=0)
    return (d_rows, d_gain)


def positive(values_in):
    return jnp.where(values_in > 0, values_in + 1.0, jnp.exp(values_in))


def local_mask(begin_row, positions, doc_ids, valid_keys):
    seg_pos = positions[begin_row : begin_row + SEG]
    seg_doc = doc_ids[begin_row : begin_row + SEG]
    seg_valid = valid_keys[begin_row : begin_row + SEG]
    same_doc = seg_doc[:, None] == seg_doc[None, :]
    causal = seg_pos[None, :] <= seg_pos[:, None]
    return same_doc & causal & (seg_valid[None, :] | (seg_pos[None, :] == seg_pos[:, None]))


def memory_mask(begin_row, doc_ids, valid_keys):
    seg_doc = doc_ids[begin_row : begin_row + SEG]
    return (seg_doc[:, None] == doc_ids[None, :begin_row]) & valid_keys[None, :begin_row]


def head_forward(query_all, key_all, value_all, share, positions, doc_ids, valid_keys):
    score_scale = DH ** (-0.5)
    pos_query = positive(query_all.astype(jnp.float32)).astype(jnp.bfloat16)
    pos_key = positive(key_all.astype(jnp.float32)).astype(jnp.bfloat16)
    dotted_parts, recalled_parts, total_parts = ([], [], [])
    for segment in range(SEGS):
        begin_row = segment * SEG
        query_seg = query_all[begin_row : begin_row + SEG]
        key_seg = key_all[begin_row : begin_row + SEG]
        value_seg = value_all[begin_row : begin_row + SEG]
        allowed = local_mask(begin_row, positions, doc_ids, valid_keys)
        scores = jnp.where(allowed, dot_rows(query_seg, key_seg) * score_scale, big_negative)
        row_top = jnp.max(scores, axis=1, keepdims=True)
        log_total = row_top + jnp.log(jnp.sum(jnp.exp(scores - row_top), axis=1, keepdims=True))
        soft_probs = jnp.exp(scores - log_total)
        dotted_parts.append(
            jnp.dot(soft_probs.astype(jnp.bfloat16), value_seg, preferred_element_type=jnp.float32)
        )
        total_parts.append(log_total)
        if segment == 0:
            recalled_parts.append(jnp.zeros((SEG, DH), jnp.float32))
        else:
            mem_allowed = memory_mask(begin_row, doc_ids, valid_keys)
            weights = jnp.where(
                mem_allowed,
                dot_rows(pos_query[begin_row : begin_row + SEG], pos_key[:begin_row]),
                0.0,
            )
            denominator = jnp.maximum(jnp.sum(weights, axis=1, keepdims=True), 1.0)
            numerator = jnp.dot(
                weights.astype(jnp.bfloat16),
                value_all[:begin_row],
                preferred_element_type=jnp.float32,
            )
            recalled_parts.append(numerator / denominator)
    dotted = jnp.concatenate(dotted_parts, axis=0)
    recalled = jnp.concatenate(recalled_parts, axis=0)
    mixed_head = share * recalled + (1.0 - share) * dotted
    return (mixed_head, dotted, recalled, jnp.concatenate(total_parts, axis=0))


def head_backward(
    query_all,
    key_all,
    value_all,
    share,
    positions,
    doc_ids,
    valid_keys,
    d_mixed,
    dotted,
    recalled,
    log_totals,
):
    score_scale = DH ** (-0.5)
    query_float = query_all.astype(jnp.float32)
    key_float = key_all.astype(jnp.float32)
    pos_query = positive(query_float).astype(jnp.bfloat16)
    pos_key = positive(key_float).astype(jnp.bfloat16)
    d_share = jnp.sum(d_mixed * (recalled - dotted)) * share * (1.0 - share)
    d_dotted = ((1.0 - share) * d_mixed).astype(jnp.bfloat16)
    d_recalled = share * d_mixed
    zeros_block = jnp.zeros((LEN, DH), jnp.float32)
    d_query, d_key, d_value, d_posq, d_posk = (
        zeros_block,
        zeros_block,
        zeros_block,
        zeros_block,
        zeros_block,
    )
    for segment in range(SEGS):
        begin_row = segment * SEG
        end_row = begin_row + SEG
        query_seg = query_all[begin_row:end_row]
        key_seg = key_all[begin_row:end_row]
        value_seg = value_all[begin_row:end_row]
        allowed = local_mask(begin_row, positions, doc_ids, valid_keys)
        scores = jnp.where(allowed, dot_rows(query_seg, key_seg) * score_scale, big_negative)
        soft_probs = jnp.exp(scores - log_totals[begin_row:end_row])
        d_dot_seg = d_dotted[begin_row:end_row]
        d_value = d_value.at[begin_row:end_row].add(
            dot_cols(soft_probs.astype(jnp.bfloat16), d_dot_seg)
        )
        d_probs = dot_rows(d_dot_seg, value_seg)
        d_scores = (
            soft_probs * (d_probs - jnp.sum(soft_probs * d_probs, axis=1, keepdims=True))
        ).astype(jnp.bfloat16)
        d_query = d_query.at[begin_row:end_row].add(
            jnp.dot(d_scores, key_seg, preferred_element_type=jnp.float32) * score_scale
        )
        d_key = d_key.at[begin_row:end_row].add(dot_cols(d_scores, query_seg) * score_scale)
        if segment > 0:
            posq_seg = pos_query[begin_row:end_row]
            posk_prev = pos_key[:begin_row]
            value_prev = value_all[:begin_row]
            mem_allowed = memory_mask(begin_row, doc_ids, valid_keys)
            weights = jnp.where(mem_allowed, dot_rows(posq_seg, posk_prev), 0.0)
            row_total = jnp.sum(weights, axis=1, keepdims=True)
            denominator = jnp.maximum(row_total, 1.0)
            weights_low = weights.astype(jnp.bfloat16)
            numerator = jnp.dot(weights_low, value_prev, preferred_element_type=jnp.float32)
            d_recall_seg = d_recalled[begin_row:end_row]
            d_numer = (d_recall_seg / denominator).astype(jnp.bfloat16)
            d_denom = jnp.where(
                row_total > 1.0,
                -jnp.sum(d_recall_seg * numerator, axis=1, keepdims=True)
                / (denominator * denominator),
                0.0,
            )
            d_weights = jnp.where(mem_allowed, dot_rows(d_numer, value_prev) + d_denom, 0.0).astype(
                jnp.bfloat16
            )
            d_posq = d_posq.at[begin_row:end_row].add(
                jnp.dot(d_weights, posk_prev, preferred_element_type=jnp.float32)
            )
            d_posk = d_posk.at[:begin_row].add(dot_cols(d_weights, posq_seg))
            d_value = d_value.at[:begin_row].add(dot_cols(weights_low, d_numer))
    d_query = d_query + d_posq * jnp.where(query_float > 0, 1.0, jnp.exp(query_float))
    d_key = d_key + d_posk * jnp.where(key_float > 0, 1.0, jnp.exp(key_float))
    return (
        d_query.astype(jnp.bfloat16),
        d_key.astype(jnp.bfloat16),
        d_value.astype(jnp.bfloat16),
        d_share,
    )


def per_device(
    tokens,
    cotangent,
    doc_lengths,
    pad_mask,
    w_query,
    w_key,
    w_value,
    w_out,
    w_gate,
    w_up,
    w_down,
    norm_attn,
    norm_mlp,
    mix_gate,
):
    local_width = w_query.shape[1]
    hidden_cols = w_gate.shape[1]
    w_qkv = jnp.concatenate([w_query, w_key, w_value], axis=1)
    w_gate_up = jnp.concatenate([w_gate, w_up], axis=1)
    shares = jax.nn.sigmoid(mix_gate)
    positions = jnp.arange(LEN, dtype=jnp.int32)
    grad_qkv = jnp.zeros(w_qkv.shape, jnp.float32)
    grad_out = jnp.zeros(w_out.shape, jnp.float32)
    grad_gate_up = jnp.zeros(w_gate_up.shape, jnp.float32)
    grad_down = jnp.zeros(w_down.shape, jnp.float32)
    grad_mix = jnp.zeros(mix_gate.shape, jnp.float32)
    grad_gain_attn = jnp.zeros(norm_attn.shape, jnp.float32)
    grad_gain_mlp = jnp.zeros(norm_mlp.shape, jnp.float32)
    out_list, grad_in_list = ([], [])
    for micro_step in range(MICRO):
        doc_ends = jnp.cumsum(doc_lengths[micro_step, 0])
        doc_ids = jnp.sum((positions[:, None] >= doc_ends[None, :]).astype(jnp.int32), axis=1)
        valid_keys = pad_mask[micro_step, 0] == 1
        x_rows = tokens[micro_step, 0].astype(jnp.float32)
        normed_attn, scale_attn = norm_rows(x_rows, norm_attn)
        low_attn = normed_attn.astype(jnp.bfloat16)
        full_attn = lax.all_gather(low_attn, "heads", axis=0, tiled=True)
        qkv_all = jnp.dot(full_attn, w_qkv, preferred_element_type=jnp.float32).astype(jnp.bfloat16)
        head_inputs, head_kept, mixed_parts = ([], [], [])
        head_index = 0
        col_begin = head_index * DH
        query_all = qkv_all[:, col_begin : col_begin + DH]
        key_all = qkv_all[:, local_width + col_begin : local_width + col_begin + DH]
        value_all = qkv_all[:, 2 * local_width + col_begin : 2 * local_width + col_begin + DH]
        result_head = head_forward(
            query_all, key_all, value_all, shares[head_index], positions, doc_ids, valid_keys
        )
        head_inputs.append((query_all, key_all, value_all))
        head_kept.append(result_head)
        mixed_parts.append(result_head[0])
        mixed_low = mixed_parts[0].astype(jnp.bfloat16)
        attn_rows = lax.psum_scatter(
            jnp.dot(mixed_low, w_out, preferred_element_type=jnp.float32),
            "heads",
            scatter_dimension=0,
            tiled=True,
        )
        mid_rows = x_rows + attn_rows
        normed_mlp, scale_mlp = norm_rows(mid_rows, norm_mlp)
        low_mlp = normed_mlp.astype(jnp.bfloat16)
        full_mlp = lax.all_gather(low_mlp, "heads", axis=0, tiled=True)
        gate_up = jnp.dot(full_mlp, w_gate_up, preferred_element_type=jnp.float32)
        gate_pre = gate_up[:, :hidden_cols]
        up_pre = gate_up[:, hidden_cols:]
        sig_gate = jax.nn.sigmoid(gate_pre)
        hidden = (gate_pre * sig_gate * up_pre).astype(jnp.bfloat16)
        mlp_rows = lax.psum_scatter(
            jnp.dot(hidden, w_down, preferred_element_type=jnp.float32).astype(jnp.bfloat16),
            "heads",
            scatter_dimension=0,
            tiled=True,
        ).astype(jnp.float32)
        out_list.append((mid_rows + mlp_rows).astype(jnp.bfloat16))
        cot_low = cotangent[micro_step, 0]
        cot_full = lax.all_gather(cot_low, "heads", axis=0, tiled=True)
        grad_down = grad_down + dot_cols(hidden, cot_full)
        d_hidden = dot_rows(cot_full, w_down)
        d_up = d_hidden * gate_pre * sig_gate
        d_gate = d_hidden * up_pre * sig_gate * (1.0 + gate_pre * (1.0 - sig_gate))
        d_gate_up = jnp.concatenate([d_gate, d_up], axis=1).astype(jnp.bfloat16)
        grad_gate_up = grad_gate_up + dot_cols(full_mlp, d_gate_up)
        d_norm_mlp = lax.psum_scatter(
            dot_rows(d_gate_up, w_gate_up), "heads", scatter_dimension=0, tiled=True
        )
        d_mid_norm, gain_mlp_part = norm_back(mid_rows, scale_mlp, norm_mlp, d_norm_mlp)
        grad_gain_mlp = grad_gain_mlp + gain_mlp_part
        d_mid = d_mid_norm + cot_low.astype(jnp.float32)
        d_attn_full = lax.all_gather(d_mid.astype(jnp.bfloat16), "heads", axis=0, tiled=True)
        grad_out = grad_out + dot_cols(mixed_low, d_attn_full)
        d_mixed_all = dot_rows(d_attn_full, w_out)
        dq_parts, dk_parts, dv_parts, dshare_parts = ([], [], [], [])
        head_index = 0
        col_begin = head_index * DH
        query_all, key_all, value_all = head_inputs[head_index]
        kept_head = head_kept[head_index]
        back_head = head_backward(
            query_all,
            key_all,
            value_all,
            shares[head_index],
            positions,
            doc_ids,
            valid_keys,
            d_mixed_all,
            kept_head[1],
            kept_head[2],
            kept_head[3],
        )
        dq_parts.append(back_head[0])
        dk_parts.append(back_head[1])
        dv_parts.append(back_head[2])
        dshare_parts.append(back_head[3])
        grad_mix = grad_mix + jnp.stack(dshare_parts)
        d_qkv = jnp.concatenate(dq_parts + dk_parts + dv_parts, axis=1)
        grad_qkv = grad_qkv + dot_cols(full_attn, d_qkv)
        d_norm_attn = lax.psum_scatter(
            dot_rows(d_qkv, w_qkv).astype(jnp.bfloat16), "heads", scatter_dimension=0, tiled=True
        ).astype(jnp.float32)
        d_x_norm, gain_attn_part = norm_back(x_rows, scale_attn, norm_attn, d_norm_attn)
        grad_gain_attn = grad_gain_attn + gain_attn_part
        grad_in_list.append(d_x_norm + d_mid)
    grad_qkv, grad_out, grad_gate_up, grad_down, grad_mix = (
        lax.psum(grad_qkv.astype(jnp.bfloat16), "batch").astype(jnp.float32),
        lax.psum(grad_out.astype(jnp.bfloat16), "batch").astype(jnp.float32),
        lax.psum(grad_gate_up.astype(jnp.bfloat16), "batch").astype(jnp.float32),
        lax.psum(grad_down.astype(jnp.bfloat16), "batch").astype(jnp.float32),
        lax.psum(grad_mix.astype(jnp.bfloat16), "batch").astype(jnp.float32),
    )
    grad_gain_attn, grad_gain_mlp = lax.psum((grad_gain_attn, grad_gain_mlp), ("heads", "batch"))
    layer_out = jnp.stack(out_list)[:, None]
    grad_tokens = jnp.stack(grad_in_list)[:, None]
    return (
        layer_out,
        grad_tokens,
        grad_qkv[:, :local_width],
        grad_qkv[:, local_width : 2 * local_width],
        grad_qkv[:, 2 * local_width :],
        grad_out,
        grad_gate_up[:, :hidden_cols],
        grad_gate_up[:, hidden_cols:],
        grad_down,
        grad_gain_attn,
        grad_gain_mlp,
        grad_mix,
    )


def solution(mesh):
    in_specs = (
        P(None, "batch", "heads", None),
        P(None, "batch", "heads", None),
        P(None, "batch", None),
        P(None, "batch", None),
        P(None, "heads"),
        P(None, "heads"),
        P(None, "heads"),
        P("heads", None),
        P(None, "heads"),
        P(None, "heads"),
        P("heads", None),
        P(),
        P(),
        P("heads"),
    )
    out_specs = (
        P(None, "batch", "heads", None),
        P(None, "batch", "heads", None),
        P(None, "heads"),
        P(None, "heads"),
        P(None, "heads"),
        P("heads", None),
        P(None, "heads"),
        P(None, "heads"),
        P("heads", None),
        P(),
        P(),
        P("heads"),
    )
    return jax.shard_map(
        per_device, mesh=mesh, in_specs=in_specs, out_specs=out_specs, check_vma=False
    )
```

profile of v0, /device:TPU:0, one launch (start us, length us, event | category | flops | bytes accessed | tf_op | source)
XLA Modules:
  0.0 1430.8 jit_solution(2356076530199268857)
XLA Ops:
  7.3 1.6 fusion.42
  9.5 2.5 fusion.36
  16.6 35.0 %all-gather.15.cloned.1.call-done = bf16[1024,2048]{1,0:T(8,128)(2,1)} async-done(((bf16[128,2048]{1,0:T(8,128)(2,1)}), bf16[1024,2048]{1,0:T(8,128)(2,1)}) %all-gather.15.cloned.1.call-update) | async-done | bytes 4194320 | tf_op jit(solution)/shard_map/all_gather | solution.py:224
  51.6 4.5 convolution_convert_fusion.4
  63.0 4.7 fusion.168
  68.3 22.5 %all-gather.11.cloned.1.call-done = bf16[1024,2048]{1,0:T(8,128)(2,1)} async-done(((bf16[128,2048]{1,0:T(8,128)(2,1)}), bf16[1024,2048]{1,0:T(8,128)(2,1)}) %all-gather.11.cloned.1.call-update) | async-done | bytes 4194320 | tf_op jit(solution)/shard_map/all_gather | solution.py:224
  90.8 4.5 convolution_convert_fusion.5
  102.3 5.7 fusion.166
  108.1 58.1 %reduce-scatter.13.cloned.1.call-done = f32[128,2048]{1,0:T(8,128)} async-done(((f32[1024,2048]{1,0:T(8,128)}), f32[128,2048]{1,0:T(8,128)}) %reduce-scatter.13.cloned.1.call-update) | async-done | bytes 1048592 | tf_op jit(solution)/shard_map/reduce_scatter | solution.py:239
  166.2 75.6 %reduce-scatter.9.cloned.1.call-done = f32[128,2048]{1,0:T(8,128)} async-done(((f32[1024,2048]{1,0:T(8,128)}), f32[128,2048]{1,0:T(8,128)}) %reduce-scatter.9.cloned.1.call-update) | async-done | bytes 1048592 | tf_op jit(solution)/shard_map/reduce_scatter | solution.py:239
  241.8 2.8 multiply_reduce_fusion.9
  244.6 1.0 multiply_convert_fusion.11
  245.6 2.3 fusion.157
  248.0 4.8 constant_dynamic-update-slice_fusion.4
  252.8 2.5 constant_dynamic-update-slice_fusion.3
  255.3 27.2 %all-gather.13.cloned.1.call-done = bf16[1024,2048]{1,0:T(8,128)(2,1)} async-done(((bf16[128,2048]{1,0:T(8,128)(2,1)}), bf16[1024,2048]{1,0:T(8,128)(2,1)}) %all-gather.13.cloned.1.call-update) | async-done | bytes 4194320 | tf_op jit(solution)/shard_map/all_gather | solution.py:248
  282.4 14.9 %fusion.167 = f32[1024,2048]{1,0:T(8,128)} fusion(bf16[1024,2048]{1,0:T(8,128)(2,1)} %all-gather.13.cloned.1.call-done, bf16[2048,2048]{1,0:T(8,128)(2,1)} %constant_dynamic-update-slice_fusion.3), kind=kOutput, calls=%fused_computation.320 | convolution fusion | flops 8589934592 | bytes 20971520 | tf_op jit(solution)/shard_map/dot_general | solution.py:249
  297.3 24.2 %all-gather.23.cloned.1.call-done = bf16[1,1,1024,2048]{3,2,1,0:T(8,128)(2,1)} async-done(((bf16[1,1,128,2048]{3,2,1,0:T(8,128)(2,1)}), bf16[1,1,1024,2048]{3,2,1,0:T(8,128)(2,1)}) %all-gather.23.cloned.1.call-update) | async-done | bytes 4194320 | tf_op jit(solution)/shard_map/all_gather | solution.py:262
  321.5 13.2 multiply_convert_fusion.3
  334.7 1.3 copy-done.108
  336.7 13.3 fusion.12
  350.1 71.3 %reduce-scatter.17.cloned.1.call-done = f32[128,2048]{1,0:T(8,128)} async-done(((f32[1024,2048]{1,0:T(8,128)}), f32[128,2048]{1,0:T(8,128)}) %reduce-scatter.17.cloned.1.call-update) | async-done | bytes 1048592 | tf_op jit(solution)/shard_map/reduce_scatter | solution.py:269
  421.5 3.0 multiply_reduce_fusion.1
  425.2 36.1 %all-gather.17.cloned.1.call-done = bf16[1024,2048]{1,0:T(8,128)(2,1)} async-done(((bf16[128,2048]{1,0:T(8,128)(2,1)}), bf16[1024,2048]{1,0:T(8,128)(2,1)}) %all-gather.17.cloned.1.call-update) | async-done | bytes 4194320 | tf_op jit(solution)/shard_map/all_gather | solution.py:248
  461.3 14.6 %fusion.169 = f32[1024,2048]{1,0:T(8,128)} fusion(bf16[1024,2048]{1,0:T(8,128)(2,1)} %all-gather.17.cloned.1.call-done, bf16[2048,2048]{1,0:T(8,128)(2,1)} %constant_dynamic-update-slice_fusion.3), kind=kOutput, calls=%fused_computation.322 | convolution fusion | flops 8589934592 | bytes 20971520 | tf_op jit(solution)/shard_map/dot_general | solution.py:249
  475.9 24.7 %all-gather.25.cloned.1.call-done = bf16[1,1,1024,2048]{3,2,1,0:T(8,128)(2,1)} async-done(((bf16[1,1,128,2048]{3,2,1,0:T(8,128)(2,1)}), bf16[1,1,1024,2048]{3,2,1,0:T(8,128)(2,1)}) %all-gather.25.cloned.1.call-update) | async-done | bytes 4194320 | tf_op jit(solution)/shard_map/all_gather | solution.py:262
  500.7 13.2 multiply_convert_fusion.1
  513.9 1.4 copy-done.111
  516.0 13.3 fusion.10
  529.8 9.7 convolution_convert_fusion.3
  539.6 10.4 convolution_convert_fusion.2
  550.1 50.7 %reduce-scatter.21.cloned.1.call-done = f32[128,2048]{1,0:T(8,128)} async-done(((f32[1024,2048]{1,0:T(8,128)}), f32[128,2048]{1,0:T(8,128)}) %reduce-scatter.21.cloned.1.call-update) | async-done | bytes 1048592 | tf_op jit(solution)/shard_map/reduce_scatter | solution.py:269
  600.8 1.5 multiply_reduce_fusion
  602.3 53.8 %reduce-scatter.11.cloned.1.call-done = bf16[128,2048]{1,0:T(8,128)(2,1)} async-done(((bf16[1024,2048]{1,0:T(8,128)(2,1)}), bf16[128,2048]{1,0:T(8,128)(2,1)}) %reduce-scatter.11.cloned.1.call-update) | async-done | bytes 524304 | tf_op jit(solution)/shard_map/reduce_scatter | solution.py:254
  656.1 55.5 %reduce-scatter.15.cloned.1.call-done = bf16[128,2048]{1,0:T(8,128)(2,1)} async-done(((bf16[1024,2048]{1,0:T(8,128)(2,1)}), bf16[128,2048]{1,0:T(8,128)(2,1)}) %reduce-scatter.15.cloned.1.call-update) | async-done | bytes 524304 | tf_op jit(solution)/shard_map/reduce_scatter | solution.py:254
  711.5 4.5 fusion.153
  716.8 36.1 %all-gather.21.cloned.1.call-done = bf16[1024,2048]{1,0:T(8,128)(2,1)} async-done(((bf16[128,2048]{1,0:T(8,128)(2,1)}), bf16[1024,2048]{1,0:T(8,128)(2,1)}) %all-gather.21.cloned.1.call-update) | async-done | bytes 4194320 | tf_op jit(solution)/shard_map/all_gather | solution.py:275
  753.0 4.6 fusion.65
  763.2 5.9 convolution_convert_fusion
  769.4 1.3 copy-done.109
  770.8 14.8 %fusion.11 = f32[2048,2048]{1,0:T(8,128)} fusion(bf16[1024,2048]{1,0:T(8,128)(2,1)} %all-gather.13.cloned.1.call-done, bf16[1024,1024]{1,0:T(8,128)(2,1)} %copy-done.110, bf16[1024,1024]{1,0:T(8,128)(2,1)S(1)} %copy-done.109), kind=kOutput, calls=%fused_computation.26 | convolution fusion | flops 8598323200 | bytes 25165824 | tf_op jit(solution)/shard_map/dot_general | solution.py:24
  785.6 6.4 all-gather.19.cloned.1.call-done
  792.0 4.6 fusion.61
  802.3 6.0 convolution_convert_fusion.1
  808.7 7.3 fusion
  816.0 6.2 add_convert_fusion.1
  822.2 16.9 %add_convert_fusion = bf16[2048,2048]{1,0:T(8,128)(2,1)} fusion(f32[2048,2048]{1,0:T(8,128)} %fusion.11, bf16[1024,2048]{1,0:T(8,128)(2,1)} %all-gather.17.cloned.1.call-done, bf16[1024,1024]{1,0:T(8,128)(2,1)} %copy-done.112, bf16[1024,1024]{1,0:T(8,128)(2,1)} %copy-done.111), kind=kOutput, calls=%fused_computation | convolution fusion | flops 8606711808 | bytes 33554432 | tf_op jit(solution)/shard_map/dot_general | solution.py:24
  839.9 1.4 copy-done.19
  841.3 1.5 fusion.13
  842.9 1.0 copy-done.101
  843.9 2.4 fusion.72
  846.3 3.6 add_convert_fusion.2
  851.0 2.1 maximum_bitcast_fusion.1
  854.4 12.8 psum.55
  867.9 34.8 %reduce-scatter.19.cloned.1.call-done = bf16[128,2048]{1,0:T(8,128)(2,1)} async-done(((bf16[1024,2048]{1,0:T(8,128)(2,1)}), bf16[128,2048]{1,0:T(8,128)(2,1)}) %reduce-scatter.19.cloned.1.call-update) | async-done | bytes 524304 | tf_op jit(solution)/shard_map/reduce_scatter | solution.py:303
  902.7 1.9 fusion.45
  904.6 45.3 %all-reduce.6 = (f32[2048]{0:T(1024)}, f32[2048]{0:T(1024)}) all-reduce(f32[2048]{0:T(1024)S(1)} %add.352, f32[2048]{0:T(1024)S(1)} %add.353), channel_id=1, replica_groups=mesh['heads'=8,'batch'=4] {'heads','batch'}, use_global_device_ids=true, to_apply=%region_42.43 | all-reduce | flops 4096 | bytes 32768 | tf_op jit(solution)/shard_map/psum | solution.py:316
  949.9 2.3 fusion.41
  952.2 1.5 maximum_bitcast_fusion
  953.6 449.8 %all-reduce.10.cloned.1.call-done = (bf16[2048,384]{1,0:T(8,128)(2,1)}, bf16[2048,2048]{1,0:T(8,128)(2,1)}, bf16[128,2048]{1,0:T(8,128)(2,1)}, bf16[1024,2048]{1,0:T(8,128)(2,1)}) async-done(((bf16[2048,384]{1,0:T(8,128)(2,1)}, bf16[2048,2048]{1,0:T(8,128)(2,1)}, bf16[128,2048]{1,0:T(8,128)(2,1)}, bf16[1024,2048]{1,0:T(8,128)(2,1)}), (bf16[2048,384]{1,0:T(8,128)(2,1)}, bf16[2048,2048]{1,0:T(8,128)(2,1)}, ...) | async-done | bytes 14680080 | tf_op jit(solution)/shard_map/psum | solution.py:310
  1403.4 11.9 fusion.155
  1415.3 4.4 convert_element_type.296
  1419.8 1.8 fusion.156
  1421.5 1.1 convert_element_type.292
  (351 shorter events, 35.2 us)
Async XLA Ops:
  7.2 55.9 %copy-start = (bf16[128,2048]{1,0:T(8,128)(2,1)S(1)}, bf16[128,2048]{1,0:T(8,128)(2,1)}, u32[]{:S(2)}) copy-start(bf16[128,2048]{1,0:T(8,128)(2,1)} %param.57) | copy-start | bytes 1572868
  7.2 6.4 copy-start.95
  7.2 6.6 copy-start.78
  7.2 6.7 copy-start.40
  7.2 7.6 copy-start.41
  7.2 8.5 copy-start.42
  7.2 44.3 %all-gather.15.cloned.1.call-start = ((), (), s32[]{:S(2)}) async-start(), calls=%async_computation.12 | async-start | bytes 4718592 | tf_op jit(solution)/shard_map/all_gather | solution.py:224
  12.0 78.8 %all-gather.11.cloned.1.call-start = ((), (), s32[]{:S(2)}) async-start(), calls=%async_computation.8 | async-start | bytes 4718592 | tf_op jit(solution)/shard_map/all_gather | solution.py:224
  12.8 153.4 %reduce-scatter.13.cloned.1.call-start = ((), (), s32[]{:S(2)}) async-start(), calls=%async_computation.13 | async-start | bytes 9437184 | tf_op jit(solution)/shard_map/reduce_scatter | solution.py:239
  13.8 44.4 %copy-start.98 = (pred[512]{0:T(512)(128)(4,1)}, pred[512]{0:T(512)(128)(4,1)S(1)}, u32[]{:S(2)}) copy-start(pred[512]{0:T(512)(128)(4,1)S(1)} %get-tuple-element.267) | copy-start | bytes 1540
  14.0 44.3 %copy-start.91 = (s32[512]{0:T(512)}, s32[512]{0:T(512)S(1)}, u32[]{:S(2)}) copy-start(s32[512]{0:T(512)S(1)} %get-tuple-element.330) | copy-start | bytes 6148
  14.0 44.3 %copy-start.93 = (s32[512]{0:T(512)}, s32[512]{0:T(512)S(1)}, u32[]{:S(2)}) copy-start(s32[512]{0:T(512)S(1)} %get-tuple-element.331) | copy-start | bytes 6148
  67.7 174.1 %reduce-scatter.9.cloned.1.call-start = ((), (), s32[]{:S(2)}) async-start(), calls=%async_computation.9 | async-start | bytes 9437184 | tf_op jit(solution)/shard_map/reduce_scatter | solution.py:239
  68.2 29.3 %copy-start.96 = (pred[512]{0:T(512)(128)(4,1)}, pred[512]{0:T(512)(128)(4,1)S(1)}, u32[]{:S(2)}) copy-start(pred[512]{0:T(512)(128)(4,1)S(1)} %get-tuple-element.265) | copy-start | bytes 1540
  68.3 29.2 %copy-start.87 = (s32[512]{0:T(512)}, s32[512]{0:T(512)S(1)}, u32[]{:S(2)}) copy-start(s32[512]{0:T(512)S(1)} %get-tuple-element.328) | copy-start | bytes 6148
  68.3 29.2 %copy-start.89 = (s32[512]{0:T(512)}, s32[512]{0:T(512)S(1)}, u32[]{:S(2)}) copy-start(s32[512]{0:T(512)S(1)} %get-tuple-element.329) | copy-start | bytes 6148
  108.0 133.8 %copy-start.9 = (bf16[2,1,128,2048]{3,2,1,0:T(8,128)(2,1)S(1)}, bf16[2,1,128,2048]{3,2,1,0:T(8,128)(2,1)}, u32[]{:S(2)}) copy-start(bf16[2,1,128,2048]{3,2,1,0:T(8,128)(2,1)} %param.50) | copy-start | bytes 3145732
  108.0 136.6 %copy-start.63 = (f32[2048]{0:T(1024)S(1)}, f32[2048]{0:T(1024)}, u32[]{:S(2)}) copy-start(f32[2048]{0:T(1024)} %param.62) | copy-start | bytes 24580
  108.0 174.4 %all-gather.13.cloned.1.call-start = ((), (), s32[]{:S(2)}) async-start(), calls=%async_computation.10 | async-start | bytes 4718592 | tf_op jit(solution)/shard_map/all_gather | solution.py:248
  245.6 75.9 %all-gather.23.cloned.1.call-start = ((), (), s32[]{:S(2)}) async-start(), calls=%async_computation.22 | async-start | bytes 4718592 | tf_op jit(solution)/shard_map/all_gather | solution.py:262
  247.9 173.5 %reduce-scatter.17.cloned.1.call-start = ((), (), s32[]{:S(2)}) async-start(), calls=%async_computation.16 | async-start | bytes 9437184 | tf_op jit(solution)/shard_map/reduce_scatter | solution.py:269
  350.0 71.4 %copy-start.11 = (f32[128,2048]{1,0:T(8,128)S(1)}, f32[128,2048]{1,0:T(8,128)}, u32[]{:S(2)}) copy-start(f32[128,2048]{1,0:T(8,128)} %get-tuple-element.304) | copy-start | bytes 3145732
  350.0 111.3 %all-gather.17.cloned.1.call-start = ((), (), s32[]{:S(2)}) async-start(), calls=%async_computation.14 | async-start | bytes 4718592 | tf_op jit(solution)/shard_map/all_gather | solution.py:248
  424.5 76.2 %all-gather.25.cloned.1.call-start = ((), (), s32[]{:S(2)}) async-start(), calls=%async_computation.23 | async-start | bytes 4718592 | tf_op jit(solution)/shard_map/all_gather | solution.py:262
  425.2 175.6 %reduce-scatter.21.cloned.1.call-start = ((), (), s32[]{:S(2)}) async-start(), calls=%async_computation.19 | async-start | bytes 9437184 | tf_op jit(solution)/shard_map/reduce_scatter | solution.py:269
  529.3 126.7 %reduce-scatter.11.cloned.1.call-start = ((), (), s32[]{:S(2)}) async-start(), calls=%async_computation.11 | async-start | bytes 4718592 | tf_op jit(solution)/shard_map/reduce_scatter | solution.py:254
  539.5 172.0 %reduce-scatter.15.cloned.1.call-start = ((), (), s32[]{:S(2)}) async-start(), calls=%async_computation.15 | async-start | bytes 4718592 | tf_op jit(solution)/shard_map/reduce_scatter | solution.py:254
  550.0 202.9 %all-gather.21.cloned.1.call-start = ((), (), s32[]{:S(2)}) async-start(), calls=%async_computation.20 | async-start | bytes 4718592 | tf_op jit(solution)/shard_map/all_gather | solution.py:275
  716.1 41.5 %copy-start.6 = (f32[512,512]{0,1:T(8,128)S(1)}, f32[512,512]{0,1:T(8,128)}, u32[]{:S(2)}) copy-start(f32[512,512]{0,1:T(8,128)} %copy-done.5) | copy-start | bytes 3145732
  716.1 41.4 %copy-start.70 = (f32[512]{0:T(512)S(1)}, f32[512]{0:T(512)}, u32[]{:S(2)}) copy-start(f32[512]{0:T(512)} %copy-done.69) | copy-start | bytes 6148
  716.1 75.9 %all-gather.19.cloned.1.call-start = ((), (), s32[]{:S(2)}) async-start(), calls=%async_computation.17 | async-start | bytes 4718592 | tf_op jit(solution)/shard_map/all_gather | solution.py:275
  716.7 41.2 %copy-start.8 = (f32[512,512]{0,1:T(8,128)S(1)}, f32[512,512]{0,1:T(8,128)}, u32[]{:S(2)}) copy-start(f32[512,512]{0,1:T(8,128)} %copy-done.7) | copy-start | bytes 3145732
  716.7 41.2 %copy-start.72 = (f32[512]{0:T(512)S(1)}, f32[512]{0:T(512)}, u32[]{:S(2)}) copy-start(f32[512]{0:T(512)} %copy-done.71) | copy-start | bytes 6148
  716.7 41.6 %copy-start.77 = (f32[512]{0:T(512)S(1)}, f32[512]{0:T(512)}, u32[]{:S(2)}) copy-start(f32[512]{0:T(512)} %copy-done.76) | copy-start | bytes 6148
  716.7 41.6 %copy-start.15 = (bf16[1024,384]{0,1:T(8,128)(2,1)S(1)}, bf16[1024,384]{0,1:T(8,128)(2,1)}, u32[]{:S(2)}) copy-start(bf16[1024,384]{0,1:T(8,128)(2,1)} %copy-done.14) | copy-start | bytes 2359300
  716.7 41.6 %copy-start.86 = (f32[512]{0:T(512)S(1)}, f32[512]{0:T(512)}, u32[]{:S(2)}) copy-start(f32[512]{0:T(512)} %copy-done.85) | copy-start | bytes 6148
  716.8 41.6 %copy-start.92 = (s32[512]{0:T(512)S(1)}, s32[512]{0:T(512)}, u32[]{:S(2)}) copy-start(s32[512]{0:T(512)} %copy-done.91) | copy-start | bytes 6148
  716.8 41.6 %copy-start.94 = (s32[512]{0:T(512)S(1)}, s32[512]{0:T(512)}, u32[]{:S(2)}) copy-start(s32[512]{0:T(512)} %copy-done.93) | copy-start | bytes 6148
  716.8 41.6 %copy-start.99 = (pred[512]{0:T(512)(128)(4,1)S(1)}, pred[512]{0:T(512)(128)(4,1)}, u32[]{:S(2)}) copy-start(pred[512]{0:T(512)(128)(4,1)} %copy-done.98) | copy-start | bytes 1540
  716.8 151.1 %reduce-scatter.23.cloned.1.call-start = ((), (), s32[]{:S(2)}) async-start(), calls=%async_computation.21 | async-start | bytes 4718592 | tf_op jit(solution)/shard_map/reduce_scatter | solution.py:303
  753.0 5.3 copy-start.54
  769.2 133.5 %reduce-scatter.19.cloned.1.call-start = ((), (), s32[]{:S(2)}) async-start(), calls=%async_computation.18 | async-start | bytes 4718592 | tf_op jit(solution)/shard_map/reduce_scatter | solution.py:303
  785.6 11.1 copy-start.2
  785.6 11.1 copy-start.66
  785.6 11.4 copy-start.4
  785.6 11.4 copy-start.68
  785.6 11.9 copy-start.75
  785.6 11.9 copy-start.13
  785.6 11.9 copy-start.84
  785.6 11.9 copy-start.88
  785.6 11.9 copy-start.90
  785.6 11.9 copy-start.97
  792.0 5.3 copy-start.53
  808.4 595.0 %all-reduce.10.cloned.1.call-start = ((), (), s32[]{:S(2)}) async-start(), calls=%async_computation.24 | async-start | bytes 29360128 | tf_op jit(solution)/shard_map/psum | solution.py:310
  808.6 7.4 copy-start.102
  808.6 7.4 copy-start.107
  822.2 16.9 %copy-start.20 = (bf16[1024,2048]{1,0:T(8,128)(2,1)S(1)}, bf16[1024,2048]{1,0:T(8,128)(2,1)}, u32[]{:S(2)}) copy-start(bf16[1024,2048]{1,0:T(8,128)(2,1)} %all-gather.19.cloned.1.call-done) | copy-start | bytes 12582916
  822.2 16.9 %copy-start.25 = (bf16[1024,128]{0,1:T(8,128)(2,1)S(1)}, bf16[1024,128]{0,1:T(8,128)(2,1)}, u32[]{:S(2)}) copy-start(bf16[1024,128]{0,1:T(8,128)(2,1)} %copy-done.24) | copy-start | bytes 786436
  850.0 52.8 %copy-start.10 = (bf16[2,1,128,2048]{3,2,1,0:T(8,128)(2,1)S(1)}, bf16[2,1,128,2048]{3,2,1,0:T(8,128)(2,1)}, u32[]{:S(2)}) copy-start(bf16[2,1,128,2048]{3,2,1,0:T(8,128)(2,1)} %param.50) | copy-start | bytes 3145732
  850.0 52.8 %copy-start.64 = (f32[2048]{0:T(1024)S(1)}, f32[2048]{0:T(1024)}, u32[]{:S(2)}) copy-start(f32[2048]{0:T(1024)} %param.61) | copy-start | bytes 24580
  850.0 52.8 %copy-start.80 = (f32[128]{0:T(128)S(1)}, f32[128]{0:T(128)}, u32[]{:S(2)}) copy-start(f32[128]{0:T(128)} %copy-done.79) | copy-start | bytes 1540
  850.0 52.7 %copy-start.82 = (f32[128]{0:T(128)S(1)}, f32[128]{0:T(128)}, u32[]{:S(2)}) copy-start(f32[128]{0:T(128)} %copy-done.81) | copy-start | bytes 1540
  850.0 99.9 %copy-start.21 = (f32[128,2048]{1,0:T(8,128)S(1)}, f32[128,2048]{1,0:T(8,128)}, u32[]{:S(2)}) copy-start(f32[128,2048]{1,0:T(8,128)} %get-tuple-element.275) | copy-start | bytes 3145732
  1403.4 11.9 copy-start.17
  (66 other events, 139.6 us)
Sparse Core Ops, SparseCore 0:
  12.1 39.4 all-gather.14
  54.1 36.7 all-gather.10
  94.8 71.3 reduce-scatter.12
  170.5 71.2 reduce-scatter.8
  245.7 36.6 all-gather.12
  284.8 36.7 all-gather.22
  350.2 71.2 reduce-scatter.16
  424.6 36.6 all-gather.16
  463.9 36.7 all-gather.24
  529.4 71.2 reduce-scatter.20
  604.7 51.3 reduce-scatter.10
  660.2 51.2 reduce-scatter.14
  716.2 36.6 all-gather.20
  755.3 36.7 all-gather.18
  795.8 51.3 reduce-scatter.22
  851.3 51.3 reduce-scatter.18
  906.6 496.7 all-reduce.9
where the time goes:
time: 1440 us; the launch traced here: 1430 us
  waiting for transfers between devices  1060 us (74%)
  matrix products  211 us (15%)
  blocking collectives  58.1 us (4%)
  local copies, waits for them, and re-layouts  42.1 us (3%)
  other arithmetic  34.4 us (2%)
  between operations  19.9 us (1%)
    psum x1, waiting for transfers between devices, per_device(): lax.psum(grad_qkv.astype(jnp.bfloat16), 'batch').astype(jnp.float32)  450 us
    reduce_scatter x2, waiting for transfers between devices, per_device(): lax.psum_scatter(jnp.dot(mixed_low, w_out, preferred_element_type=jnp.flo...  134 us
    reduce_scatter x2, waiting for transfers between devices, per_device(): lax.psum_scatter(dot_rows(d_gate_up, w_gate_up), 'heads', scatter_dimensi...  122 us
    reduce_scatter x2, waiting for transfers between devices, per_device(): lax.psum_scatter(jnp.dot(hidden, w_down, preferred_element_type=jnp.float...  109 us
    dot_general x20, matrix products, dot_rows(): lax.dot_general(left_mat, right_mat, (((1,), (1,)), ((), ())), preferred_...  79.7 us
    all_gather x2, waiting for transfers between devices, per_device(): full_mlp = lax.all_gather(low_mlp, 'heads', axis=0, tiled=True)  63.2 us
    all_gather x2, waiting for transfers between devices, per_device(): full_attn = lax.all_gather(low_attn, 'heads', axis=0, tiled=True)  57.5 us
    dot_general x20, matrix products, dot_cols(): lax.dot_general(left_mat, right_mat, (((0,), (0,)), ((), ())), preferred_...  57.2 us
  transfers between devices with their start and end apart: 17, of which 16 were waited for; matrix products, arithmetic and copies ran while one was open for 13% of the time, Pallas kernels for 0%

commit v1 on v0

v1 whole, which is shorter than its diff:
```python
import jax
import jax.numpy as jnp
from jax import lax
from jax.sharding import PartitionSpec as P

DH = 128
SEG = 512
SEGS = 2
LEN = 1024
MICRO = 2


epsilon = 1e-05
big_negative = -1e30


def dot_rows(left_mat, right_mat):
    return lax.dot_general(
        left_mat, right_mat, (((1,), (1,)), ((), ())), preferred_element_type=jnp.float32
    )


def dot_cols(left_mat, right_mat):
    return lax.dot_general(
        left_mat, right_mat, (((0,), (0,)), ((), ())), preferred_element_type=jnp.float32
    )


def batch_mm(left, right):
    return lax.dot_general(
        left, right, (((2,), (1,)), ((0,), (0,))), preferred_element_type=jnp.float32
    )


def batch_mt(left, right):
    return lax.dot_general(
        left, right, (((2,), (2,)), ((0,), (0,))), preferred_element_type=jnp.float32
    )


def batch_tm(left, right):
    return lax.dot_general(
        left, right, (((1,), (1,)), ((0,), (0,))), preferred_element_type=jnp.float32
    )


def norm_scale(row_block):
    return lax.rsqrt(jnp.mean(row_block * row_block, axis=-1, keepdims=True) + epsilon)


def norm_back(row_block, row_scale, gain_vec, upstream):
    shaped = upstream * gain_vec
    inner = jnp.mean(shaped * row_block, axis=-1, keepdims=True)
    d_rows = row_scale * shaped - row_block * row_scale * row_scale * row_scale * inner
    d_gain = jnp.sum(upstream * row_block * row_scale, axis=0)
    return (d_rows, d_gain)


def positive(values_in):
    return jnp.where(values_in > 0, values_in + 1.0, jnp.exp(values_in))


def local_mask(begin_row, positions, doc_ids, valid_keys):
    seg_pos = positions[begin_row : begin_row + SEG]
    seg_doc = doc_ids[:, begin_row : begin_row + SEG]
    seg_valid = valid_keys[:, begin_row : begin_row + SEG]
    same_doc = seg_doc[:, :, None] == seg_doc[:, None, :]
    causal = (seg_pos[None, :] <= seg_pos[:, None])[None]
    diagonal = (seg_pos[None, :] == seg_pos[:, None])[None]
    return same_doc & causal & (seg_valid[:, None, :] | diagonal)


def memory_mask(begin_row, doc_ids, valid_keys):
    seg_doc = doc_ids[:, begin_row : begin_row + SEG]
    return (seg_doc[:, :, None] == doc_ids[:, None, :begin_row]) & valid_keys[:, None, :begin_row]


def head_forward(query_all, key_all, value_all, share, positions, doc_ids, valid_keys):
    score_scale = DH ** (-0.5)
    pos_query = positive(query_all.astype(jnp.float32)).astype(jnp.bfloat16)
    pos_key = positive(key_all.astype(jnp.float32)).astype(jnp.bfloat16)
    kept = []
    dotted_parts, recalled_parts = ([], [])
    for segment in range(SEGS):
        rows = slice(segment * SEG, (segment + 1) * SEG)
        before = slice(0, segment * SEG)
        allowed = local_mask(segment * SEG, positions, doc_ids, valid_keys)
        scores = jnp.where(
            allowed, batch_mt(query_all[:, rows], key_all[:, rows]) * score_scale, big_negative
        )
        shifted = jnp.exp(scores - jnp.max(scores, axis=2, keepdims=True))
        soft_probs = shifted / jnp.sum(shifted, axis=2, keepdims=True)
        dotted_parts.append(batch_mm(soft_probs.astype(jnp.bfloat16), value_all[:, rows]))
        if segment == 0:
            recalled_parts.append(jnp.zeros((query_all.shape[0], SEG, DH), jnp.float32))
            kept.append((soft_probs,))
        else:
            mem_allowed = memory_mask(segment * SEG, doc_ids, valid_keys)
            weights = jnp.where(mem_allowed, batch_mt(pos_query[:, rows], pos_key[:, before]), 0.0)
            row_total = jnp.sum(weights, axis=2, keepdims=True)
            denominator = jnp.maximum(row_total, 1.0)
            weights_low = weights.astype(jnp.bfloat16)
            numerator = batch_mm(weights_low, value_all[:, before])
            recalled_parts.append(numerator / denominator)
            kept.append((soft_probs, mem_allowed, row_total, weights_low, numerator))
    dotted = jnp.concatenate(dotted_parts, axis=1)
    recalled = jnp.concatenate(recalled_parts, axis=1)
    mixed_head = share * recalled + (1.0 - share) * dotted
    return (mixed_head, dotted, recalled, pos_query, pos_key, kept)


def head_backward(query_all, key_all, value_all, share, d_mixed, forward_kept):
    _, dotted, recalled, pos_query, pos_key, kept = forward_kept
    score_scale = DH ** (-0.5)
    query_float = query_all.astype(jnp.float32)
    key_float = key_all.astype(jnp.float32)
    d_share = jnp.sum(d_mixed * (recalled - dotted)) * share * (1.0 - share)
    d_dotted = ((1.0 - share) * d_mixed).astype(jnp.bfloat16)
    d_recalled = share * d_mixed
    nothing = jnp.zeros((query_all.shape[0], SEG, DH), jnp.float32)
    d_query, d_key, d_value, d_posq, d_posk = [
        [nothing for _ in range(SEGS)] for _ in range(5)
    ]
    for segment in range(SEGS):
        rows = slice(segment * SEG, (segment + 1) * SEG)
        before = slice(0, segment * SEG)
        soft_probs = kept[segment][0]
        d_dot_seg = d_dotted[:, rows]
        d_value[segment] += batch_tm(soft_probs.astype(jnp.bfloat16), d_dot_seg)
        d_probs = batch_mt(d_dot_seg, value_all[:, rows])
        d_scores = (
            soft_probs * (d_probs - jnp.sum(soft_probs * d_probs, axis=2, keepdims=True))
        ).astype(jnp.bfloat16)
        d_query[segment] += batch_mm(d_scores, key_all[:, rows]) * score_scale
        d_key[segment] += batch_tm(d_scores, query_all[:, rows]) * score_scale
        if segment > 0:
            _, mem_allowed, row_total, weights_low, numerator = kept[segment]
            denominator = jnp.maximum(row_total, 1.0)
            d_recall_seg = d_recalled[:, rows]
            d_numer = (d_recall_seg / denominator).astype(jnp.bfloat16)
            d_denom = jnp.where(
                row_total > 1.0,
                -jnp.sum(d_recall_seg * numerator, axis=2, keepdims=True)
                / (denominator * denominator),
                0.0,
            )
            d_weights = jnp.where(
                mem_allowed, batch_mt(d_numer, value_all[:, before]) + d_denom, 0.0
            ).astype(jnp.bfloat16)
            d_posq[segment] += batch_mm(d_weights, pos_key[:, before])
            d_posk_all = batch_tm(d_weights, pos_query[:, rows])
            d_value_all = batch_tm(weights_low, d_numer)
            for earlier in range(segment):
                part = slice(earlier * SEG, (earlier + 1) * SEG)
                d_posk[earlier] += d_posk_all[:, part]
                d_value[earlier] += d_value_all[:, part]
    d_query, d_key, d_value, d_posq, d_posk = [
        jnp.concatenate(parts, axis=1) for parts in (d_query, d_key, d_value, d_posq, d_posk)
    ]
    d_query = d_query + d_posq * jnp.where(query_float > 0, 1.0, jnp.exp(query_float))
    d_key = d_key + d_posk * jnp.where(key_float > 0, 1.0, jnp.exp(key_float))
    return (
        d_query.astype(jnp.bfloat16),
        d_key.astype(jnp.bfloat16),
        d_value.astype(jnp.bfloat16),
        d_share,
    )


class Chain:
    def __init__(self, axis, size, depth):
        self.axis, self.size, self.depth = axis, size, depth
        self.place = lax.axis_index(axis)
        half = size // 2
        self.stages = [("in", [(s - 1, s), (size - s, size - 1 - s)]) for s in range(1, half)]
        self.stages.append(("in", [(half - 1, half), (half, half - 1)]))
        self.stages += [("out", [(s, s - 1), (size - 1 - s, size - s)]) for s in range(half - 1, 0, -1)]
        self.entered = []
        self.last = [None] * len(self.stages)

    def add(self, array):
        if self.size == 1:
            return array
        if self.size % 2:
            return lax.psum(array, self.axis)
        if len(self.entered) >= self.depth:
            array, _ = lax.optimization_barrier((array, self.entered[-self.depth]))
        for number, (kind, pairs) in enumerate(self.stages):
            arrived = lax.ppermute(array, self.axis, pairs)
            if self.last[number] is not None:
                array, arrived, _ = lax.optimization_barrier((array, arrived, self.last[number]))
            if kind == "in":
                array = array + arrived
            else:
                receives = jnp.zeros((), jnp.bool_)
                for _, target in pairs:
                    receives = receives | (self.place == target)
                array = jnp.where(receives, arrived, array)
            self.last[number] = array
            if number == 0:
                self.entered.append(array)
        return array


def per_device(
    tokens,
    cotangent,
    doc_lengths,
    pad_mask,
    w_query,
    w_key,
    w_value,
    w_out,
    w_gate,
    w_up,
    w_down,
    norm_attn,
    norm_mlp,
    mix_gate,
    *,
    n_heads,
    n_batch,
):
    width = tokens.shape[-1]
    rows = tokens.shape[2]
    own_rows = MICRO * rows
    all_rows = n_heads * own_rows
    hidden_cols = w_gate.shape[1]
    here = lax.axis_index("heads")
    low = jnp.bfloat16

    def by_sequence(array):
        cols = array.shape[-1]
        return array.reshape(n_heads, MICRO, rows, cols).transpose(1, 0, 2, 3).reshape(MICRO, LEN, cols)

    def by_device(array):
        cols = array.shape[-1]
        return (
            array.reshape(MICRO, n_heads, rows, cols).transpose(1, 0, 2, 3).reshape(all_rows, cols)
        )

    def gather(array):
        return lax.all_gather(array, "heads", axis=0, tiled=True)

    def scatter(array):
        return lax.psum_scatter(array, "heads", scatter_dimension=0, tiled=True)

    def own(array):
        return lax.dynamic_slice_in_dim(array, here * own_rows, own_rows, 0)

    w_qkv = jnp.concatenate([w_query, w_key, w_value], axis=1)
    w_gate_up = jnp.concatenate([w_gate, w_up], axis=1)
    share = jax.nn.sigmoid(mix_gate)[0]
    positions = jnp.arange(LEN, dtype=jnp.int32)
    doc_ends = jnp.cumsum(doc_lengths[:, 0], axis=1)
    doc_ids = jnp.sum((positions[None, :, None] >= doc_ends[:, None, :]).astype(jnp.int32), axis=2)
    valid_keys = pad_mask[:, 0] == 1

    tok_own = tokens.reshape(own_rows, width)
    cot_own = cotangent.reshape(own_rows, width)
    tok_all = gather(tok_own)
    w_out_all = gather(w_out)
    x_all = tok_all.astype(jnp.float32)
    h1_all = (x_all * norm_scale(x_all) * norm_attn).astype(low)
    qkv = jnp.dot(h1_all, w_qkv, preferred_element_type=jnp.float32).astype(low)
    query, key, value = [by_sequence(qkv[:, i * DH : (i + 1) * DH]) for i in range(3)]
    head_kept = head_forward(query, key, value, share, positions, doc_ids, valid_keys)
    mixed = by_device(head_kept[0].astype(low))
    mixed_all = lax.all_gather(mixed, "heads", axis=1, tiled=True)
    cot_all = gather(cot_own)

    y1_all = x_all + jnp.dot(mixed_all, w_out_all, preferred_element_type=jnp.float32)
    h2_all = (y1_all * norm_scale(y1_all) * norm_mlp).astype(low)
    x_own = tok_own.astype(jnp.float32)
    y1_own = own(y1_all)
    gate_up = jnp.dot(h2_all, w_gate_up, preferred_element_type=jnp.float32)
    gate_pre = gate_up[:, :hidden_cols]
    up_pre = gate_up[:, hidden_cols:]
    sig_gate = jax.nn.sigmoid(gate_pre)
    hidden = (gate_pre * sig_gate * up_pre).astype(low)
    d_hidden = dot_rows(cot_all, w_down)
    d_up = d_hidden * gate_pre * sig_gate
    d_gate = d_hidden * up_pre * sig_gate * (1.0 + gate_pre * (1.0 - sig_gate))
    d_gate_up = jnp.concatenate([d_gate, d_up], axis=1).astype(low)

    chain = Chain("batch", n_batch, 3)
    d_h2 = scatter(dot_rows(d_gate_up, w_gate_up).astype(low)).astype(jnp.float32)
    down_parts, gate_up_parts = ([], [])
    step = hidden_cols // 4
    for begin in range(0, hidden_cols, step):
        down_parts.append(chain.add(dot_cols(hidden[:, begin : begin + step], cot_all).astype(low)))
    step = width // 8
    for begin in range(0, width, step):
        gate_up_parts.append(
            chain.add(dot_cols(h2_all[:, begin : begin + step], d_gate_up).astype(low))
        )
    mlp_own = scatter(jnp.dot(hidden, w_down, preferred_element_type=jnp.float32).astype(low))
    layer_out = (y1_own + mlp_own.astype(jnp.float32)).astype(low)

    scale_mlp = norm_scale(y1_own)
    d_y1, gain_mlp_part = norm_back(y1_own, scale_mlp, norm_mlp, d_h2)
    d_y1 = d_y1 + cot_own.astype(jnp.float32)
    d_attn = d_y1.astype(low)
    d_mixed_own = dot_rows(d_attn, w_out_all).astype(low)
    d_mixed = lax.all_to_all(d_mixed_own, "heads", split_axis=1, concat_axis=0, tiled=True)
    grad_out = scatter(dot_cols(own(mixed_all), d_attn).astype(low))

    d_query, d_key, d_value, d_share = head_backward(
        query, key, value, share, by_sequence(d_mixed).astype(jnp.float32), head_kept
    )
    d_qkv = jnp.concatenate([by_device(d_query), by_device(d_key), by_device(d_value)], axis=1)
    d_h1 = scatter(dot_rows(d_qkv, w_qkv).astype(low)).astype(jnp.float32)
    grad_out = chain.add(grad_out)
    grad_qkv = chain.add(dot_cols(h1_all, d_qkv).astype(low))

    d_x, gain_attn_part = norm_back(x_own, norm_scale(x_own), norm_attn, d_h1)
    grad_tokens = (d_x + d_y1).reshape(tokens.shape)
    slots = jnp.where(jnp.arange(n_heads) == here, d_share, 0.0)
    sums = lax.psum(jnp.concatenate([gain_attn_part, gain_mlp_part, slots]), ("heads", "batch"))
    grad_mix = lax.dynamic_slice_in_dim(sums, 2 * width + here, 1, 0)

    wide = jnp.float32
    grad_qkv = grad_qkv.astype(wide)
    grad_gate_up = jnp.concatenate([p.astype(wide) for p in gate_up_parts], axis=0)
    grad_down = jnp.concatenate([p.astype(wide) for p in down_parts], axis=0)
    return (
        layer_out.reshape(tokens.shape),
        grad_tokens,
        grad_qkv[:, :DH],
        grad_qkv[:, DH : 2 * DH],
        grad_qkv[:, 2 * DH :],
        grad_out.astype(wide),
        grad_gate_up[:, :hidden_cols],
        grad_gate_up[:, hidden_cols:],
        grad_down,
        sums[:width],
        sums[width : 2 * width],
        grad_mix,
    )


def solution(mesh):
    in_specs = (
        P(None, "batch", "heads", None),
        P(None, "batch", "heads", None),
        P(None, "batch", None),
        P(None, "batch", None),
        P(None, "heads"),
        P(None, "heads"),
        P(None, "heads"),
        P("heads", None),
        P(None, "heads"),
        P(None, "heads"),
        P("heads", None),
        P(),
        P(),
        P("heads"),
    )
    out_specs = (
        P(None, "batch", "heads", None),
        P(None, "batch", "heads", None),
        P(None, "heads"),
        P(None, "heads"),
        P(None, "heads"),
        P("heads", None),
        P(None, "heads"),
        P(None, "heads"),
        P("heads", None),
        P(),
        P(),
        P("heads"),
    )

    def program(*arrays):
        return per_device(*arrays, n_heads=mesh.shape["heads"], n_batch=mesh.shape["batch"])

    return jax.shard_map(
        program, mesh=mesh, in_specs=in_specs, out_specs=out_specs, check_vma=False
    )
```

time: 1440 us -> 862 us (0.60)
  waiting for transfers between devices: 1060 us -> 344 us
  starting transfers between devices: 1.7 us -> 109 us
  other arithmetic: 34.4 us -> 95.5 us
  blocking collectives: 58.1 us -> 38 us
    psum x1 -> x0, waiting for transfers between devices: 450 us -> none  [per_device(): lax.psum(grad_qkv.astype(jnp.bfloat16), 'batch').astype(jnp.float32)]
    reduce_scatter x8 -> x4, waiting for transfers between devices: 400 us -> 56.8 us  [scatter(): return lax.psum_scatter(array, 'heads', scatter_dimension=0, tiled=True)]
    ppermute x0 -> x42, waiting for transfers between devices: none -> 181 us  [add(): arrived = lax.ppermute(array, self.axis, pairs)]
    all_gather x8 -> x4, waiting for transfers between devices: 212 us -> 104 us  [the longest x3 64.4 us: gather(): return lax.all_gather(array, 'heads', axis=0, tiled=True)]
    ppermute x0 -> x42, starting transfers between devices: none -> 104 us  [add(): arrived = lax.ppermute(array, self.axis, pairs)]
    add x6 -> x30, other arithmetic: 0.03 us -> 42.2 us  [the longest x28 34.3 us: add(): array = array + arrived]
    dot_general x20 -> x4, matrix products: 79.7 us -> 53.9 us  [dot_rows(): lax.dot_general(left_mat, right_mat, (((1,), (1,)), ((), ())), preferred_...]
    dot_general x20 -> x14, matrix products: 57.2 us -> 78 us  [dot_cols(): lax.dot_general(left_mat, right_mat, (((0,), (0,)), ((), ())), preferred_...]
  transfers between devices with their start and end apart: 17 -> 51, of which waited for: 16 -> 17; matrix products, arithmetic and copies ran while one was open for 13% -> 33% of each run, Pallas kernels for 0% -> 0%
where the time goes in v1:
time: 862 us; the launch traced here: 853 us
  waiting for transfers between devices  344 us (40%)
  matrix products  207 us (24%)
  starting transfers between devices  109 us (13%)
  other arithmetic  95.5 us (11%)
  local copies, waits for them, and re-layouts  41.3 us (5%)
  blocking collectives  38 us (4%)
  between operations  17.9 us (2%)
    ppermute x42, waiting for transfers between devices, add(): arrived = lax.ppermute(array, self.axis, pairs)  181 us
    ppermute x42, starting transfers between devices, add(): arrived = lax.ppermute(array, self.axis, pairs)  104 us
    dot_general x14, matrix products, dot_cols(): lax.dot_general(left_mat, right_mat, (((0,), (0,)), ((), ())), preferred_...  78 us
    all_gather x3, waiting for transfers between devices, gather(): return lax.all_gather(array, 'heads', axis=0, tiled=True)  64.4 us
    reduce_scatter x4, waiting for transfers between devices, scatter(): return lax.psum_scatter(array, 'heads', scatter_dimension=0, tiled=True)  56.8 us
    dot_general x4, matrix products, dot_rows(): lax.dot_general(left_mat, right_mat, (((1,), (1,)), ((), ())), preferred_...  53.9 us
    all_gather x1, waiting for transfers between devices, per_device(): mixed_all = lax.all_gather(mixed, 'heads', axis=1, tiled=True)  39.9 us
    psum x1, blocking collectives, per_device(): lax.psum(jnp.concatenate([gain_attn_part, gain_mlp_part, slots]), ('heads...  38 us
  transfers between devices with their start and end apart: 51, of which 17 were waited for; matrix products, arithmetic and copies ran while one was open for 33% of the time, Pallas kernels for 0%

profile of v1, /device:TPU:0, one launch (start us, length us, event | category | flops | bytes accessed | tf_op | source)
XLA Modules:
  0.0 852.8 jit_solution(9633711189530872917)
XLA Ops:
  16.1 50.9 %all-gather.5.cloned.1.call-done = bf16[2048,2048]{1,0:T(8,128)(2,1)} async-done(((bf16[256,2048]{1,0:T(8,128)(2,1)}), bf16[2048,2048]{1,0:T(8,128)(2,1)}) %all-gather.5.cloned.1.call-update) | async-done | bytes 8388624 | tf_op jit(solution)/shard_map/all_gather | solution.py:243
  67.0 5.2 fusion.2
  72.8 4.8 convolution_convert_fusion.5
  87.0 2.9 fusion.56
  92.9 4.8 constant_dynamic-update-slice_fusion.4
  100.2 5.5 all-gather.9.cloned.1.call-done
  105.7 39.9 %all-gather.7.cloned.1.call-done = bf16[2048,1024]{1,0:T(8,128)(2,1)} async-done(((bf16[2048,128]{1,0:T(8,128)(2,1)}), bf16[2048,1024]{1,0:T(8,128)(2,1)}) %all-gather.7.cloned.1.call-update) | async-done | bytes 4194320 | tf_op jit(solution)/shard_map/all_gather | solution.py:269
  145.6 13.5 %multiply_reduce_fusion = (f32[2048]{0:T(1024)S(1)}, f32[2048,2048]{1,0:T(8,128)S(1)}) fusion(bf16[2048,1024]{1,0:T(8,128)(2,1)} %all-gather.7.cloned.1.call-done, bf16[1024,2048]{1,0:T(8,128)(2,1)} %all-gather.9.cloned.1.call-done, bf16[2048,2048]{1,0:T(8,128)(2,1)} %all-gather.5.cloned.1.call-done), kind=kOutput, calls=%fused_computation.9 | convolution fusion | flops 8606709760 | bytes 33562624 | tf_op jit(solution)/shard_map/dot_general | solution.py:272
  159.1 5.8 copy-done
  164.9 4.4 multiply_convert_fusion
  169.3 24.3 %fusion.125 = f32[2048,2048]{0,1:T(8,128)} fusion(bf16[2048,2048]{1,0:T(8,128)(2,1)} %multiply_convert_fusion, bf16[2048,2048]{1,0:T(8,128)(2,1)} %constant_dynamic-update-slice_fusion.3), kind=kOutput, calls=%fused_computation.223 | convolution fusion | flops 17179869184 | bytes 33554432 | tf_op jit(solution)/shard_map/dot_general | solution.py:276
  193.7 8.1 all-gather.11.cloned.1.call-done
  201.8 22.9 %multiply_convert_fusion.2 = (bf16[2048,1024]{0,1:T(8,128)(2,1)S(1)}, bf16[2048,1024]{0,1:T(8,128)(2,1)}, bf16[2048,1024]{0,1:T(8,128)(2,1)}) fusion(f32[2048,2048]{0,1:T(8,128)} %fusion.125, bf16[2048,2048]{1,0:T(8,128)(2,1)} %all-gather.11.cloned.1.call-done, bf16[1024,2048]{1,0:T(8,128)(2,1)} %param.24), kind=kOutput, calls=%fused_computation.12 | convolution fusion | flops 8623489024 | bytes 41943040 | tf_op jit(solution)/shard_map/dot_general | solution.py:18
  226.7 22.9 %convolution_convert_fusion.1 = bf16[2048,2048]{1,0:T(8,128)(2,1)} fusion(bf16[2048,2048]{1,0:T(8,128)(2,1)} %constant_dynamic-update-slice_fusion.3, bf16[2048,1024]{0,1:T(8,128)(2,1)} %get-tuple-element.249, bf16[2048,1024]{0,1:T(8,128)(2,1)S(1)} %get-tuple-element.248), kind=kOutput, calls=%fused_computation.16 | convolution fusion | flops 17200840704 | bytes 25165824 | tf_op jit(solution)/shard_map/dot_general | solution.py:18
  249.6 14.7 %convolution_convert_fusion.2 = bf16[2048,2048]{1,0:T(8,128)(2,1)} fusion(bf16[2048,1024]{0,1:T(8,128)(2,1)} %get-tuple-element.252, bf16[1024,2048]{1,0:T(8,128)(2,1)} %param.24), kind=kOutput, calls=%fused_computation.17 | convolution fusion | flops 8594128896 | bytes 16777216 | tf_op jit(solution)/shard_map/dot_general | solution.py:297
  266.5 6.2 convolution_convert_fusion.13
  272.8 3.9 collective-permute-start.1
  276.7 6.4 convolution_convert_fusion.14
  285.5 3.4 convolution_convert_fusion.15
  288.9 3.4 convolution_convert_fusion.9
  292.3 5.7 convolution_convert_fusion.10
  298.1 7.1 convolution_convert_fusion.16
  305.2 4.8 convolution_convert_fusion.11
  310.0 7.2 convolution_convert_fusion.7
  321.3 4.5 convolution_convert_fusion.12
  331.0 3.5 collective-permute-start.3
  336.7 3.1 fusion.16
  339.8 56.7 %reduce-scatter.5.cloned.1.call-done = bf16[256,2048]{1,0:T(8,128)(2,1)} async-done(((bf16[2048,2048]{1,0:T(8,128)(2,1)}), bf16[256,2048]{1,0:T(8,128)(2,1)}) %reduce-scatter.5.cloned.1.call-update) | async-done | bytes 1048592 | tf_op jit(solution)/shard_map/reduce_scatter | solution.py:246
  396.6 4.6 fusion.13
  403.4 4.2 all-to-all-start
  407.6 7.1 convolution_convert_fusion.8
  414.7 3.0 add.211
  419.3 6.1 collective-permute-start.7
  429.8 2.9 add.224
  437.6 2.9 add.213
  440.5 4.3 convolution_convert_fusion.3
  460.3 6.8 convolution_convert_fusion
  468.0 6.3 convolution_convert_fusion.17
  480.8 11.6 %collective-permute-start.6 = (bf16[256,2048]{1,0:T(8,128)(2,1)S(1)}, bf16[256,2048]{1,0:T(8,128)(2,1)S(1)}, u32[]{:S(2)}, u32[]{:S(2)}) collective-permute-start(bf16[256,2048]{1,0:T(8,128)(2,1)S(1)} %copy-done.22), channel_id=1, source_target_pairs={{0,1},{3,2},{4,5},{7,6},{8,9},{11,10},{12,13},{15,14},{16,17},{19,... | collective-permute-start | bytes 3145736 | tf_op jit(solution)/shard_map/ppermute | solution.py:189
  493.8 5.0 convolution_convert_fusion.6
  498.8 3.8 collective-permute-start.10
  507.3 8.6 %collective-permute-done.6 = bf16[256,2048]{1,0:T(8,128)(2,1)S(1)} collective-permute-done((bf16[256,2048]{1,0:T(8,128)(2,1)S(1)}, bf16[256,2048]{1,0:T(8,128)(2,1)S(1)}, u32[]{:S(2)}, u32[]{:S(2)}) %collective-permute-start.6) | collective-permute-done | bytes 1048608 | tf_op jit(solution)/shard_map/ppermute | solution.py:189
  519.4 19.1 %collective-permute-done.5 = bf16[256,2048]{1,0:T(8,128)(2,1)S(1)} collective-permute-done((bf16[256,2048]{1,0:T(8,128)(2,1)S(1)}, bf16[256,2048]{1,0:T(8,128)(2,1)S(1)}, u32[]{:S(2)}, u32[]{:S(2)}) %collective-permute-start.5) | collective-permute-done | bytes 1048608 | tf_op jit(solution)/shard_map/ppermute | solution.py:189
  540.9 18.0 %collective-permute-done.10 = bf16[256,2048]{1,0:T(8,128)(2,1)S(1)} collective-permute-done((bf16[256,2048]{1,0:T(8,128)(2,1)S(1)}, bf16[256,2048]{1,0:T(8,128)(2,1)S(1)}, u32[]{:S(2)}, u32[]{:S(2)}) %collective-permute-start.10) | collective-permute-done | bytes 1048608 | tf_op jit(solution)/shard_map/ppermute | solution.py:189
  561.0 8.7 %collective-permute-done.37 = bf16[256,2048]{1,0:T(8,128)(2,1)S(1)} collective-permute-done((bf16[256,2048]{1,0:T(8,128)(2,1)S(1)}, bf16[256,2048]{1,0:T(8,128)(2,1)S(1)}, u32[]{:S(2)}, u32[]{:S(2)}) %collective-permute-start.37) | collective-permute-done | bytes 1048608 | tf_op jit(solution)/shard_map/ppermute | solution.py:189
  571.1 18.9 %collective-permute-done.36 = bf16[256,2048]{1,0:T(8,128)(2,1)S(1)} collective-permute-done((bf16[256,2048]{1,0:T(8,128)(2,1)S(1)}, bf16[256,2048]{1,0:T(8,128)(2,1)S(1)}, u32[]{:S(2)}, u32[]{:S(2)}) %collective-permute-start.36) | collective-permute-done | bytes 1048608 | tf_op jit(solution)/shard_map/ppermute | solution.py:189
  600.2 14.9 %collective-permute-done.8 = bf16[256,2048]{1,0:T(8,128)(2,1)S(1)} collective-permute-done((bf16[256,2048]{1,0:T(8,128)(2,1)S(1)}, bf16[256,2048]{1,0:T(8,128)(2,1)S(1)}, u32[]{:S(2)}, u32[]{:S(2)}) %collective-permute-start.8) | collective-permute-done | bytes 1048608 | tf_op jit(solution)/shard_map/ppermute | solution.py:189
  616.2 18.6 %collective-permute-done.13 = bf16[256,2048]{1,0:T(8,128)(2,1)S(1)} collective-permute-done((bf16[256,2048]{1,0:T(8,128)(2,1)S(1)}, bf16[256,2048]{1,0:T(8,128)(2,1)S(1)}, u32[]{:S(2)}, u32[]{:S(2)}) %collective-permute-start.13) | collective-permute-done | bytes 1048608 | tf_op jit(solution)/shard_map/ppermute | solution.py:189
  636.1 4.6 maximum_convert_fusion
  642.9 6.4 convolution_convert_fusion.4
  649.3 9.9 %collective-permute-start.11 = (bf16[2048,384]{1,0:T(8,128)(2,1)}, bf16[2048,384]{1,0:T(8,128)(2,1)}, u32[]{:S(2)}, u32[]{:S(2)}) collective-permute-start(bf16[2048,384]{1,0:T(8,128)(2,1)} %convolution_convert_fusion.4), channel_id=1, source_target_pairs={{0,1},{3,2},{4,5},{7,6},{8,9},{11,10},{12,13},{15,14},{16,17},{19,... | collective-permute-start | bytes 4718600 | tf_op jit(solution)/shard_map/ppermute | solution.py:189
  670.0 20.0 %collective-permute-start.12 = (bf16[128,2048]{1,0:T(8,128)(2,1)}, bf16[128,2048]{1,0:T(8,128)(2,1)S(1)}, u32[]{:S(2)}, u32[]{:S(2)}) collective-permute-start(bf16[128,2048]{1,0:T(8,128)(2,1)} %reduce-scatter.11.cloned.1.call-done), channel_id=1, source_target_pairs={{0,1},{3,2},{4,5},{7,6},{8,9},{11,10},{12,13},{15,14},{16,17},{19,... | collective-permute-start | bytes 1572872 | tf_op jit(solution)/shard_map/ppermute | solution.py:189
  690.0 2.6 constant_dynamic-update-slice_fusion.8
  692.6 7.6 collective-permute-done.12
  704.5 2.6 constant_dynamic-update-slice_fusion.7
  707.2 5.6 collective-permute-done.31
  712.7 2.6 constant_dynamic-update-slice_fusion.6
  715.4 15.5 %collective-permute-done.30 = bf16[256,2048]{1,0:T(8,128)(2,1)} collective-permute-done((bf16[256,2048]{1,0:T(8,128)(2,1)}, bf16[256,2048]{1,0:T(8,128)(2,1)}, u32[]{:S(2)}, u32[]{:S(2)}) %collective-permute-start.30) | collective-permute-done | bytes 1048608 | tf_op jit(solution)/shard_map/ppermute | solution.py:189
  731.6 2.6 constant_dynamic-update-slice_fusion.5
  738.5 11.8 %fusion.109 = (f32[2048,1024]{1,0:T(8,128)}, f32[2048,1024]{1,0:T(8,128)}) fusion(bf16[2048,2048]{1,0:T(8,128)(2,1)} %constant_dynamic-update-slice_fusion.5), kind=kLoop, calls=%fused_computation.215 | loop fusion | bytes 33554432 | tf_op jit(solution)/shard_map/slice | solution.py:334
  750.9 16.7 %collective-permute-done.29 = bf16[128,2048]{1,0:T(8,128)(2,1)S(1)} collective-permute-done((bf16[128,2048]{1,0:T(8,128)(2,1)S(1)}, bf16[128,2048]{1,0:T(8,128)(2,1)S(1)}, u32[]{:S(2)}, u32[]{:S(2)}) %collective-permute-start.29) | collective-permute-done | bytes 524320 | tf_op jit(solution)/shard_map/ppermute | solution.py:189
  768.7 29.0 %collective-permute-done.28 = bf16[2048,384]{1,0:T(8,128)(2,1)} collective-permute-done((bf16[2048,384]{1,0:T(8,128)(2,1)}, bf16[2048,384]{1,0:T(8,128)(2,1)}, u32[]{:S(2)}, u32[]{:S(2)}) %collective-permute-start.28) | collective-permute-done | bytes 1572896 | tf_op jit(solution)/shard_map/ppermute | solution.py:189
  803.0 38.0 %psum.7 = f32[4104]{0:T(1024)S(1)} all-reduce(f32[4104]{0:T(1024)S(1)} %pad_maximum_fusion.6), channel_id=1, replica_groups=mesh['heads'=8,'batch'=4] {'heads','batch'}, use_global_device_ids=true, to_apply=%region_23.24 | all-reduce | flops 4104 | bytes 32832 | tf_op jit(solution)/shard_map/psum | solution.py:319
  842.2 3.3 fusion.11
  (344 shorter events, 133.6 us)
Async XLA Ops:
  7.2 59.8 %all-gather.5.cloned.1.call-start = ((), (), s32[]{:S(2)}) async-start(), calls=%async_computation.5 | async-start | bytes 9437184 | tf_op jit(solution)/shard_map/all_gather | solution.py:243
  7.9 97.7 %all-gather.9.cloned.1.call-start = ((), (), s32[]{:S(2)}) async-start(), calls=%async_computation.7 | async-start | bytes 4718592 | tf_op jit(solution)/shard_map/all_gather | solution.py:243
  8.7 136.9 %all-gather.7.cloned.1.call-start = ((), (), s32[]{:S(2)}) async-start(), calls=%async_computation.6 | async-start | bytes 4718592 | tf_op jit(solution)/shard_map/all_gather | solution.py:269
  10.8 71.6 %copy-start.56 = (s32[2,512]{1,0:T(2,128)}, s32[2,512]{1,0:T(2,128)S(1)}, u32[]{:S(2)}) copy-start(s32[2,512]{1,0:T(2,128)S(1)} %get-tuple-element.266) | copy-start | bytes 12292
  10.8 73.9 %copy-start.54 = (s32[2,512]{1,0:T(2,128)}, s32[2,512]{1,0:T(2,128)S(1)}, u32[]{:S(2)}) copy-start(s32[2,512]{1,0:T(2,128)S(1)} %get-tuple-element.265) | copy-start | bytes 12292
  13.5 68.9 %copy-start.58 = (pred[2,512]{1,0:T(4,128)(4,1)}, pred[2,512]{1,0:T(4,128)(4,1)S(1)}, u32[]{:S(2)}) copy-start(pred[2,512]{1,0:T(4,128)(4,1)S(1)} %get-tuple-element.268) | copy-start | bytes 3076
  14.7 57.6 %copy-start.37 = (bf16[2048,384]{1,0:T(8,128)(2,1)}, bf16[2048,384]{1,0:T(8,128)(2,1)S(1)}, u32[]{:S(2)}) copy-start(bf16[2048,384]{1,0:T(8,128)(2,1)S(1)} %constant_dynamic-update-slice_fusion) | copy-start | bytes 4718596
  16.1 56.1 %copy-start.41 = (f32[2048]{0:T(1024)S(1)}, f32[2048]{0:T(1024)}, u32[]{:S(2)}) copy-start(f32[2048]{0:T(1024)} %param.25) | copy-start | bytes 24580
  92.3 109.5 %all-gather.11.cloned.1.call-start = ((), (), s32[]{:S(2)}) async-start(), calls=%async_computation.9 | async-start | bytes 9437184 | tf_op jit(solution)/shard_map/all_gather | solution.py:243
  92.9 243.8 %reduce-scatter.7.cloned.1.call-start = ((), (), s32[]{:S(2)}) async-start(), calls=%async_computation.10 | async-start | bytes 9437184 | tf_op jit(solution)/shard_map/reduce_scatter | solution.py:246
  100.2 64.7 %copy-start.39 = (f32[2048]{0:T(1024)S(1)}, f32[2048]{0:T(1024)}, u32[]{:S(2)}) copy-start(f32[2048]{0:T(1024)} %param.26) | copy-start | bytes 24580
  249.6 147.0 %reduce-scatter.5.cloned.1.call-start = ((), (), s32[]{:S(2)}) async-start(), calls=%async_computation.8 | async-start | bytes 9437184 | tf_op jit(solution)/shard_map/reduce_scatter | solution.py:246
  266.5 19.0 %slice-start.2 = ((s8[8388608]{0:T(1024)(128)(4,1)}), s8[4194304]{0:T(1024)(128)(4,1)S(1)}, s32[]{:S(2)}) async-start(s8[8388608]{0:T(1024)(128)(4,1)} %bitcast.109), calls=%async_computation.15 | async-start | bytes 8388608
  272.8 53.1 %collective-permute-start.1 = (bf16[256,2048]{1,0:T(8,128)(2,1)S(1)}, bf16[256,2048]{1,0:T(8,128)(2,1)S(1)}, u32[]{:S(2)}, u32[]{:S(2)}) collective-permute-start(bf16[256,2048]{1,0:T(8,128)(2,1)S(1)} %convolution_convert_fusion.13), channel_id=1, source_target_pairs={{0,1},{3,2},{4,5},{7,6},{8,9},{11,10},{12,13},{15,14},{16,17},{19,... | collective-permute-start | bytes 3145736 | tf_op jit(solution)/shard_map/ppermute | solution.py:189
  283.1 44.9 %collective-permute-start = (bf16[256,2048]{1,0:T(8,128)(2,1)S(1)}, bf16[256,2048]{1,0:T(8,128)(2,1)S(1)}, u32[]{:S(2)}, u32[]{:S(2)}) collective-permute-start(bf16[256,2048]{1,0:T(8,128)(2,1)S(1)} %convolution_convert_fusion.14), channel_id=1, source_target_pairs={{0,1},{3,2},{4,5},{7,6},{8,9},{11,10},{12,13},{15,14},{16,17},{19,... | collective-permute-start | bytes 3145736 | tf_op jit(solution)/shard_map/ppermute | solution.py:189
  292.3 12.8 %slice-start.4 = ((s8[8388608]{0:T(1024)(128)(4,1)}), s8[4194304]{0:T(1024)(128)(4,1)S(1)}, s32[]{:S(2)}) async-start(s8[8388608]{0:T(1024)(128)(4,1)} %bitcast.141), calls=%async_computation.17 | async-start | bytes 8388608
  317.2 97.5 %collective-permute-start.4 = (bf16[256,2048]{1,0:T(8,128)(2,1)}, bf16[256,2048]{1,0:T(8,128)(2,1)}, u32[]{:S(2)}, u32[]{:S(2)}) collective-permute-start(bf16[256,2048]{1,0:T(8,128)(2,1)} %convolution_convert_fusion.11), channel_id=1, source_target_pairs={{0,1},{3,2},{4,5},{7,6},{8,9},{11,10},{12,13},{15,14},{16,17},{19,... | collective-permute-start | bytes 3145736 | tf_op jit(solution)/shard_map/ppermute | solution.py:189
  326.3 93.0 %collective-permute-start.27 = (bf16[256,2048]{1,0:T(8,128)(2,1)S(1)}, bf16[256,2048]{1,0:T(8,128)(2,1)}, u32[]{:S(2)}, u32[]{:S(2)}) collective-permute-start(bf16[256,2048]{1,0:T(8,128)(2,1)S(1)} %add.209), channel_id=1, source_target_pairs={{1,2},{2,1},{5,6},{6,5},{9,10},{10,9},{13,14},{14,13},{17,18},{18,... | collective-permute-start | bytes 3145736 | tf_op jit(solution)/shard_map/ppermute | solution.py:189
  329.3 98.7 %collective-permute-start.26 = (bf16[256,2048]{1,0:T(8,128)(2,1)}, bf16[256,2048]{1,0:T(8,128)(2,1)}, u32[]{:S(2)}, u32[]{:S(2)}) collective-permute-start(bf16[256,2048]{1,0:T(8,128)(2,1)} %add.210), channel_id=1, source_target_pairs={{1,2},{2,1},{5,6},{6,5},{9,10},{10,9},{13,14},{14,13},{17,18},{18,... | collective-permute-start | bytes 3145736 | tf_op jit(solution)/shard_map/ppermute | solution.py:189
  331.0 101.7 %collective-permute-start.3 = (bf16[256,2048]{1,0:T(8,128)(2,1)}, bf16[256,2048]{1,0:T(8,128)(2,1)}, u32[]{:S(2)}, u32[]{:S(2)}) collective-permute-start(bf16[256,2048]{1,0:T(8,128)(2,1)} %convolution_convert_fusion.12), channel_id=1, source_target_pairs={{0,1},{3,2},{4,5},{7,6},{8,9},{11,10},{12,13},{15,14},{16,17},{19,... | collective-permute-start | bytes 3145736 | tf_op jit(solution)/shard_map/ppermute | solution.py:189
  334.4 101.5 %collective-permute-start.2 = (bf16[256,2048]{1,0:T(8,128)(2,1)}, bf16[256,2048]{1,0:T(8,128)(2,1)}, u32[]{:S(2)}, u32[]{:S(2)}) collective-permute-start(bf16[256,2048]{1,0:T(8,128)(2,1)} %convolution_convert_fusion.15), channel_id=1, source_target_pairs={{0,1},{3,2},{4,5},{7,6},{8,9},{11,10},{12,13},{15,14},{16,17},{19,... | collective-permute-start | bytes 3145736 | tf_op jit(solution)/shard_map/ppermute | solution.py:189
  403.4 41.6 %all-to-all-start = ((bf16[256,8,128]{2,0,1:T(8,128)(2,1)}), bf16[256,8,128]{2,0,1:T(8,128)(2,1)}, u32[]{:S(2)}, u32[]{:S(2)}) async-start(bf16[256,8,128]{2,0,1:T(8,128)(2,1)} %bitcast.119), calls=%async_computation.2 | async-start | bytes 1048576 | tf_op jit(solution)/shard_map/all_to_all | solution.py:305
  407.5 262.5 %reduce-scatter.11.cloned.1.call-start = ((), (), s32[]{:S(2)}) async-start(), calls=%async_computation.12 | async-start | bytes 4718592 | tf_op jit(solution)/shard_map/reduce_scatter | solution.py:246
  417.7 49.4 %collective-permute-start.25 = (bf16[256,2048]{1,0:T(8,128)(2,1)}, bf16[256,2048]{1,0:T(8,128)(2,1)}, u32[]{:S(2)}, u32[]{:S(2)}) collective-permute-start(bf16[256,2048]{1,0:T(8,128)(2,1)} %add.211), channel_id=1, source_target_pairs={{1,2},{2,1},{5,6},{6,5},{9,10},{10,9},{13,14},{14,13},{17,18},{18,... | collective-permute-start | bytes 3145736 | tf_op jit(solution)/shard_map/ppermute | solution.py:189
  419.3 57.2 %collective-permute-start.7 = (bf16[256,2048]{1,0:T(8,128)(2,1)}, bf16[256,2048]{1,0:T(8,128)(2,1)}, u32[]{:S(2)}, u32[]{:S(2)}) collective-permute-start(bf16[256,2048]{1,0:T(8,128)(2,1)} %convolution_convert_fusion.9), channel_id=1, source_target_pairs={{0,1},{3,2},{4,5},{7,6},{8,9},{11,10},{12,13},{15,14},{16,17},{19,... | collective-permute-start | bytes 3145736 | tf_op jit(solution)/shard_map/ppermute | solution.py:189
  428.1 51.8 %collective-permute-start.41 = (bf16[256,2048]{1,0:T(8,128)(2,1)}, bf16[256,2048]{1,0:T(8,128)(2,1)}, u32[]{:S(2)}, u32[]{:S(2)}) collective-permute-start(bf16[256,2048]{1,0:T(8,128)(2,1)} %add.223), channel_id=1, source_target_pairs={{1,0},{2,3},{5,4},{6,7},{9,8},{10,11},{13,12},{14,15},{17,16},{18,... | collective-permute-start | bytes 3145736 | tf_op jit(solution)/shard_map/ppermute | solution.py:189
  432.7 48.1 %collective-permute-start.40 = (bf16[256,2048]{1,0:T(8,128)(2,1)}, bf16[256,2048]{1,0:T(8,128)(2,1)}, u32[]{:S(2)}, u32[]{:S(2)}) collective-permute-start(bf16[256,2048]{1,0:T(8,128)(2,1)} %add.224), channel_id=1, source_target_pairs={{1,0},{2,3},{5,4},{6,7},{9,8},{10,11},{13,12},{14,15},{17,16},{18,... | collective-permute-start | bytes 3145736 | tf_op jit(solution)/shard_map/ppermute | solution.py:189
  435.9 56.5 %collective-permute-start.24 = (bf16[256,2048]{1,0:T(8,128)(2,1)S(1)}, bf16[256,2048]{1,0:T(8,128)(2,1)}, u32[]{:S(2)}, u32[]{:S(2)}) collective-permute-start(bf16[256,2048]{1,0:T(8,128)(2,1)S(1)} %add.212), channel_id=1, source_target_pairs={{1,2},{2,1},{5,6},{6,5},{9,10},{10,9},{13,14},{14,13},{17,18},{18,... | collective-permute-start | bytes 3145736 | tf_op jit(solution)/shard_map/ppermute | solution.py:189
  444.9 356.2 %reduce-scatter.9.cloned.1.call-start = ((), (), s32[]{:S(2)}) async-start(), calls=%async_computation.11 | async-start | bytes 9437184 | tf_op jit(solution)/shard_map/reduce_scatter | solution.py:246
  467.1 31.7 %collective-permute-start.23 = (bf16[256,2048]{1,0:T(8,128)(2,1)}, bf16[256,2048]{1,0:T(8,128)(2,1)S(1)}, u32[]{:S(2)}, u32[]{:S(2)}) collective-permute-start(bf16[256,2048]{1,0:T(8,128)(2,1)} %add.213), channel_id=1, source_target_pairs={{1,2},{2,1},{5,6},{6,5},{9,10},{10,9},{13,14},{14,13},{17,18},{18,... | collective-permute-start | bytes 3145736 | tf_op jit(solution)/shard_map/ppermute | solution.py:189
  474.4 18.1 %copy-start.21 = (bf16[256,2048]{1,0:T(8,128)(2,1)S(1)}, bf16[256,2048]{1,0:T(8,128)(2,1)}, u32[]{:S(2)}) copy-start(bf16[256,2048]{1,0:T(8,128)(2,1)} %convolution_convert_fusion.16) | copy-start | bytes 3145732
  474.4 19.4 %copy-start.65 = (bf16[2048,1024]{0,1:T(8,128)(2,1)S(1)}, bf16[2048,1024]{0,1:T(8,128)(2,1)}, u32[]{:S(2)}) copy-start(bf16[2048,1024]{0,1:T(8,128)(2,1)} %copy-done.63) | copy-start | bytes 12582916
  476.5 41.5 %collective-permute-start.39 = (bf16[256,2048]{1,0:T(8,128)(2,1)S(1)}, bf16[256,2048]{1,0:T(8,128)(2,1)S(1)}, u32[]{:S(2)}, u32[]{:S(2)}) collective-permute-start(bf16[256,2048]{1,0:T(8,128)(2,1)S(1)} %add.225), channel_id=1, source_target_pairs={{1,0},{2,3},{5,4},{6,7},{9,8},{10,11},{13,12},{14,15},{17,16},{18,... | collective-permute-start | bytes 3145736 | tf_op jit(solution)/shard_map/ppermute | solution.py:189
  479.9 18.9 %copy-start.19 = (bf16[256,2048]{1,0:T(8,128)(2,1)S(1)}, bf16[256,2048]{1,0:T(8,128)(2,1)}, u32[]{:S(2)}) copy-start(bf16[256,2048]{1,0:T(8,128)(2,1)} %convolution_convert_fusion.7) | copy-start | bytes 3145732
  479.9 26.1 %collective-permute-start.22 = (bf16[256,2048]{1,0:T(8,128)(2,1)S(1)}, bf16[256,2048]{1,0:T(8,128)(2,1)S(1)}, u32[]{:S(2)}, u32[]{:S(2)}) collective-permute-start(bf16[256,2048]{1,0:T(8,128)(2,1)S(1)} %add.214), channel_id=1, source_target_pairs={{1,2},{2,1},{5,6},{6,5},{9,10},{10,9},{13,14},{14,13},{17,18},{18,... | collective-permute-start | bytes 3145736 | tf_op jit(solution)/shard_map/ppermute | solution.py:189
  480.8 35.2 %collective-permute-start.6 = (bf16[256,2048]{1,0:T(8,128)(2,1)S(1)}, bf16[256,2048]{1,0:T(8,128)(2,1)S(1)}, u32[]{:S(2)}, u32[]{:S(2)}) collective-permute-start(bf16[256,2048]{1,0:T(8,128)(2,1)S(1)} %copy-done.22), channel_id=1, source_target_pairs={{0,1},{3,2},{4,5},{7,6},{8,9},{11,10},{12,13},{15,14},{16,17},{19,... | collective-permute-start | bytes 3145736 | tf_op jit(solution)/shard_map/ppermute | solution.py:189
  492.5 46.0 %collective-permute-start.5 = (bf16[256,2048]{1,0:T(8,128)(2,1)S(1)}, bf16[256,2048]{1,0:T(8,128)(2,1)S(1)}, u32[]{:S(2)}, u32[]{:S(2)}) collective-permute-start(bf16[256,2048]{1,0:T(8,128)(2,1)S(1)} %copy-done.21), channel_id=1, source_target_pairs={{0,1},{3,2},{4,5},{7,6},{8,9},{11,10},{12,13},{15,14},{16,17},{19,... | collective-permute-start | bytes 3145736 | tf_op jit(solution)/shard_map/ppermute | solution.py:189
  498.8 60.1 %collective-permute-start.10 = (bf16[256,2048]{1,0:T(8,128)(2,1)S(1)}, bf16[256,2048]{1,0:T(8,128)(2,1)S(1)}, u32[]{:S(2)}, u32[]{:S(2)}) collective-permute-start(bf16[256,2048]{1,0:T(8,128)(2,1)S(1)} %copy-done.19), channel_id=1, source_target_pairs={{0,1},{3,2},{4,5},{7,6},{8,9},{11,10},{12,13},{15,14},{16,17},{19,... | collective-permute-start | bytes 3145736 | tf_op jit(solution)/shard_map/ppermute | solution.py:189
  506.0 54.2 %collective-permute-start.38 = (bf16[256,2048]{1,0:T(8,128)(2,1)S(1)}, bf16[256,2048]{1,0:T(8,128)(2,1)S(1)}, u32[]{:S(2)}, u32[]{:S(2)}) collective-permute-start(bf16[256,2048]{1,0:T(8,128)(2,1)S(1)} %add.226), channel_id=1, source_target_pairs={{1,0},{2,3},{5,4},{6,7},{9,8},{10,11},{13,12},{14,15},{17,16},{18,... | collective-permute-start | bytes 3145736 | tf_op jit(solution)/shard_map/ppermute | solution.py:189
  516.0 53.6 %collective-permute-start.37 = (bf16[256,2048]{1,0:T(8,128)(2,1)S(1)}, bf16[256,2048]{1,0:T(8,128)(2,1)S(1)}, u32[]{:S(2)}, u32[]{:S(2)}) collective-permute-start(bf16[256,2048]{1,0:T(8,128)(2,1)S(1)} %add.227), channel_id=1, source_target_pairs={{1,0},{2,3},{5,4},{6,7},{9,8},{10,11},{13,12},{14,15},{17,16},{18,... | collective-permute-start | bytes 3145736 | tf_op jit(solution)/shard_map/ppermute | solution.py:189
  518.1 72.0 %collective-permute-start.36 = (bf16[256,2048]{1,0:T(8,128)(2,1)S(1)}, bf16[256,2048]{1,0:T(8,128)(2,1)S(1)}, u32[]{:S(2)}, u32[]{:S(2)}) collective-permute-start(bf16[256,2048]{1,0:T(8,128)(2,1)S(1)} %add.228), channel_id=1, source_target_pairs={{1,0},{2,3},{5,4},{6,7},{9,8},{10,11},{13,12},{14,15},{17,16},{18,... | collective-permute-start | bytes 3145736 | tf_op jit(solution)/shard_map/ppermute | solution.py:189
  538.4 53.1 %collective-permute-start.21 = (bf16[256,2048]{1,0:T(8,128)(2,1)S(1)}, bf16[256,2048]{1,0:T(8,128)(2,1)S(1)}, u32[]{:S(2)}, u32[]{:S(2)}) collective-permute-start(bf16[256,2048]{1,0:T(8,128)(2,1)S(1)} %add.215), channel_id=1, source_target_pairs={{1,2},{2,1},{5,6},{6,5},{9,10},{10,9},{13,14},{14,13},{17,18},{18,... | collective-permute-start | bytes 3145736 | tf_op jit(solution)/shard_map/ppermute | solution.py:189
  540.5 29.1 %copy-start.20 = (bf16[256,2048]{1,0:T(8,128)(2,1)S(1)}, bf16[256,2048]{1,0:T(8,128)(2,1)}, u32[]{:S(2)}) copy-start(bf16[256,2048]{1,0:T(8,128)(2,1)} %convolution_convert_fusion.8) | copy-start | bytes 3145732
  559.0 34.5 %collective-permute-start.20 = (bf16[256,2048]{1,0:T(8,128)(2,1)S(1)}, bf16[256,2048]{1,0:T(8,128)(2,1)S(1)}, u32[]{:S(2)}, u32[]{:S(2)}) collective-permute-start(bf16[256,2048]{1,0:T(8,128)(2,1)S(1)} %add.216), channel_id=1, source_target_pairs={{1,2},{2,1},{5,6},{6,5},{9,10},{10,9},{13,14},{14,13},{17,18},{18,... | collective-permute-start | bytes 3145736 | tf_op jit(solution)/shard_map/ppermute | solution.py:189
  560.2 36.6 %collective-permute-start.19 = (bf16[256,2048]{1,0:T(8,128)(2,1)S(1)}, bf16[256,2048]{1,0:T(8,128)(2,1)S(1)}, u32[]{:S(2)}, u32[]{:S(2)}) collective-permute-start(bf16[256,2048]{1,0:T(8,128)(2,1)S(1)} %add.217), channel_id=1, source_target_pairs={{1,2},{2,1},{5,6},{6,5},{9,10},{10,9},{13,14},{14,13},{17,18},{18,... | collective-permute-start | bytes 3145736 | tf_op jit(solution)/shard_map/ppermute | solution.py:189
  569.6 28.9 %collective-permute-start.9 = (bf16[256,2048]{1,0:T(8,128)(2,1)S(1)}, bf16[256,2048]{1,0:T(8,128)(2,1)S(1)}, u32[]{:S(2)}, u32[]{:S(2)}) collective-permute-start(bf16[256,2048]{1,0:T(8,128)(2,1)S(1)} %copy-done.20), channel_id=1, source_target_pairs={{0,1},{3,2},{4,5},{7,6},{8,9},{11,10},{12,13},{15,14},{16,17},{19,... | collective-permute-start | bytes 3145736 | tf_op jit(solution)/shard_map/ppermute | solution.py:189
  590.1 25.0 %collective-permute-start.8 = (bf16[256,2048]{1,0:T(8,128)(2,1)S(1)}, bf16[256,2048]{1,0:T(8,128)(2,1)S(1)}, u32[]{:S(2)}, u32[]{:S(2)}) collective-permute-start(bf16[256,2048]{1,0:T(8,128)(2,1)S(1)} %convolution_convert_fusion.17), channel_id=1, source_target_pairs={{0,1},{3,2},{4,5},{7,6},{8,9},{11,10},{12,13},{15,14},{16,17},{19,... | collective-permute-start | bytes 3145736 | tf_op jit(solution)/shard_map/ppermute | solution.py:189
  591.6 43.3 %collective-permute-start.13 = (bf16[256,2048]{1,0:T(8,128)(2,1)S(1)}, bf16[256,2048]{1,0:T(8,128)(2,1)S(1)}, u32[]{:S(2)}, u32[]{:S(2)}) collective-permute-start(bf16[256,2048]{1,0:T(8,128)(2,1)S(1)} %convolution_convert_fusion.6), channel_id=1, source_target_pairs={{0,1},{3,2},{4,5},{7,6},{8,9},{11,10},{12,13},{15,14},{16,17},{19,... | collective-permute-start | bytes 3145736 | tf_op jit(solution)/shard_map/ppermute | solution.py:189
  593.5 48.6 %collective-permute-start.35 = (bf16[256,2048]{1,0:T(8,128)(2,1)S(1)}, bf16[256,2048]{1,0:T(8,128)(2,1)S(1)}, u32[]{:S(2)}, u32[]{:S(2)}) collective-permute-start(bf16[256,2048]{1,0:T(8,128)(2,1)S(1)} %add.229), channel_id=1, source_target_pairs={{1,0},{2,3},{5,4},{6,7},{9,8},{10,11},{13,12},{14,15},{17,16},{18,... | collective-permute-start | bytes 3145736 | tf_op jit(solution)/shard_map/ppermute | solution.py:189
  596.8 52.5 %collective-permute-start.34 = (bf16[256,2048]{1,0:T(8,128)(2,1)S(1)}, bf16[256,2048]{1,0:T(8,128)(2,1)S(1)}, u32[]{:S(2)}, u32[]{:S(2)}) collective-permute-start(bf16[256,2048]{1,0:T(8,128)(2,1)S(1)} %add.230), channel_id=1, source_target_pairs={{1,0},{2,3},{5,4},{6,7},{9,8},{10,11},{13,12},{14,15},{17,16},{18,... | collective-permute-start | bytes 3145736 | tf_op jit(solution)/shard_map/ppermute | solution.py:189
  598.5 66.2 %collective-permute-start.33 = (bf16[256,2048]{1,0:T(8,128)(2,1)S(1)}, bf16[256,2048]{1,0:T(8,128)(2,1)S(1)}, u32[]{:S(2)}, u32[]{:S(2)}) collective-permute-start(bf16[256,2048]{1,0:T(8,128)(2,1)S(1)} %add.231), channel_id=1, source_target_pairs={{1,0},{2,3},{5,4},{6,7},{9,8},{10,11},{13,12},{14,15},{17,16},{18,... | collective-permute-start | bytes 3145736 | tf_op jit(solution)/shard_map/ppermute | solution.py:189
  615.1 45.5 %collective-permute-start.18 = (bf16[256,2048]{1,0:T(8,128)(2,1)S(1)}, bf16[256,2048]{1,0:T(8,128)(2,1)S(1)}, u32[]{:S(2)}, u32[]{:S(2)}) collective-permute-start(bf16[256,2048]{1,0:T(8,128)(2,1)S(1)} %add.218), channel_id=1, source_target_pairs={{1,2},{2,1},{5,6},{6,5},{9,10},{10,9},{13,14},{14,13},{17,18},{18,... | collective-permute-start | bytes 3145736 | tf_op jit(solution)/shard_map/ppermute | solution.py:189
  615.8 27.0 %slice-start = ((s8[8388608]{0:T(1024)(128)(4,1)}), s8[4194304]{0:T(1024)(128)(4,1)S(1)}, s32[]{:S(2)}) async-start(s8[8388608]{0:T(1024)(128)(4,1)} %bitcast.107), calls=%async_computation.13 | async-start | bytes 8388608
  634.9 29.8 %collective-permute-start.17 = (bf16[256,2048]{1,0:T(8,128)(2,1)S(1)}, bf16[256,2048]{1,0:T(8,128)(2,1)S(1)}, u32[]{:S(2)}, u32[]{:S(2)}) collective-permute-start(bf16[256,2048]{1,0:T(8,128)(2,1)S(1)} %add.219), channel_id=1, source_target_pairs={{1,2},{2,1},{5,6},{6,5},{9,10},{10,9},{13,14},{14,13},{17,18},{18,... | collective-permute-start | bytes 3145736 | tf_op jit(solution)/shard_map/ppermute | solution.py:189
  642.1 25.3 %collective-permute-start.16 = (bf16[256,2048]{1,0:T(8,128)(2,1)S(1)}, bf16[256,2048]{1,0:T(8,128)(2,1)S(1)}, u32[]{:S(2)}, u32[]{:S(2)}) collective-permute-start(bf16[256,2048]{1,0:T(8,128)(2,1)S(1)} %add.220), channel_id=1, source_target_pairs={{1,2},{2,1},{5,6},{6,5},{9,10},{10,9},{13,14},{14,13},{17,18},{18,... | collective-permute-start | bytes 3145736 | tf_op jit(solution)/shard_map/ppermute | solution.py:189
  649.3 52.1 %collective-permute-start.11 = (bf16[2048,384]{1,0:T(8,128)(2,1)}, bf16[2048,384]{1,0:T(8,128)(2,1)}, u32[]{:S(2)}, u32[]{:S(2)}) collective-permute-start(bf16[2048,384]{1,0:T(8,128)(2,1)} %convolution_convert_fusion.4), channel_id=1, source_target_pairs={{0,1},{3,2},{4,5},{7,6},{8,9},{11,10},{12,13},{15,14},{16,17},{19,... | collective-permute-start | bytes 4718600 | tf_op jit(solution)/shard_map/ppermute | solution.py:189
  662.0 30.7 %collective-permute-start.32 = (bf16[256,2048]{1,0:T(8,128)(2,1)}, bf16[256,2048]{1,0:T(8,128)(2,1)}, u32[]{:S(2)}, u32[]{:S(2)}) collective-permute-start(bf16[256,2048]{1,0:T(8,128)(2,1)} %add.232), channel_id=1, source_target_pairs={{1,0},{2,3},{5,4},{6,7},{9,8},{10,11},{13,12},{14,15},{17,16},{18,... | collective-permute-start | bytes 3145736 | tf_op jit(solution)/shard_map/ppermute | solution.py:189
  666.0 46.7 %collective-permute-start.31 = (bf16[256,2048]{1,0:T(8,128)(2,1)}, bf16[256,2048]{1,0:T(8,128)(2,1)}, u32[]{:S(2)}, u32[]{:S(2)}) collective-permute-start(bf16[256,2048]{1,0:T(8,128)(2,1)} %add.233), channel_id=1, source_target_pairs={{1,0},{2,3},{5,4},{6,7},{9,8},{10,11},{13,12},{14,15},{17,16},{18,... | collective-permute-start | bytes 3145736 | tf_op jit(solution)/shard_map/ppermute | solution.py:189
  668.7 62.2 %collective-permute-start.30 = (bf16[256,2048]{1,0:T(8,128)(2,1)}, bf16[256,2048]{1,0:T(8,128)(2,1)}, u32[]{:S(2)}, u32[]{:S(2)}) collective-permute-start(bf16[256,2048]{1,0:T(8,128)(2,1)} %add.234), channel_id=1, source_target_pairs={{1,0},{2,3},{5,4},{6,7},{9,8},{10,11},{13,12},{14,15},{17,16},{18,... | collective-permute-start | bytes 3145736 | tf_op jit(solution)/shard_map/ppermute | solution.py:189
  670.0 30.2 %collective-permute-start.12 = (bf16[128,2048]{1,0:T(8,128)(2,1)}, bf16[128,2048]{1,0:T(8,128)(2,1)S(1)}, u32[]{:S(2)}, u32[]{:S(2)}) collective-permute-start(bf16[128,2048]{1,0:T(8,128)(2,1)} %reduce-scatter.11.cloned.1.call-done), channel_id=1, source_target_pairs={{0,1},{3,2},{4,5},{7,6},{8,9},{11,10},{12,13},{15,14},{16,17},{19,... | collective-permute-start | bytes 1572872 | tf_op jit(solution)/shard_map/ppermute | solution.py:189
  703.7 31.9 %collective-permute-start.14 = (bf16[2048,384]{1,0:T(8,128)(2,1)S(1)}, bf16[2048,384]{1,0:T(8,128)(2,1)S(1)}, u32[]{:S(2)}, u32[]{:S(2)}) collective-permute-start(bf16[2048,384]{1,0:T(8,128)(2,1)S(1)} %add.222), channel_id=1, source_target_pairs={{1,2},{2,1},{5,6},{6,5},{9,10},{10,9},{13,14},{14,13},{17,18},{18,... | collective-permute-start | bytes 4718600 | tf_op jit(solution)/shard_map/ppermute | solution.py:189
  730.9 3.3 collective-permute-start.15
  734.3 33.4 %collective-permute-start.29 = (bf16[128,2048]{1,0:T(8,128)(2,1)S(1)}, bf16[128,2048]{1,0:T(8,128)(2,1)S(1)}, u32[]{:S(2)}, u32[]{:S(2)}) collective-permute-start(bf16[128,2048]{1,0:T(8,128)(2,1)S(1)} %add.235), channel_id=1, source_target_pairs={{1,0},{2,3},{5,4},{6,7},{9,8},{10,11},{13,12},{14,15},{17,16},{18,... | collective-permute-start | bytes 1572872 | tf_op jit(solution)/shard_map/ppermute | solution.py:189
  737.2 60.5 %collective-permute-start.28 = (bf16[2048,384]{1,0:T(8,128)(2,1)}, bf16[2048,384]{1,0:T(8,128)(2,1)}, u32[]{:S(2)}, u32[]{:S(2)}) collective-permute-start(bf16[2048,384]{1,0:T(8,128)(2,1)} %add.236), channel_id=1, source_target_pairs={{1,0},{2,3},{5,4},{6,7},{9,8},{10,11},{13,12},{14,15},{17,16},{18,... | collective-permute-start | bytes 4718600 | tf_op jit(solution)/shard_map/ppermute | solution.py:189
  (60 other events, 248.6 us)
Sparse Core Ops, SparseCore 0:
  9.9 57.0 all-gather.4
  68.9 36.7 all-gather.8
  108.1 37.4 all-gather.6
  147.3 54.3 all-gather.10
  249.7 71.2 reduce-scatter.6
  325.3 71.2 reduce-scatter.4
  445.0 55.6 reduce-scatter.10
  504.5 71.2 reduce-scatter.8

commit v2 on v1

v2 whole, which is shorter than its diff:
```python
import functools

import jax
import jax.numpy as jnp
from jax import lax
from jax.experimental import pallas as pl
from jax.experimental.pallas import tpu as pltpu
from jax.sharding import PartitionSpec as P

DH = 128
SEG = 512
SEGS = 2
LEN = 1024
MICRO = 2
FFN_CHUNKS = 4
WAITS = (225, 57, 57, 1)
ROW_BLOCK = 512
MIB = 1 << 20
VMEM_ALONE = 60
IN_VMEM = pl.BlockSpec(memory_space=pltpu.VMEM)
ANYWHERE = pl.BlockSpec(memory_space=pl.ANY)
SMALL = pl.CostEstimate(flops=1, bytes_accessed=1, transcendentals=0)
def busy(microseconds):
    return pl.CostEstimate(flops=int(microseconds * 10**9), bytes_accessed=1, transcendentals=0)


epsilon = 1e-05
big_negative = -1e30
low = jnp.bfloat16
wide = jnp.float32


def mm(left_mat, right_mat):
    return jnp.dot(left_mat, right_mat, preferred_element_type=wide)


def dot_rows(left_mat, right_mat):
    return lax.dot_general(
        left_mat, right_mat, (((1,), (1,)), ((), ())), preferred_element_type=wide
    )


def dot_cols(left_mat, right_mat):
    return lax.dot_general(
        left_mat, right_mat, (((0,), (0,)), ((), ())), preferred_element_type=wide
    )


def norm_scale(row_block):
    return lax.rsqrt(jnp.mean(row_block * row_block, axis=-1, keepdims=True) + epsilon)


def norm_back(row_block, row_scale, gain_vec, upstream):
    shaped = upstream * gain_vec
    inner = jnp.mean(shaped * row_block, axis=-1, keepdims=True)
    d_rows = row_scale * shaped - row_block * row_scale * row_scale * row_scale * inner
    d_gain = jnp.sum(upstream * row_block * row_scale, axis=0)
    return (d_rows, d_gain)


def positive(values_in):
    return jnp.where(values_in > 0, values_in + 1.0, jnp.exp(values_in))


def positive_slope(values_in):
    return jnp.where(values_in > 0, 1.0, jnp.exp(values_in))


def params(mebibytes):
    return pltpu.CompilerParams(vmem_limit_bytes=mebibytes * MIB)


def kept_block(shape):
    return pl.BlockSpec(shape, lambda *_: (0,) * len(shape), pipeline_mode=pl.Buffered(1))


def qkv_kernel(x_ref, gain_ref, w_ref, h1_ref, qkv_ref):
    rows = x_ref[...].astype(wide)
    h1 = (rows * norm_scale(rows) * gain_ref[...]).astype(low)
    h1_ref[...] = h1
    qkv_ref[...] = mm(h1, w_ref[...]).astype(low)


def qkv_rows(x_all, gain, w_qkv):
    count, width = x_all.shape
    cols = w_qkv.shape[1]
    block = min(ROW_BLOCK, count)
    return pl.pallas_call(
        qkv_kernel,
        name="qkv_rows",
        grid=(count // block,),
        in_specs=[
            pl.BlockSpec((block, width), lambda i: (i, 0)),
            kept_block((1, width)),
            kept_block((width, cols)),
        ],
        out_specs=[
            pl.BlockSpec((block, width), lambda i: (i, 0)),
            pl.BlockSpec((block, cols), lambda i: (i, 0)),
        ],
        out_shape=[
            jax.ShapeDtypeStruct((count, width), low),
            jax.ShapeDtypeStruct((count, cols), low),
        ],
        compiler_params=params(VMEM_ALONE),
        cost_estimate=SMALL,
    )(x_all, gain.reshape(1, width), w_qkv)


def seg_of(array, segment):
    return array[segment * SEG : (segment + 1) * SEG]


def local_probs(query_seg, key_seg, doc_rows, doc_cols):
    row_ids = lax.broadcasted_iota(jnp.int32, (SEG, SEG), 0)
    col_ids = lax.broadcasted_iota(jnp.int32, (SEG, SEG), 1)
    allowed = ((doc_rows == doc_cols) & (col_ids <= row_ids)) | (col_ids == row_ids)
    scores = jnp.where(allowed, dot_rows(query_seg, key_seg) * DH ** (-0.5), big_negative)
    shifted = jnp.exp(scores - jnp.max(scores, axis=1, keepdims=True))
    return shifted * (1.0 / jnp.sum(shifted, axis=1, keepdims=True))


def head_kernel(share_ref, qkv_ref, doc_rows_ref, doc_cols_ref, mixed_ref):
    share = share_ref[0]
    qkv = qkv_ref[...].reshape(LEN, 3 * DH)
    query, key, value = [qkv[:, i * DH : (i + 1) * DH] for i in range(3)]
    parts = []
    for segment in range(SEGS):
        begin = segment * SEG
        query_seg = seg_of(query, segment)
        doc_rows = doc_rows_ref[begin : begin + SEG]
        probs = local_probs(
            query_seg, seg_of(key, segment), doc_rows, doc_cols_ref[:, begin : begin + SEG]
        )
        result = (1.0 - share) * mm(probs.astype(low), seg_of(value, segment))
        if segment > 0:
            allowed = doc_rows == doc_cols_ref[:, :begin]
            pos_query = positive(query_seg.astype(wide)).astype(low)
            pos_key = positive(key[:begin].astype(wide)).astype(low)
            weights = jnp.where(allowed, dot_rows(pos_query, pos_key), 0.0)
            den = jnp.maximum(jnp.sum(weights, axis=1, keepdims=True), 1.0)
            result = result + share * (mm(weights.astype(low), value[:begin]) / den)
        parts.append(result.astype(low))
    mixed_ref[...] = jnp.concatenate(parts, axis=0).reshape(mixed_ref.shape)


def micro_spec(n_heads, rows, cols):
    return pl.BlockSpec((n_heads, None, rows, cols), lambda m: (0, m, 0, 0))


def doc_specs():
    return [
        pl.BlockSpec((None, LEN, 1), lambda m: (m, 0, 0)),
        pl.BlockSpec((None, 1, LEN), lambda m: (m, 0, 0)),
    ]


def head_forward(share, qkv, doc_rows, doc_cols):
    n_heads, micro, rows, cols = qkv.shape
    pairs = micro * LEN * SEG * 2
    return pl.pallas_call(
        head_kernel,
        name="head_forward",
        grid=(micro,),
        in_specs=[pl.BlockSpec(memory_space=pltpu.SMEM), micro_spec(n_heads, rows, cols), *doc_specs()],
        out_specs=micro_spec(n_heads, rows, DH),
        out_shape=jax.ShapeDtypeStruct((n_heads, micro, rows, DH), low),
        compiler_params=params(VMEM_ALONE),
        cost_estimate=SMALL,
    )(share, qkv, doc_rows, doc_cols)


def head_back_kernel(
    share_ref, qkv_ref, d_mixed_ref, doc_rows_ref, doc_cols_ref, _, d_qkv_ref, d_share_ref
):
    share = share_ref[0]
    scale = DH ** (-0.5)
    qkv = qkv_ref[...].reshape(LEN, 3 * DH)
    query, key, value = [qkv[:, i * DH : (i + 1) * DH] for i in range(3)]
    d_mixed = d_mixed_ref[...].reshape(LEN, DH).astype(wide)
    d_query, d_key, d_value = [[None] * SEGS for _ in range(3)]
    d_share = jnp.zeros((1, 1), wide)
    for segment in range(SEGS):
        begin = segment * SEG
        query_seg, key_seg, value_seg = [seg_of(a, segment) for a in (query, key, value)]
        doc_rows = doc_rows_ref[begin : begin + SEG]
        probs = local_probs(query_seg, key_seg, doc_rows, doc_cols_ref[:, begin : begin + SEG])
        probs_low = probs.astype(low)
        d_mixed_seg = seg_of(d_mixed, segment)
        d_dotted = ((1.0 - share) * d_mixed_seg).astype(low)
        gap = -mm(probs_low, value_seg)
        d_probs = dot_rows(d_dotted, value_seg)
        d_scores = (
            probs * (d_probs - jnp.sum(probs * d_probs, axis=1, keepdims=True))
        ).astype(low)
        d_value[segment] = dot_cols(probs_low, d_dotted)
        d_query[segment] = mm(d_scores, key_seg) * scale
        d_key[segment] = dot_cols(d_scores, query_seg) * scale
        if segment > 0:
            allowed = doc_rows == doc_cols_ref[:, :begin]
            query_float = query_seg.astype(wide)
            key_float = key[:begin].astype(wide)
            pos_query = positive(query_float).astype(low)
            pos_key = positive(key_float).astype(low)
            weights = jnp.where(allowed, dot_rows(pos_query, pos_key), 0.0)
            row_total = jnp.sum(weights, axis=1, keepdims=True)
            inverse = 1.0 / jnp.maximum(row_total, 1.0)
            weights_low = weights.astype(low)
            numerator = mm(weights_low, value[:begin])
            gap = gap + numerator * inverse
            d_recalled = share * d_mixed_seg
            d_numer = (d_recalled * inverse).astype(low)
            d_denom = jnp.where(
                row_total > 1.0,
                -jnp.sum(d_recalled * numerator, axis=1, keepdims=True) * inverse * inverse,
                0.0,
            )
            d_weights = jnp.where(
                allowed, dot_rows(d_numer, value[:begin]) + d_denom, 0.0
            ).astype(low)
            d_query[segment] += mm(d_weights, pos_key) * positive_slope(query_float)
            d_pos_key = dot_cols(d_weights, pos_query) * positive_slope(key_float)
            d_value_before = dot_cols(weights_low, d_numer)
            for earlier in range(segment):
                d_key[earlier] += seg_of(d_pos_key, earlier)
                d_value[earlier] += seg_of(d_value_before, earlier)
        d_share = d_share + jnp.sum(
            jnp.sum(d_mixed_seg * gap, axis=1, keepdims=True), axis=0, keepdims=True
        )
    whole = jnp.concatenate(
        [jnp.concatenate(parts, axis=0).astype(low) for parts in (d_query, d_key, d_value)], axis=1
    )
    d_qkv_ref[...] = whole.reshape(d_qkv_ref.shape)
    d_share_ref[...] = jnp.broadcast_to(d_share * (share * (1.0 - share)), d_share_ref.shape)


def head_backward(share, qkv, d_mixed, doc_rows, doc_cols, token):
    n_heads, micro, rows, cols = qkv.shape
    pairs = micro * LEN * SEG * 2
    return pl.pallas_call(
        head_back_kernel,
        name="head_backward",
        grid=(micro,),
        in_specs=[
            pl.BlockSpec(memory_space=pltpu.SMEM),
            micro_spec(n_heads, rows, cols),
            micro_spec(n_heads, rows, DH),
            *doc_specs(),
            ANYWHERE,
        ],
        out_specs=[
            micro_spec(n_heads, rows, cols),
            pl.BlockSpec((None, 8, 128), lambda m: (m, 0, 0)),
        ],
        out_shape=[
            jax.ShapeDtypeStruct((n_heads, micro, rows, cols), low),
            jax.ShapeDtypeStruct((micro, 8, 128), wide),
        ],
        compiler_params=params(VMEM_ALONE),
        cost_estimate=SMALL,
    )(share, qkv, d_mixed, doc_rows, doc_cols, token)


def mid_kernel(heads, place_ref, x_ref, *refs):
    mixed_refs = refs[:heads]
    w_ref, gain_ref, h2_ref, y1_ref, mixed_own_ref, w_near = refs[heads:]
    step = pl.program_id(0)
    def owner(number):
        return pl.multiple_of((place_ref[1] ^ number) * DH, DH)

    @pl.when(step == 0)
    def _():
        for number in range(heads):
            w_near[number * DH : (number + 1) * DH] = w_ref[pl.ds(owner(number), DH)]

    mixed = jnp.concatenate([ref[...] for ref in mixed_refs], axis=1)
    y1 = x_ref[...].astype(wide) + mm(mixed, w_near[...])
    h2_ref[...] = (y1 * norm_scale(y1) * gain_ref[...]).astype(low)

    @pl.when(step == place_ref[0])
    def _():
        y1_ref[...] = y1
        for number in range(heads):
            mixed_own_ref[:, pl.ds(owner(number), DH)] = mixed_refs[number][...]


def mid_rows(place, x_all, mixed_pieces, w_out_all, gain):
    count, width = x_all.shape
    heads = len(mixed_pieces)
    inner = w_out_all.shape[0]
    block = count // heads
    return pl.pallas_call(
        functools.partial(mid_kernel, heads),
        name="mid_rows",
        grid_spec=pltpu.PrefetchScalarGridSpec(
            num_scalar_prefetch=1,
            grid=(heads,),
            in_specs=[
                pl.BlockSpec((block, width), lambda i, _: (i, 0)),
                *[pl.BlockSpec((block, DH), lambda i, _: (i, 0))] * heads,
                kept_block((inner, width)),
                kept_block((1, width)),
            ],
            out_specs=[
                pl.BlockSpec((block, width), lambda i, _: (i, 0)),
                pl.BlockSpec((block, width), lambda i, _: (0, 0)),
                pl.BlockSpec((block, inner), lambda i, _: (0, 0)),
            ],
            scratch_shapes=[pltpu.VMEM((inner, width), low)],
        ),
        out_shape=[
            jax.ShapeDtypeStruct((count, width), low),
            jax.ShapeDtypeStruct((block, width), wide),
            jax.ShapeDtypeStruct((block, inner), low),
        ],
        compiler_params=params(30),
        cost_estimate=SMALL,
    )(place, x_all, *mixed_pieces, w_out_all, gain.reshape(1, width))


def ffn_rows(h2_ref, cot_ref, w_gate, w_up, w_down):
    h2 = h2_ref[...]
    gate = mm(h2, w_gate)
    up = mm(h2, w_up)
    d_hidden = dot_rows(cot_ref[...], w_down)
    sig = jax.nn.sigmoid(gate)
    act = gate * sig
    hidden = (act * up).astype(low)
    d_up = (d_hidden * act).astype(low)
    d_gate = (d_hidden * up * sig * (1.0 + gate * (1.0 - sig))).astype(low)
    return hidden, d_gate, d_up


def ffn_grads(step, hidden, d_both, h2_ref, cot_ref, top_ref, bottom_ref):
    cols = hidden.shape[1]
    side = 2 * cols
    half = cols // 2
    span = pl.ds(pl.multiple_of(step * side, side), side)
    top_ref[:cols, span] = dot_cols(hidden[...], cot_ref[...]).astype(low)
    square = dot_cols(h2_ref[...], d_both[...]).astype(low)
    top_ref[cols:, span] = square[:half]
    bottom_ref[:, span] = square[half:]


def first_kernel(
    blocks, h2_ref, cot_ref, h2_col_ref, cot_col_ref, wg_ref, wu_ref, wd_ref, _, *refs
):
    hid_ref, dg_ref, du_ref, top_ref, bottom_ref, hid_all, both_all = refs
    step = pl.program_id(0)
    block, cols = hid_ref.shape

    @pl.when(step < blocks)
    def _():
        rows = pl.ds(pl.multiple_of(step * block, block), block)
        hidden, d_gate, d_up = ffn_rows(h2_ref, cot_ref, wg_ref[...], wu_ref[...], wd_ref[...])
        hid_ref[...] = hid_all[rows] = hidden
        dg_ref[...] = both_all[rows, :cols] = d_gate
        du_ref[...] = both_all[rows, cols:] = d_up

    @pl.when(step >= blocks)
    def _():
        ffn_grads(step - blocks, hid_all, both_all, h2_col_ref, cot_col_ref, top_ref, bottom_ref)


def ffn_first(number, cols, h2_all, cot_all, w_gate, w_up, w_down, token):
    count, width = h2_all.shape
    block = min(ROW_BLOCK, count // 2)
    blocks = count // block
    side = 2 * cols
    row_spec = pl.BlockSpec((block, width), lambda i: (jnp.minimum(i, blocks - 1), 0))
    side_spec = pl.BlockSpec((count, side), lambda i: (0, jnp.maximum(i - blocks, 0)))
    col_spec = pl.BlockSpec((width, cols), lambda i: (0, number), pipeline_mode=pl.Buffered(1))
    down_spec = pl.BlockSpec((cols, width), lambda i: (number, 0), pipeline_mode=pl.Buffered(1))
    out_spec = pl.BlockSpec((block, cols), lambda i: (jnp.minimum(i, blocks - 1), 0))
    piece = (3 * cols // 2, width)
    return pl.pallas_call(
        functools.partial(first_kernel, blocks),
        name="ffn_first",
        grid=(blocks + width // side,),
        in_specs=[row_spec, row_spec, side_spec, side_spec, col_spec, col_spec, down_spec, ANYWHERE],
        out_specs=[out_spec] * 3 + [kept_out(piece)] * 2,
        out_shape=[jax.ShapeDtypeStruct((count, cols), low)] * 3
        + [jax.ShapeDtypeStruct(piece, low)] * 2,
        scratch_shapes=[pltpu.VMEM((count, cols), low), pltpu.VMEM((count, side), low)],
        compiler_params=params(VMEM_ALONE),
        cost_estimate=SMALL,
    )(h2_all, cot_all, h2_all, cot_all, w_gate, w_up, w_down, token)


def rest_kernel(h2_ref, cot_ref, wg_ref, wu_ref, wd_ref, _, *refs):
    results = ffn_rows(h2_ref, cot_ref, wg_ref[...], wu_ref[...], wd_ref[...])
    for ref, result in zip(refs, results):
        ref[...] = result


def ffn_rest(h2_all, cot_all, w_gate, w_up, w_down, token):
    count, width = h2_all.shape
    block = min(ROW_BLOCK, count // 2)
    cols = w_gate.shape[1] // 2
    row_spec = pl.BlockSpec((block, width), lambda i: (i, 0))
    col_spec = pl.BlockSpec((width, cols), lambda i: (0, 1), pipeline_mode=pl.Buffered(1))
    down_spec = pl.BlockSpec((cols, width), lambda i: (1, 0), pipeline_mode=pl.Buffered(1))
    return pl.pallas_call(
        rest_kernel,
        name="ffn_rest",
        grid=(count // block,),
        in_specs=[row_spec, row_spec, col_spec, col_spec, down_spec, ANYWHERE],
        out_specs=[pl.BlockSpec((block, cols), lambda i: (i, 0))] * 3,
        out_shape=[jax.ShapeDtypeStruct((count, cols), low)] * 3,
        compiler_params=params(VMEM_ALONE),
        cost_estimate=SMALL,
    )(h2_all, cot_all, w_gate, w_up, w_down, token)


def grads_kernel(h2_ref, cot_ref, hid_ref, dg_ref, du_ref, _, top_ref, bottom_ref, both_all):
    step = pl.program_id(0)
    cols = hid_ref.shape[1]

    @pl.when(step == 0)
    def _():
        both_all[:, :cols] = dg_ref[...]
        both_all[:, cols:] = du_ref[...]

    ffn_grads(step, hid_ref, both_all, h2_ref, cot_ref, top_ref, bottom_ref)


def ffn_weights(number, cols, h2_all, cot_all, hidden, d_gate, d_up, token):
    count, width = h2_all.shape
    side = 2 * cols
    side_spec = pl.BlockSpec((count, side), lambda i: (0, i))
    col_spec = pl.BlockSpec((count, cols), lambda i: (0, number), pipeline_mode=pl.Buffered(1))
    piece = (3 * cols // 2, width)
    return pl.pallas_call(
        grads_kernel,
        name="ffn_weights",
        grid=(width // side,),
        in_specs=[side_spec, side_spec, col_spec, col_spec, col_spec, ANYWHERE],
        out_specs=[kept_out(piece)] * 2,
        out_shape=[jax.ShapeDtypeStruct(piece, low)] * 2,
        scratch_shapes=[pltpu.VMEM((count, side), low)],
        compiler_params=params(VMEM_ALONE),
        cost_estimate=SMALL,
    )(h2_all, cot_all, hidden, d_gate, d_up, token)


def is_one_of(place_ref, takers):
    found = place_ref[2] == takers[0]
    for taker in takers[1:]:
        found = found | (place_ref[2] == taker)
    return found


def chosen(takers, place_ref, array_ref, arrived_ref):
    if not takers:
        return array_ref[...].astype(wide)
    return jnp.where(is_one_of(place_ref, takers), arrived_ref[...], array_ref[...]).astype(wide)


def top_kernel(takers, place_ref, array_ref, arrived_ref, *refs):
    down_ref, gate_ref, up_ref, token_ref = refs[-4:]
    step = pl.program_id(0)
    cols = gate_ref.shape[2]

    @pl.when(step < 2)
    def _():
        down_ref[...] = chosen(takers, place_ref, array_ref, arrived_ref)

    @pl.when(step == 2)
    def _():
        spread(chosen(takers, place_ref, array_ref, arrived_ref), gate_ref, up_ref)
        token_ref[...] = jnp.zeros_like(token_ref)


def bottom_kernel(takers, place_ref, array_ref, arrived_ref, *refs):
    gate_ref, up_ref, token_ref = refs[-3:]
    spread(chosen(takers, place_ref, array_ref, arrived_ref), gate_ref, up_ref)
    token_ref[...] = jnp.zeros_like(token_ref)


def spread(value, gate_ref, up_ref):
    cols = gate_ref.shape[2]
    for number in range(gate_ref.shape[0]):
        begin = number * 2 * cols
        gate_ref[number] = value[:, begin : begin + cols]
        up_ref[number] = value[:, begin + cols : begin + 2 * cols]


def finish_ffn(is_top, number, cols, hidden_cols, token, place, takers, array, arrived, grads):
    width = array.shape[1]
    half = cols // 2
    squares = width // (2 * cols)
    in_spec = pl.BlockSpec((half, width), lambda i: (i, 0))
    square_shape = jax.ShapeDtypeStruct((squares, 2 * cols, hidden_cols), wide)
    first = 0 if is_top else 1
    square_spec = pl.BlockSpec(
        (squares, half, cols), lambda i: (0, 0 if is_top else i + first, number)
    )
    out_specs = [square_spec, square_spec, kept_out((8, 128))]
    out_shape = [square_shape, square_shape, jax.ShapeDtypeStruct((8, 128), wide)]
    names = ["gate", "up"]
    if is_top:
        out_specs.insert(
            0, pl.BlockSpec((half, width), lambda i: (2 * number + jnp.minimum(i, 1), 0))
        )
        out_shape.insert(0, jax.ShapeDtypeStruct((hidden_cols, width), wide))
        names.insert(0, "down")
    carried = [(i, grads[name]) for i, name in enumerate(names) if name in grads]
    *buffers, token = pl.pallas_call(
        functools.partial(top_kernel if is_top else bottom_kernel, takers),
        name="finish_ffn",
        grid=(3,),
        in_specs=[pl.BlockSpec(memory_space=pltpu.SMEM), in_spec, in_spec, ANYWHERE]
        + [ANYWHERE] * len(carried),
        out_specs=out_specs,
        out_shape=out_shape,
        input_output_aliases={4 + i: target for i, (target, _) in enumerate(carried)},
        compiler_params=params(VMEM_ALONE),
        cost_estimate=SMALL,
    )(place, array, arrived, token, *[buffer for _, buffer in carried])
    grads.update(zip(names, buffers))
    return token


def cut_kernel(takers, place_ref, array_ref, arrived_ref, _, *outs):
    value = chosen(takers, place_ref, array_ref, arrived_ref)
    cols = outs[0].shape[1]
    for number, out in enumerate(outs[:-1]):
        out[...] = value[:, number * cols : (number + 1) * cols]
    outs[-1][...] = jnp.zeros_like(outs[-1])


def finish_cut(pieces, token, place, takers, array, arrived):
    count, width = array.shape
    block = count // 2
    cols = width // pieces
    in_spec = pl.BlockSpec((block, width), lambda i: (i, 0))
    out_spec = pl.BlockSpec((block, cols), lambda i: (i, 0))
    return pl.pallas_call(
        functools.partial(cut_kernel, takers),
        name="finish_cut",
        grid=(2,),
        in_specs=[pl.BlockSpec(memory_space=pltpu.SMEM), in_spec, in_spec, ANYWHERE],
        out_specs=[out_spec] * pieces + [kept_out((8, 128))],
        out_shape=[jax.ShapeDtypeStruct((count, cols), wide)] * pieces
        + [jax.ShapeDtypeStruct((8, 128), wide)],
        compiler_params=params(VMEM_ALONE),
        cost_estimate=SMALL,
    )(place, array, arrived, token)


def tie_kernel(*refs):
    refs[-1][...] = jnp.zeros_like(refs[-1])


def tie(*arrays, estimate=SMALL):
    return pl.pallas_call(
        tie_kernel,
        name="tie",
        in_specs=[ANYWHERE] * len(arrays),
        out_specs=IN_VMEM,
        out_shape=jax.ShapeDtypeStruct((8, 128), wide),
        compiler_params=params(VMEM_ALONE),
        cost_estimate=estimate,
    )(*arrays)


def hold_kernel(*_):
    pass


def hold(array, token, estimate=SMALL):
    return pl.pallas_call(
        hold_kernel,
        name="hold",
        in_specs=[ANYWHERE] * 2,
        out_specs=ANYWHERE,
        out_shape=jax.ShapeDtypeStruct(array.shape, array.dtype),
        input_output_aliases={0: 0},
        compiler_params=params(VMEM_ALONE),
        cost_estimate=estimate,
    )(array, token)


def last_kernel(d_h1_ref, x_ref, d_y1_ref, gain_ref, _, out_ref, d_gain_ref):
    rows = x_ref[...].astype(wide)
    d_rows, d_gain = norm_back(rows, norm_scale(rows), gain_ref[...], d_h1_ref[...].astype(wide))
    out_ref[...] = d_rows + d_y1_ref[...]
    d_gain_ref[...] = d_gain[None]


def last_rows(token, d_h1, x_own, d_y1, gain):
    count, width = d_y1.shape
    return pl.pallas_call(
        last_kernel,
        name="last_rows",
        in_specs=[IN_VMEM] * 4 + [ANYWHERE],
        out_specs=[IN_VMEM] * 2,
        out_shape=[
            jax.ShapeDtypeStruct((count, width), wide),
            jax.ShapeDtypeStruct((1, width), wide),
        ],
        compiler_params=params(VMEM_ALONE),
        cost_estimate=SMALL,
    )(d_h1, x_own, d_y1, gain.reshape(1, width), token)


def kept_out(shape):
    return pl.BlockSpec(shape, lambda *_: (0,) * len(shape))


def sums_kernel(count, wg_ref, wu_ref, wd_ref, *refs):
    hidden, d_gate, d_up = [
        jnp.concatenate([ref[...] for ref in refs[i * count : (i + 1) * count]], axis=1)
        for i in range(3)
    ]
    out_ref = refs[-1]
    devices, both_rows, width = out_ref.shape
    own_rows = both_rows // 2
    d_h2 = dot_rows(d_gate, wg_ref[...]) + dot_rows(d_up, wu_ref[...])
    out_ref[:, :own_rows] = d_h2.astype(low).reshape(devices, own_rows, width)
    mlp = mm(hidden, wd_ref[...])
    out_ref[:, own_rows:] = mlp.astype(low).reshape(devices, own_rows, width)


def ffn_sums(own_rows, w_gate, w_up, w_down, hidden, d_gate, d_up, token):
    count = hidden[0].shape[0]
    width = w_gate.shape[0]
    devices = max(1, 256 // own_rows)

    def row_spec(part):
        return pl.BlockSpec((devices * own_rows, part.shape[1]), lambda i: (i, 0))

    parts = [*hidden, *d_gate, *d_up]
    return pl.pallas_call(
        functools.partial(sums_kernel, len(hidden)),
        name="ffn_sums",
        grid=(count // (devices * own_rows),),
        in_specs=[kept_block(w_gate.shape), kept_block(w_up.shape), kept_block(w_down.shape)]
        + [row_spec(part) for part in parts]
        + [ANYWHERE],
        out_specs=pl.BlockSpec((devices, 2 * own_rows, width), lambda i: (i, 0, 0)),
        out_shape=jax.ShapeDtypeStruct((count // own_rows, 2 * own_rows, width), low),
        compiler_params=params(VMEM_ALONE),
        cost_estimate=SMALL,
    )(w_gate, w_up, w_down, *parts, token)


def own_kernel(sums_ref, y1_ref, cot_ref, gain_ref, w_ref, mixed_ref, _, *refs):
    d_y1_ref, d_mixed_ref, d_w_ref, d_gain_ref, layer_ref = refs
    count = y1_ref.shape[0]
    y1 = y1_ref[...]
    layer_ref[...] = (y1 + sums_ref[count:].astype(wide)).astype(low)
    d_rows, d_gain = norm_back(y1, norm_scale(y1), gain_ref[...], sums_ref[:count].astype(wide))
    d_y1 = d_rows + cot_ref[...].astype(wide)
    d_attn = d_y1.astype(low)
    d_y1_ref[...] = d_y1
    d_gain_ref[...] = d_gain[None]
    d_mixed_ref[...] = dot_rows(d_attn, w_ref[...]).astype(low)
    d_w_ref[...] = dot_cols(mixed_ref[...], d_attn).astype(low)


def own_rows_back(token, sums, y1_own, cot_own, gain, w_out_all, mixed_own):
    count, width = y1_own.shape
    inner = w_out_all.shape[0]
    once = [sums.shape, y1_own.shape, cot_own.shape, (1, width), w_out_all.shape, mixed_own.shape]
    return pl.pallas_call(
        own_kernel,
        name="own_rows_back",
        grid=(1,),
        in_specs=[kept_block(shape) for shape in once] + [ANYWHERE],
        out_specs=[
            kept_block((count, width)),
            kept_block((count, inner)),
            kept_block((inner, width)),
            kept_block((1, width)),
            kept_block((count, width)),
        ],
        out_shape=[
            jax.ShapeDtypeStruct((count, width), wide),
            jax.ShapeDtypeStruct((count, inner), low),
            jax.ShapeDtypeStruct((inner, width), low),
            jax.ShapeDtypeStruct((1, width), wide),
            jax.ShapeDtypeStruct((count, width), low),
        ],
        compiler_params=params(VMEM_ALONE),
        cost_estimate=SMALL,
    )(sums, y1_own, cot_own, gain.reshape(1, width), w_out_all, mixed_own, token)


def qkv_back_kernel(d_qkv_ref, h1_ref, w_ref, d_h1_ref, d_w_ref, total):
    step = pl.program_id(0)
    d_qkv = d_qkv_ref[...]
    d_h1_ref[...] = dot_rows(d_qkv, w_ref[...]).astype(low)
    part = dot_cols(h1_ref[...], d_qkv)

    @pl.when(step == 0)
    def _():
        total[...] = part

    @pl.when(step > 0)
    def _():
        total[...] += part

    @pl.when(step == pl.num_programs(0) - 1)
    def _():
        d_w_ref[...] = total[...].astype(low)


def qkv_back(d_qkv, h1_all, w_qkv):
    count, width = h1_all.shape
    cols = w_qkv.shape[1]
    block = min(ROW_BLOCK, count)
    return pl.pallas_call(
        qkv_back_kernel,
        name="qkv_back",
        grid=(count // block,),
        in_specs=[
            pl.BlockSpec((block, cols), lambda i: (i, 0)),
            pl.BlockSpec((block, width), lambda i: (i, 0)),
            kept_block((width, cols)),
        ],
        out_specs=[pl.BlockSpec((block, width), lambda i: (i, 0)), kept_out((width, cols))],
        out_shape=[
            jax.ShapeDtypeStruct((count, width), low),
            jax.ShapeDtypeStruct((width, cols), low),
        ],
        scratch_shapes=[pltpu.VMEM((width, cols), wide)],
        compiler_params=params(VMEM_ALONE),
        cost_estimate=SMALL,
    )(d_qkv, h1_all, w_qkv)


def join_kernel(takers, place_ref, array_ref, arrived_ref, _, out_ref):
    array, arrived = array_ref[...], arrived_ref[...]
    if takers:
        out_ref[...] = jnp.where(is_one_of(place_ref, takers), arrived, array)
    else:
        out_ref[...] = array + arrived


def join(token, place, takers, array, arrived):
    count, width = array.shape
    block = count // 2
    spec = pl.BlockSpec((block, width), lambda i: (i, 0))
    return pl.pallas_call(
        functools.partial(join_kernel, takers),
        name="join",
        grid=(2,),
        in_specs=[pl.BlockSpec(memory_space=pltpu.SMEM), spec, spec, ANYWHERE],
        out_specs=spec,
        out_shape=jax.ShapeDtypeStruct((count, width), low),
        compiler_params=params(VMEM_ALONE),
        cost_estimate=SMALL,
    )(place, array, arrived, token)


def butterfly(array, axis, size):
    if size & (size - 1):
        return lax.psum(array, axis)
    step = 1
    while step < size:
        array = array + lax.ppermute(array, axis, [(i, i ^ step) for i in range(size)])
        step *= 2
    return array


class Chain:
    def __init__(self, axis, size, place, token):
        self.axis, self.size, self.place, self.token = axis, size, place, token
        half = size // 2
        self.stages = [("in", [(s - 1, s), (size - s, size - 1 - s)]) for s in range(1, half)]
        self.stages.append(("in", [(half - 1, half), (half, half - 1)]))
        self.stages += [("out", [(s, s - 1), (size - 1 - s, size - s)]) for s in range(half - 1, 0, -1)]
        self.waiting = []
        self.moving = [[] for _ in self.stages]

    def push(self, array, land):
        self.waiting.append((land, array))

    def send(self, stage, land, array):
        arrived = lax.ppermute(array, self.axis, self.stages[stage][1])
        self.moving[stage].append((land, array, arrived))

    def move(self, stage):
        land, array, arrived = self.moving[stage].pop(0)
        kind, pairs = self.stages[stage]
        takers = tuple(target for _, target in pairs) if kind == "out" else ()
        last = stage + 1 == len(self.stages)
        if kind == "in" or not last:
            array = join(self.token, self.place, takers, array, arrived)
            arrived, takers = array, ()
            self.token = array
        if last:
            self.token = land(self.token, self.place, takers, array, arrived)
        else:
            self.send(stage + 1, land, array)

    def tick(self, estimate=SMALL):
        if self.size == 1 or self.size % 2:
            for land, array in self.waiting:
                array = lax.psum(array, self.axis)
                self.token = land(self.token, self.place, (), array, array)
            self.waiting = []
            return
        ready = [bool(moving) for moving in self.moving]
        if self.waiting:
            land, array = self.waiting.pop(0)
            array = self.token = hold(array, self.token, estimate)
            self.send(0, land, array)
        for stage, can_move in enumerate(ready):
            if can_move:
                self.move(stage)

    def drain(self):
        while self.waiting or any(self.moving):
            self.tick()


def assemble_kernel(place_ref, *refs):
    *pieces, out_ref = refs
    rows = pieces[0].shape[0]
    for number, piece in enumerate(pieces):
        begin = pl.multiple_of((place_ref[1] ^ number) * rows, rows)
        out_ref[pl.ds(begin, rows)] = piece[...]


def assemble(place, pieces):
    count = len(pieces)
    rows, cols = pieces[0].shape
    return pl.pallas_call(
        assemble_kernel,
        name="assemble",
        in_specs=[pl.BlockSpec(memory_space=pltpu.SMEM)]
        + [pl.BlockSpec(memory_space=pltpu.VMEM)] * count,
        out_specs=pl.BlockSpec(memory_space=pltpu.VMEM),
        out_shape=jax.ShapeDtypeStruct((count * rows, cols), pieces[0].dtype),
        compiler_params=params(24),
        cost_estimate=SMALL,
    )(place, *pieces)


def gather_pieces(array, axis, size):
    if size != 8:
        gathered = lax.all_gather(array, axis, axis=0)
        return [gathered[i] for i in range(size)]

    def flip(value, bits):
        return lax.ppermute(value, axis, [(i, i ^ bits) for i in range(size)])

    half = array.shape[0] // 2
    side_a, side_b = flip(array, 2), flip(array, 4)
    far_a, far_b = flip(side_a[:half], 4), flip(side_b[half:], 2)
    mine = [array, side_a, side_b, jnp.concatenate([far_a, far_b], axis=0)]
    pieces = []
    for piece in mine:
        pieces += [piece, flip(piece, 1)]
    return pieces


def per_device(
    tokens,
    cotangent,
    doc_lengths,
    pad_mask,
    w_query,
    w_key,
    w_value,
    w_out,
    w_gate,
    w_up,
    w_down,
    norm_attn,
    norm_mlp,
    mix_gate,
    *,
    n_heads,
    n_batch,
):
    width = tokens.shape[-1]
    rows = tokens.shape[2]
    own_rows = MICRO * rows
    here = lax.axis_index("heads")

    def gather(array):
        return lax.all_gather(array, "heads", axis=0, tiled=True)

    def scatter(array):
        return lax.psum_scatter(array, "heads", scatter_dimension=0, tiled=True)

    def grouped(array):
        return array.reshape(n_heads, MICRO, rows, array.shape[-1])

    def flat(array):
        return array.reshape(n_heads * own_rows, array.shape[-1])

    w_qkv = jnp.concatenate([w_query, w_key, w_value], axis=1)
    share = jax.nn.sigmoid(mix_gate)
    positions = jnp.arange(LEN, dtype=jnp.int32)
    doc_ends = jnp.cumsum(doc_lengths[:, 0], axis=1)
    doc_ids = jnp.sum((positions[None, :, None] >= doc_ends[:, None, :]).astype(jnp.int32), axis=2)
    doc_rows = doc_ids[:, :, None]
    doc_cols = jnp.where(pad_mask[:, 0] == 1, doc_ids, -1)[:, None, :]

    tok_own = tokens.reshape(own_rows, width)
    cot_own = cotangent.reshape(own_rows, width)
    place = jnp.stack(
        [here, here if n_heads == 8 else jnp.zeros_like(here), lax.axis_index("batch")]
    )
    tok_all = gather(tok_own)
    w_out_all = assemble(place, gather_pieces(w_out, "heads", n_heads))
    tok_all, w_out_all = lax.optimization_barrier((tok_all, w_out_all))
    cot_all = gather(lax.optimization_barrier((cot_own, tok_all))[0])
    h1_all, qkv = qkv_rows(tok_all, norm_attn, w_qkv)
    qkv = grouped(qkv)
    mixed = flat(head_forward(share, qkv, doc_rows, doc_cols))
    mixed_pieces = gather_pieces(mixed, "heads", n_heads)
    h2_all, y1_own, mixed_own = mid_rows(place, tok_all, mixed_pieces, w_out_all, norm_mlp)

    chain = Chain("batch", n_batch, place, norm_mlp)
    hidden_cols = w_gate.shape[1]
    cols = hidden_cols // FFN_CHUNKS
    grads = {}

    def push_ffn(number, top, bottom):
        for is_top, part in ((True, top), (False, bottom)):
            chain.push(
                part,
                lambda *moved, is_top=is_top: finish_ffn(
                    is_top, number, cols, hidden_cols, *moved, grads
                ),
            )

    def land_qkv(*moved):
        *grads["qkv"], token = finish_cut(3, *moved)
        return token

    def land_out(*moved):
        grads["out"], token = finish_cut(1, *moved)
        return token

    def first(number):
        *parts, top, bottom = ffn_first(
            number, cols, h2_all, cot_all, w_gate, w_up, w_down, chain.token
        )
        chain.token = top
        push_ffn(number, top, bottom)
        return parts

    def weights(number, parts):
        top, bottom = ffn_weights(number - 2, cols, h2_all, cot_all, *parts, chain.token)
        chain.token = top
        push_ffn(number, top, bottom)

    def wait_for(microseconds):
        chain.token = tie(chain.token, estimate=busy(microseconds))

    part_a = first(0)
    chain.tick()
    part_b = first(1)
    chain.tick()
    part_c = ffn_rest(h2_all, cot_all, w_gate, w_up, w_down, chain.token)
    chain.token = part_c[0]
    chain.tick()
    sums = chain.token = ffn_sums(
        own_rows, w_gate, w_up, w_down, *zip(part_a, part_b, part_c), chain.token
    )
    sums = scatter(sums.reshape(-1, width))
    chain.tick()
    weights(2, part_c)
    weights(3, part_c)
    chain.tick()
    chain.tick()
    chain.tick()

    wait_for(WAITS[0])
    d_y1, d_mixed_own, grad_out, gain_mlp_part, layer_out = own_rows_back(
        chain.token, sums, y1_own, cot_own, norm_mlp, w_out_all, mixed_own
    )
    chain.token = d_y1
    d_mixed = lax.all_to_all(d_mixed_own, "heads", split_axis=1, concat_axis=0, tiled=True)
    grad_out = scatter(grad_out)
    chain.tick()
    wait_for(WAITS[3])
    d_qkv, d_share = head_backward(
        share, qkv, grouped(d_mixed), doc_rows, doc_cols, chain.token
    )
    d_h1, grad_qkv = qkv_back(flat(d_qkv), h1_all, w_qkv)
    chain.token = grad_qkv
    d_h1 = scatter(d_h1)
    chain.push(grad_qkv, land_qkv)
    chain.tick()
    wait_for(WAITS[1])
    chain.push(grad_out, land_out)
    chain.tick()
    chain.tick()

    wait_for(WAITS[2])
    grad_tokens, gain_attn_part = last_rows(chain.token, d_h1, tok_own, d_y1, norm_attn)
    grad_tokens = grad_tokens.reshape(tokens.shape)
    chain.token = gain_attn_part
    slots = jnp.where(jnp.arange(n_heads) == here, jnp.sum(d_share[:, 0, 0]), 0.0)
    sums = jnp.concatenate([gain_attn_part[0], gain_mlp_part[0], slots])
    sums = butterfly(butterfly(sums, "heads", n_heads), "batch", n_batch)
    grad_mix = lax.dynamic_slice_in_dim(sums, 2 * width + here, 1, 0)
    chain.drain()

    return (
        layer_out.reshape(tokens.shape),
        grad_tokens,
        *grads["qkv"],
        grads["out"],
        grads["gate"].reshape(w_gate.shape),
        grads["up"].reshape(w_up.shape),
        grads["down"],
        sums[:width],
        sums[width : 2 * width],
        grad_mix,
    )


def solution(mesh):
    in_specs = (
        P(None, "batch", "heads", None),
        P(None, "batch", "heads", None),
        P(None, "batch", None),
        P(None, "batch", None),
        P(None, "heads"),
        P(None, "heads"),
        P(None, "heads"),
        P("heads", None),
        P(None, "heads"),
        P(None, "heads"),
        P("heads", None),
        P(),
        P(),
        P("heads"),
    )
    out_specs = (
        P(None, "batch", "heads", None),
        P(None, "batch", "heads", None),
        P(None, "heads"),
        P(None, "heads"),
        P(None, "heads"),
        P("heads", None),
        P(None, "heads"),
        P(None, "heads"),
        P("heads", None),
        P(),
        P(),
        P("heads"),
    )

    def program(*arrays):
        return per_device(*arrays, n_heads=mesh.shape["heads"], n_batch=mesh.shape["batch"])

    return jax.shard_map(
        program, mesh=mesh, in_specs=in_specs, out_specs=out_specs, check_vma=False
    )
```

time: 862 us -> 697 us (0.81)
  Pallas kernels: 0 us -> 304 us
  matrix products: 207 us -> 0 us
  waiting for transfers between devices: 344 us -> 223 us
  other arithmetic: 95.5 us -> 3.73 us
  blocking collectives: 38 us -> 0 us
    pallas_call x0 -> x58, Pallas kernels: none -> 304 us  [the longest x20 57.9 us: join(): pl.pallas_call(functools.partial(join_kernel, takers), name='join', grid=...]
    dot_general x38 -> x0, matrix products: 202 us -> none  [the longest x14 78 us: dot_cols(): lax.dot_general(left_mat, right_mat, (((0,), (0,)), ((), ())), preferred_...]
    reduce_scatter x4 -> x3, waiting for transfers between devices: 56.8 us -> 0.01 us  [scatter(): return lax.psum_scatter(array, 'heads', scatter_dimension=0, tiled=True)]
    add x30 -> x5, other arithmetic: 42.2 us -> 0.02 us  [butterfly(): array + lax.ppermute(array, axis, [(i, i ^ step) for i in range(size)])]
    all_gather x1 -> x0, waiting for transfers between devices: 39.9 us -> none  [per_device(): mixed_all = lax.all_gather(mixed, 'heads', axis=1, tiled=True)]
    psum x1 -> x0, blocking collectives: 38 us -> none  [per_device(): lax.psum(jnp.concatenate([gain_attn_part, gain_mlp_part, slots]), ('heads...]
    all_gather x3 -> x2, waiting for transfers between devices: 64.4 us -> 28.2 us  [gather(): return lax.all_gather(array, 'heads', axis=0, tiled=True)]
    slice x7 -> x4, local copies, waits for them, and re-layouts: 13.8 us -> 0.07 us  [gather_pieces(): far_a, far_b = (flip(side_a[:half], 4), flip(side_b[half:], 2))]
  transfers between devices with their start and end apart: 51 -> 57, of which waited for: 17 -> 25; matrix products, arithmetic and copies ran while one was open for 33% -> 1% of each run, Pallas kernels for 0% -> 39%
where the time goes in v2:
time: 697 us; the launch traced here: 685 us
  Pallas kernels  304 us (44%)
  waiting for transfers between devices  223 us (32%)
  starting transfers between devices  102 us (15%)
  local copies, waits for them, and re-layouts  36.9 us (5%)
  between operations  15.7 us (2%)
    ppermute x30, waiting for transfers between devices, send(): arrived = lax.ppermute(array, self.axis, self.stages[stage][1])  106 us
    ppermute x30, starting transfers between devices, send(): arrived = lax.ppermute(array, self.axis, self.stages[stage][1])  83.2 us
    ppermute x16, waiting for transfers between devices, flip(): return lax.ppermute(value, axis, [(i, i ^ bits) for i in range(size)])  61.3 us
    pallas_call x20, Pallas kernels, join(): pl.pallas_call(functools.partial(join_kernel, takers), name='join', grid=...  57.9 us
    pallas_call x2, Pallas kernels, ffn_first(): pl.pallas_call(functools.partial(first_kernel, blocks), name='ffn_first',...  47.2 us
    pallas_call x8, Pallas kernels, finish_ffn(): pl.pallas_call(functools.partial(top_kernel if is_top else bottom_kernel,...  35.8 us
    pallas_call x1, Pallas kernels, ffn_sums(): pl.pallas_call(functools.partial(sums_kernel, len(hidden)), name='ffn_sum...  34.7 us
    unnamed x78, local copies, waits for them, and re-layouts  33.2 us
  transfers between devices with their start and end apart: 57, of which 25 were waited for; matrix products, arithmetic and copies ran while one was open for 1% of the time, Pallas kernels for 39%

profile of v2, /device:TPU:0, one launch (start us, length us, event | category | flops | bytes accessed | tf_op | source)
XLA Modules:
  0.0 684.7 jit_solution(17483975095395298097)
XLA Ops:
  8.0 3.0 collective-permute-start.1
  12.5 12.4 %collective-permute-done.1.refs_2_ = bf16[128,2048]{1,0:T(8,128)(2,1)S(1)} collective-permute-done((bf16[128,2048]{1,0:T(8,128)(2,1)}, bf16[128,2048]{1,0:T(8,128)(2,1)S(1)}, u32[]{:S(2)}, u32[]{:S(2)}) %collective-permute-start.1) | collective-permute-done | bytes 524320 | tf_op jit(solution)/shard_map/ppermute | solution.py:848
  29.3 9.3 %collective-permute-done.5 = bf16[64,2048]{1,0:T(8,128)(2,1)S(1)} collective-permute-done((bf16[64,2048]{1,0:T(8,128)(2,1)S(1)}, bf16[64,2048]{1,0:T(8,128)(2,1)S(1)}, u32[]{:S(2)}, u32[]{:S(2)}) %collective-permute-start.5) | collective-permute-done | bytes 262176 | tf_op jit(solution)/shard_map/ppermute | solution.py:848
  45.7 28.2 %all-gather.3.cloned.1.call-done.x_ref = bf16[2048,2048]{1,0:T(8,128)(2,1)} async-done(((bf16[256,2048]{1,0:T(8,128)(2,1)}), bf16[2048,2048]{1,0:T(8,128)(2,1)}) %all-gather.3.cloned.1.call-update) | async-done | bytes 8388624 | tf_op jit(solution)/shard_map/all_gather | solution.py:885
  78.5 10.6 %qkv_rows.1 = (bf16[2048,2048]{1,0:T(8,128)(2,1)}, bf16[2048,384]{1,0:T(8,128)(2,1)}) custom-call(bf16[2048,2048]{1,0:T(8,128)(2,1)} %all-gather.3.cloned.1.call-done.x_ref, f32[1,2048]{1,0:T(1,128)} %bitcast.52, bf16[2048,384]{1,0:T(8,128)(2,1)} %copy-done.11), custom_call_target="tpu_custom_call" | custom-call | flops 1 | bytes 1 | tf_op jit(solution)/shard_map/qkv_rows/pallas_call | solution.py:88
  89.1 5.8 head_forward.1
  96.5 17.0 %collective-permute-done.9.refs_2_ = bf16[2048,128]{1,0:T(8,128)(2,1)S(1)} collective-permute-done((bf16[2048,128]{1,0:T(8,128)(2,1)}, bf16[2048,128]{1,0:T(8,128)(2,1)S(1)}, u32[]{:S(2)}, u32[]{:S(2)}) %collective-permute-start.9) | collective-permute-done | bytes 524320 | tf_op jit(solution)/shard_map/ppermute | solution.py:848
  117.3 10.3 %collective-permute-done.13 = bf16[1024,128]{1,0:T(8,128)(2,1)S(1)} collective-permute-done((bf16[1024,128]{1,0:T(8,128)(2,1)S(1)}, bf16[1024,128]{1,0:T(8,128)(2,1)S(1)}, u32[]{:S(2)}, u32[]{:S(2)}) %collective-permute-start.13) | collective-permute-done | bytes 262176 | tf_op jit(solution)/shard_map/ppermute | solution.py:848
  134.4 14.9 %mid_rows.1 = (bf16[2048,2048]{1,0:T(8,128)(2,1)S(1)}, f32[256,2048]{1,0:T(8,128)S(1)}, bf16[256,1024]{1,0:T(8,128)(2,1)S(1)}) custom-call(s32[3]{0:T(128)S(1)} %pad_add_fusion.place_ref, bf16[2048,2048]{1,0:T(8,128)(2,1)} %all-gather.3.cloned.1.call-done.x_ref, bf16[2048,128]{1,0:T(8,128)(2,1)S(1)} %bitcast.33, ...), custom_call_target="tpu_custom_call" | custom-call | flops 1 | bytes 1 | tf_op jit(solution)/shard_map/mid_rows/pallas_call | solution.py:292
  149.3 3.3 copy-done
  154.7 23.6 %ffn_first.2 = (bf16[2048,256]{1,0:T(8,128)(2,1)}, bf16[2048,256]{1,0:T(8,128)(2,1)}, bf16[2048,256]{1,0:T(8,128)(2,1)}, bf16[384,2048]{1,0:T(8,128)(2,1)}, bf16[384,2048]{1,0:T(8,128)(2,1)}) custom-call(bf16[2048,2048]{1,0:T(8,128)(2,1)} %copy-done, bf16[2048,2048]{1,0:T(8,128)(2,1)} %all-gather.5.cloned.1.call-done.cot_ref.cot_col_ref, ...), custom_call_target="tpu_custom_call" | custom-call | flops 1 | bytes 1 | tf_op jit(solution)/shard_map/ffn_first/pallas_call | solution.py:376
  181.0 3.6 collective-permute-start.16
  184.7 23.6 %ffn_first.3 = (bf16[2048,256]{1,0:T(8,128)(2,1)}, bf16[2048,256]{1,0:T(8,128)(2,1)}, bf16[2048,256]{1,0:T(8,128)(2,1)}, bf16[384,2048]{1,0:T(8,128)(2,1)}, bf16[384,2048]{1,0:T(8,128)(2,1)}) custom-call(bf16[2048,2048]{1,0:T(8,128)(2,1)} %copy-done, bf16[2048,2048]{1,0:T(8,128)(2,1)} %all-gather.5.cloned.1.call-done.cot_ref.cot_col_ref, ...), custom_call_target="tpu_custom_call" | custom-call | flops 1 | bytes 1 | tf_op jit(solution)/shard_map/ffn_first/pallas_call | solution.py:376
  209.7 9.8 %collective-permute-done.16.arrived_ref = bf16[384,2048]{1,0:T(8,128)(2,1)S(1)} collective-permute-done((bf16[384,2048]{1,0:T(8,128)(2,1)}, bf16[384,2048]{1,0:T(8,128)(2,1)S(1)}, u32[]{:S(2)}, u32[]{:S(2)}) %collective-permute-start.16) | collective-permute-done | bytes 1572896 | tf_op jit(solution)/shard_map/ppermute | solution.py:781
  220.6 2.9 join.20._.array_ref
  225.2 19.5 %ffn_rest.1 = (bf16[2048,512]{1,0:T(8,128)(2,1)}, bf16[2048,512]{1,0:T(8,128)(2,1)}, bf16[2048,512]{1,0:T(8,128)(2,1)}) custom-call(bf16[2048,2048]{1,0:T(8,128)(2,1)} %copy-done, bf16[2048,2048]{1,0:T(8,128)(2,1)} %all-gather.5.cloned.1.call-done.cot_ref.cot_col_ref, bf16[2048,1024]{1,0:T(8,128)(2,1)} %wg_ref.7, bf16[2048,1024]{1,0:T(8,128)(2,1)} %wu_ref.7, ...), custom_call_target="tpu_custom_call" | custom-call | flops 1 | bytes 1 | tf_op jit(solution)/shard_map/ffn_rest/pallas_call | solution.py:403
  244.8 6.0 collective-permute-start.22
  254.3 2.8 join.21._.array_ref
  257.9 2.9 join.22.refs_9_.array_ref
  262.1 34.7 %ffn_sums.1.__1_ = bf16[8,512,2048]{2,1,0:T(8,128)(2,1)} custom-call(bf16[2048,1024]{1,0:T(8,128)(2,1)} %wg_ref.7, bf16[2048,1024]{1,0:T(8,128)(2,1)} %wu_ref.7, bf16[1024,2048]{1,0:T(8,128)(2,1)} %wd_ref.7, bf16[2048,256]{1,0:T(8,128)(2,1)} %get-tuple-element.86.refs_0_, bf16[2048,256]{1,0:T(8,128)(2,1)} %get-tuple-element.88.refs_1_, ...), custom_call_target="tpu_custom_call" | custom-call | flops 1 | bytes 1 | tf_op jit(solution)/shard_map/ffn_sums/pallas_call | solution.py:634
  296.8 9.2 %collective-permute-start.19 = (bf16[384,2048]{1,0:T(8,128)(2,1)}, bf16[384,2048]{1,0:T(8,128)(2,1)}, u32[]{:S(2)}, u32[]{:S(2)}) collective-permute-start(bf16[384,2048]{1,0:T(8,128)(2,1)} %hold.13._.array_ref), channel_id=1, source_target_pairs={{0,1},{3,2},{4,5},{7,6},{8,9},{11,10},{12,13},{15,14},{16,17},{19,... | collective-permute-start | bytes 4718600 | tf_op jit(solution)/shard_map/ppermute | solution.py:781
  307.2 2.8 join.23._.array_ref
  312.0 3.5 join.24.refs_0_.array_ref
  316.9 4.9 finish_ffn.8
  321.8 14.8 %ffn_weights.2 = (bf16[384,2048]{1,0:T(8,128)(2,1)}, bf16[384,2048]{1,0:T(8,128)(2,1)}) custom-call(bf16[2048,2048]{1,0:T(8,128)(2,1)} %copy-done, bf16[2048,2048]{1,0:T(8,128)(2,1)} %all-gather.5.cloned.1.call-done.cot_ref.cot_col_ref, bf16[2048,512]{1,0:T(8,128)(2,1)} %get-tuple-element.91.__1_.refs_2_.hid_ref, ...), custom_call_target="tpu_custom_call" | custom-call | flops 1 | bytes 1 | tf_op jit(solution)/shard_map/ffn_weights/pallas_call | solution.py:433
  336.6 12.9 %ffn_weights.3 = (bf16[384,2048]{1,0:T(8,128)(2,1)}, bf16[384,2048]{1,0:T(8,128)(2,1)}) custom-call(bf16[2048,2048]{1,0:T(8,128)(2,1)} %copy-done, bf16[2048,2048]{1,0:T(8,128)(2,1)} %all-gather.5.cloned.1.call-done.cot_ref.cot_col_ref, bf16[2048,512]{1,0:T(8,128)(2,1)} %get-tuple-element.91.__1_.refs_2_.hid_ref, ...), custom_call_target="tpu_custom_call" | custom-call | flops 1 | bytes 1 | tf_op jit(solution)/shard_map/ffn_weights/pallas_call | solution.py:433
  349.5 5.4 collective-permute-start.24
  355.0 3.0 join.25._.array_ref
  361.0 2.9 join.26.refs_0_.array_ref
  366.3 4.5 finish_ffn.9
  370.9 5.7 collective-permute-start.29
  376.6 12.3 %collective-permute-done.24.arrived_ref = bf16[384,2048]{1,0:T(8,128)(2,1)} collective-permute-done((bf16[384,2048]{1,0:T(8,128)(2,1)}, bf16[384,2048]{1,0:T(8,128)(2,1)}, u32[]{:S(2)}, u32[]{:S(2)}) %collective-permute-start.24) | collective-permute-done | bytes 1572896 | tf_op jit(solution)/shard_map/ppermute | solution.py:781
  388.9 2.8 join.27._.array_ref
  393.6 3.5 join.28.refs_0_.array_ref
  398.4 4.9 collective-permute-done.30.arrived_ref
  404.5 4.5 finish_ffn.10
  408.9 10.9 %collective-permute-done.29.arrived_ref = bf16[384,2048]{1,0:T(8,128)(2,1)} collective-permute-done((bf16[384,2048]{1,0:T(8,128)(2,1)}, bf16[384,2048]{1,0:T(8,128)(2,1)}, u32[]{:S(2)}, u32[]{:S(2)}) %collective-permute-start.29) | collective-permute-done | bytes 1572896 | tf_op jit(solution)/shard_map/ppermute | solution.py:781
  419.8 2.9 join.29._.array_ref
  422.7 2.8 join.30.refs_0_.array_ref
  425.6 8.1 %collective-permute-done.27.arrived_ref = bf16[384,2048]{1,0:T(8,128)(2,1)S(1)} collective-permute-done((bf16[384,2048]{1,0:T(8,128)(2,1)}, bf16[384,2048]{1,0:T(8,128)(2,1)S(1)}, u32[]{:S(2)}, u32[]{:S(2)}) %collective-permute-start.27) | collective-permute-done | bytes 1572896 | tf_op jit(solution)/shard_map/ppermute | solution.py:781
  434.8 4.4 finish_ffn.11
  439.7 9.3 %own_rows_back.1 = (f32[256,2048]{1,0:T(8,128)}, bf16[256,1024]{1,0:T(8,128)(2,1)}, bf16[1024,2048]{1,0:T(8,128)(2,1)}, f32[1,2048]{1,0:T(1,128)}, bf16[256,2048]{1,0:T(8,128)(2,1)}) custom-call(bf16[512,2048]{1,0:T(8,128)(2,1)} %reduce-scatter.4.cloned.1.call-done.sums_ref, f32[256,2048]{1,0:T(8,128)} %copy-done.4, bf16[256,2048]{1,0:T(8,128)(2,1)} %bitcast.44, ...), custom_call_target="tpu_custom_call" | custom-call | flops 1 | bytes 1 | tf_op jit(solution)/shard_map/own_rows_back/pallas_call | solution.py:666
  456.3 6.8 collective-permute-start.34
  463.1 23.8 %collective-permute-done.33.arrived_ref = bf16[384,2048]{1,0:T(8,128)(2,1)} collective-permute-done((bf16[384,2048]{1,0:T(8,128)(2,1)S(1)}, bf16[384,2048]{1,0:T(8,128)(2,1)}, u32[]{:S(2)}, u32[]{:S(2)}) %collective-permute-start.33) | collective-permute-done | bytes 1572896 | tf_op jit(solution)/shard_map/ppermute | solution.py:781
  491.7 2.8 join.32.refs_0_.array_ref
  496.7 3.5 all-to-all-start
  500.5 4.4 finish_ffn.12
  505.5 4.4 all-to-all-done
  510.7 10.6 %head_backward.1 = (bf16[8,2,128,384]{3,2,1,0:T(8,128)(2,1)}, f32[2,8,128]{2,1,0:T(8,128)}) custom-call(f32[1]{0:T(128)S(6)} %div.3.share_ref, bf16[8,2,128,384]{3,2,1,0:T(8,128)(2,1)} %bitcast.40, bf16[8,2,128,128]{3,2,1,0:T(8,128)(2,1)} %bitcast.45, s32[2,1024,1]{2,1,0:T(8,128)} %copy.61.doc_rows_ref, s32[2,1,1024]{2,1,0:T(1,128)} %compare_select_fusion.doc_cols_ref, ...), custom_call_target="tpu_custom_call" | custom-call | flops 1 | bytes 1 | tf_op jit(solution)/shard_map/head_backward/pallas_call | solution.py:240
  521.3 14.9 %qkv_back.1 = (bf16[2048,2048]{1,0:T(8,128)(2,1)}, bf16[2048,384]{1,0:T(8,128)(2,1)}) custom-call(bf16[2048,384]{1,0:T(8,128)(2,1)} %bitcast.46, bf16[2048,2048]{1,0:T(8,128)(2,1)} %get-tuple-element.124.h1_ref, bf16[2048,384]{1,0:T(8,128)(2,1)} %copy-done.11), custom_call_target="tpu_custom_call" | custom-call | flops 1 | bytes 1 | tf_op jit(solution)/shard_map/qkv_back/pallas_call | solution.py:713
  538.8 7.1 %collective-permute-start.36 = (bf16[2048,384]{1,0:T(8,128)(2,1)}, bf16[2048,384]{1,0:T(8,128)(2,1)S(1)}, u32[]{:S(2)}, u32[]{:S(2)}) collective-permute-start(bf16[2048,384]{1,0:T(8,128)(2,1)} %hold.18._.array_ref), channel_id=1, source_target_pairs={{0,1},{3,2},{4,5},{7,6},{8,9},{11,10},{12,13},{15,14},{16,17},{19,... | collective-permute-start | bytes 4718600 | tf_op jit(solution)/shard_map/ppermute | solution.py:781
  545.9 3.5 join.33._.array_ref
  551.2 3.3 join.34.refs_0_.array_ref
  555.9 4.4 finish_ffn.13
  560.9 16.5 %collective-permute-done.36.arrived_ref = bf16[2048,384]{1,0:T(8,128)(2,1)S(1)} collective-permute-done((bf16[2048,384]{1,0:T(8,128)(2,1)}, bf16[2048,384]{1,0:T(8,128)(2,1)S(1)}, u32[]{:S(2)}, u32[]{:S(2)}) %collective-permute-start.36) | collective-permute-done | bytes 1572896 | tf_op jit(solution)/shard_map/ppermute | solution.py:781
  578.5 2.9 join.35._.array_ref
  587.5 6.2 collective-permute-start.41
  596.8 4.3 finish_ffn.14
  604.6 2.9 join.38.refs_0_.array_ref
  608.8 17.4 %collective-permute-done.39.arrived_ref = bf16[384,2048]{1,0:T(8,128)(2,1)S(1)} collective-permute-done((bf16[384,2048]{1,0:T(8,128)(2,1)}, bf16[384,2048]{1,0:T(8,128)(2,1)S(1)}, u32[]{:S(2)}, u32[]{:S(2)}) %collective-permute-start.39) | collective-permute-done | bytes 1572896 | tf_op jit(solution)/shard_map/ppermute | solution.py:781
  627.4 4.4 finish_ffn.15
  632.4 5.5 last_rows.1
  652.4 16.6 %collective-permute-done.49 = f32[4104]{0:T(1024)S(1)} collective-permute-done((f32[4104]{0:T(1024)S(1)}, f32[4104]{0:T(1024)S(1)}, u32[]{:S(2)}, u32[]{:S(2)}) %collective-permute-start.49) | collective-permute-done | bytes 16448 | tf_op jit(solution)/shard_map/ppermute | solution.py:762
  670.1 3.2 finish_cut.2
  (214 shorter events, 119.2 us)
Async XLA Ops:
  7.2 21.6 %copy-start.5 = (bf16[128,2048]{1,0:T(8,128)(2,1)S(1)}, bf16[128,2048]{1,0:T(8,128)(2,1)}, u32[]{:S(2)}) copy-start(bf16[128,2048]{1,0:T(8,128)(2,1)} %refs_0_.1) | copy-start | bytes 1572868
  7.2 66.7 %all-gather.3.cloned.1.call-start = ((), (), s32[]{:S(2)}) async-start(), calls=%async_computation.4 | async-start | bytes 9437184 | tf_op jit(solution)/shard_map/all_gather | solution.py:885
  7.9 146.8 %all-gather.5.cloned.1.call-start = ((), (), s32[]{:S(2)}) async-start(), calls=%async_computation.5 | async-start | bytes 9437184 | tf_op jit(solution)/shard_map/all_gather | solution.py:885
  8.0 16.9 %collective-permute-start.1 = (bf16[128,2048]{1,0:T(8,128)(2,1)}, bf16[128,2048]{1,0:T(8,128)(2,1)S(1)}, u32[]{:S(2)}, u32[]{:S(2)}) collective-permute-start(bf16[128,2048]{1,0:T(8,128)(2,1)} %refs_0_.1), channel_id=1, source_target_pairs={{0,8},{4,12},{8,0},{12,4},{16,24},{20,28},{24,16},{28,20},{1,9},{5... | collective-permute-start | bytes 1572872 | tf_op jit(solution)/shard_map/ppermute | solution.py:848
  11.0 17.2 %collective-permute-start.3 = (bf16[128,2048]{1,0:T(8,128)(2,1)}, bf16[128,2048]{1,0:T(8,128)(2,1)S(1)}, u32[]{:S(2)}, u32[]{:S(2)}) collective-permute-start(bf16[128,2048]{1,0:T(8,128)(2,1)} %refs_0_.1), channel_id=1, source_target_pairs={{0,16},{4,20},{8,24},{12,28},{16,0},{20,4},{24,8},{28,12},{1,17},{... | collective-permute-start | bytes 1572872 | tf_op jit(solution)/shard_map/ppermute | solution.py:848
  24.9 13.7 %collective-permute-start.5 = (bf16[64,2048]{1,0:T(8,128)(2,1)S(1)}, bf16[64,2048]{1,0:T(8,128)(2,1)S(1)}, u32[]{:S(2)}, u32[]{:S(2)}) collective-permute-start(bf16[64,2048]{1,0:T(8,128)(2,1)S(1)} %slice.28), channel_id=1, source_target_pairs={{0,16},{4,20},{8,24},{12,28},{16,0},{20,4},{24,8},{28,12},{1,17},{... | collective-permute-start | bytes 786440 | tf_op jit(solution)/shard_map/ppermute | solution.py:848
  28.2 11.8 %collective-permute-start.6 = (bf16[64,2048]{1,0:T(8,128)(2,1)S(1)}, bf16[64,2048]{1,0:T(8,128)(2,1)S(1)}, u32[]{:S(2)}, u32[]{:S(2)}) collective-permute-start(bf16[64,2048]{1,0:T(8,128)(2,1)S(1)} %slice.29), channel_id=1, source_target_pairs={{0,8},{4,12},{8,0},{12,4},{16,24},{20,28},{24,16},{28,20},{1,9},{5... | collective-permute-start | bytes 786440 | tf_op jit(solution)/shard_map/ppermute | solution.py:848
  28.8 11.4 %collective-permute-start = (bf16[128,2048]{1,0:T(8,128)(2,1)S(1)}, bf16[128,2048]{1,0:T(8,128)(2,1)S(1)}, u32[]{:S(2)}, u32[]{:S(2)}) collective-permute-start(bf16[128,2048]{1,0:T(8,128)(2,1)S(1)} %copy-done.5), channel_id=1, source_target_pairs={{0,4},{4,0},{8,12},{12,8},{16,20},{20,16},{24,28},{28,24},{1,5},{5... | collective-permute-start | bytes 1572872 | tf_op jit(solution)/shard_map/ppermute | solution.py:848
  28.8 11.4 %collective-permute-start.2 = (bf16[128,2048]{1,0:T(8,128)(2,1)S(1)}, bf16[128,2048]{1,0:T(8,128)(2,1)S(1)}, u32[]{:S(2)}, u32[]{:S(2)}) collective-permute-start(bf16[128,2048]{1,0:T(8,128)(2,1)S(1)} %collective-permute-done.1.refs_2_), channel_id=1, source_target_pairs={{0,4},{4,0},{8,12},{12,8},{16,20},{20,16},{24,28},{28,24},{1,5},{5... | collective-permute-start | bytes 1572872 | tf_op jit(solution)/shard_map/ppermute | solution.py:848
  29.3 10.9 %collective-permute-start.4 = (bf16[128,2048]{1,0:T(8,128)(2,1)S(1)}, bf16[128,2048]{1,0:T(8,128)(2,1)}, u32[]{:S(2)}, u32[]{:S(2)}) collective-permute-start(bf16[128,2048]{1,0:T(8,128)(2,1)S(1)} %collective-permute-done.3.refs_4_), channel_id=1, source_target_pairs={{0,4},{4,0},{8,12},{12,8},{16,20},{20,16},{24,28},{28,24},{1,5},{5... | collective-permute-start | bytes 1572872 | tf_op jit(solution)/shard_map/ppermute | solution.py:848
  40.0 2.1 collective-permute-start.7
  40.2 92.0 %copy-start.7 = (s32[3]{0:T(128)}, s32[3]{0:T(128)S(1)}, u32[]{:S(2)}) copy-start(s32[3]{0:T(128)S(1)} %pad_add_fusion.place_ref) | copy-start | bytes 40
  40.2 34.6 %copy-start.35 = (s32[2,1,4]{2,1,0:T(1,128)S(1)}, s32[2,1,4]{2,1,0:T(1,128)}, u32[]{:S(2)}) copy-start(s32[2,1,4]{2,1,0:T(1,128)} %param.16) | copy-start | bytes 100
  45.7 30.7 %copy-start.34 = (s32[2,1,1024]{2,1,0:T(1,128)S(1)}, s32[2,1,1024]{2,1,0:T(1,128)}, u32[]{:S(2)}) copy-start(s32[2,1,1024]{2,1,0:T(1,128)} %param.17) | copy-start | bytes 24580
  45.7 31.3 %copy-start.27 = (bf16[2048,128]{1,0:T(8,128)(2,1)S(1)}, bf16[2048,128]{1,0:T(8,128)(2,1)}, u32[]{:S(2)}) copy-start(bf16[2048,128]{1,0:T(8,128)(2,1)} %param.18) | copy-start | bytes 1572868
  73.9 365.8 %reduce-scatter.4.cloned.1.call-start = ((), (), s32[]{:S(2)}) async-start(), calls=%async_computation.6 | async-start | bytes 18874368 | tf_op jit(solution)/shard_map/reduce_scatter | solution.py:888
  94.9 37.2 %copy-start.3 = (bf16[8,2,128,128]{3,2,1,0:T(8,128)(2,1)S(1)}, bf16[8,2,128,128]{3,2,1,0:T(8,128)(2,1)}, u32[]{:S(2)}) copy-start(bf16[8,2,128,128]{3,2,1,0:T(8,128)(2,1)} %head_forward.1) | copy-start | bytes 1572868
  94.9 37.2 %copy-start.8 = (f32[2048]{0:T(1024)S(1)}, f32[2048]{0:T(1024)}, u32[]{:S(2)}) copy-start(f32[2048]{0:T(1024)} %_.1) | copy-start | bytes 24580
  94.9 18.6 %collective-permute-start.9 = (bf16[2048,128]{1,0:T(8,128)(2,1)}, bf16[2048,128]{1,0:T(8,128)(2,1)S(1)}, u32[]{:S(2)}, u32[]{:S(2)}) collective-permute-start(bf16[2048,128]{1,0:T(8,128)(2,1)} %bitcast.30), channel_id=1, source_target_pairs={{0,8},{4,12},{8,0},{12,4},{16,24},{20,28},{24,16},{28,20},{1,9},{5... | collective-permute-start | bytes 1572872 | tf_op jit(solution)/shard_map/ppermute | solution.py:848
  96.4 20.1 %collective-permute-start.11 = (bf16[2048,128]{1,0:T(8,128)(2,1)}, bf16[2048,128]{1,0:T(8,128)(2,1)S(1)}, u32[]{:S(2)}, u32[]{:S(2)}) collective-permute-start(bf16[2048,128]{1,0:T(8,128)(2,1)} %bitcast.31), channel_id=1, source_target_pairs={{0,16},{4,20},{8,24},{12,28},{16,0},{20,4},{24,8},{28,12},{1,17},{... | collective-permute-start | bytes 1572872 | tf_op jit(solution)/shard_map/ppermute | solution.py:848
  113.5 14.1 %collective-permute-start.13 = (bf16[1024,128]{1,0:T(8,128)(2,1)S(1)}, bf16[1024,128]{1,0:T(8,128)(2,1)S(1)}, u32[]{:S(2)}, u32[]{:S(2)}) collective-permute-start(bf16[1024,128]{1,0:T(8,128)(2,1)S(1)} %slice.30), channel_id=1, source_target_pairs={{0,16},{4,20},{8,24},{12,28},{16,0},{20,4},{24,8},{28,12},{1,17},{... | collective-permute-start | bytes 786440 | tf_op jit(solution)/shard_map/ppermute | solution.py:848
  116.5 13.4 %collective-permute-start.14 = (bf16[1024,128]{1,0:T(8,128)(2,1)S(1)}, bf16[1024,128]{1,0:T(8,128)(2,1)S(1)}, u32[]{:S(2)}, u32[]{:S(2)}) collective-permute-start(bf16[1024,128]{1,0:T(8,128)(2,1)S(1)} %slice.31), channel_id=1, source_target_pairs={{0,8},{4,12},{8,0},{12,4},{16,24},{20,28},{24,16},{28,20},{1,9},{5... | collective-permute-start | bytes 786440 | tf_op jit(solution)/shard_map/ppermute | solution.py:848
  116.6 13.5 %collective-permute-start.8 = (bf16[2048,128]{1,0:T(8,128)(2,1)}, bf16[2048,128]{1,0:T(8,128)(2,1)S(1)}, u32[]{:S(2)}, u32[]{:S(2)}) collective-permute-start(bf16[2048,128]{1,0:T(8,128)(2,1)} %bitcast.32), channel_id=1, source_target_pairs={{0,4},{4,0},{8,12},{12,8},{16,20},{20,16},{24,28},{28,24},{1,5},{5... | collective-permute-start | bytes 1572872 | tf_op jit(solution)/shard_map/ppermute | solution.py:848
  116.7 13.4 %collective-permute-start.12 = (bf16[2048,128]{1,0:T(8,128)(2,1)S(1)}, bf16[2048,128]{1,0:T(8,128)(2,1)S(1)}, u32[]{:S(2)}, u32[]{:S(2)}) collective-permute-start(bf16[2048,128]{1,0:T(8,128)(2,1)S(1)} %collective-permute-done.11.refs_4_), channel_id=1, source_target_pairs={{0,4},{4,0},{8,12},{12,8},{16,20},{20,16},{24,28},{28,24},{1,5},{5... | collective-permute-start | bytes 1572872 | tf_op jit(solution)/shard_map/ppermute | solution.py:848
  117.2 12.9 %collective-permute-start.10 = (bf16[2048,128]{1,0:T(8,128)(2,1)S(1)}, bf16[2048,128]{1,0:T(8,128)(2,1)S(1)}, u32[]{:S(2)}, u32[]{:S(2)}) collective-permute-start(bf16[2048,128]{1,0:T(8,128)(2,1)S(1)} %collective-permute-done.9.refs_2_), channel_id=1, source_target_pairs={{0,4},{4,0},{8,12},{12,8},{16,20},{20,16},{24,28},{28,24},{1,5},{5... | collective-permute-start | bytes 1572872 | tf_op jit(solution)/shard_map/ppermute | solution.py:848
  130.0 2.1 collective-permute-start.15
  181.0 38.4 %collective-permute-start.16 = (bf16[384,2048]{1,0:T(8,128)(2,1)}, bf16[384,2048]{1,0:T(8,128)(2,1)S(1)}, u32[]{:S(2)}, u32[]{:S(2)}) collective-permute-start(bf16[384,2048]{1,0:T(8,128)(2,1)} %hold.10._.array_ref), channel_id=1, source_target_pairs={{0,1},{3,2},{4,5},{7,6},{8,9},{11,10},{12,13},{15,14},{16,17},{19,... | collective-permute-start | bytes 4718600 | tf_op jit(solution)/shard_map/ppermute | solution.py:781
  208.3 44.9 %collective-permute-start.18 = (bf16[384,2048]{1,0:T(8,128)(2,1)}, bf16[384,2048]{1,0:T(8,128)(2,1)S(1)}, u32[]{:S(2)}, u32[]{:S(2)}) collective-permute-start(bf16[384,2048]{1,0:T(8,128)(2,1)} %hold.11._.array_ref), channel_id=1, source_target_pairs={{0,1},{3,2},{4,5},{7,6},{8,9},{11,10},{12,13},{15,14},{16,17},{19,... | collective-permute-start | bytes 4718600 | tf_op jit(solution)/shard_map/ppermute | solution.py:781
  223.4 34.4 %collective-permute-start.17 = (bf16[384,2048]{1,0:T(8,128)(2,1)}, bf16[384,2048]{1,0:T(8,128)(2,1)}, u32[]{:S(2)}, u32[]{:S(2)}) collective-permute-start(bf16[384,2048]{1,0:T(8,128)(2,1)} %join.20._.array_ref), channel_id=1, source_target_pairs={{1,2},{2,1},{5,6},{6,5},{9,10},{10,9},{13,14},{14,13},{17,18},{18,... | collective-permute-start | bytes 4718600 | tf_op jit(solution)/shard_map/ppermute | solution.py:781
  244.8 61.3 %collective-permute-start.22 = (bf16[384,2048]{1,0:T(8,128)(2,1)}, bf16[384,2048]{1,0:T(8,128)(2,1)S(1)}, u32[]{:S(2)}, u32[]{:S(2)}) collective-permute-start(bf16[384,2048]{1,0:T(8,128)(2,1)} %hold.12._.array_ref), channel_id=1, source_target_pairs={{0,1},{3,2},{4,5},{7,6},{8,9},{11,10},{12,13},{15,14},{16,17},{19,... | collective-permute-start | bytes 4718600 | tf_op jit(solution)/shard_map/ppermute | solution.py:781
  257.1 53.7 %collective-permute-start.21 = (bf16[384,2048]{1,0:T(8,128)(2,1)}, bf16[384,2048]{1,0:T(8,128)(2,1)S(1)}, u32[]{:S(2)}, u32[]{:S(2)}) collective-permute-start(bf16[384,2048]{1,0:T(8,128)(2,1)} %join.21._.array_ref), channel_id=1, source_target_pairs={{1,2},{2,1},{5,6},{6,5},{9,10},{10,9},{13,14},{14,13},{17,18},{18,... | collective-permute-start | bytes 4718600 | tf_op jit(solution)/shard_map/ppermute | solution.py:781
  260.8 56.2 %collective-permute-start.20 = (bf16[384,2048]{1,0:T(8,128)(2,1)}, bf16[384,2048]{1,0:T(8,128)(2,1)}, u32[]{:S(2)}, u32[]{:S(2)}) collective-permute-start(bf16[384,2048]{1,0:T(8,128)(2,1)} %join.22.refs_9_.array_ref), channel_id=1, source_target_pairs={{1,0},{2,3},{5,4},{6,7},{9,8},{10,11},{13,12},{14,15},{17,16},{18,... | collective-permute-start | bytes 4718600 | tf_op jit(solution)/shard_map/ppermute | solution.py:781
  296.8 58.2 %collective-permute-start.19 = (bf16[384,2048]{1,0:T(8,128)(2,1)}, bf16[384,2048]{1,0:T(8,128)(2,1)}, u32[]{:S(2)}, u32[]{:S(2)}) collective-permute-start(bf16[384,2048]{1,0:T(8,128)(2,1)} %hold.13._.array_ref), channel_id=1, source_target_pairs={{0,1},{3,2},{4,5},{7,6},{8,9},{11,10},{12,13},{15,14},{16,17},{19,... | collective-permute-start | bytes 4718600 | tf_op jit(solution)/shard_map/ppermute | solution.py:781
  306.0 254.8 %reduce-scatter.8.cloned.1.call-start = ((), (), s32[]{:S(2)}) async-start(), calls=%async_computation.8 | async-start | bytes 4718592 | tf_op jit(solution)/shard_map/reduce_scatter | solution.py:888
  310.0 49.7 %collective-permute-start.26 = (bf16[384,2048]{1,0:T(8,128)(2,1)}, bf16[384,2048]{1,0:T(8,128)(2,1)S(1)}, u32[]{:S(2)}, u32[]{:S(2)}) collective-permute-start(bf16[384,2048]{1,0:T(8,128)(2,1)} %join.23._.array_ref), channel_id=1, source_target_pairs={{1,2},{2,1},{5,6},{6,5},{9,10},{10,9},{13,14},{14,13},{17,18},{18,... | collective-permute-start | bytes 4718600 | tf_op jit(solution)/shard_map/ppermute | solution.py:781
  315.4 49.8 %collective-permute-start.25 = (bf16[384,2048]{1,0:T(8,128)(2,1)}, bf16[384,2048]{1,0:T(8,128)(2,1)S(1)}, u32[]{:S(2)}, u32[]{:S(2)}) collective-permute-start(bf16[384,2048]{1,0:T(8,128)(2,1)} %join.24.refs_0_.array_ref), channel_id=1, source_target_pairs={{1,0},{2,3},{5,4},{6,7},{9,8},{10,11},{13,12},{14,15},{17,16},{18,... | collective-permute-start | bytes 4718600 | tf_op jit(solution)/shard_map/ppermute | solution.py:781
  349.5 39.4 %collective-permute-start.24 = (bf16[384,2048]{1,0:T(8,128)(2,1)}, bf16[384,2048]{1,0:T(8,128)(2,1)}, u32[]{:S(2)}, u32[]{:S(2)}) collective-permute-start(bf16[384,2048]{1,0:T(8,128)(2,1)} %hold.14._.array_ref), channel_id=1, source_target_pairs={{0,1},{3,2},{4,5},{7,6},{8,9},{11,10},{12,13},{15,14},{16,17},{19,... | collective-permute-start | bytes 4718600 | tf_op jit(solution)/shard_map/ppermute | solution.py:781
  358.0 35.6 %collective-permute-start.23 = (bf16[384,2048]{1,0:T(8,128)(2,1)}, bf16[384,2048]{1,0:T(8,128)(2,1)}, u32[]{:S(2)}, u32[]{:S(2)}) collective-permute-start(bf16[384,2048]{1,0:T(8,128)(2,1)} %join.25._.array_ref), channel_id=1, source_target_pairs={{1,2},{2,1},{5,6},{6,5},{9,10},{10,9},{13,14},{14,13},{17,18},{18,... | collective-permute-start | bytes 4718600 | tf_op jit(solution)/shard_map/ppermute | solution.py:781
  363.9 39.4 %collective-permute-start.30 = (bf16[384,2048]{1,0:T(8,128)(2,1)}, bf16[384,2048]{1,0:T(8,128)(2,1)S(1)}, u32[]{:S(2)}, u32[]{:S(2)}) collective-permute-start(bf16[384,2048]{1,0:T(8,128)(2,1)} %join.26.refs_0_.array_ref), channel_id=1, source_target_pairs={{1,0},{2,3},{5,4},{6,7},{9,8},{10,11},{13,12},{14,15},{17,16},{18,... | collective-permute-start | bytes 4718600 | tf_op jit(solution)/shard_map/ppermute | solution.py:781
  370.9 49.0 %collective-permute-start.29 = (bf16[384,2048]{1,0:T(8,128)(2,1)}, bf16[384,2048]{1,0:T(8,128)(2,1)}, u32[]{:S(2)}, u32[]{:S(2)}) collective-permute-start(bf16[384,2048]{1,0:T(8,128)(2,1)} %hold.15._.array_ref), channel_id=1, source_target_pairs={{0,1},{3,2},{4,5},{7,6},{8,9},{11,10},{12,13},{15,14},{16,17},{19,... | collective-permute-start | bytes 4718600 | tf_op jit(solution)/shard_map/ppermute | solution.py:781
  391.8 31.0 %collective-permute-start.28 = (bf16[384,2048]{1,0:T(8,128)(2,1)}, bf16[384,2048]{1,0:T(8,128)(2,1)}, u32[]{:S(2)}, u32[]{:S(2)}) collective-permute-start(bf16[384,2048]{1,0:T(8,128)(2,1)} %join.27._.array_ref), channel_id=1, source_target_pairs={{1,2},{2,1},{5,6},{6,5},{9,10},{10,9},{13,14},{14,13},{17,18},{18,... | collective-permute-start | bytes 4718600 | tf_op jit(solution)/shard_map/ppermute | solution.py:781
  397.1 36.6 %collective-permute-start.27 = (bf16[384,2048]{1,0:T(8,128)(2,1)}, bf16[384,2048]{1,0:T(8,128)(2,1)S(1)}, u32[]{:S(2)}, u32[]{:S(2)}) collective-permute-start(bf16[384,2048]{1,0:T(8,128)(2,1)} %join.28.refs_0_.array_ref), channel_id=1, source_target_pairs={{1,0},{2,3},{5,4},{6,7},{9,8},{10,11},{13,12},{14,15},{17,16},{18,... | collective-permute-start | bytes 4718600 | tf_op jit(solution)/shard_map/ppermute | solution.py:781
  450.5 36.4 %collective-permute-start.33 = (bf16[384,2048]{1,0:T(8,128)(2,1)S(1)}, bf16[384,2048]{1,0:T(8,128)(2,1)}, u32[]{:S(2)}, u32[]{:S(2)}) collective-permute-start(bf16[384,2048]{1,0:T(8,128)(2,1)S(1)} %copy-done.9), channel_id=1, source_target_pairs={{0,1},{3,2},{4,5},{7,6},{8,9},{11,10},{12,13},{15,14},{16,17},{19,... | collective-permute-start | bytes 4718600 | tf_op jit(solution)/shard_map/ppermute | solution.py:781
  453.2 38.5 %collective-permute-start.32 = (bf16[384,2048]{1,0:T(8,128)(2,1)}, bf16[384,2048]{1,0:T(8,128)(2,1)}, u32[]{:S(2)}, u32[]{:S(2)}) collective-permute-start(bf16[384,2048]{1,0:T(8,128)(2,1)} %join.29._.array_ref), channel_id=1, source_target_pairs={{1,2},{2,1},{5,6},{6,5},{9,10},{10,9},{13,14},{14,13},{17,18},{18,... | collective-permute-start | bytes 4718600 | tf_op jit(solution)/shard_map/ppermute | solution.py:781
  455.0 45.5 %collective-permute-start.31 = (bf16[384,2048]{1,0:T(8,128)(2,1)S(1)}, bf16[384,2048]{1,0:T(8,128)(2,1)}, u32[]{:S(2)}, u32[]{:S(2)}) collective-permute-start(bf16[384,2048]{1,0:T(8,128)(2,1)S(1)} %copy-done.10), channel_id=1, source_target_pairs={{1,0},{2,3},{5,4},{6,7},{9,8},{10,11},{13,12},{14,15},{17,16},{18,... | collective-permute-start | bytes 4718600 | tf_op jit(solution)/shard_map/ppermute | solution.py:781
  456.3 89.6 %collective-permute-start.34 = (bf16[384,2048]{1,0:T(8,128)(2,1)}, bf16[384,2048]{1,0:T(8,128)(2,1)}, u32[]{:S(2)}, u32[]{:S(2)}) collective-permute-start(bf16[384,2048]{1,0:T(8,128)(2,1)} %hold.17._.array_ref), channel_id=1, source_target_pairs={{0,1},{3,2},{4,5},{7,6},{8,9},{11,10},{12,13},{15,14},{16,17},{19,... | collective-permute-start | bytes 4718600 | tf_op jit(solution)/shard_map/ppermute | solution.py:781
  489.7 61.5 %collective-permute-start.38 = (bf16[384,2048]{1,0:T(8,128)(2,1)}, bf16[384,2048]{1,0:T(8,128)(2,1)}, u32[]{:S(2)}, u32[]{:S(2)}) collective-permute-start(bf16[384,2048]{1,0:T(8,128)(2,1)} %join.31._.array_ref), channel_id=1, source_target_pairs={{1,2},{2,1},{5,6},{6,5},{9,10},{10,9},{13,14},{14,13},{17,18},{18,... | collective-permute-start | bytes 4718600 | tf_op jit(solution)/shard_map/ppermute | solution.py:781
  494.5 61.3 %collective-permute-start.37 = (bf16[384,2048]{1,0:T(8,128)(2,1)}, bf16[384,2048]{1,0:T(8,128)(2,1)}, u32[]{:S(2)}, u32[]{:S(2)}) collective-permute-start(bf16[384,2048]{1,0:T(8,128)(2,1)} %join.32.refs_0_.array_ref), channel_id=1, source_target_pairs={{1,0},{2,3},{5,4},{6,7},{9,8},{10,11},{13,12},{14,15},{17,16},{18,... | collective-permute-start | bytes 4718600 | tf_op jit(solution)/shard_map/ppermute | solution.py:781
  496.7 13.2 %all-to-all-start = ((bf16[256,8,128]{2,0,1:T(8,128)(2,1)}), bf16[256,8,128]{2,0,1:T(8,128)(2,1)S(1)}, u32[]{:S(2)}, u32[]{:S(2)}) async-start(bf16[256,8,128]{2,0,1:T(8,128)(2,1)} %copy_bitcast_fusion), calls=%async_computation.1 | async-start | bytes 1048576 | tf_op jit(solution)/shard_map/all_to_all | solution.py:980
  500.2 132.2 %reduce-scatter.6.cloned.1.call-start = ((), (), s32[]{:S(2)}) async-start(), calls=%async_computation.7 | async-start | bytes 9437184 | tf_op jit(solution)/shard_map/reduce_scatter | solution.py:888
  538.8 38.6 %collective-permute-start.36 = (bf16[2048,384]{1,0:T(8,128)(2,1)}, bf16[2048,384]{1,0:T(8,128)(2,1)S(1)}, u32[]{:S(2)}, u32[]{:S(2)}) collective-permute-start(bf16[2048,384]{1,0:T(8,128)(2,1)} %hold.18._.array_ref), channel_id=1, source_target_pairs={{0,1},{3,2},{4,5},{7,6},{8,9},{11,10},{12,13},{15,14},{16,17},{19,... | collective-permute-start | bytes 4718600 | tf_op jit(solution)/shard_map/ppermute | solution.py:781
  549.4 34.0 %collective-permute-start.35 = (bf16[384,2048]{1,0:T(8,128)(2,1)}, bf16[384,2048]{1,0:T(8,128)(2,1)}, u32[]{:S(2)}, u32[]{:S(2)}) collective-permute-start(bf16[384,2048]{1,0:T(8,128)(2,1)} %join.33._.array_ref), channel_id=1, source_target_pairs={{1,2},{2,1},{5,6},{6,5},{9,10},{10,9},{13,14},{14,13},{17,18},{18,... | collective-permute-start | bytes 4718600 | tf_op jit(solution)/shard_map/ppermute | solution.py:781
  554.6 41.1 %collective-permute-start.42 = (bf16[384,2048]{1,0:T(8,128)(2,1)}, bf16[384,2048]{1,0:T(8,128)(2,1)S(1)}, u32[]{:S(2)}, u32[]{:S(2)}) collective-permute-start(bf16[384,2048]{1,0:T(8,128)(2,1)} %join.34.refs_0_.array_ref), channel_id=1, source_target_pairs={{1,0},{2,3},{5,4},{6,7},{9,8},{10,11},{13,12},{14,15},{17,16},{18,... | collective-permute-start | bytes 4718600 | tf_op jit(solution)/shard_map/ppermute | solution.py:781
  581.4 23.2 %collective-permute-start.40 = (bf16[2048,384]{1,0:T(8,128)(2,1)}, bf16[2048,384]{1,0:T(8,128)(2,1)}, u32[]{:S(2)}, u32[]{:S(2)}) collective-permute-start(bf16[2048,384]{1,0:T(8,128)(2,1)} %join.35._.array_ref), channel_id=1, source_target_pairs={{1,2},{2,1},{5,6},{6,5},{9,10},{10,9},{13,14},{14,13},{17,18},{18,... | collective-permute-start | bytes 4718600 | tf_op jit(solution)/shard_map/ppermute | solution.py:781
  586.2 40.0 %collective-permute-start.39 = (bf16[384,2048]{1,0:T(8,128)(2,1)}, bf16[384,2048]{1,0:T(8,128)(2,1)S(1)}, u32[]{:S(2)}, u32[]{:S(2)}) collective-permute-start(bf16[384,2048]{1,0:T(8,128)(2,1)} %join.36.refs_0_.array_ref), channel_id=1, source_target_pairs={{1,0},{2,3},{5,4},{6,7},{9,8},{10,11},{13,12},{14,15},{17,16},{18,... | collective-permute-start | bytes 4718600 | tf_op jit(solution)/shard_map/ppermute | solution.py:781
  587.5 13.7 %collective-permute-start.41 = (bf16[128,2048]{1,0:T(8,128)(2,1)S(1)}, bf16[128,2048]{1,0:T(8,128)(2,1)}, u32[]{:S(2)}, u32[]{:S(2)}) collective-permute-start(bf16[128,2048]{1,0:T(8,128)(2,1)S(1)} %copy-done.13), channel_id=1, source_target_pairs={{0,1},{3,2},{4,5},{7,6},{8,9},{11,10},{12,13},{15,14},{16,17},{19,... | collective-permute-start | bytes 1572872 | tf_op jit(solution)/shard_map/ppermute | solution.py:781
  603.1 35.6 %collective-permute-start.44 = (bf16[128,2048]{1,0:T(8,128)(2,1)}, bf16[128,2048]{1,0:T(8,128)(2,1)}, u32[]{:S(2)}, u32[]{:S(2)}) collective-permute-start(bf16[128,2048]{1,0:T(8,128)(2,1)} %join.37._.array_ref), channel_id=1, source_target_pairs={{1,2},{2,1},{5,6},{6,5},{9,10},{10,9},{13,14},{14,13},{17,18},{18,... | collective-permute-start | bytes 1572872 | tf_op jit(solution)/shard_map/ppermute | solution.py:781
  607.5 61.4 %collective-permute-start.43 = (bf16[2048,384]{1,0:T(8,128)(2,1)}, bf16[2048,384]{1,0:T(8,128)(2,1)S(1)}, u32[]{:S(2)}, u32[]{:S(2)}) collective-permute-start(bf16[2048,384]{1,0:T(8,128)(2,1)} %join.38.refs_0_.array_ref), channel_id=1, source_target_pairs={{1,0},{2,3},{5,4},{6,7},{9,8},{10,11},{13,12},{14,15},{17,16},{18,... | collective-permute-start | bytes 4718600 | tf_op jit(solution)/shard_map/ppermute | solution.py:781
  638.7 3.2 collective-permute-start.46
  640.6 34.2 %collective-permute-start.45 = (bf16[128,2048]{1,0:T(8,128)(2,1)}, bf16[128,2048]{1,0:T(8,128)(2,1)S(1)}, u32[]{:S(2)}, u32[]{:S(2)}) collective-permute-start(bf16[128,2048]{1,0:T(8,128)(2,1)} %join.39._.array_ref), channel_id=1, source_target_pairs={{1,0},{2,3},{5,4},{6,7},{9,8},{10,11},{13,12},{14,15},{17,16},{18,... | collective-permute-start | bytes 1572872 | tf_op jit(solution)/shard_map/ppermute | solution.py:781
  642.0 3.8 collective-permute-start.47
  645.8 3.8 collective-permute-start.48
  649.6 19.3 %collective-permute-start.49 = (f32[4104]{0:T(1024)S(1)}, f32[4104]{0:T(1024)S(1)}, u32[]{:S(2)}, u32[]{:S(2)}) collective-permute-start(f32[4104]{0:T(1024)S(1)} %add.32), channel_id=1, source_target_pairs={{0,1},{1,0},{2,3},{3,2},{4,5},{5,4},{6,7},{7,6},{8,9},{9,8},{10,11... | collective-permute-start | bytes 49256 | tf_op jit(solution)/shard_map/ppermute | solution.py:762
  669.0 4.7 collective-permute-start.50
  (29 other events, 62.3 us)
Sparse Core Ops, SparseCore 0:
  9.9 63.9 all-gather.2
  75.8 64.7 all-gather.4
  306.1 114.3 reduce-scatter.3
  449.2 49.3 reduce-scatter.7
  536.4 72.3 reduce-scatter.5

commit v3 on v2

--- a/solution.py
+++ b/solution.py
@@ -13,7 +13,7 @@
 LEN = 1024
 MICRO = 2
 FFN_CHUNKS = 4
-WAITS = (225, 57, 57, 1)
+WAITS = (102, 108, 5, 172)
 ROW_BLOCK = 512
 MIB = 1 << 20
 VMEM_ALONE = 60
@@ -313,7 +313,7 @@
             jax.ShapeDtypeStruct((block, width), wide),
             jax.ShapeDtypeStruct((block, inner), low),
         ],
-        compiler_params=params(30),
+        compiler_params=params(VMEM_ALONE),
         cost_estimate=SMALL,
     )(place, x_all, *mixed_pieces, w_out_all, gain.reshape(1, width))
 
@@ -338,8 +338,8 @@
     span = pl.ds(pl.multiple_of(step * side, side), side)
     top_ref[:cols, span] = dot_cols(hidden[...], cot_ref[...]).astype(low)
     square = dot_cols(h2_ref[...], d_both[...]).astype(low)
-    top_ref[cols:, span] = square[:half]
-    bottom_ref[:, span] = square[half:]
+    top_ref[cols:, span] = square[3 * half :]
+    bottom_ref[:, span] = square[: 3 * half]
 
 
 def first_kernel(
@@ -456,59 +456,40 @@
     return jnp.where(is_one_of(place_ref, takers), arrived_ref[...], array_ref[...]).astype(wide)
 
 
-def top_kernel(takers, place_ref, array_ref, arrived_ref, *refs):
-    down_ref, gate_ref, up_ref, token_ref = refs[-4:]
-    step = pl.program_id(0)
-    cols = gate_ref.shape[2]
-
-    @pl.when(step < 2)
-    def _():
-        down_ref[...] = chosen(takers, place_ref, array_ref, arrived_ref)
-
-    @pl.when(step == 2)
-    def _():
-        spread(chosen(takers, place_ref, array_ref, arrived_ref), gate_ref, up_ref)
-        token_ref[...] = jnp.zeros_like(token_ref)
-
-
-def bottom_kernel(takers, place_ref, array_ref, arrived_ref, *refs):
-    gate_ref, up_ref, token_ref = refs[-3:]
-    spread(chosen(takers, place_ref, array_ref, arrived_ref), gate_ref, up_ref)
-    token_ref[...] = jnp.zeros_like(token_ref)
-
-
-def spread(value, gate_ref, up_ref):
-    cols = gate_ref.shape[2]
+def finish_kernel(cols, has_down, takers, place_ref, array_ref, arrived_ref, *refs):
+    *_, gate_ref, up_ref, token_ref = refs
+    value = chosen(takers, place_ref, array_ref, arrived_ref)
+    if has_down:
+        refs[-4][...] = value[:cols]
+        value = value[cols:]
     for number in range(gate_ref.shape[0]):
         begin = number * 2 * cols
         gate_ref[number] = value[:, begin : begin + cols]
         up_ref[number] = value[:, begin + cols : begin + 2 * cols]
+    token_ref[...] = jnp.zeros_like(token_ref)
 
 
 def finish_ffn(is_top, number, cols, hidden_cols, token, place, takers, array, arrived, grads):
-    width = array.shape[1]
-    half = cols // 2
+    count, width = array.shape
     squares = width // (2 * cols)
-    in_spec = pl.BlockSpec((half, width), lambda i: (i, 0))
+    in_spec = kept_block((count, width))
     square_shape = jax.ShapeDtypeStruct((squares, 2 * cols, hidden_cols), wide)
-    first = 0 if is_top else 1
-    square_spec = pl.BlockSpec(
-        (squares, half, cols), lambda i: (0, 0 if is_top else i + first, number)
-    )
+    if is_top:
+        square_spec = pl.BlockSpec((squares, cols // 2, cols), lambda i: (0, 3, number))
+    else:
+        square_spec = pl.BlockSpec((squares, count, cols), lambda i: (0, 0, number))
     out_specs = [square_spec, square_spec, kept_out((8, 128))]
     out_shape = [square_shape, square_shape, jax.ShapeDtypeStruct((8, 128), wide)]
     names = ["gate", "up"]
     if is_top:
-        out_specs.insert(
-            0, pl.BlockSpec((half, width), lambda i: (2 * number + jnp.minimum(i, 1), 0))
-        )
+        out_specs.insert(0, pl.BlockSpec((cols, width), lambda i: (number, 0)))
         out_shape.insert(0, jax.ShapeDtypeStruct((hidden_cols, width), wide))
         names.insert(0, "down")
     carried = [(i, grads[name]) for i, name in enumerate(names) if name in grads]
     *buffers, token = pl.pallas_call(
-        functools.partial(top_kernel if is_top else bottom_kernel, takers),
+        functools.partial(finish_kernel, cols, is_top, takers),
         name="finish_ffn",
-        grid=(3,),
+        grid=(1,),
         in_specs=[pl.BlockSpec(memory_space=pltpu.SMEM), in_spec, in_spec, ANYWHERE]
         + [ANYWHERE] * len(carried),
         out_specs=out_specs,
@@ -581,113 +562,135 @@
     )(array, token)
 
 
-def last_kernel(d_h1_ref, x_ref, d_y1_ref, gain_ref, _, out_ref, d_gain_ref):
+def last_kernel(d_h1_ref, x_ref, d_y1_ref, gain_ref, y1_ref, mlp_ref, _, out_ref, d_gain_ref, layer_ref):
     rows = x_ref[...].astype(wide)
     d_rows, d_gain = norm_back(rows, norm_scale(rows), gain_ref[...], d_h1_ref[...].astype(wide))
     out_ref[...] = d_rows + d_y1_ref[...]
     d_gain_ref[...] = d_gain[None]
-
-
-def last_rows(token, d_h1, x_own, d_y1, gain):
+    layer_ref[...] = (y1_ref[...] + mlp_ref[...].astype(wide)).astype(low)
+
+
+def last_rows(token, d_h1, x_own, d_y1, gain, y1_own, mlp_own):
     count, width = d_y1.shape
     return pl.pallas_call(
         last_kernel,
         name="last_rows",
-        in_specs=[IN_VMEM] * 4 + [ANYWHERE],
-        out_specs=[IN_VMEM] * 2,
+        grid=(1,),
+        in_specs=[kept_block((count, width))] * 3
+        + [kept_block((1, width))]
+        + [kept_block((count, width))] * 2
+        + [ANYWHERE],
+        out_specs=[kept_block((count, width)), kept_block((1, width)), kept_block((count, width))],
         out_shape=[
             jax.ShapeDtypeStruct((count, width), wide),
             jax.ShapeDtypeStruct((1, width), wide),
-        ],
-        compiler_params=params(VMEM_ALONE),
-        cost_estimate=SMALL,
-    )(d_h1, x_own, d_y1, gain.reshape(1, width), token)
+            jax.ShapeDtypeStruct((count, width), low),
+        ],
+        compiler_params=params(VMEM_ALONE),
+        cost_estimate=SMALL,
+    )(d_h1, x_own, d_y1, gain.reshape(1, width), y1_own, mlp_own, token)
 
 
 def kept_out(shape):
     return pl.BlockSpec(shape, lambda *_: (0,) * len(shape))
 
 
-def sums_kernel(count, wg_ref, wu_ref, wd_ref, *refs):
-    hidden, d_gate, d_up = [
-        jnp.concatenate([ref[...] for ref in refs[i * count : (i + 1) * count]], axis=1)
-        for i in range(3)
-    ]
-    out_ref = refs[-1]
-    devices, both_rows, width = out_ref.shape
-    own_rows = both_rows // 2
-    d_h2 = dot_rows(d_gate, wg_ref[...]) + dot_rows(d_up, wu_ref[...])
-    out_ref[:, :own_rows] = d_h2.astype(low).reshape(devices, own_rows, width)
-    mlp = mm(hidden, wd_ref[...])
-    out_ref[:, own_rows:] = mlp.astype(low).reshape(devices, own_rows, width)
-
-
-def ffn_sums(own_rows, w_gate, w_up, w_down, hidden, d_gate, d_up, token):
+def together(refs):
+    return jnp.concatenate([ref[...] for ref in refs], axis=1)
+
+
+def back_kernel(count, wg_ref, wu_ref, *refs):
+    total = dot_rows(together(refs[:count]), wg_ref[...])
+    total = total + dot_rows(together(refs[count : 2 * count]), wu_ref[...])
+    refs[-1][...] = total.astype(low)
+
+
+def ffn_back(w_gate, w_up, d_gate, d_up, token):
+    count = d_gate[0].shape[0]
+    width = w_gate.shape[0]
+    block = min(ROW_BLOCK, count)
+    parts = [*d_gate, *d_up]
+    return pl.pallas_call(
+        functools.partial(back_kernel, len(d_gate)),
+        name="ffn_back",
+        grid=(count // block,),
+        in_specs=[kept_block(w_gate.shape), kept_block(w_up.shape)]
+        + [pl.BlockSpec((block, part.shape[1]), lambda i: (i, 0)) for part in parts]
+        + [ANYWHERE],
+        out_specs=pl.BlockSpec((block, width), lambda i: (i, 0)),
+        out_shape=jax.ShapeDtypeStruct((count, width), low),
+        compiler_params=params(VMEM_ALONE),
+        cost_estimate=SMALL,
+    )(w_gate, w_up, *parts, token)
+
+
+def mlp_kernel(w_ref, *refs):
+    result = mm(together(refs[:-2]), w_ref[...])
+    refs[-1][...] = result.astype(low).reshape(refs[-1].shape)
+
+
+def ffn_out(own_rows, w_down, hidden, token):
     count = hidden[0].shape[0]
-    width = w_gate.shape[0]
-    devices = max(1, 256 // own_rows)
-
-    def row_spec(part):
-        return pl.BlockSpec((devices * own_rows, part.shape[1]), lambda i: (i, 0))
-
-    parts = [*hidden, *d_gate, *d_up]
-    return pl.pallas_call(
-        functools.partial(sums_kernel, len(hidden)),
-        name="ffn_sums",
-        grid=(count // (devices * own_rows),),
-        in_specs=[kept_block(w_gate.shape), kept_block(w_up.shape), kept_block(w_down.shape)]
-        + [row_spec(part) for part in parts]
+    width = w_down.shape[1]
+    devices = max(1, ROW_BLOCK // own_rows)
+    block = devices * own_rows
+    return pl.pallas_call(
+        mlp_kernel,
+        name="ffn_out",
+        grid=(count // block,),
+        in_specs=[kept_block(w_down.shape)]
+        + [pl.BlockSpec((block, part.shape[1]), lambda i: (i, 0)) for part in hidden]
         + [ANYWHERE],
-        out_specs=pl.BlockSpec((devices, 2 * own_rows, width), lambda i: (i, 0, 0)),
-        out_shape=jax.ShapeDtypeStruct((count // own_rows, 2 * own_rows, width), low),
-        compiler_params=params(VMEM_ALONE),
-        cost_estimate=SMALL,
-    )(w_gate, w_up, w_down, *parts, token)
-
-
-def own_kernel(sums_ref, y1_ref, cot_ref, gain_ref, w_ref, mixed_ref, _, *refs):
-    d_y1_ref, d_mixed_ref, d_w_ref, d_gain_ref, layer_ref = refs
-    count = y1_ref.shape[0]
+        out_specs=pl.BlockSpec((devices, own_rows, width), lambda i: (i, 0, 0)),
+        out_shape=jax.ShapeDtypeStruct((count // own_rows, own_rows + DH, width), low),
+        compiler_params=params(VMEM_ALONE),
+        cost_estimate=SMALL,
+    )(w_down, *hidden, token)
+
+
+def own_kernel(d_h2_ref, y1_ref, cot_ref, gain_ref, w_ref, mixed_ref, *refs):
+    d_y1_ref, d_mixed_ref, d_w_ref, d_gain_ref = refs[-4:]
     y1 = y1_ref[...]
-    layer_ref[...] = (y1 + sums_ref[count:].astype(wide)).astype(low)
-    d_rows, d_gain = norm_back(y1, norm_scale(y1), gain_ref[...], sums_ref[:count].astype(wide))
+    d_rows, d_gain = norm_back(y1, norm_scale(y1), gain_ref[...], d_h2_ref[...].astype(wide))
     d_y1 = d_rows + cot_ref[...].astype(wide)
     d_attn = d_y1.astype(low)
     d_y1_ref[...] = d_y1
     d_gain_ref[...] = d_gain[None]
     d_mixed_ref[...] = dot_rows(d_attn, w_ref[...]).astype(low)
-    d_w_ref[...] = dot_cols(mixed_ref[...], d_attn).astype(low)
-
-
-def own_rows_back(token, sums, y1_own, cot_own, gain, w_out_all, mixed_own):
+    d_w_ref[...] = dot_cols(mixed_ref[...], d_attn).astype(low).reshape(d_w_ref.shape)
+
+
+def own_rows_back(token, d_h2, y1_own, cot_own, gain, w_out_all, mixed_own, buffer):
     count, width = y1_own.shape
     inner = w_out_all.shape[0]
-    once = [sums.shape, y1_own.shape, cot_own.shape, (1, width), w_out_all.shape, mixed_own.shape]
+    heads = buffer.shape[0]
+    once = [d_h2.shape, y1_own.shape, cot_own.shape, (1, width), w_out_all.shape, mixed_own.shape]
     return pl.pallas_call(
         own_kernel,
         name="own_rows_back",
         grid=(1,),
-        in_specs=[kept_block(shape) for shape in once] + [ANYWHERE],
+        in_specs=[kept_block(shape) for shape in once] + [ANYWHERE] * 2,
         out_specs=[
             kept_block((count, width)),
             kept_block((count, inner)),
-            kept_block((inner, width)),
+            pl.BlockSpec(
+                (heads, DH, width), lambda i: (0, count // DH, 0), pipeline_mode=pl.Buffered(1)
+            ),
             kept_block((1, width)),
-            kept_block((count, width)),
         ],
         out_shape=[
             jax.ShapeDtypeStruct((count, width), wide),
             jax.ShapeDtypeStruct((count, inner), low),
-            jax.ShapeDtypeStruct((inner, width), low),
+            jax.ShapeDtypeStruct(buffer.shape, low),
             jax.ShapeDtypeStruct((1, width), wide),
-            jax.ShapeDtypeStruct((count, width), low),
-        ],
-        compiler_params=params(VMEM_ALONE),
-        cost_estimate=SMALL,
-    )(sums, y1_own, cot_own, gain.reshape(1, width), w_out_all, mixed_own, token)
-
-
-def qkv_back_kernel(d_qkv_ref, h1_ref, w_ref, d_h1_ref, d_w_ref, total):
+        ],
+        input_output_aliases={7: 2},
+        compiler_params=params(VMEM_ALONE),
+        cost_estimate=SMALL,
+    )(d_h2, y1_own, cot_own, gain.reshape(1, width), w_out_all, mixed_own, token, buffer)
+
+
+def qkv_back_kernel(d_qkv_ref, h1_ref, w_ref, _, d_h1_ref, d_w_ref, total):
     step = pl.program_id(0)
     d_qkv = d_qkv_ref[...]
     d_h1_ref[...] = dot_rows(d_qkv, w_ref[...]).astype(low)
@@ -706,7 +709,7 @@
         d_w_ref[...] = total[...].astype(low)
 
 
-def qkv_back(d_qkv, h1_all, w_qkv):
+def qkv_back(d_qkv, h1_all, w_qkv, token):
     count, width = h1_all.shape
     cols = w_qkv.shape[1]
     block = min(ROW_BLOCK, count)
@@ -718,6 +721,7 @@
             pl.BlockSpec((block, cols), lambda i: (i, 0)),
             pl.BlockSpec((block, width), lambda i: (i, 0)),
             kept_block((width, cols)),
+            ANYWHERE,
         ],
         out_specs=[pl.BlockSpec((block, width), lambda i: (i, 0)), kept_out((width, cols))],
         out_shape=[
@@ -727,7 +731,7 @@
         scratch_shapes=[pltpu.VMEM((width, cols), wide)],
         compiler_params=params(VMEM_ALONE),
         cost_estimate=SMALL,
-    )(d_qkv, h1_all, w_qkv)
+    )(d_qkv, h1_all, w_qkv, token)
 
 
 def join_kernel(takers, place_ref, array_ref, arrived_ref, _, out_ref):
@@ -745,7 +749,7 @@
     return pl.pallas_call(
         functools.partial(join_kernel, takers),
         name="join",
-        grid=(2,),
+        grid=(count // block,),
         in_specs=[pl.BlockSpec(memory_space=pltpu.SMEM), spec, spec, ANYWHERE],
         out_specs=spec,
         out_shape=jax.ShapeDtypeStruct((count, width), low),
@@ -795,21 +799,25 @@
         else:
             self.send(stage + 1, land, array)
 
-    def tick(self, estimate=SMALL):
+    def tick(self, between=None):
         if self.size == 1 or self.size % 2:
             for land, array in self.waiting:
                 array = lax.psum(array, self.axis)
                 self.token = land(self.token, self.place, (), array, array)
             self.waiting = []
-            return
+            return between() if between else None
+        result = None
         ready = [bool(moving) for moving in self.moving]
         if self.waiting:
             land, array = self.waiting.pop(0)
-            array = self.token = hold(array, self.token, estimate)
+            array = self.token = hold(array, self.token)
             self.send(0, land, array)
         for stage, can_move in enumerate(ready):
             if can_move:
                 self.move(stage)
+            if stage == 0 and between:
+                result = between()
+        return result
 
     def drain(self):
         while self.waiting or any(self.moving):
@@ -942,13 +950,13 @@
         *parts, top, bottom = ffn_first(
             number, cols, h2_all, cot_all, w_gate, w_up, w_down, chain.token
         )
-        chain.token = top
+        chain.token = parts[0]
         push_ffn(number, top, bottom)
         return parts
 
     def weights(number, parts):
         top, bottom = ffn_weights(number - 2, cols, h2_all, cot_all, *parts, chain.token)
-        chain.token = top
+        chain.token = bottom
         push_ffn(number, top, bottom)
 
     def wait_for(microseconds):
@@ -961,41 +969,49 @@
     part_c = ffn_rest(h2_all, cot_all, w_gate, w_up, w_down, chain.token)
     chain.token = part_c[0]
     chain.tick()
-    sums = chain.token = ffn_sums(
-        own_rows, w_gate, w_up, w_down, *zip(part_a, part_b, part_c), chain.token
-    )
-    sums = scatter(sums.reshape(-1, width))
+    hidden, d_gate, d_up = zip(part_a, part_b, part_c)
+    d_h2 = chain.token = ffn_back(w_gate, w_up, d_gate, d_up, chain.token)
+    d_h2 = scatter(d_h2)
     chain.tick()
     weights(2, part_c)
-    weights(3, part_c)
     chain.tick()
+    parts = chain.token = ffn_out(own_rows, w_down, hidden, chain.token)
+
     chain.tick()
-    chain.tick()
-
     wait_for(WAITS[0])
-    d_y1, d_mixed_own, grad_out, gain_mlp_part, layer_out = own_rows_back(
-        chain.token, sums, y1_own, cot_own, norm_mlp, w_out_all, mixed_own
+    d_y1, d_mixed_own, parts, gain_mlp_part = own_rows_back(
+        chain.token, d_h2, y1_own, cot_own, norm_mlp, w_out_all, mixed_own, parts
     )
     chain.token = d_y1
     d_mixed = lax.all_to_all(d_mixed_own, "heads", split_axis=1, concat_axis=0, tiled=True)
-    grad_out = scatter(grad_out)
+    parts = scatter(parts.reshape(-1, width))
+    weights(3, part_c)
     chain.tick()
-    wait_for(WAITS[3])
+    wait_for(WAITS[2])
     d_qkv, d_share = head_backward(
         share, qkv, grouped(d_mixed), doc_rows, doc_cols, chain.token
     )
-    d_h1, grad_qkv = qkv_back(flat(d_qkv), h1_all, w_qkv)
-    chain.token = grad_qkv
-    d_h1 = scatter(d_h1)
+    chain.token = d_share
+    chain.tick()
+    d_h1, grad_qkv = qkv_back(flat(d_qkv), h1_all, w_qkv, chain.token)
+    chain.token = d_h1
     chain.push(grad_qkv, land_qkv)
-    chain.tick()
-    wait_for(WAITS[1])
-    chain.push(grad_out, land_out)
+
+    def scatter_last():
+        wait_for(WAITS[3])
+        chain.token = tie(chain.token, parts)
+        chain.token = hold(d_h1, chain.token)
+        return scatter(chain.token)
+
+    d_h1 = chain.tick(scatter_last)
+    chain.push(parts[own_rows:], land_out)
     chain.tick()
     chain.tick()
 
-    wait_for(WAITS[2])
-    grad_tokens, gain_attn_part = last_rows(chain.token, d_h1, tok_own, d_y1, norm_attn)
+    wait_for(WAITS[1])
+    grad_tokens, gain_attn_part, layer_out = last_rows(
+        chain.token, d_h1, tok_own, d_y1, norm_attn, y1_own, parts
+    )
     grad_tokens = grad_tokens.reshape(tokens.shape)
     chain.token = gain_attn_part
     slots = jnp.where(jnp.arange(n_heads) == here, jnp.sum(d_share[:, 0, 0]), 0.0)

time: 697 us -> 628 us (0.901)
  waiting for transfers between devices: 223 us -> 171 us
  local copies, waits for them, and re-layouts: 36.9 us -> 24.7 us
    ppermute x30, waiting for transfers between devices: 106 us -> 58.3 us  [send(): arrived = lax.ppermute(array, self.axis, self.stages[stage][1])]
    unnamed x78 -> x70, local copies, waits for them, and re-layouts: 33.2 us -> 19.1 us
    pallas_call x10 -> x11, Pallas kernels: 76 us -> 75.9 us  [the longest x8 31.7 us: finish_ffn(): pl.pallas_call(functools.partial(finish_kernel, cols, is_top, takers), na...]
  transfers between devices with their start and end apart: 57 -> 57, of which waited for: 25 -> 24; matrix products, arithmetic and copies ran while one was open for 1% -> 2% of each run, Pallas kernels for 39% -> 45%
where the time goes in v3:
time: 628 us; the launch traced here: 619 us
  Pallas kernels  307 us (49%)
  waiting for transfers between devices  171 us (27%)
  starting transfers between devices  97.7 us (16%)
  local copies, waits for them, and re-layouts  24.7 us (4%)
  between operations  15.5 us (2%)
    ppermute x30, starting transfers between devices, send(): arrived = lax.ppermute(array, self.axis, self.stages[stage][1])  78.4 us
    ppermute x16, waiting for transfers between devices, flip(): return lax.ppermute(value, axis, [(i, i ^ bits) for i in range(size)])  61.2 us
    ppermute x30, waiting for transfers between devices, send(): arrived = lax.ppermute(array, self.axis, self.stages[stage][1])  58.3 us
    pallas_call x20, Pallas kernels, join(): pl.pallas_call(functools.partial(join_kernel, takers), name='join', grid=...  55.4 us
    pallas_call x2, Pallas kernels, ffn_first(): pl.pallas_call(functools.partial(first_kernel, blocks), name='ffn_first',...  46.9 us
    pallas_call x8, Pallas kernels, finish_ffn(): pl.pallas_call(functools.partial(finish_kernel, cols, is_top, takers), na...  31.7 us
    pallas_call x2, Pallas kernels, ffn_weights(): pl.pallas_call(grads_kernel, name='ffn_weights', grid=(width // side,), i...  29.5 us
    all_gather x2, waiting for transfers between devices, gather(): return lax.all_gather(array, 'heads', axis=0, tiled=True)  28.4 us
  transfers between devices with their start and end apart: 57, of which 24 were waited for; matrix products, arithmetic and copies ran while one was open for 2% of the time, Pallas kernels for 45%

profile of v3, /device:TPU:0, one launch (start us, length us, event | category | flops | bytes accessed | tf_op | source)
XLA Modules:
  0.0 618.9 jit_solution(17805958906419356326)
XLA Ops:
  8.0 3.0 collective-permute-start.1
  12.5 12.4 %collective-permute-done.1.refs_2_ = bf16[128,2048]{1,0:T(8,128)(2,1)S(1)} collective-permute-done((bf16[128,2048]{1,0:T(8,128)(2,1)}, bf16[128,2048]{1,0:T(8,128)(2,1)S(1)}, u32[]{:S(2)}, u32[]{:S(2)}) %collective-permute-start.1) | collective-permute-done | bytes 524320 | tf_op jit(solution)/shard_map/ppermute | solution.py:856
  29.3 9.3 %collective-permute-done.5 = bf16[64,2048]{1,0:T(8,128)(2,1)S(1)} collective-permute-done((bf16[64,2048]{1,0:T(8,128)(2,1)S(1)}, bf16[64,2048]{1,0:T(8,128)(2,1)S(1)}, u32[]{:S(2)}, u32[]{:S(2)}) %collective-permute-start.5) | collective-permute-done | bytes 262176 | tf_op jit(solution)/shard_map/ppermute | solution.py:856
  45.5 28.3 %all-gather.3.cloned.1.call-done.x_ref = bf16[2048,2048]{1,0:T(8,128)(2,1)} async-done(((bf16[256,2048]{1,0:T(8,128)(2,1)}), bf16[2048,2048]{1,0:T(8,128)(2,1)}) %all-gather.3.cloned.1.call-update) | async-done | bytes 8388624 | tf_op jit(solution)/shard_map/all_gather | solution.py:893
  78.5 10.5 %qkv_rows.1 = (bf16[2048,2048]{1,0:T(8,128)(2,1)}, bf16[2048,384]{1,0:T(8,128)(2,1)}) custom-call(bf16[2048,2048]{1,0:T(8,128)(2,1)} %all-gather.3.cloned.1.call-done.x_ref, f32[1,2048]{1,0:T(1,128)} %bitcast.52, bf16[2048,384]{1,0:T(8,128)(2,1)} %copy-done.3), custom_call_target="tpu_custom_call" | custom-call | flops 1 | bytes 1 | tf_op jit(solution)/shard_map/qkv_rows/pallas_call | solution.py:88
  89.1 5.8 head_forward.1
  96.5 16.9 %collective-permute-done.9.refs_2_ = bf16[2048,128]{1,0:T(8,128)(2,1)S(1)} collective-permute-done((bf16[2048,128]{1,0:T(8,128)(2,1)}, bf16[2048,128]{1,0:T(8,128)(2,1)S(1)}, u32[]{:S(2)}, u32[]{:S(2)}) %collective-permute-start.9) | collective-permute-done | bytes 524320 | tf_op jit(solution)/shard_map/ppermute | solution.py:856
  113.6 2.8 collective-permute-done.11.refs_4_
  117.2 10.3 %collective-permute-done.13 = bf16[1024,128]{1,0:T(8,128)(2,1)S(1)} collective-permute-done((bf16[1024,128]{1,0:T(8,128)(2,1)S(1)}, bf16[1024,128]{1,0:T(8,128)(2,1)S(1)}, u32[]{:S(2)}, u32[]{:S(2)}) %collective-permute-start.13) | collective-permute-done | bytes 262176 | tf_op jit(solution)/shard_map/ppermute | solution.py:856
  132.8 18.9 %mid_rows.1 = (bf16[2048,2048]{1,0:T(8,128)(2,1)}, f32[256,2048]{1,0:T(8,128)}, bf16[256,1024]{1,0:T(8,128)(2,1)}) custom-call(s32[3]{0:T(128)} %copy-done.2, bf16[2048,2048]{1,0:T(8,128)(2,1)} %all-gather.3.cloned.1.call-done.x_ref, bf16[2048,128]{1,0:T(8,128)(2,1)} %bitcast.42, bf16[2048,128]{1,0:T(8,128)(2,1)} %copy-done.19, ...), custom_call_target="tpu_custom_call" | custom-call | flops 1 | bytes 1 | tf_op jit(solution)/shard_map/mid_rows/pallas_call | solution.py:292
  151.7 23.4 %ffn_first.2 = (bf16[2048,256]{1,0:T(8,128)(2,1)}, bf16[2048,256]{1,0:T(8,128)(2,1)}, bf16[2048,256]{1,0:T(8,128)(2,1)}, bf16[384,2048]{1,0:T(8,128)(2,1)}, bf16[384,2048]{1,0:T(8,128)(2,1)}) custom-call(bf16[2048,2048]{1,0:T(8,128)(2,1)} %get-tuple-element.84.h2_ref.h2_col_ref, bf16[2048,2048]{1,0:T(8,128)(2,1)} %all-gather.5.cloned.1.call-done.cot_ref.cot_col_ref, ...), custom_call_target="tpu_custom_call" | custom-call | flops 1 | bytes 1 | tf_op jit(solution)/shard_map/ffn_first/pallas_call | solution.py:376
  175.2 3.7 collective-permute-start.16
  178.9 23.5 %ffn_first.3 = (bf16[2048,256]{1,0:T(8,128)(2,1)}, bf16[2048,256]{1,0:T(8,128)(2,1)}, bf16[2048,256]{1,0:T(8,128)(2,1)}, bf16[384,2048]{1,0:T(8,128)(2,1)}, bf16[384,2048]{1,0:T(8,128)(2,1)}) custom-call(bf16[2048,2048]{1,0:T(8,128)(2,1)} %get-tuple-element.84.h2_ref.h2_col_ref, bf16[2048,2048]{1,0:T(8,128)(2,1)} %all-gather.5.cloned.1.call-done.cot_ref.cot_col_ref, ...), custom_call_target="tpu_custom_call" | custom-call | flops 1 | bytes 1 | tf_op jit(solution)/shard_map/ffn_first/pallas_call | solution.py:376
  203.8 9.9 %collective-permute-done.16.arrived_ref = bf16[384,2048]{1,0:T(8,128)(2,1)S(1)} collective-permute-done((bf16[384,2048]{1,0:T(8,128)(2,1)}, bf16[384,2048]{1,0:T(8,128)(2,1)S(1)}, u32[]{:S(2)}, u32[]{:S(2)}) %collective-permute-start.16) | collective-permute-done | bytes 1572896 | tf_op jit(solution)/shard_map/ppermute | solution.py:785
  214.8 2.8 join.20._.array_ref
  219.5 19.5 %ffn_rest.1 = (bf16[2048,512]{1,0:T(8,128)(2,1)}, bf16[2048,512]{1,0:T(8,128)(2,1)}, bf16[2048,512]{1,0:T(8,128)(2,1)}) custom-call(bf16[2048,2048]{1,0:T(8,128)(2,1)} %get-tuple-element.84.h2_ref.h2_col_ref, bf16[2048,2048]{1,0:T(8,128)(2,1)} %all-gather.5.cloned.1.call-done.cot_ref.cot_col_ref, bf16[2048,1024]{1,0:T(8,128)(2,1)} %wg_ref.7, ...), custom_call_target="tpu_custom_call" | custom-call | flops 1 | bytes 1 | tf_op jit(solution)/shard_map/ffn_rest/pallas_call | solution.py:403
  239.0 7.1 %collective-permute-start.19 = (bf16[384,2048]{1,0:T(8,128)(2,1)}, bf16[384,2048]{1,0:T(8,128)(2,1)}, u32[]{:S(2)}, u32[]{:S(2)}) collective-permute-start(bf16[384,2048]{1,0:T(8,128)(2,1)} %hold.13._.array_ref), channel_id=1, source_target_pairs={{0,1},{3,2},{4,5},{7,6},{8,9},{11,10},{12,13},{15,14},{16,17},{19,... | collective-permute-start | bytes 4718600 | tf_op jit(solution)/shard_map/ppermute | solution.py:785
  248.5 2.9 join.21._.array_ref
  252.2 2.8 join.22.refs_6_.array_ref
  256.3 23.8 %ffn_back.1.__1_ = bf16[2048,2048]{1,0:T(8,128)(2,1)} custom-call(bf16[2048,1024]{1,0:T(8,128)(2,1)} %wg_ref.7, bf16[2048,1024]{1,0:T(8,128)(2,1)} %wu_ref.7, bf16[2048,256]{1,0:T(8,128)(2,1)} %get-tuple-element.86.refs_0_, bf16[2048,256]{1,0:T(8,128)(2,1)} %get-tuple-element.89.refs_1_, bf16[2048,512]{1,0:T(8,128)(2,1)} %get-tuple-element.92.refs_2_.dg_ref, ...), custom_call_target="tpu_custom_call" | custom-call | flops 1 | bytes 1 | tf_op jit(solution)/shard_map/ffn_back/pallas_call | solution.py:613
  280.2 8.2 %collective-permute-start.21 = (bf16[384,2048]{1,0:T(8,128)(2,1)}, bf16[384,2048]{1,0:T(8,128)(2,1)}, u32[]{:S(2)}, u32[]{:S(2)}) collective-permute-start(bf16[384,2048]{1,0:T(8,128)(2,1)} %hold.14._.array_ref), channel_id=1, source_target_pairs={{0,1},{3,2},{4,5},{7,6},{8,9},{11,10},{12,13},{15,14},{16,17},{19,... | collective-permute-start | bytes 4718600 | tf_op jit(solution)/shard_map/ppermute | solution.py:785
  288.3 2.8 join.23._.array_ref
  294.2 2.8 join.24.refs_0_.array_ref
  299.5 4.3 finish_ffn.8
  303.8 13.9 %ffn_weights.2 = (bf16[384,2048]{1,0:T(8,128)(2,1)}, bf16[384,2048]{1,0:T(8,128)(2,1)}) custom-call(bf16[2048,2048]{1,0:T(8,128)(2,1)} %get-tuple-element.84.h2_ref.h2_col_ref, bf16[2048,2048]{1,0:T(8,128)(2,1)} %all-gather.5.cloned.1.call-done.cot_ref.cot_col_ref, bf16[2048,512]{1,0:T(8,128)(2,1)} %get-tuple-element.97.__1_.hid_ref.refs_2_, ...), custom_call_target="tpu_custom_call" | custom-call | flops 1 | bytes 1 | tf_op jit(solution)/shard_map/ffn_weights/pallas_call | solution.py:433
  317.7 5.9 collective-permute-start.26
  323.7 2.8 join.25._.array_ref
  328.3 3.0 join.26.refs_0_.array_ref
  334.2 3.9 finish_ffn.9
  338.1 13.6 %ffn_out.1.__1_.refs_1_ = bf16[8,384,2048]{2,1,0:T(8,128)(2,1)} custom-call(bf16[1024,2048]{1,0:T(8,128)(2,1)} %w_ref.1, bf16[2048,256]{1,0:T(8,128)(2,1)} %get-tuple-element.88.__1_.refs_0_, bf16[2048,256]{1,0:T(8,128)(2,1)} %get-tuple-element.91.__1_.refs_1_, bf16[2048,512]{1,0:T(8,128)(2,1)} %get-tuple-element.97.__1_.hid_ref.refs_2_, ...), custom_call_target="tpu_custom_call" | custom-call | flops 1 | bytes 1 | tf_op jit(solution)/shard_map/ffn_out/pallas_call | solution.py:637
  351.7 4.2 collective-permute-start.30
  356.0 2.9 join.27._.array_ref
  360.7 2.8 join.28.refs_0_.array_ref
  364.8 3.9 collective-permute-done.24.arrived_ref
  369.9 3.7 finish_ffn.10
  374.2 8.8 %own_rows_back.1 = (f32[256,2048]{1,0:T(8,128)}, bf16[256,1024]{1,0:T(8,128)(2,1)}, bf16[8,384,2048]{2,1,0:T(8,128)(2,1)}, f32[1,2048]{1,0:T(1,128)}) custom-call(bf16[256,2048]{1,0:T(8,128)(2,1)} %reduce-scatter.4.cloned.1.call-done.d_h2_ref, f32[256,2048]{1,0:T(8,128)} %get-tuple-element.98.y1_ref, ...), custom_call_target="tpu_custom_call", output_to_operand_aliasing={{2}: (7, {})} | custom-call | flops 1 | bytes 1 | tf_op jit(solution)/shard_map/own_rows_back/pallas_call | solution.py:668
  385.0 3.5 all-to-all-start
  388.6 15.6 %ffn_weights.3 = (bf16[384,2048]{1,0:T(8,128)(2,1)}, bf16[384,2048]{1,0:T(8,128)(2,1)}) custom-call(bf16[2048,2048]{1,0:T(8,128)(2,1)} %get-tuple-element.84.h2_ref.h2_col_ref, bf16[2048,2048]{1,0:T(8,128)(2,1)} %all-gather.5.cloned.1.call-done.cot_ref.cot_col_ref, bf16[2048,512]{1,0:T(8,128)(2,1)} %get-tuple-element.97.__1_.hid_ref.refs_2_, ...), custom_call_target="tpu_custom_call" | custom-call | flops 1 | bytes 1 | tf_op jit(solution)/shard_map/ffn_weights/pallas_call | solution.py:433
  404.1 3.1 collective-permute-start.33
  408.4 2.8 join.29._.array_ref
  413.0 2.8 join.30.refs_0_.array_ref
  417.3 3.9 finish_ffn.11
  422.7 10.9 %head_backward.1 = (bf16[8,2,128,384]{3,2,1,0:T(8,128)(2,1)}, f32[2,8,128]{2,1,0:T(8,128)}) custom-call(f32[1]{0:T(128)S(6)} %div.3.share_ref, bf16[8,2,128,384]{3,2,1,0:T(8,128)(2,1)} %bitcast.34, bf16[8,2,128,128]{3,2,1,0:T(8,128)(2,1)} %bitcast.43, s32[2,1024,1]{2,1,0:T(8,128)} %copy.63.doc_rows_ref, s32[2,1,1024]{2,1,0:T(1,128)} %compare_select_fusion.doc_cols_ref, ...), custom_call_target="tpu_custom_call" | custom-call | flops 1 | bytes 1 | tf_op jit(solution)/shard_map/head_backward/pallas_call | solution.py:240
  433.6 5.7 collective-permute-start.34
  441.1 2.8 join.31._.array_ref
  445.8 2.9 join.32.refs_0_.array_ref
  449.9 4.7 collective-permute-done.31.arrived_ref
  455.8 3.7 finish_ffn.12
  459.5 14.9 %qkv_back.1 = (bf16[2048,2048]{1,0:T(8,128)(2,1)}, bf16[2048,384]{1,0:T(8,128)(2,1)}) custom-call(bf16[2048,384]{1,0:T(8,128)(2,1)} %bitcast.44, bf16[2048,2048]{1,0:T(8,128)(2,1)} %get-tuple-element.119.h1_ref, bf16[2048,384]{1,0:T(8,128)(2,1)} %copy-done.3, f32[8,128]{1,0:T(8,128)} %get-tuple-element.124._), custom_call_target="tpu_custom_call" | custom-call | flops 1 | bytes 1 | tf_op jit(solution)/shard_map/qkv_back/pallas_call | solution.py:716
  474.4 3.5 collective-permute-start.36
  477.9 2.9 join.33.refs_0_.array_ref
  483.8 2.8 join.34.refs_0_.array_ref
  488.0 4.6 finish_ffn.13
  494.6 15.9 %collective-permute-done.36.arrived_ref = bf16[2048,384]{1,0:T(8,128)(2,1)} collective-permute-done((bf16[2048,384]{1,0:T(8,128)(2,1)}, bf16[2048,384]{1,0:T(8,128)(2,1)}, u32[]{:S(2)}, u32[]{:S(2)}) %collective-permute-start.36) | collective-permute-done | bytes 1572896 | tf_op jit(solution)/shard_map/ppermute | solution.py:785
  510.5 2.9 join.35._.array_ref
  515.3 2.9 join.36.refs_0_.array_ref
  519.5 6.3 %collective-permute-start.41 = (bf16[128,2048]{1,0:T(8,128)(2,1)S(1)}, bf16[128,2048]{1,0:T(8,128)(2,1)}, u32[]{:S(2)}, u32[]{:S(2)}) collective-permute-start(bf16[128,2048]{1,0:T(8,128)(2,1)S(1)} %copy-done.4), channel_id=1, source_target_pairs={{0,1},{3,2},{4,5},{7,6},{8,9},{11,10},{12,13},{15,14},{16,17},{19,... | collective-permute-start | bytes 1572872 | tf_op jit(solution)/shard_map/ppermute | solution.py:785
  528.9 3.8 finish_ffn.14
  537.2 2.9 join.38.refs_0_.array_ref
  541.6 18.2 %collective-permute-done.39.arrived_ref = bf16[384,2048]{1,0:T(8,128)(2,1)S(1)} collective-permute-done((bf16[384,2048]{1,0:T(8,128)(2,1)}, bf16[384,2048]{1,0:T(8,128)(2,1)S(1)}, u32[]{:S(2)}, u32[]{:S(2)}) %collective-permute-start.39) | collective-permute-done | bytes 1572896 | tf_op jit(solution)/shard_map/ppermute | solution.py:785
  561.0 3.9 finish_ffn.15
  565.5 6.7 %last_rows.1 = (f32[256,2048]{1,0:T(8,128)}, f32[1,2048]{1,0:T(1,128)}, bf16[256,2048]{1,0:T(8,128)(2,1)}) custom-call(bf16[256,2048]{1,0:T(8,128)(2,1)} %reduce-scatter.8.cloned.1.call-done.d_h1_ref, bf16[256,2048]{1,0:T(8,128)(2,1)} %bitcast.38, f32[256,2048]{1,0:T(8,128)} %get-tuple-element.112._.d_y1_ref, f32[1,2048]{1,0:T(1,128)} %bitcast.53, ...), custom_call_target="tpu_custom_call" | custom-call | flops 1 | bytes 1 | tf_op jit(solution)/shard_map/last_rows/pallas_call | solution.py:575
  587.4 16.1 %collective-permute-done.49 = f32[4104]{0:T(1024)S(1)} collective-permute-done((f32[4104]{0:T(1024)S(1)}, f32[4104]{0:T(1024)S(1)}, u32[]{:S(2)}, u32[]{:S(2)}) %collective-permute-start.49) | collective-permute-done | bytes 16448 | tf_op jit(solution)/shard_map/ppermute | solution.py:766
  603.5 3.2 finish_cut.2
  (210 shorter events, 103.9 us)
Async XLA Ops:
  7.2 21.6 %copy-start.1 = (bf16[128,2048]{1,0:T(8,128)(2,1)S(1)}, bf16[128,2048]{1,0:T(8,128)(2,1)}, u32[]{:S(2)}) copy-start(bf16[128,2048]{1,0:T(8,128)(2,1)} %refs_0_.1) | copy-start | bytes 1572868
  7.2 66.7 %all-gather.3.cloned.1.call-start = ((), (), s32[]{:S(2)}) async-start(), calls=%async_computation.4 | async-start | bytes 9437184 | tf_op jit(solution)/shard_map/all_gather | solution.py:893
  7.9 143.8 %all-gather.5.cloned.1.call-start = ((), (), s32[]{:S(2)}) async-start(), calls=%async_computation.5 | async-start | bytes 9437184 | tf_op jit(solution)/shard_map/all_gather | solution.py:893
  8.0 16.9 %collective-permute-start.1 = (bf16[128,2048]{1,0:T(8,128)(2,1)}, bf16[128,2048]{1,0:T(8,128)(2,1)S(1)}, u32[]{:S(2)}, u32[]{:S(2)}) collective-permute-start(bf16[128,2048]{1,0:T(8,128)(2,1)} %refs_0_.1), channel_id=1, source_target_pairs={{0,8},{4,12},{8,0},{12,4},{16,24},{20,28},{24,16},{28,20},{1,9},{5... | collective-permute-start | bytes 1572872 | tf_op jit(solution)/shard_map/ppermute | solution.py:856
  11.0 17.2 %collective-permute-start.3 = (bf16[128,2048]{1,0:T(8,128)(2,1)}, bf16[128,2048]{1,0:T(8,128)(2,1)S(1)}, u32[]{:S(2)}, u32[]{:S(2)}) collective-permute-start(bf16[128,2048]{1,0:T(8,128)(2,1)} %refs_0_.1), channel_id=1, source_target_pairs={{0,16},{4,20},{8,24},{12,28},{16,0},{20,4},{24,8},{28,12},{1,17},{... | collective-permute-start | bytes 1572872 | tf_op jit(solution)/shard_map/ppermute | solution.py:856
  24.9 13.7 %collective-permute-start.5 = (bf16[64,2048]{1,0:T(8,128)(2,1)S(1)}, bf16[64,2048]{1,0:T(8,128)(2,1)S(1)}, u32[]{:S(2)}, u32[]{:S(2)}) collective-permute-start(bf16[64,2048]{1,0:T(8,128)(2,1)S(1)} %slice.32), channel_id=1, source_target_pairs={{0,16},{4,20},{8,24},{12,28},{16,0},{20,4},{24,8},{28,12},{1,17},{... | collective-permute-start | bytes 786440 | tf_op jit(solution)/shard_map/ppermute | solution.py:856
  28.2 11.8 %collective-permute-start.6 = (bf16[64,2048]{1,0:T(8,128)(2,1)S(1)}, bf16[64,2048]{1,0:T(8,128)(2,1)S(1)}, u32[]{:S(2)}, u32[]{:S(2)}) collective-permute-start(bf16[64,2048]{1,0:T(8,128)(2,1)S(1)} %slice.33), channel_id=1, source_target_pairs={{0,8},{4,12},{8,0},{12,4},{16,24},{20,28},{24,16},{28,20},{1,9},{5... | collective-permute-start | bytes 786440 | tf_op jit(solution)/shard_map/ppermute | solution.py:856
  28.8 11.4 %collective-permute-start = (bf16[128,2048]{1,0:T(8,128)(2,1)S(1)}, bf16[128,2048]{1,0:T(8,128)(2,1)S(1)}, u32[]{:S(2)}, u32[]{:S(2)}) collective-permute-start(bf16[128,2048]{1,0:T(8,128)(2,1)S(1)} %copy-done.1), channel_id=1, source_target_pairs={{0,4},{4,0},{8,12},{12,8},{16,20},{20,16},{24,28},{28,24},{1,5},{5... | collective-permute-start | bytes 1572872 | tf_op jit(solution)/shard_map/ppermute | solution.py:856
  28.8 11.4 %collective-permute-start.2 = (bf16[128,2048]{1,0:T(8,128)(2,1)S(1)}, bf16[128,2048]{1,0:T(8,128)(2,1)S(1)}, u32[]{:S(2)}, u32[]{:S(2)}) collective-permute-start(bf16[128,2048]{1,0:T(8,128)(2,1)S(1)} %collective-permute-done.1.refs_2_), channel_id=1, source_target_pairs={{0,4},{4,0},{8,12},{12,8},{16,20},{20,16},{24,28},{28,24},{1,5},{5... | collective-permute-start | bytes 1572872 | tf_op jit(solution)/shard_map/ppermute | solution.py:856
  29.3 10.9 %collective-permute-start.4 = (bf16[128,2048]{1,0:T(8,128)(2,1)S(1)}, bf16[128,2048]{1,0:T(8,128)(2,1)}, u32[]{:S(2)}, u32[]{:S(2)}) collective-permute-start(bf16[128,2048]{1,0:T(8,128)(2,1)S(1)} %collective-permute-done.3.refs_4_), channel_id=1, source_target_pairs={{0,4},{4,0},{8,12},{12,8},{16,20},{20,16},{24,28},{28,24},{1,5},{5... | collective-permute-start | bytes 1572872 | tf_op jit(solution)/shard_map/ppermute | solution.py:856
  40.0 2.1 collective-permute-start.7
  40.2 34.6 %copy-start.32 = (s32[2,1,4]{2,1,0:T(1,128)S(1)}, s32[2,1,4]{2,1,0:T(1,128)}, u32[]{:S(2)}) copy-start(s32[2,1,4]{2,1,0:T(1,128)} %param.16) | copy-start | bytes 100
  45.5 30.8 %copy-start.31 = (s32[2,1,1024]{2,1,0:T(1,128)S(1)}, s32[2,1,1024]{2,1,0:T(1,128)}, u32[]{:S(2)}) copy-start(s32[2,1,1024]{2,1,0:T(1,128)} %param.17) | copy-start | bytes 24580
  45.5 31.5 %copy-start.23 = (bf16[2048,128]{1,0:T(8,128)(2,1)S(1)}, bf16[2048,128]{1,0:T(8,128)(2,1)}, u32[]{:S(2)}) copy-start(bf16[2048,128]{1,0:T(8,128)(2,1)} %param.18) | copy-start | bytes 1572868
  73.9 300.3 %reduce-scatter.4.cloned.1.call-start = ((), (), s32[]{:S(2)}) async-start(), calls=%async_computation.6 | async-start | bytes 9437184 | tf_op jit(solution)/shard_map/reduce_scatter | solution.py:896
  94.9 18.5 %collective-permute-start.9 = (bf16[2048,128]{1,0:T(8,128)(2,1)}, bf16[2048,128]{1,0:T(8,128)(2,1)S(1)}, u32[]{:S(2)}, u32[]{:S(2)}) collective-permute-start(bf16[2048,128]{1,0:T(8,128)(2,1)} %bitcast.39), channel_id=1, source_target_pairs={{0,8},{4,12},{8,0},{12,4},{16,24},{20,28},{24,16},{28,20},{1,9},{5... | collective-permute-start | bytes 1572872 | tf_op jit(solution)/shard_map/ppermute | solution.py:856
  96.3 20.1 %collective-permute-start.11 = (bf16[2048,128]{1,0:T(8,128)(2,1)}, bf16[2048,128]{1,0:T(8,128)(2,1)S(1)}, u32[]{:S(2)}, u32[]{:S(2)}) collective-permute-start(bf16[2048,128]{1,0:T(8,128)(2,1)} %bitcast.40), channel_id=1, source_target_pairs={{0,16},{4,20},{8,24},{12,28},{16,0},{20,4},{24,8},{28,12},{1,17},{... | collective-permute-start | bytes 1572872 | tf_op jit(solution)/shard_map/ppermute | solution.py:856
  113.4 18.7 %copy-start.16 = (bf16[2048,128]{1,0:T(8,128)(2,1)}, bf16[2048,128]{1,0:T(8,128)(2,1)S(1)}, u32[]{:S(2)}) copy-start(bf16[2048,128]{1,0:T(8,128)(2,1)S(1)} %collective-permute-done.9.refs_2_) | copy-start | bytes 1572868
  113.4 14.1 %collective-permute-start.13 = (bf16[1024,128]{1,0:T(8,128)(2,1)S(1)}, bf16[1024,128]{1,0:T(8,128)(2,1)S(1)}, u32[]{:S(2)}, u32[]{:S(2)}) collective-permute-start(bf16[1024,128]{1,0:T(8,128)(2,1)S(1)} %slice.34), channel_id=1, source_target_pairs={{0,16},{4,20},{8,24},{12,28},{16,0},{20,4},{24,8},{28,12},{1,17},{... | collective-permute-start | bytes 786440 | tf_op jit(solution)/shard_map/ppermute | solution.py:856
  116.4 15.6 %copy-start.17 = (bf16[2048,128]{1,0:T(8,128)(2,1)}, bf16[2048,128]{1,0:T(8,128)(2,1)S(1)}, u32[]{:S(2)}) copy-start(bf16[2048,128]{1,0:T(8,128)(2,1)S(1)} %collective-permute-done.11.refs_4_) | copy-start | bytes 1572868
  116.4 13.4 %collective-permute-start.14 = (bf16[1024,128]{1,0:T(8,128)(2,1)S(1)}, bf16[1024,128]{1,0:T(8,128)(2,1)S(1)}, u32[]{:S(2)}, u32[]{:S(2)}) collective-permute-start(bf16[1024,128]{1,0:T(8,128)(2,1)S(1)} %slice.35), channel_id=1, source_target_pairs={{0,8},{4,12},{8,0},{12,4},{16,24},{20,28},{24,16},{28,20},{1,9},{5... | collective-permute-start | bytes 786440 | tf_op jit(solution)/shard_map/ppermute | solution.py:856
  116.5 13.5 %collective-permute-start.8 = (bf16[2048,128]{1,0:T(8,128)(2,1)}, bf16[2048,128]{1,0:T(8,128)(2,1)S(1)}, u32[]{:S(2)}, u32[]{:S(2)}) collective-permute-start(bf16[2048,128]{1,0:T(8,128)(2,1)} %bitcast.41), channel_id=1, source_target_pairs={{0,4},{4,0},{8,12},{12,8},{16,20},{20,16},{24,28},{28,24},{1,5},{5... | collective-permute-start | bytes 1572872 | tf_op jit(solution)/shard_map/ppermute | solution.py:856
  116.6 13.4 %collective-permute-start.10 = (bf16[2048,128]{1,0:T(8,128)(2,1)S(1)}, bf16[2048,128]{1,0:T(8,128)(2,1)S(1)}, u32[]{:S(2)}, u32[]{:S(2)}) collective-permute-start(bf16[2048,128]{1,0:T(8,128)(2,1)S(1)} %collective-permute-done.9.refs_2_), channel_id=1, source_target_pairs={{0,4},{4,0},{8,12},{12,8},{16,20},{20,16},{24,28},{28,24},{1,5},{5... | collective-permute-start | bytes 1572872 | tf_op jit(solution)/shard_map/ppermute | solution.py:856
  117.1 12.9 %collective-permute-start.12 = (bf16[2048,128]{1,0:T(8,128)(2,1)S(1)}, bf16[2048,128]{1,0:T(8,128)(2,1)S(1)}, u32[]{:S(2)}, u32[]{:S(2)}) collective-permute-start(bf16[2048,128]{1,0:T(8,128)(2,1)S(1)} %collective-permute-done.11.refs_4_), channel_id=1, source_target_pairs={{0,4},{4,0},{8,12},{12,8},{16,20},{20,16},{24,28},{28,24},{1,5},{5... | collective-permute-start | bytes 1572872 | tf_op jit(solution)/shard_map/ppermute | solution.py:856
  129.9 2.2 collective-permute-start.15
  175.2 38.5 %collective-permute-start.16 = (bf16[384,2048]{1,0:T(8,128)(2,1)}, bf16[384,2048]{1,0:T(8,128)(2,1)S(1)}, u32[]{:S(2)}, u32[]{:S(2)}) collective-permute-start(bf16[384,2048]{1,0:T(8,128)(2,1)} %hold.11._.array_ref), channel_id=1, source_target_pairs={{0,1},{3,2},{4,5},{7,6},{8,9},{11,10},{12,13},{15,14},{16,17},{19,... | collective-permute-start | bytes 4718600 | tf_op jit(solution)/shard_map/ppermute | solution.py:785
  202.4 45.0 %collective-permute-start.18 = (bf16[384,2048]{1,0:T(8,128)(2,1)}, bf16[384,2048]{1,0:T(8,128)(2,1)S(1)}, u32[]{:S(2)}, u32[]{:S(2)}) collective-permute-start(bf16[384,2048]{1,0:T(8,128)(2,1)} %hold.12._.array_ref), channel_id=1, source_target_pairs={{0,1},{3,2},{4,5},{7,6},{8,9},{11,10},{12,13},{15,14},{16,17},{19,... | collective-permute-start | bytes 4718600 | tf_op jit(solution)/shard_map/ppermute | solution.py:785
  217.7 34.5 %collective-permute-start.17 = (bf16[384,2048]{1,0:T(8,128)(2,1)}, bf16[384,2048]{1,0:T(8,128)(2,1)}, u32[]{:S(2)}, u32[]{:S(2)}) collective-permute-start(bf16[384,2048]{1,0:T(8,128)(2,1)} %join.20._.array_ref), channel_id=1, source_target_pairs={{1,2},{2,1},{5,6},{6,5},{9,10},{10,9},{13,14},{14,13},{17,18},{18,... | collective-permute-start | bytes 4718600 | tf_op jit(solution)/shard_map/ppermute | solution.py:785
  239.0 49.3 %collective-permute-start.19 = (bf16[384,2048]{1,0:T(8,128)(2,1)}, bf16[384,2048]{1,0:T(8,128)(2,1)}, u32[]{:S(2)}, u32[]{:S(2)}) collective-permute-start(bf16[384,2048]{1,0:T(8,128)(2,1)} %hold.13._.array_ref), channel_id=1, source_target_pairs={{0,1},{3,2},{4,5},{7,6},{8,9},{11,10},{12,13},{15,14},{16,17},{19,... | collective-permute-start | bytes 4718600 | tf_op jit(solution)/shard_map/ppermute | solution.py:785
  251.4 41.6 %collective-permute-start.23 = (bf16[384,2048]{1,0:T(8,128)(2,1)}, bf16[384,2048]{1,0:T(8,128)(2,1)S(1)}, u32[]{:S(2)}, u32[]{:S(2)}) collective-permute-start(bf16[384,2048]{1,0:T(8,128)(2,1)} %join.21._.array_ref), channel_id=1, source_target_pairs={{1,2},{2,1},{5,6},{6,5},{9,10},{10,9},{13,14},{14,13},{17,18},{18,... | collective-permute-start | bytes 4718600 | tf_op jit(solution)/shard_map/ppermute | solution.py:785
  255.0 43.3 %collective-permute-start.22 = (bf16[384,2048]{1,0:T(8,128)(2,1)}, bf16[384,2048]{1,0:T(8,128)(2,1)S(1)}, u32[]{:S(2)}, u32[]{:S(2)}) collective-permute-start(bf16[384,2048]{1,0:T(8,128)(2,1)} %join.22.refs_6_.array_ref), channel_id=1, source_target_pairs={{1,0},{2,3},{5,4},{6,7},{9,8},{10,11},{13,12},{14,15},{17,16},{18,... | collective-permute-start | bytes 4718600 | tf_op jit(solution)/shard_map/ppermute | solution.py:785
  280.2 43.5 %collective-permute-start.21 = (bf16[384,2048]{1,0:T(8,128)(2,1)}, bf16[384,2048]{1,0:T(8,128)(2,1)}, u32[]{:S(2)}, u32[]{:S(2)}) collective-permute-start(bf16[384,2048]{1,0:T(8,128)(2,1)} %hold.14._.array_ref), channel_id=1, source_target_pairs={{0,1},{3,2},{4,5},{7,6},{8,9},{11,10},{12,13},{15,14},{16,17},{19,... | collective-permute-start | bytes 4718600 | tf_op jit(solution)/shard_map/ppermute | solution.py:785
  291.2 37.1 %collective-permute-start.20 = (bf16[384,2048]{1,0:T(8,128)(2,1)}, bf16[384,2048]{1,0:T(8,128)(2,1)}, u32[]{:S(2)}, u32[]{:S(2)}) collective-permute-start(bf16[384,2048]{1,0:T(8,128)(2,1)} %join.23._.array_ref), channel_id=1, source_target_pairs={{1,2},{2,1},{5,6},{6,5},{9,10},{10,9},{13,14},{14,13},{17,18},{18,... | collective-permute-start | bytes 4718600 | tf_op jit(solution)/shard_map/ppermute | solution.py:785
  293.0 190.2 %reduce-scatter.6.cloned.1.call-start = ((), (), s32[]{:S(2)}) async-start(), calls=%async_computation.7 | async-start | bytes 14155776 | tf_op jit(solution)/shard_map/reduce_scatter | solution.py:896
  297.0 36.0 %collective-permute-start.27 = (bf16[384,2048]{1,0:T(8,128)(2,1)}, bf16[384,2048]{1,0:T(8,128)(2,1)S(1)}, u32[]{:S(2)}, u32[]{:S(2)}) collective-permute-start(bf16[384,2048]{1,0:T(8,128)(2,1)} %join.24.refs_0_.array_ref), channel_id=1, source_target_pairs={{1,0},{2,3},{5,4},{6,7},{9,8},{10,11},{13,12},{14,15},{17,16},{18,... | collective-permute-start | bytes 4718600 | tf_op jit(solution)/shard_map/ppermute | solution.py:785
  317.7 38.2 %collective-permute-start.26 = (bf16[384,2048]{1,0:T(8,128)(2,1)}, bf16[384,2048]{1,0:T(8,128)(2,1)}, u32[]{:S(2)}, u32[]{:S(2)}) collective-permute-start(bf16[384,2048]{1,0:T(8,128)(2,1)} %hold.15._.array_ref), channel_id=1, source_target_pairs={{0,1},{3,2},{4,5},{7,6},{8,9},{11,10},{12,13},{15,14},{16,17},{19,... | collective-permute-start | bytes 4718600 | tf_op jit(solution)/shard_map/ppermute | solution.py:785
  326.5 34.2 %collective-permute-start.25 = (bf16[384,2048]{1,0:T(8,128)(2,1)}, bf16[384,2048]{1,0:T(8,128)(2,1)}, u32[]{:S(2)}, u32[]{:S(2)}) collective-permute-start(bf16[384,2048]{1,0:T(8,128)(2,1)} %join.25._.array_ref), channel_id=1, source_target_pairs={{1,2},{2,1},{5,6},{6,5},{9,10},{10,9},{13,14},{14,13},{17,18},{18,... | collective-permute-start | bytes 4718600 | tf_op jit(solution)/shard_map/ppermute | solution.py:785
  331.3 37.5 %collective-permute-start.24 = (bf16[384,2048]{1,0:T(8,128)(2,1)}, bf16[384,2048]{1,0:T(8,128)(2,1)S(1)}, u32[]{:S(2)}, u32[]{:S(2)}) collective-permute-start(bf16[384,2048]{1,0:T(8,128)(2,1)} %join.26.refs_0_.array_ref), channel_id=1, source_target_pairs={{1,0},{2,3},{5,4},{6,7},{9,8},{10,11},{13,12},{14,15},{17,16},{18,... | collective-permute-start | bytes 4718600 | tf_op jit(solution)/shard_map/ppermute | solution.py:785
  351.7 55.5 %collective-permute-start.30 = (bf16[384,2048]{1,0:T(8,128)(2,1)}, bf16[384,2048]{1,0:T(8,128)(2,1)S(1)}, u32[]{:S(2)}, u32[]{:S(2)}) collective-permute-start(bf16[384,2048]{1,0:T(8,128)(2,1)} %hold.16._.array_ref), channel_id=1, source_target_pairs={{0,1},{3,2},{4,5},{7,6},{8,9},{11,10},{12,13},{15,14},{16,17},{19,... | collective-permute-start | bytes 4718600 | tf_op jit(solution)/shard_map/ppermute | solution.py:785
  358.9 54.2 %collective-permute-start.29 = (bf16[384,2048]{1,0:T(8,128)(2,1)}, bf16[384,2048]{1,0:T(8,128)(2,1)}, u32[]{:S(2)}, u32[]{:S(2)}) collective-permute-start(bf16[384,2048]{1,0:T(8,128)(2,1)} %join.27._.array_ref), channel_id=1, source_target_pairs={{1,2},{2,1},{5,6},{6,5},{9,10},{10,9},{13,14},{14,13},{17,18},{18,... | collective-permute-start | bytes 4718600 | tf_op jit(solution)/shard_map/ppermute | solution.py:785
  363.6 53.8 %collective-permute-start.28 = (bf16[384,2048]{1,0:T(8,128)(2,1)}, bf16[384,2048]{1,0:T(8,128)(2,1)}, u32[]{:S(2)}, u32[]{:S(2)}) collective-permute-start(bf16[384,2048]{1,0:T(8,128)(2,1)} %join.28.refs_0_.array_ref), channel_id=1, source_target_pairs={{1,0},{2,3},{5,4},{6,7},{9,8},{10,11},{13,12},{14,15},{17,16},{18,... | collective-permute-start | bytes 4718600 | tf_op jit(solution)/shard_map/ppermute | solution.py:785
  385.0 36.9 %all-to-all-start = ((bf16[256,8,128]{2,0,1:T(8,128)(2,1)}), bf16[256,8,128]{2,0,1:T(8,128)(2,1)S(1)}, u32[]{:S(2)}, u32[]{:S(2)}) async-start(bf16[256,8,128]{2,0,1:T(8,128)(2,1)} %copy_bitcast_fusion), calls=%async_computation.1 | async-start | bytes 1048576 | tf_op jit(solution)/shard_map/all_to_all | solution.py:986
  388.5 177.0 %reduce-scatter.8.cloned.1.call-start = ((), (), s32[]{:S(2)}) async-start(), calls=%async_computation.8 | async-start | bytes 9437184 | tf_op jit(solution)/shard_map/reduce_scatter | solution.py:896
  404.1 37.0 %collective-permute-start.33 = (bf16[384,2048]{1,0:T(8,128)(2,1)}, bf16[384,2048]{1,0:T(8,128)(2,1)}, u32[]{:S(2)}, u32[]{:S(2)}) collective-permute-start(bf16[384,2048]{1,0:T(8,128)(2,1)} %hold.17._.array_ref), channel_id=1, source_target_pairs={{0,1},{3,2},{4,5},{7,6},{8,9},{11,10},{12,13},{15,14},{16,17},{19,... | collective-permute-start | bytes 4718600 | tf_op jit(solution)/shard_map/ppermute | solution.py:785
  411.2 34.5 %collective-permute-start.32 = (bf16[384,2048]{1,0:T(8,128)(2,1)}, bf16[384,2048]{1,0:T(8,128)(2,1)}, u32[]{:S(2)}, u32[]{:S(2)}) collective-permute-start(bf16[384,2048]{1,0:T(8,128)(2,1)} %join.29._.array_ref), channel_id=1, source_target_pairs={{1,2},{2,1},{5,6},{6,5},{9,10},{10,9},{13,14},{14,13},{17,18},{18,... | collective-permute-start | bytes 4718600 | tf_op jit(solution)/shard_map/ppermute | solution.py:785
  415.9 38.8 %collective-permute-start.31 = (bf16[384,2048]{1,0:T(8,128)(2,1)}, bf16[384,2048]{1,0:T(8,128)(2,1)S(1)}, u32[]{:S(2)}, u32[]{:S(2)}) collective-permute-start(bf16[384,2048]{1,0:T(8,128)(2,1)} %join.30.refs_0_.array_ref), channel_id=1, source_target_pairs={{1,0},{2,3},{5,4},{6,7},{9,8},{10,11},{13,12},{14,15},{17,16},{18,... | collective-permute-start | bytes 4718600 | tf_op jit(solution)/shard_map/ppermute | solution.py:785
  433.6 44.3 %collective-permute-start.34 = (bf16[384,2048]{1,0:T(8,128)(2,1)}, bf16[384,2048]{1,0:T(8,128)(2,1)}, u32[]{:S(2)}, u32[]{:S(2)}) collective-permute-start(bf16[384,2048]{1,0:T(8,128)(2,1)} %hold.18._.array_ref), channel_id=1, source_target_pairs={{0,1},{3,2},{4,5},{7,6},{8,9},{11,10},{12,13},{15,14},{16,17},{19,... | collective-permute-start | bytes 4718600 | tf_op jit(solution)/shard_map/ppermute | solution.py:785
  444.0 39.9 %collective-permute-start.38 = (bf16[384,2048]{1,0:T(8,128)(2,1)}, bf16[384,2048]{1,0:T(8,128)(2,1)}, u32[]{:S(2)}, u32[]{:S(2)}) collective-permute-start(bf16[384,2048]{1,0:T(8,128)(2,1)} %join.31._.array_ref), channel_id=1, source_target_pairs={{1,2},{2,1},{5,6},{6,5},{9,10},{10,9},{13,14},{14,13},{17,18},{18,... | collective-permute-start | bytes 4718600 | tf_op jit(solution)/shard_map/ppermute | solution.py:785
  448.6 39.4 %collective-permute-start.37 = (bf16[384,2048]{1,0:T(8,128)(2,1)}, bf16[384,2048]{1,0:T(8,128)(2,1)}, u32[]{:S(2)}, u32[]{:S(2)}) collective-permute-start(bf16[384,2048]{1,0:T(8,128)(2,1)} %join.32.refs_0_.array_ref), channel_id=1, source_target_pairs={{1,0},{2,3},{5,4},{6,7},{9,8},{10,11},{13,12},{14,15},{17,16},{18,... | collective-permute-start | bytes 4718600 | tf_op jit(solution)/shard_map/ppermute | solution.py:785
  474.4 36.1 %collective-permute-start.36 = (bf16[2048,384]{1,0:T(8,128)(2,1)}, bf16[2048,384]{1,0:T(8,128)(2,1)}, u32[]{:S(2)}, u32[]{:S(2)}) collective-permute-start(bf16[2048,384]{1,0:T(8,128)(2,1)} %hold.19._.array_ref), channel_id=1, source_target_pairs={{0,1},{3,2},{4,5},{7,6},{8,9},{11,10},{12,13},{15,14},{16,17},{19,... | collective-permute-start | bytes 4718600 | tf_op jit(solution)/shard_map/ppermute | solution.py:785
  480.8 34.5 %collective-permute-start.35 = (bf16[384,2048]{1,0:T(8,128)(2,1)}, bf16[384,2048]{1,0:T(8,128)(2,1)}, u32[]{:S(2)}, u32[]{:S(2)}) collective-permute-start(bf16[384,2048]{1,0:T(8,128)(2,1)} %join.33.refs_0_.array_ref), channel_id=1, source_target_pairs={{1,2},{2,1},{5,6},{6,5},{9,10},{10,9},{13,14},{14,13},{17,18},{18,... | collective-permute-start | bytes 4718600 | tf_op jit(solution)/shard_map/ppermute | solution.py:785
  486.7 41.1 %collective-permute-start.42 = (bf16[384,2048]{1,0:T(8,128)(2,1)}, bf16[384,2048]{1,0:T(8,128)(2,1)S(1)}, u32[]{:S(2)}, u32[]{:S(2)}) collective-permute-start(bf16[384,2048]{1,0:T(8,128)(2,1)} %join.34.refs_0_.array_ref), channel_id=1, source_target_pairs={{1,0},{2,3},{5,4},{6,7},{9,8},{10,11},{13,12},{14,15},{17,16},{18,... | collective-permute-start | bytes 4718600 | tf_op jit(solution)/shard_map/ppermute | solution.py:785
  513.3 23.8 %collective-permute-start.40 = (bf16[2048,384]{1,0:T(8,128)(2,1)}, bf16[2048,384]{1,0:T(8,128)(2,1)}, u32[]{:S(2)}, u32[]{:S(2)}) collective-permute-start(bf16[2048,384]{1,0:T(8,128)(2,1)} %join.35._.array_ref), channel_id=1, source_target_pairs={{1,2},{2,1},{5,6},{6,5},{9,10},{10,9},{13,14},{14,13},{17,18},{18,... | collective-permute-start | bytes 4718600 | tf_op jit(solution)/shard_map/ppermute | solution.py:785
  518.2 41.6 %collective-permute-start.39 = (bf16[384,2048]{1,0:T(8,128)(2,1)}, bf16[384,2048]{1,0:T(8,128)(2,1)S(1)}, u32[]{:S(2)}, u32[]{:S(2)}) collective-permute-start(bf16[384,2048]{1,0:T(8,128)(2,1)} %join.36.refs_0_.array_ref), channel_id=1, source_target_pairs={{1,0},{2,3},{5,4},{6,7},{9,8},{10,11},{13,12},{14,15},{17,16},{18,... | collective-permute-start | bytes 4718600 | tf_op jit(solution)/shard_map/ppermute | solution.py:785
  519.5 15.0 %collective-permute-start.41 = (bf16[128,2048]{1,0:T(8,128)(2,1)S(1)}, bf16[128,2048]{1,0:T(8,128)(2,1)}, u32[]{:S(2)}, u32[]{:S(2)}) collective-permute-start(bf16[128,2048]{1,0:T(8,128)(2,1)S(1)} %copy-done.4), channel_id=1, source_target_pairs={{0,1},{3,2},{4,5},{7,6},{8,9},{11,10},{12,13},{15,14},{16,17},{19,... | collective-permute-start | bytes 1572872 | tf_op jit(solution)/shard_map/ppermute | solution.py:785
  536.5 36.5 %collective-permute-start.44 = (bf16[128,2048]{1,0:T(8,128)(2,1)}, bf16[128,2048]{1,0:T(8,128)(2,1)S(1)}, u32[]{:S(2)}, u32[]{:S(2)}) collective-permute-start(bf16[128,2048]{1,0:T(8,128)(2,1)} %join.37._.array_ref), channel_id=1, source_target_pairs={{1,2},{2,1},{5,6},{6,5},{9,10},{10,9},{13,14},{14,13},{17,18},{18,... | collective-permute-start | bytes 1572872 | tf_op jit(solution)/shard_map/ppermute | solution.py:785
  540.1 63.4 %collective-permute-start.43 = (bf16[2048,384]{1,0:T(8,128)(2,1)}, bf16[2048,384]{1,0:T(8,128)(2,1)}, u32[]{:S(2)}, u32[]{:S(2)}) collective-permute-start(bf16[2048,384]{1,0:T(8,128)(2,1)} %join.38.refs_0_.array_ref), channel_id=1, source_target_pairs={{1,0},{2,3},{5,4},{6,7},{9,8},{10,11},{13,12},{14,15},{17,16},{18,... | collective-permute-start | bytes 4718600 | tf_op jit(solution)/shard_map/ppermute | solution.py:785
  565.5 6.8 %copy-start.30 = (f32[1,2048]{1,0:T(1,128)S(1)}, f32[1,2048]{1,0:T(1,128)}, u32[]{:S(2)}) copy-start(f32[1,2048]{1,0:T(1,128)} %get-tuple-element.149) | copy-start | bytes 24580
  573.0 4.0 collective-permute-start.46
  575.7 33.6 %collective-permute-start.45 = (bf16[128,2048]{1,0:T(8,128)(2,1)}, bf16[128,2048]{1,0:T(8,128)(2,1)S(1)}, u32[]{:S(2)}, u32[]{:S(2)}) collective-permute-start(bf16[128,2048]{1,0:T(8,128)(2,1)} %join.39._.array_ref), channel_id=1, source_target_pairs={{1,0},{2,3},{5,4},{6,7},{9,8},{10,11},{13,12},{14,15},{17,16},{18,... | collective-permute-start | bytes 1572872 | tf_op jit(solution)/shard_map/ppermute | solution.py:785
  577.1 3.8 collective-permute-start.47
  580.9 3.8 collective-permute-start.48
  584.7 18.7 %collective-permute-start.49 = (f32[4104]{0:T(1024)S(1)}, f32[4104]{0:T(1024)S(1)}, u32[]{:S(2)}, u32[]{:S(2)}) collective-permute-start(f32[4104]{0:T(1024)S(1)} %add.32), channel_id=1, source_target_pairs={{0,1},{1,0},{2,3},{3,2},{4,5},{5,4},{6,7},{7,6},{8,9},{9,8},{10,11... | collective-permute-start | bytes 49256 | tf_op jit(solution)/shard_map/ppermute | solution.py:766
  603.4 4.7 collective-permute-start.50
  (26 other events, 47.1 us)
Sparse Core Ops, SparseCore 0:
  9.9 63.9 all-gather.2
  75.8 64.6 all-gather.4
  293.1 69.5 reduce-scatter.3
  383.2 91.3 reduce-scatter.5
  483.9 71.3 reduce-scatter.7

commit v4 on v3

--- a/solution.py
+++ b/solution.py
@@ -265,6 +265,9 @@
     mixed_refs = refs[:heads]
     w_ref, gain_ref, h2_ref, y1_ref, mixed_own_ref, w_near = refs[heads:]
     step = pl.program_id(0)
+    own_rows = y1_ref.shape[0]
+    devices = x_ref.shape[0] // own_rows
+
     def owner(number):
         return pl.multiple_of((place_ref[1] ^ number) * DH, DH)
 
@@ -276,25 +279,30 @@
     mixed = jnp.concatenate([ref[...] for ref in mixed_refs], axis=1)
     y1 = x_ref[...].astype(wide) + mm(mixed, w_near[...])
     h2_ref[...] = (y1 * norm_scale(y1) * gain_ref[...]).astype(low)
-
-    @pl.when(step == place_ref[0])
-    def _():
-        y1_ref[...] = y1
-        for number in range(heads):
-            mixed_own_ref[:, pl.ds(owner(number), DH)] = mixed_refs[number][...]
+    for device in range(devices):
+        begin = device * own_rows
+
+        @pl.when(step * devices + device == place_ref[0])
+        def _():
+            y1_ref[...] = y1[begin : begin + own_rows]
+            for number in range(heads):
+                mixed_own_ref[:, pl.ds(owner(number), DH)] = mixed_refs[number][
+                    begin : begin + own_rows
+                ]
 
 
 def mid_rows(place, x_all, mixed_pieces, w_out_all, gain):
     count, width = x_all.shape
     heads = len(mixed_pieces)
     inner = w_out_all.shape[0]
-    block = count // heads
+    own_rows = count // heads
+    block = max(1, ROW_BLOCK // own_rows) * own_rows
     return pl.pallas_call(
         functools.partial(mid_kernel, heads),
         name="mid_rows",
         grid_spec=pltpu.PrefetchScalarGridSpec(
             num_scalar_prefetch=1,
-            grid=(heads,),
+            grid=(count // block,),
             in_specs=[
                 pl.BlockSpec((block, width), lambda i, _: (i, 0)),
                 *[pl.BlockSpec((block, DH), lambda i, _: (i, 0))] * heads,
@@ -303,15 +311,15 @@
             ],
             out_specs=[
                 pl.BlockSpec((block, width), lambda i, _: (i, 0)),
-                pl.BlockSpec((block, width), lambda i, _: (0, 0)),
-                pl.BlockSpec((block, inner), lambda i, _: (0, 0)),
+                pl.BlockSpec((own_rows, width), lambda i, _: (0, 0)),
+                pl.BlockSpec((own_rows, inner), lambda i, _: (0, 0)),
             ],
             scratch_shapes=[pltpu.VMEM((inner, width), low)],
         ),
         out_shape=[
             jax.ShapeDtypeStruct((count, width), low),
-            jax.ShapeDtypeStruct((block, width), wide),
-            jax.ShapeDtypeStruct((block, inner), low),
+            jax.ShapeDtypeStruct((own_rows, width), wide),
+            jax.ShapeDtypeStruct((own_rows, inner), low),
         ],
         compiler_params=params(VMEM_ALONE),
         cost_estimate=SMALL,
@@ -393,13 +401,12 @@
         ref[...] = result
 
 
-def ffn_rest(h2_all, cot_all, w_gate, w_up, w_down, token):
+def ffn_rest(number, cols, h2_all, cot_all, w_gate, w_up, w_down, token):
     count, width = h2_all.shape
     block = min(ROW_BLOCK, count // 2)
-    cols = w_gate.shape[1] // 2
     row_spec = pl.BlockSpec((block, width), lambda i: (i, 0))
-    col_spec = pl.BlockSpec((width, cols), lambda i: (0, 1), pipeline_mode=pl.Buffered(1))
-    down_spec = pl.BlockSpec((cols, width), lambda i: (1, 0), pipeline_mode=pl.Buffered(1))
+    col_spec = pl.BlockSpec((width, cols), lambda i: (0, number), pipeline_mode=pl.Buffered(1))
+    down_spec = pl.BlockSpec((cols, width), lambda i: (number, 0), pipeline_mode=pl.Buffered(1))
     return pl.pallas_call(
         rest_kernel,
         name="ffn_rest",
@@ -815,7 +822,7 @@
         for stage, can_move in enumerate(ready):
             if can_move:
                 self.move(stage)
-            if stage == 0 and between:
+            if stage == max(len(ready) - 2, 0) and between:
                 result = between()
         return result
 
@@ -954,8 +961,13 @@
         push_ffn(number, top, bottom)
         return parts
 
+    def rest(number):
+        results = ffn_rest(number, cols, h2_all, cot_all, w_gate, w_up, w_down, chain.token)
+        chain.token = results[0]
+        return results
+
     def weights(number, parts):
-        top, bottom = ffn_weights(number - 2, cols, h2_all, cot_all, *parts, chain.token)
+        top, bottom = ffn_weights(0, cols, h2_all, cot_all, *parts, chain.token)
         chain.token = bottom
         push_ffn(number, top, bottom)
 
@@ -965,18 +977,18 @@
     part_a = first(0)
     chain.tick()
     part_b = first(1)
+    part_c = rest(2)
     chain.tick()
-    part_c = ffn_rest(h2_all, cot_all, w_gate, w_up, w_down, chain.token)
-    chain.token = part_c[0]
+    part_d = rest(3)
+    weights(2, part_c)
     chain.tick()
-    hidden, d_gate, d_up = zip(part_a, part_b, part_c)
+    hidden, d_gate, d_up = zip(part_a, part_b, part_c, part_d)
     d_h2 = chain.token = ffn_back(w_gate, w_up, d_gate, d_up, chain.token)
     d_h2 = scatter(d_h2)
     chain.tick()
-    weights(2, part_c)
+    parts = chain.token = ffn_out(own_rows, w_down, hidden, chain.token)
     chain.tick()
-    parts = chain.token = ffn_out(own_rows, w_down, hidden, chain.token)
-
+    weights(3, part_d)
     chain.tick()
     wait_for(WAITS[0])
     d_y1, d_mixed_own, parts, gain_mlp_part = own_rows_back(
@@ -985,7 +997,6 @@
     chain.token = d_y1
     d_mixed = lax.all_to_all(d_mixed_own, "heads", split_axis=1, concat_axis=0, tiled=True)
     parts = scatter(parts.reshape(-1, width))
-    weights(3, part_c)
     chain.tick()
     wait_for(WAITS[2])
     d_qkv, d_share = head_backward(

time: 628 us -> 627 us (level)
  waiting for transfers between devices: 171 us -> 164 us
    ppermute x30, waiting for transfers between devices: 58.3 us -> 46.5 us  [send(): arrived = lax.ppermute(array, self.axis, self.stages[stage][1])]
    pallas_call x1 -> x2, Pallas kernels: 19.5 us -> 24.4 us  [ffn_rest(): pl.pallas_call(rest_kernel, name='ffn_rest', grid=(count // block,), in_s...]
    unnamed x70 -> x72, local copies, waits for them, and re-layouts: 19.1 us -> 20.5 us
  transfers between devices with their start and end apart: 57 -> 57, of which waited for: 24 -> 22; matrix products, arithmetic and copies ran while one was open for 2% -> 2% of each run, Pallas kernels for 45% -> 46%
where the time goes in v4:
time: 627 us; the launch traced here: 617 us
  Pallas kernels  310 us (49%)
  waiting for transfers between devices  164 us (26%)
  starting transfers between devices  97 us (15%)
  local copies, waits for them, and re-layouts  26.1 us (4%)
  between operations  15.4 us (2%)
    ppermute x30, starting transfers between devices, send(): arrived = lax.ppermute(array, self.axis, self.stages[stage][1])  76.4 us
    ppermute x16, waiting for transfers between devices, flip(): return lax.ppermute(value, axis, [(i, i ^ bits) for i in range(size)])  61.1 us
    pallas_call x20, Pallas kernels, join(): pl.pallas_call(functools.partial(join_kernel, takers), name='join', grid=...  58.3 us
    pallas_call x2, Pallas kernels, ffn_first(): pl.pallas_call(functools.partial(first_kernel, blocks), name='ffn_first',...  46.9 us
    ppermute x30, waiting for transfers between devices, send(): arrived = lax.ppermute(array, self.axis, self.stages[stage][1])  46.5 us
    pallas_call x8, Pallas kernels, finish_ffn(): pl.pallas_call(functools.partial(finish_kernel, cols, is_top, takers), na...  31.4 us
    all_gather x2, waiting for transfers between devices, gather(): return lax.all_gather(array, 'heads', axis=0, tiled=True)  28.4 us
    pallas_call x2, Pallas kernels, ffn_weights(): pl.pallas_call(grads_kernel, name='ffn_weights', grid=(width // side,), i...  26.1 us
  transfers between devices with their start and end apart: 57, of which 22 were waited for; matrix products, arithmetic and copies ran while one was open for 2% of the time, Pallas kernels for 46%

profile of v4, /device:TPU:0, one launch (start us, length us, event | category | flops | bytes accessed | tf_op | source)
XLA Modules:
  0.0 617.1 jit_solution(7529639491479353879)
XLA Ops:
  8.0 3.0 collective-permute-start.1
  12.5 12.4 %collective-permute-done.1.refs_2_ = bf16[128,2048]{1,0:T(8,128)(2,1)S(1)} collective-permute-done((bf16[128,2048]{1,0:T(8,128)(2,1)}, bf16[128,2048]{1,0:T(8,128)(2,1)S(1)}, u32[]{:S(2)}, u32[]{:S(2)}) %collective-permute-start.1) | collective-permute-done | bytes 524320 | tf_op jit(solution)/shard_map/ppermute | solution.py:863
  29.3 9.3 %collective-permute-done.5 = bf16[64,2048]{1,0:T(8,128)(2,1)S(1)} collective-permute-done((bf16[64,2048]{1,0:T(8,128)(2,1)S(1)}, bf16[64,2048]{1,0:T(8,128)(2,1)S(1)}, u32[]{:S(2)}, u32[]{:S(2)}) %collective-permute-start.5) | collective-permute-done | bytes 262176 | tf_op jit(solution)/shard_map/ppermute | solution.py:863
  45.5 28.3 %all-gather.3.cloned.1.call-done.x_ref = bf16[2048,2048]{1,0:T(8,128)(2,1)} async-done(((bf16[256,2048]{1,0:T(8,128)(2,1)}), bf16[2048,2048]{1,0:T(8,128)(2,1)}) %all-gather.3.cloned.1.call-update) | async-done | bytes 8388624 | tf_op jit(solution)/shard_map/all_gather | solution.py:900
  78.5 10.6 %qkv_rows.1 = (bf16[2048,2048]{1,0:T(8,128)(2,1)}, bf16[2048,384]{1,0:T(8,128)(2,1)}) custom-call(bf16[2048,2048]{1,0:T(8,128)(2,1)} %all-gather.3.cloned.1.call-done.x_ref, f32[1,2048]{1,0:T(1,128)} %bitcast.52, bf16[2048,384]{1,0:T(8,128)(2,1)} %copy-done.3), custom_call_target="tpu_custom_call" | custom-call | flops 1 | bytes 1 | tf_op jit(solution)/shard_map/qkv_rows/pallas_call | solution.py:88
  89.1 5.8 head_forward.1
  96.5 16.8 %collective-permute-done.9.refs_2_ = bf16[2048,128]{1,0:T(8,128)(2,1)S(1)} collective-permute-done((bf16[2048,128]{1,0:T(8,128)(2,1)}, bf16[2048,128]{1,0:T(8,128)(2,1)S(1)}, u32[]{:S(2)}, u32[]{:S(2)}) %collective-permute-start.9) | collective-permute-done | bytes 524320 | tf_op jit(solution)/shard_map/ppermute | solution.py:863
  117.1 10.4 %collective-permute-done.13 = bf16[1024,128]{1,0:T(8,128)(2,1)S(1)} collective-permute-done((bf16[1024,128]{1,0:T(8,128)(2,1)S(1)}, bf16[1024,128]{1,0:T(8,128)(2,1)S(1)}, u32[]{:S(2)}, u32[]{:S(2)}) %collective-permute-start.13) | collective-permute-done | bytes 262176 | tf_op jit(solution)/shard_map/ppermute | solution.py:863
  132.8 18.2 %mid_rows.1 = (bf16[2048,2048]{1,0:T(8,128)(2,1)}, f32[256,2048]{1,0:T(8,128)}, bf16[256,1024]{1,0:T(8,128)(2,1)}) custom-call(s32[3]{0:T(128)} %copy-done.2, bf16[2048,2048]{1,0:T(8,128)(2,1)} %all-gather.3.cloned.1.call-done.x_ref, bf16[2048,128]{1,0:T(8,128)(2,1)} %bitcast.42, bf16[2048,128]{1,0:T(8,128)(2,1)} %copy-done.20, ...), custom_call_target="tpu_custom_call" | custom-call | flops 1 | bytes 1 | tf_op jit(solution)/shard_map/mid_rows/pallas_call | solution.py:300
  151.0 23.4 %ffn_first.2 = (bf16[2048,256]{1,0:T(8,128)(2,1)}, bf16[2048,256]{1,0:T(8,128)(2,1)}, bf16[2048,256]{1,0:T(8,128)(2,1)}, bf16[384,2048]{1,0:T(8,128)(2,1)}, bf16[384,2048]{1,0:T(8,128)(2,1)}) custom-call(bf16[2048,2048]{1,0:T(8,128)(2,1)} %get-tuple-element.87.h2_ref.h2_col_ref, bf16[2048,2048]{1,0:T(8,128)(2,1)} %all-gather.5.cloned.1.call-done.cot_ref.cot_col_ref, ...), custom_call_target="tpu_custom_call" | custom-call | flops 1 | bytes 1 | tf_op jit(solution)/shard_map/ffn_first/pallas_call | solution.py:384
  174.5 3.8 collective-permute-start.16
  178.2 23.5 %ffn_first.3 = (bf16[2048,256]{1,0:T(8,128)(2,1)}, bf16[2048,256]{1,0:T(8,128)(2,1)}, bf16[2048,256]{1,0:T(8,128)(2,1)}, bf16[384,2048]{1,0:T(8,128)(2,1)}, bf16[384,2048]{1,0:T(8,128)(2,1)}) custom-call(bf16[2048,2048]{1,0:T(8,128)(2,1)} %get-tuple-element.87.h2_ref.h2_col_ref, bf16[2048,2048]{1,0:T(8,128)(2,1)} %all-gather.5.cloned.1.call-done.cot_ref.cot_col_ref, ...), custom_call_target="tpu_custom_call" | custom-call | flops 1 | bytes 1 | tf_op jit(solution)/shard_map/ffn_first/pallas_call | solution.py:384
  201.7 12.2 %ffn_rest.2 = (bf16[2048,256]{1,0:T(8,128)(2,1)}, bf16[2048,256]{1,0:T(8,128)(2,1)}, bf16[2048,256]{1,0:T(8,128)(2,1)}) custom-call(bf16[2048,2048]{1,0:T(8,128)(2,1)} %get-tuple-element.87.h2_ref.h2_col_ref, bf16[2048,2048]{1,0:T(8,128)(2,1)} %all-gather.5.cloned.1.call-done.cot_ref.cot_col_ref, bf16[2048,1024]{1,0:T(8,128)(2,1)} %wg_ref.9, ...), custom_call_target="tpu_custom_call" | custom-call | flops 1 | bytes 1 | tf_op jit(solution)/shard_map/ffn_rest/pallas_call | solution.py:410
  216.5 2.8 join.20._.array_ref
  221.1 12.2 %ffn_rest.3 = (bf16[2048,256]{1,0:T(8,128)(2,1)}, bf16[2048,256]{1,0:T(8,128)(2,1)}, bf16[2048,256]{1,0:T(8,128)(2,1)}) custom-call(bf16[2048,2048]{1,0:T(8,128)(2,1)} %get-tuple-element.87.h2_ref.h2_col_ref, bf16[2048,2048]{1,0:T(8,128)(2,1)} %all-gather.5.cloned.1.call-done.cot_ref.cot_col_ref, bf16[2048,1024]{1,0:T(8,128)(2,1)} %wg_ref.9, ...), custom_call_target="tpu_custom_call" | custom-call | flops 1 | bytes 1 | tf_op jit(solution)/shard_map/ffn_rest/pallas_call | solution.py:410
  233.4 12.8 %ffn_weights.2 = (bf16[384,2048]{1,0:T(8,128)(2,1)}, bf16[384,2048]{1,0:T(8,128)(2,1)}) custom-call(bf16[2048,2048]{1,0:T(8,128)(2,1)} %get-tuple-element.87.h2_ref.h2_col_ref, bf16[2048,2048]{1,0:T(8,128)(2,1)} %all-gather.5.cloned.1.call-done.cot_ref.cot_col_ref, bf16[2048,256]{1,0:T(8,128)(2,1)} %get-tuple-element.96.__1_.hid_ref.refs_2_, ...), custom_call_target="tpu_custom_call" | custom-call | flops 1 | bytes 1 | tf_op jit(solution)/shard_map/ffn_weights/pallas_call | solution.py:440
  246.1 3.9 collective-permute-start.19
  251.2 2.8 join.21._.array_ref
  254.8 2.8 join.22.refs_8_.array_ref
  258.9 24.0 %ffn_back.1.__1_ = bf16[2048,2048]{1,0:T(8,128)(2,1)} custom-call(bf16[2048,1024]{1,0:T(8,128)(2,1)} %wg_ref.9, bf16[2048,1024]{1,0:T(8,128)(2,1)} %wu_ref.9, bf16[2048,256]{1,0:T(8,128)(2,1)} %get-tuple-element.89.refs_0_, bf16[2048,256]{1,0:T(8,128)(2,1)} %get-tuple-element.92.refs_1_, bf16[2048,256]{1,0:T(8,128)(2,1)} %get-tuple-element.94.dg_ref.refs_2_, ...), custom_call_target="tpu_custom_call" | custom-call | flops 1 | bytes 1 | tf_op jit(solution)/shard_map/ffn_back/pallas_call | solution.py:620
  282.9 8.5 %collective-permute-start.21 = (bf16[384,2048]{1,0:T(8,128)(2,1)}, bf16[384,2048]{1,0:T(8,128)(2,1)}, u32[]{:S(2)}, u32[]{:S(2)}) collective-permute-start(bf16[384,2048]{1,0:T(8,128)(2,1)} %hold.14._.array_ref), channel_id=1, source_target_pairs={{0,1},{3,2},{4,5},{7,6},{8,9},{11,10},{12,13},{15,14},{16,17},{19,... | collective-permute-start | bytes 4718600 | tf_op jit(solution)/shard_map/ppermute | solution.py:792
  291.4 2.8 join.23._.array_ref
  297.7 3.5 join.24.refs_0_.array_ref
  303.7 4.4 finish_ffn.8
  308.1 13.9 %ffn_out.1.__1_.refs_1_ = bf16[8,384,2048]{2,1,0:T(8,128)(2,1)} custom-call(bf16[1024,2048]{1,0:T(8,128)(2,1)} %w_ref.1, bf16[2048,256]{1,0:T(8,128)(2,1)} %get-tuple-element.91.__1_.refs_0_, bf16[2048,256]{1,0:T(8,128)(2,1)} %get-tuple-element.93._.refs_1_, bf16[2048,256]{1,0:T(8,128)(2,1)} %get-tuple-element.96.__1_.hid_ref.refs_2_, ...), custom_call_target="tpu_custom_call" | custom-call | flops 1 | bytes 1 | tf_op jit(solution)/shard_map/ffn_out/pallas_call | solution.py:644
  322.0 5.6 collective-permute-start.26
  327.5 2.9 join.25._.array_ref
  332.3 3.1 join.26.refs_0_.array_ref
  338.2 4.0 finish_ffn.9
  342.2 13.3 %ffn_weights.3 = (bf16[384,2048]{1,0:T(8,128)(2,1)}, bf16[384,2048]{1,0:T(8,128)(2,1)}) custom-call(bf16[2048,2048]{1,0:T(8,128)(2,1)} %get-tuple-element.87.h2_ref.h2_col_ref, bf16[2048,2048]{1,0:T(8,128)(2,1)} %all-gather.5.cloned.1.call-done.cot_ref.cot_col_ref, bf16[2048,256]{1,0:T(8,128)(2,1)} %get-tuple-element.103._.refs_3_.hid_ref, ...), custom_call_target="tpu_custom_call" | custom-call | flops 1 | bytes 1 | tf_op jit(solution)/shard_map/ffn_weights/pallas_call | solution.py:440
  355.5 4.2 collective-permute-start.30
  360.0 2.8 join.27._.array_ref
  364.6 2.9 join.28.refs_0_.array_ref
  368.7 4.4 collective-permute-done.24.arrived_ref
  374.3 3.7 finish_ffn.10
  378.6 8.9 %own_rows_back.1 = (f32[256,2048]{1,0:T(8,128)}, bf16[256,1024]{1,0:T(8,128)(2,1)}, bf16[8,384,2048]{2,1,0:T(8,128)(2,1)}, f32[1,2048]{1,0:T(1,128)}) custom-call(bf16[256,2048]{1,0:T(8,128)(2,1)} %reduce-scatter.4.cloned.1.call-done.d_h2_ref, f32[256,2048]{1,0:T(8,128)} %get-tuple-element.105.y1_ref, ...), custom_call_target="tpu_custom_call", output_to_operand_aliasing={{2}: (7, {})} | custom-call | flops 1 | bytes 1 | tf_op jit(solution)/shard_map/own_rows_back/pallas_call | solution.py:675
  387.5 2.9 collective-permute-start.33
  392.3 3.5 all-to-all-start
  397.1 3.6 join.29._.array_ref
  402.6 3.7 join.30.refs_0_.array_ref
  407.7 4.1 finish_ffn.11
  413.2 10.6 %head_backward.1 = (bf16[8,2,128,384]{3,2,1,0:T(8,128)(2,1)}, f32[2,8,128]{2,1,0:T(8,128)}) custom-call(f32[1]{0:T(128)S(6)} %div.3.share_ref, bf16[8,2,128,384]{3,2,1,0:T(8,128)(2,1)} %bitcast.34, bf16[8,2,128,128]{3,2,1,0:T(8,128)(2,1)} %bitcast.43, s32[2,1024,1]{2,1,0:T(8,128)} %copy.63.doc_rows_ref, s32[2,1,1024]{2,1,0:T(1,128)} %compare_select_fusion.doc_cols_ref, ...), custom_call_target="tpu_custom_call" | custom-call | flops 1 | bytes 1 | tf_op jit(solution)/shard_map/head_backward/pallas_call | solution.py:240
  423.8 5.8 collective-permute-start.35
  429.6 3.1 join.31._.array_ref
  434.6 2.9 join.32.refs_0_.array_ref
  438.7 6.8 %collective-permute-done.31.arrived_ref = bf16[384,2048]{1,0:T(8,128)(2,1)S(1)} collective-permute-done((bf16[384,2048]{1,0:T(8,128)(2,1)}, bf16[384,2048]{1,0:T(8,128)(2,1)S(1)}, u32[]{:S(2)}, u32[]{:S(2)}) %collective-permute-start.31) | collective-permute-done | bytes 1572896 | tf_op jit(solution)/shard_map/ppermute | solution.py:792
  446.7 3.7 finish_ffn.12
  450.4 15.0 %qkv_back.1 = (bf16[2048,2048]{1,0:T(8,128)(2,1)}, bf16[2048,384]{1,0:T(8,128)(2,1)}) custom-call(bf16[2048,384]{1,0:T(8,128)(2,1)} %bitcast.44, bf16[2048,2048]{1,0:T(8,128)(2,1)} %get-tuple-element.125.h1_ref, bf16[2048,384]{1,0:T(8,128)(2,1)} %copy-done.3, f32[8,128]{1,0:T(8,128)} %get-tuple-element.130._), custom_call_target="tpu_custom_call" | custom-call | flops 1 | bytes 1 | tf_op jit(solution)/shard_map/qkv_back/pallas_call | solution.py:723
  465.5 3.0 collective-permute-start.37
  468.4 2.9 join.33._.array_ref
  473.1 2.8 join.34.refs_0_.array_ref
  476.5 5.0 reduce-scatter.6.cloned.1.call-done.refs_1_.mlp_ref
  484.8 3.9 finish_ffn.13
  490.5 9.6 %collective-permute-done.37.arrived_ref = bf16[2048,384]{1,0:T(8,128)(2,1)} collective-permute-done((bf16[2048,384]{1,0:T(8,128)(2,1)}, bf16[2048,384]{1,0:T(8,128)(2,1)}, u32[]{:S(2)}, u32[]{:S(2)}) %collective-permute-start.37) | collective-permute-done | bytes 1572896 | tf_op jit(solution)/shard_map/ppermute | solution.py:792
  500.2 3.0 join.35._.array_ref
  509.2 8.3 %collective-permute-start.41 = (bf16[128,2048]{1,0:T(8,128)(2,1)S(1)}, bf16[128,2048]{1,0:T(8,128)(2,1)}, u32[]{:S(2)}, u32[]{:S(2)}) collective-permute-start(bf16[128,2048]{1,0:T(8,128)(2,1)S(1)} %copy-done.4), channel_id=1, source_target_pairs={{0,1},{3,2},{4,5},{7,6},{8,9},{11,10},{12,13},{15,14},{16,17},{19,... | collective-permute-start | bytes 1572872 | tf_op jit(solution)/shard_map/ppermute | solution.py:792
  519.5 3.1 collective-permute-done.42.arrived_ref
  523.8 3.8 finish_ffn.14
  530.3 2.9 join.38.refs_0_.array_ref
  534.7 21.7 %collective-permute-done.39.arrived_ref = bf16[384,2048]{1,0:T(8,128)(2,1)} collective-permute-done((bf16[384,2048]{1,0:T(8,128)(2,1)}, bf16[384,2048]{1,0:T(8,128)(2,1)}, u32[]{:S(2)}, u32[]{:S(2)}) %collective-permute-start.39) | collective-permute-done | bytes 1572896 | tf_op jit(solution)/shard_map/ppermute | solution.py:792
  556.4 3.9 finish_ffn.15
  560.9 6.7 %last_rows.1 = (f32[256,2048]{1,0:T(8,128)}, f32[1,2048]{1,0:T(1,128)}, bf16[256,2048]{1,0:T(8,128)(2,1)}) custom-call(bf16[256,2048]{1,0:T(8,128)(2,1)} %reduce-scatter.8.cloned.1.call-done.d_h1_ref, bf16[256,2048]{1,0:T(8,128)(2,1)} %bitcast.38, f32[256,2048]{1,0:T(8,128)} %get-tuple-element.120.__1_.d_y1_ref, f32[1,2048]{1,0:T(1,128)} %bitcast.53, ...), custom_call_target="tpu_custom_call" | custom-call | flops 1 | bytes 1 | tf_op jit(solution)/shard_map/last_rows/pallas_call | solution.py:582
  582.8 17.7 %collective-permute-done.49 = f32[4104]{0:T(1024)S(1)} collective-permute-done((f32[4104]{0:T(1024)S(1)}, f32[4104]{0:T(1024)S(1)}, u32[]{:S(2)}, u32[]{:S(2)}) %collective-permute-start.49) | collective-permute-done | bytes 16448 | tf_op jit(solution)/shard_map/ppermute | solution.py:773
  603.1 3.2 finish_cut.2
  (213 shorter events, 106.4 us)
Async XLA Ops:
  7.2 21.6 %copy-start.1 = (bf16[128,2048]{1,0:T(8,128)(2,1)S(1)}, bf16[128,2048]{1,0:T(8,128)(2,1)}, u32[]{:S(2)}) copy-start(bf16[128,2048]{1,0:T(8,128)(2,1)} %refs_0_.1) | copy-start | bytes 1572868
  7.2 66.7 %all-gather.3.cloned.1.call-start = ((), (), s32[]{:S(2)}) async-start(), calls=%async_computation.4 | async-start | bytes 9437184 | tf_op jit(solution)/shard_map/all_gather | solution.py:900
  7.9 143.1 %all-gather.5.cloned.1.call-start = ((), (), s32[]{:S(2)}) async-start(), calls=%async_computation.5 | async-start | bytes 9437184 | tf_op jit(solution)/shard_map/all_gather | solution.py:900
  8.0 16.9 %collective-permute-start.1 = (bf16[128,2048]{1,0:T(8,128)(2,1)}, bf16[128,2048]{1,0:T(8,128)(2,1)S(1)}, u32[]{:S(2)}, u32[]{:S(2)}) collective-permute-start(bf16[128,2048]{1,0:T(8,128)(2,1)} %refs_0_.1), channel_id=1, source_target_pairs={{0,8},{4,12},{8,0},{12,4},{16,24},{20,28},{24,16},{28,20},{1,9},{5... | collective-permute-start | bytes 1572872 | tf_op jit(solution)/shard_map/ppermute | solution.py:863
  11.0 17.2 %collective-permute-start.3 = (bf16[128,2048]{1,0:T(8,128)(2,1)}, bf16[128,2048]{1,0:T(8,128)(2,1)S(1)}, u32[]{:S(2)}, u32[]{:S(2)}) collective-permute-start(bf16[128,2048]{1,0:T(8,128)(2,1)} %refs_0_.1), channel_id=1, source_target_pairs={{0,16},{4,20},{8,24},{12,28},{16,0},{20,4},{24,8},{28,12},{1,17},{... | collective-permute-start | bytes 1572872 | tf_op jit(solution)/shard_map/ppermute | solution.py:863
  24.9 13.7 %collective-permute-start.5 = (bf16[64,2048]{1,0:T(8,128)(2,1)S(1)}, bf16[64,2048]{1,0:T(8,128)(2,1)S(1)}, u32[]{:S(2)}, u32[]{:S(2)}) collective-permute-start(bf16[64,2048]{1,0:T(8,128)(2,1)S(1)} %slice.32), channel_id=1, source_target_pairs={{0,16},{4,20},{8,24},{12,28},{16,0},{20,4},{24,8},{28,12},{1,17},{... | collective-permute-start | bytes 786440 | tf_op jit(solution)/shard_map/ppermute | solution.py:863
  28.2 11.8 %collective-permute-start.6 = (bf16[64,2048]{1,0:T(8,128)(2,1)S(1)}, bf16[64,2048]{1,0:T(8,128)(2,1)S(1)}, u32[]{:S(2)}, u32[]{:S(2)}) collective-permute-start(bf16[64,2048]{1,0:T(8,128)(2,1)S(1)} %slice.33), channel_id=1, source_target_pairs={{0,8},{4,12},{8,0},{12,4},{16,24},{20,28},{24,16},{28,20},{1,9},{5... | collective-permute-start | bytes 786440 | tf_op jit(solution)/shard_map/ppermute | solution.py:863
  28.8 11.4 %collective-permute-start = (bf16[128,2048]{1,0:T(8,128)(2,1)S(1)}, bf16[128,2048]{1,0:T(8,128)(2,1)S(1)}, u32[]{:S(2)}, u32[]{:S(2)}) collective-permute-start(bf16[128,2048]{1,0:T(8,128)(2,1)S(1)} %copy-done.1), channel_id=1, source_target_pairs={{0,4},{4,0},{8,12},{12,8},{16,20},{20,16},{24,28},{28,24},{1,5},{5... | collective-permute-start | bytes 1572872 | tf_op jit(solution)/shard_map/ppermute | solution.py:863
  28.8 11.4 %collective-permute-start.2 = (bf16[128,2048]{1,0:T(8,128)(2,1)S(1)}, bf16[128,2048]{1,0:T(8,128)(2,1)S(1)}, u32[]{:S(2)}, u32[]{:S(2)}) collective-permute-start(bf16[128,2048]{1,0:T(8,128)(2,1)S(1)} %collective-permute-done.1.refs_2_), channel_id=1, source_target_pairs={{0,4},{4,0},{8,12},{12,8},{16,20},{20,16},{24,28},{28,24},{1,5},{5... | collective-permute-start | bytes 1572872 | tf_op jit(solution)/shard_map/ppermute | solution.py:863
  29.3 10.9 %collective-permute-start.4 = (bf16[128,2048]{1,0:T(8,128)(2,1)S(1)}, bf16[128,2048]{1,0:T(8,128)(2,1)}, u32[]{:S(2)}, u32[]{:S(2)}) collective-permute-start(bf16[128,2048]{1,0:T(8,128)(2,1)S(1)} %collective-permute-done.3.refs_4_), channel_id=1, source_target_pairs={{0,4},{4,0},{8,12},{12,8},{16,20},{20,16},{24,28},{28,24},{1,5},{5... | collective-permute-start | bytes 1572872 | tf_op jit(solution)/shard_map/ppermute | solution.py:863
  40.0 2.1 collective-permute-start.7
  40.2 34.6 %copy-start.33 = (s32[2,1,4]{2,1,0:T(1,128)S(1)}, s32[2,1,4]{2,1,0:T(1,128)}, u32[]{:S(2)}) copy-start(s32[2,1,4]{2,1,0:T(1,128)} %param.16) | copy-start | bytes 100
  45.5 30.8 %copy-start.32 = (s32[2,1,1024]{2,1,0:T(1,128)S(1)}, s32[2,1,1024]{2,1,0:T(1,128)}, u32[]{:S(2)}) copy-start(s32[2,1,1024]{2,1,0:T(1,128)} %param.17) | copy-start | bytes 24580
  45.5 31.4 %copy-start.24 = (bf16[2048,128]{1,0:T(8,128)(2,1)S(1)}, bf16[2048,128]{1,0:T(8,128)(2,1)}, u32[]{:S(2)}) copy-start(bf16[2048,128]{1,0:T(8,128)(2,1)} %param.18) | copy-start | bytes 1572868
  73.9 304.7 %reduce-scatter.4.cloned.1.call-start = ((), (), s32[]{:S(2)}) async-start(), calls=%async_computation.6 | async-start | bytes 9437184 | tf_op jit(solution)/shard_map/reduce_scatter | solution.py:903
  94.9 18.4 %collective-permute-start.9 = (bf16[2048,128]{1,0:T(8,128)(2,1)}, bf16[2048,128]{1,0:T(8,128)(2,1)S(1)}, u32[]{:S(2)}, u32[]{:S(2)}) collective-permute-start(bf16[2048,128]{1,0:T(8,128)(2,1)} %bitcast.39), channel_id=1, source_target_pairs={{0,8},{4,12},{8,0},{12,4},{16,24},{20,28},{24,16},{28,20},{1,9},{5... | collective-permute-start | bytes 1572872 | tf_op jit(solution)/shard_map/ppermute | solution.py:863
  96.3 20.0 %collective-permute-start.11 = (bf16[2048,128]{1,0:T(8,128)(2,1)}, bf16[2048,128]{1,0:T(8,128)(2,1)S(1)}, u32[]{:S(2)}, u32[]{:S(2)}) collective-permute-start(bf16[2048,128]{1,0:T(8,128)(2,1)} %bitcast.40), channel_id=1, source_target_pairs={{0,16},{4,20},{8,24},{12,28},{16,0},{20,4},{24,8},{28,12},{1,17},{... | collective-permute-start | bytes 1572872 | tf_op jit(solution)/shard_map/ppermute | solution.py:863
  113.3 18.7 %copy-start.17 = (bf16[2048,128]{1,0:T(8,128)(2,1)}, bf16[2048,128]{1,0:T(8,128)(2,1)S(1)}, u32[]{:S(2)}) copy-start(bf16[2048,128]{1,0:T(8,128)(2,1)S(1)} %collective-permute-done.9.refs_2_) | copy-start | bytes 1572868
  113.4 14.1 %collective-permute-start.13 = (bf16[1024,128]{1,0:T(8,128)(2,1)S(1)}, bf16[1024,128]{1,0:T(8,128)(2,1)S(1)}, u32[]{:S(2)}, u32[]{:S(2)}) collective-permute-start(bf16[1024,128]{1,0:T(8,128)(2,1)S(1)} %slice.34), channel_id=1, source_target_pairs={{0,16},{4,20},{8,24},{12,28},{16,0},{20,4},{24,8},{28,12},{1,17},{... | collective-permute-start | bytes 786440 | tf_op jit(solution)/shard_map/ppermute | solution.py:863
  116.3 15.7 %copy-start.18 = (bf16[2048,128]{1,0:T(8,128)(2,1)}, bf16[2048,128]{1,0:T(8,128)(2,1)S(1)}, u32[]{:S(2)}) copy-start(bf16[2048,128]{1,0:T(8,128)(2,1)S(1)} %collective-permute-done.11.refs_4_) | copy-start | bytes 1572868
  116.3 13.5 %collective-permute-start.14 = (bf16[1024,128]{1,0:T(8,128)(2,1)S(1)}, bf16[1024,128]{1,0:T(8,128)(2,1)S(1)}, u32[]{:S(2)}, u32[]{:S(2)}) collective-permute-start(bf16[1024,128]{1,0:T(8,128)(2,1)S(1)} %slice.35), channel_id=1, source_target_pairs={{0,8},{4,12},{8,0},{12,4},{16,24},{20,28},{24,16},{28,20},{1,9},{5... | collective-permute-start | bytes 786440 | tf_op jit(solution)/shard_map/ppermute | solution.py:863
  116.4 13.5 %collective-permute-start.8 = (bf16[2048,128]{1,0:T(8,128)(2,1)}, bf16[2048,128]{1,0:T(8,128)(2,1)S(1)}, u32[]{:S(2)}, u32[]{:S(2)}) collective-permute-start(bf16[2048,128]{1,0:T(8,128)(2,1)} %bitcast.41), channel_id=1, source_target_pairs={{0,4},{4,0},{8,12},{12,8},{16,20},{20,16},{24,28},{28,24},{1,5},{5... | collective-permute-start | bytes 1572872 | tf_op jit(solution)/shard_map/ppermute | solution.py:863
  116.5 13.5 %collective-permute-start.12 = (bf16[2048,128]{1,0:T(8,128)(2,1)S(1)}, bf16[2048,128]{1,0:T(8,128)(2,1)S(1)}, u32[]{:S(2)}, u32[]{:S(2)}) collective-permute-start(bf16[2048,128]{1,0:T(8,128)(2,1)S(1)} %collective-permute-done.11.refs_4_), channel_id=1, source_target_pairs={{0,4},{4,0},{8,12},{12,8},{16,20},{20,16},{24,28},{28,24},{1,5},{5... | collective-permute-start | bytes 1572872 | tf_op jit(solution)/shard_map/ppermute | solution.py:863
  117.0 13.0 %collective-permute-start.10 = (bf16[2048,128]{1,0:T(8,128)(2,1)S(1)}, bf16[2048,128]{1,0:T(8,128)(2,1)S(1)}, u32[]{:S(2)}, u32[]{:S(2)}) collective-permute-start(bf16[2048,128]{1,0:T(8,128)(2,1)S(1)} %collective-permute-done.9.refs_2_), channel_id=1, source_target_pairs={{0,4},{4,0},{8,12},{12,8},{16,20},{20,16},{24,28},{28,24},{1,5},{5... | collective-permute-start | bytes 1572872 | tf_op jit(solution)/shard_map/ppermute | solution.py:863
  129.9 2.2 collective-permute-start.15
  174.5 40.8 %collective-permute-start.16 = (bf16[384,2048]{1,0:T(8,128)(2,1)}, bf16[384,2048]{1,0:T(8,128)(2,1)S(1)}, u32[]{:S(2)}, u32[]{:S(2)}) collective-permute-start(bf16[384,2048]{1,0:T(8,128)(2,1)} %hold.11._.array_ref), channel_id=1, source_target_pairs={{0,1},{3,2},{4,5},{7,6},{8,9},{11,10},{12,13},{15,14},{16,17},{19,... | collective-permute-start | bytes 4718600 | tf_op jit(solution)/shard_map/ppermute | solution.py:792
  213.9 36.1 %collective-permute-start.18 = (bf16[384,2048]{1,0:T(8,128)(2,1)}, bf16[384,2048]{1,0:T(8,128)(2,1)S(1)}, u32[]{:S(2)}, u32[]{:S(2)}) collective-permute-start(bf16[384,2048]{1,0:T(8,128)(2,1)} %hold.12._.array_ref), channel_id=1, source_target_pairs={{0,1},{3,2},{4,5},{7,6},{8,9},{11,10},{12,13},{15,14},{16,17},{19,... | collective-permute-start | bytes 4718600 | tf_op jit(solution)/shard_map/ppermute | solution.py:792
  219.3 35.5 %collective-permute-start.17 = (bf16[384,2048]{1,0:T(8,128)(2,1)}, bf16[384,2048]{1,0:T(8,128)(2,1)}, u32[]{:S(2)}, u32[]{:S(2)}) collective-permute-start(bf16[384,2048]{1,0:T(8,128)(2,1)} %join.20._.array_ref), channel_id=1, source_target_pairs={{1,2},{2,1},{5,6},{6,5},{9,10},{10,9},{13,14},{14,13},{17,18},{18,... | collective-permute-start | bytes 4718600 | tf_op jit(solution)/shard_map/ppermute | solution.py:792
  246.1 45.3 %collective-permute-start.19 = (bf16[384,2048]{1,0:T(8,128)(2,1)}, bf16[384,2048]{1,0:T(8,128)(2,1)}, u32[]{:S(2)}, u32[]{:S(2)}) collective-permute-start(bf16[384,2048]{1,0:T(8,128)(2,1)} %hold.13._.array_ref), channel_id=1, source_target_pairs={{0,1},{3,2},{4,5},{7,6},{8,9},{11,10},{12,13},{15,14},{16,17},{19,... | collective-permute-start | bytes 4718600 | tf_op jit(solution)/shard_map/ppermute | solution.py:792
  254.0 42.6 %collective-permute-start.23 = (bf16[384,2048]{1,0:T(8,128)(2,1)}, bf16[384,2048]{1,0:T(8,128)(2,1)S(1)}, u32[]{:S(2)}, u32[]{:S(2)}) collective-permute-start(bf16[384,2048]{1,0:T(8,128)(2,1)} %join.21._.array_ref), channel_id=1, source_target_pairs={{1,2},{2,1},{5,6},{6,5},{9,10},{10,9},{13,14},{14,13},{17,18},{18,... | collective-permute-start | bytes 4718600 | tf_op jit(solution)/shard_map/ppermute | solution.py:792
  257.6 44.9 %collective-permute-start.22 = (bf16[384,2048]{1,0:T(8,128)(2,1)}, bf16[384,2048]{1,0:T(8,128)(2,1)S(1)}, u32[]{:S(2)}, u32[]{:S(2)}) collective-permute-start(bf16[384,2048]{1,0:T(8,128)(2,1)} %join.22.refs_8_.array_ref), channel_id=1, source_target_pairs={{1,0},{2,3},{5,4},{6,7},{9,8},{10,11},{13,12},{14,15},{17,16},{18,... | collective-permute-start | bytes 4718600 | tf_op jit(solution)/shard_map/ppermute | solution.py:792
  282.9 44.6 %collective-permute-start.21 = (bf16[384,2048]{1,0:T(8,128)(2,1)}, bf16[384,2048]{1,0:T(8,128)(2,1)}, u32[]{:S(2)}, u32[]{:S(2)}) collective-permute-start(bf16[384,2048]{1,0:T(8,128)(2,1)} %hold.14._.array_ref), channel_id=1, source_target_pairs={{0,1},{3,2},{4,5},{7,6},{8,9},{11,10},{12,13},{15,14},{16,17},{19,... | collective-permute-start | bytes 4718600 | tf_op jit(solution)/shard_map/ppermute | solution.py:792
  294.2 38.0 %collective-permute-start.20 = (bf16[384,2048]{1,0:T(8,128)(2,1)}, bf16[384,2048]{1,0:T(8,128)(2,1)}, u32[]{:S(2)}, u32[]{:S(2)}) collective-permute-start(bf16[384,2048]{1,0:T(8,128)(2,1)} %join.23._.array_ref), channel_id=1, source_target_pairs={{1,2},{2,1},{5,6},{6,5},{9,10},{10,9},{13,14},{14,13},{17,18},{18,... | collective-permute-start | bytes 4718600 | tf_op jit(solution)/shard_map/ppermute | solution.py:792
  296.1 185.3 %reduce-scatter.6.cloned.1.call-start = ((), (), s32[]{:S(2)}) async-start(), calls=%async_computation.7 | async-start | bytes 14155776 | tf_op jit(solution)/shard_map/reduce_scatter | solution.py:903
  301.2 35.8 %collective-permute-start.27 = (bf16[384,2048]{1,0:T(8,128)(2,1)}, bf16[384,2048]{1,0:T(8,128)(2,1)S(1)}, u32[]{:S(2)}, u32[]{:S(2)}) collective-permute-start(bf16[384,2048]{1,0:T(8,128)(2,1)} %join.24.refs_0_.array_ref), channel_id=1, source_target_pairs={{1,0},{2,3},{5,4},{6,7},{9,8},{10,11},{13,12},{14,15},{17,16},{18,... | collective-permute-start | bytes 4718600 | tf_op jit(solution)/shard_map/ppermute | solution.py:792
  322.0 38.0 %collective-permute-start.26 = (bf16[384,2048]{1,0:T(8,128)(2,1)}, bf16[384,2048]{1,0:T(8,128)(2,1)}, u32[]{:S(2)}, u32[]{:S(2)}) collective-permute-start(bf16[384,2048]{1,0:T(8,128)(2,1)} %hold.15._.array_ref), channel_id=1, source_target_pairs={{0,1},{3,2},{4,5},{7,6},{8,9},{11,10},{12,13},{15,14},{16,17},{19,... | collective-permute-start | bytes 4718600 | tf_op jit(solution)/shard_map/ppermute | solution.py:792
  330.5 34.1 %collective-permute-start.25 = (bf16[384,2048]{1,0:T(8,128)(2,1)}, bf16[384,2048]{1,0:T(8,128)(2,1)}, u32[]{:S(2)}, u32[]{:S(2)}) collective-permute-start(bf16[384,2048]{1,0:T(8,128)(2,1)} %join.25._.array_ref), channel_id=1, source_target_pairs={{1,2},{2,1},{5,6},{6,5},{9,10},{10,9},{13,14},{14,13},{17,18},{18,... | collective-permute-start | bytes 4718600 | tf_op jit(solution)/shard_map/ppermute | solution.py:792
  335.4 37.8 %collective-permute-start.24 = (bf16[384,2048]{1,0:T(8,128)(2,1)}, bf16[384,2048]{1,0:T(8,128)(2,1)S(1)}, u32[]{:S(2)}, u32[]{:S(2)}) collective-permute-start(bf16[384,2048]{1,0:T(8,128)(2,1)} %join.26.refs_0_.array_ref), channel_id=1, source_target_pairs={{1,0},{2,3},{5,4},{6,7},{9,8},{10,11},{13,12},{14,15},{17,16},{18,... | collective-permute-start | bytes 4718600 | tf_op jit(solution)/shard_map/ppermute | solution.py:792
  355.5 40.4 %collective-permute-start.30 = (bf16[384,2048]{1,0:T(8,128)(2,1)}, bf16[384,2048]{1,0:T(8,128)(2,1)S(1)}, u32[]{:S(2)}, u32[]{:S(2)}) collective-permute-start(bf16[384,2048]{1,0:T(8,128)(2,1)} %hold.16._.array_ref), channel_id=1, source_target_pairs={{0,1},{3,2},{4,5},{7,6},{8,9},{11,10},{12,13},{15,14},{16,17},{19,... | collective-permute-start | bytes 4718600 | tf_op jit(solution)/shard_map/ppermute | solution.py:792
  362.8 39.8 %collective-permute-start.29 = (bf16[384,2048]{1,0:T(8,128)(2,1)}, bf16[384,2048]{1,0:T(8,128)(2,1)}, u32[]{:S(2)}, u32[]{:S(2)}) collective-permute-start(bf16[384,2048]{1,0:T(8,128)(2,1)} %join.27._.array_ref), channel_id=1, source_target_pairs={{1,2},{2,1},{5,6},{6,5},{9,10},{10,9},{13,14},{14,13},{17,18},{18,... | collective-permute-start | bytes 4718600 | tf_op jit(solution)/shard_map/ppermute | solution.py:792
  367.4 40.3 %collective-permute-start.28 = (bf16[384,2048]{1,0:T(8,128)(2,1)}, bf16[384,2048]{1,0:T(8,128)(2,1)}, u32[]{:S(2)}, u32[]{:S(2)}) collective-permute-start(bf16[384,2048]{1,0:T(8,128)(2,1)} %join.28.refs_0_.array_ref), channel_id=1, source_target_pairs={{1,0},{2,3},{5,4},{6,7},{9,8},{10,11},{13,12},{14,15},{17,16},{18,... | collective-permute-start | bytes 4718600 | tf_op jit(solution)/shard_map/ppermute | solution.py:792
  387.5 42.1 %collective-permute-start.33 = (bf16[384,2048]{1,0:T(8,128)(2,1)}, bf16[384,2048]{1,0:T(8,128)(2,1)}, u32[]{:S(2)}, u32[]{:S(2)}) collective-permute-start(bf16[384,2048]{1,0:T(8,128)(2,1)} %hold.17._.array_ref), channel_id=1, source_target_pairs={{0,1},{3,2},{4,5},{7,6},{8,9},{11,10},{12,13},{15,14},{16,17},{19,... | collective-permute-start | bytes 4718600 | tf_op jit(solution)/shard_map/ppermute | solution.py:792
  392.3 20.1 %all-to-all-start = ((bf16[256,8,128]{2,0,1:T(8,128)(2,1)}), bf16[256,8,128]{2,0,1:T(8,128)(2,1)S(1)}, u32[]{:S(2)}, u32[]{:S(2)}) async-start(bf16[256,8,128]{2,0,1:T(8,128)(2,1)} %copy_bitcast_fusion), calls=%async_computation.1 | async-start | bytes 1048576 | tf_op jit(solution)/shard_map/all_to_all | solution.py:998
  395.8 165.1 %reduce-scatter.8.cloned.1.call-start = ((), (), s32[]{:S(2)}) async-start(), calls=%async_computation.8 | async-start | bytes 9437184 | tf_op jit(solution)/shard_map/reduce_scatter | solution.py:903
  400.8 33.8 %collective-permute-start.32 = (bf16[384,2048]{1,0:T(8,128)(2,1)}, bf16[384,2048]{1,0:T(8,128)(2,1)}, u32[]{:S(2)}, u32[]{:S(2)}) collective-permute-start(bf16[384,2048]{1,0:T(8,128)(2,1)} %join.29._.array_ref), channel_id=1, source_target_pairs={{1,2},{2,1},{5,6},{6,5},{9,10},{10,9},{13,14},{14,13},{17,18},{18,... | collective-permute-start | bytes 4718600 | tf_op jit(solution)/shard_map/ppermute | solution.py:792
  406.3 39.3 %collective-permute-start.31 = (bf16[384,2048]{1,0:T(8,128)(2,1)}, bf16[384,2048]{1,0:T(8,128)(2,1)S(1)}, u32[]{:S(2)}, u32[]{:S(2)}) collective-permute-start(bf16[384,2048]{1,0:T(8,128)(2,1)} %join.30.refs_0_.array_ref), channel_id=1, source_target_pairs={{1,0},{2,3},{5,4},{6,7},{9,8},{10,11},{13,12},{14,15},{17,16},{18,... | collective-permute-start | bytes 4718600 | tf_op jit(solution)/shard_map/ppermute | solution.py:792
  423.8 44.6 %collective-permute-start.35 = (bf16[384,2048]{1,0:T(8,128)(2,1)}, bf16[384,2048]{1,0:T(8,128)(2,1)}, u32[]{:S(2)}, u32[]{:S(2)}) collective-permute-start(bf16[384,2048]{1,0:T(8,128)(2,1)} %hold.18._.array_ref), channel_id=1, source_target_pairs={{0,1},{3,2},{4,5},{7,6},{8,9},{11,10},{12,13},{15,14},{16,17},{19,... | collective-permute-start | bytes 4718600 | tf_op jit(solution)/shard_map/ppermute | solution.py:792
  432.7 40.4 %collective-permute-start.34 = (bf16[384,2048]{1,0:T(8,128)(2,1)}, bf16[384,2048]{1,0:T(8,128)(2,1)}, u32[]{:S(2)}, u32[]{:S(2)}) collective-permute-start(bf16[384,2048]{1,0:T(8,128)(2,1)} %join.31._.array_ref), channel_id=1, source_target_pairs={{1,2},{2,1},{5,6},{6,5},{9,10},{10,9},{13,14},{14,13},{17,18},{18,... | collective-permute-start | bytes 4718600 | tf_op jit(solution)/shard_map/ppermute | solution.py:792
  437.4 47.3 %collective-permute-start.38 = (bf16[384,2048]{1,0:T(8,128)(2,1)}, bf16[384,2048]{1,0:T(8,128)(2,1)}, u32[]{:S(2)}, u32[]{:S(2)}) collective-permute-start(bf16[384,2048]{1,0:T(8,128)(2,1)} %join.32.refs_0_.array_ref), channel_id=1, source_target_pairs={{1,0},{2,3},{5,4},{6,7},{9,8},{10,11},{13,12},{14,15},{17,16},{18,... | collective-permute-start | bytes 4718600 | tf_op jit(solution)/shard_map/ppermute | solution.py:792
  465.5 34.7 %collective-permute-start.37 = (bf16[2048,384]{1,0:T(8,128)(2,1)}, bf16[2048,384]{1,0:T(8,128)(2,1)}, u32[]{:S(2)}, u32[]{:S(2)}) collective-permute-start(bf16[2048,384]{1,0:T(8,128)(2,1)} %hold.19._.array_ref), channel_id=1, source_target_pairs={{0,1},{3,2},{4,5},{7,6},{8,9},{11,10},{12,13},{15,14},{16,17},{19,... | collective-permute-start | bytes 4718600 | tf_op jit(solution)/shard_map/ppermute | solution.py:792
  471.3 33.8 %collective-permute-start.36 = (bf16[384,2048]{1,0:T(8,128)(2,1)}, bf16[384,2048]{1,0:T(8,128)(2,1)}, u32[]{:S(2)}, u32[]{:S(2)}) collective-permute-start(bf16[384,2048]{1,0:T(8,128)(2,1)} %join.33._.array_ref), channel_id=1, source_target_pairs={{1,2},{2,1},{5,6},{6,5},{9,10},{10,9},{13,14},{14,13},{17,18},{18,... | collective-permute-start | bytes 4718600 | tf_op jit(solution)/shard_map/ppermute | solution.py:792
  483.5 39.2 %collective-permute-start.42 = (bf16[384,2048]{1,0:T(8,128)(2,1)S(1)}, bf16[384,2048]{1,0:T(8,128)(2,1)S(1)}, u32[]{:S(2)}, u32[]{:S(2)}) collective-permute-start(bf16[384,2048]{1,0:T(8,128)(2,1)S(1)} %copy-done.5), channel_id=1, source_target_pairs={{1,0},{2,3},{5,4},{6,7},{9,8},{10,11},{13,12},{14,15},{17,16},{18,... | collective-permute-start | bytes 4718600 | tf_op jit(solution)/shard_map/ppermute | solution.py:792
  503.2 27.1 %collective-permute-start.40 = (bf16[2048,384]{1,0:T(8,128)(2,1)}, bf16[2048,384]{1,0:T(8,128)(2,1)}, u32[]{:S(2)}, u32[]{:S(2)}) collective-permute-start(bf16[2048,384]{1,0:T(8,128)(2,1)} %join.35._.array_ref), channel_id=1, source_target_pairs={{1,2},{2,1},{5,6},{6,5},{9,10},{10,9},{13,14},{14,13},{17,18},{18,... | collective-permute-start | bytes 4718600 | tf_op jit(solution)/shard_map/ppermute | solution.py:792
  508.0 48.5 %collective-permute-start.39 = (bf16[384,2048]{1,0:T(8,128)(2,1)}, bf16[384,2048]{1,0:T(8,128)(2,1)}, u32[]{:S(2)}, u32[]{:S(2)}) collective-permute-start(bf16[384,2048]{1,0:T(8,128)(2,1)} %join.36.refs_0_.array_ref), channel_id=1, source_target_pairs={{1,0},{2,3},{5,4},{6,7},{9,8},{10,11},{13,12},{14,15},{17,16},{18,... | collective-permute-start | bytes 4718600 | tf_op jit(solution)/shard_map/ppermute | solution.py:792
  509.2 18.4 %collective-permute-start.41 = (bf16[128,2048]{1,0:T(8,128)(2,1)S(1)}, bf16[128,2048]{1,0:T(8,128)(2,1)}, u32[]{:S(2)}, u32[]{:S(2)}) collective-permute-start(bf16[128,2048]{1,0:T(8,128)(2,1)S(1)} %copy-done.4), channel_id=1, source_target_pairs={{0,1},{3,2},{4,5},{7,6},{8,9},{11,10},{12,13},{15,14},{16,17},{19,... | collective-permute-start | bytes 1572872 | tf_op jit(solution)/shard_map/ppermute | solution.py:792
  529.6 38.9 %collective-permute-start.44 = (bf16[128,2048]{1,0:T(8,128)(2,1)}, bf16[128,2048]{1,0:T(8,128)(2,1)S(1)}, u32[]{:S(2)}, u32[]{:S(2)}) collective-permute-start(bf16[128,2048]{1,0:T(8,128)(2,1)} %join.37._.array_ref), channel_id=1, source_target_pairs={{1,2},{2,1},{5,6},{6,5},{9,10},{10,9},{13,14},{14,13},{17,18},{18,... | collective-permute-start | bytes 1572872 | tf_op jit(solution)/shard_map/ppermute | solution.py:792
  533.2 68.8 %collective-permute-start.43 = (bf16[2048,384]{1,0:T(8,128)(2,1)}, bf16[2048,384]{1,0:T(8,128)(2,1)S(1)}, u32[]{:S(2)}, u32[]{:S(2)}) collective-permute-start(bf16[2048,384]{1,0:T(8,128)(2,1)} %join.38.refs_0_.array_ref), channel_id=1, source_target_pairs={{1,0},{2,3},{5,4},{6,7},{9,8},{10,11},{13,12},{14,15},{17,16},{18,... | collective-permute-start | bytes 4718600 | tf_op jit(solution)/shard_map/ppermute | solution.py:792
  560.9 6.8 %copy-start.31 = (f32[1,2048]{1,0:T(1,128)S(1)}, f32[1,2048]{1,0:T(1,128)}, u32[]{:S(2)}) copy-start(f32[1,2048]{1,0:T(1,128)} %get-tuple-element.155) | copy-start | bytes 24580
  568.4 4.0 collective-permute-start.46
  571.2 36.3 %collective-permute-start.45 = (bf16[128,2048]{1,0:T(8,128)(2,1)}, bf16[128,2048]{1,0:T(8,128)(2,1)S(1)}, u32[]{:S(2)}, u32[]{:S(2)}) collective-permute-start(bf16[128,2048]{1,0:T(8,128)(2,1)} %join.39._.array_ref), channel_id=1, source_target_pairs={{1,0},{2,3},{5,4},{6,7},{9,8},{10,11},{13,12},{14,15},{17,16},{18,... | collective-permute-start | bytes 1572872 | tf_op jit(solution)/shard_map/ppermute | solution.py:792
  572.5 3.8 collective-permute-start.47
  576.4 3.8 collective-permute-start.48
  580.2 20.4 %collective-permute-start.49 = (f32[4104]{0:T(1024)S(1)}, f32[4104]{0:T(1024)S(1)}, u32[]{:S(2)}, u32[]{:S(2)}) collective-permute-start(f32[4104]{0:T(1024)S(1)} %add.32), channel_id=1, source_target_pairs={{0,1},{1,0},{2,3},{3,2},{4,5},{5,4},{6,7},{7,6},{8,9},{9,8},{10,11... | collective-permute-start | bytes 49256 | tf_op jit(solution)/shard_map/ppermute | solution.py:773
  600.5 5.8 collective-permute-start.50
  (27 other events, 48.5 us)
Sparse Core Ops, SparseCore 0:
  9.9 63.9 all-gather.2
  75.8 64.6 all-gather.4
  296.3 68.2 reduce-scatter.3
  390.5 90.9 reduce-scatter.5
  485.2 71.2 reduce-scatter.7

commit v5 on v4

--- a/solution.py
+++ b/solution.py
@@ -986,15 +986,19 @@
     d_h2 = chain.token = ffn_back(w_gate, w_up, d_gate, d_up, chain.token)
     d_h2 = scatter(d_h2)
     chain.tick()
-    parts = chain.token = ffn_out(own_rows, w_down, hidden, chain.token)
+    out_parts = chain.token = ffn_out(own_rows, w_down, hidden, chain.token)
     chain.tick()
     weights(3, part_d)
-    chain.tick()
-    wait_for(WAITS[0])
-    d_y1, d_mixed_own, parts, gain_mlp_part = own_rows_back(
-        chain.token, d_h2, y1_own, cot_own, norm_mlp, w_out_all, mixed_own, parts
-    )
-    chain.token = d_y1
+
+    def own_part():
+        wait_for(WAITS[0])
+        results = own_rows_back(
+            chain.token, d_h2, y1_own, cot_own, norm_mlp, w_out_all, mixed_own, out_parts
+        )
+        chain.token = results[0]
+        return results
+
+    d_y1, d_mixed_own, parts, gain_mlp_part = chain.tick(own_part)
     d_mixed = lax.all_to_all(d_mixed_own, "heads", split_axis=1, concat_axis=0, tiled=True)
     parts = scatter(parts.reshape(-1, width))
     chain.tick()
@@ -1027,7 +1031,14 @@
     chain.token = gain_attn_part
     slots = jnp.where(jnp.arange(n_heads) == here, jnp.sum(d_share[:, 0, 0]), 0.0)
     sums = jnp.concatenate([gain_attn_part[0], gain_mlp_part[0], slots])
-    sums = butterfly(butterfly(sums, "heads", n_heads), "batch", n_batch)
+    sums = butterfly(sums, "heads", n_heads)
+    if n_batch == 4:
+        sums = sums + lax.ppermute(sums, "batch", [(i, i ^ 1) for i in range(4)])
+        chain.tick()
+        sums = chain.token = hold(sums, chain.token)
+        sums = sums + lax.ppermute(sums, "batch", [(i, i ^ 2) for i in range(4)])
+    else:
+        sums = butterfly(sums, "batch", n_batch)
     grad_mix = lax.dynamic_slice_in_dim(sums, 2 * width + here, 1, 0)
     chain.drain()
 

time: 627 us -> 627 us (level)
    ppermute x5 -> x3, waiting for transfers between devices: 22.7 us -> 4.96 us  [butterfly(): lax.ppermute(array, axis, [(i, i ^ step) for i in range(size)])]
    ppermute x0 -> x2, waiting for transfers between devices: none -> 9.63 us  [the longest x1 6.17 us: per_device(): sums = sums + lax.ppermute(sums, 'batch', [(i, i ^ 1) for i in range(4)])]
  transfers between devices with their start and end apart: 57 -> 57, of which waited for: 22 -> 24; matrix products, arithmetic and copies ran while one was open for 2% -> 2% of each run, Pallas kernels for 46% -> 46%
where the time goes in v5:
time: 627 us; the launch traced here: 617 us
  Pallas kernels  310 us (49%)
  waiting for transfers between devices  162 us (26%)
  starting transfers between devices  98.2 us (16%)
  local copies, waits for them, and re-layouts  26 us (4%)
  between operations  15.5 us (2%)
    ppermute x30, starting transfers between devices, send(): arrived = lax.ppermute(array, self.axis, self.stages[stage][1])  78 us
    ppermute x16, waiting for transfers between devices, flip(): return lax.ppermute(value, axis, [(i, i ^ bits) for i in range(size)])  61.1 us
    pallas_call x20, Pallas kernels, join(): pl.pallas_call(functools.partial(join_kernel, takers), name='join', grid=...  58.2 us
    ppermute x30, waiting for transfers between devices, send(): arrived = lax.ppermute(array, self.axis, self.stages[stage][1])  52.2 us
    pallas_call x2, Pallas kernels, ffn_first(): pl.pallas_call(functools.partial(first_kernel, blocks), name='ffn_first',...  46.9 us
    pallas_call x8, Pallas kernels, finish_ffn(): pl.pallas_call(functools.partial(finish_kernel, cols, is_top, takers), na...  30.9 us
    all_gather x2, waiting for transfers between devices, gather(): return lax.all_gather(array, 'heads', axis=0, tiled=True)  28.4 us
    pallas_call x2, Pallas kernels, ffn_weights(): pl.pallas_call(grads_kernel, name='ffn_weights', grid=(width // side,), i...  26.3 us
  transfers between devices with their start and end apart: 57, of which 24 were waited for; matrix products, arithmetic and copies ran while one was open for 2% of the time, Pallas kernels for 46%

profile of v5, /device:TPU:0, one launch (start us, length us, event | category | flops | bytes accessed | tf_op | source)
XLA Modules:
  0.0 616.5 jit_solution(16315513887452071313)
XLA Ops:
  8.0 3.0 collective-permute-start.1
  12.5 12.4 %collective-permute-done.1.refs_2_ = bf16[128,2048]{1,0:T(8,128)(2,1)S(1)} collective-permute-done((bf16[128,2048]{1,0:T(8,128)(2,1)}, bf16[128,2048]{1,0:T(8,128)(2,1)S(1)}, u32[]{:S(2)}, u32[]{:S(2)}) %collective-permute-start.1) | collective-permute-done | bytes 524320 | tf_op jit(solution)/shard_map/ppermute | solution.py:863
  29.3 9.3 %collective-permute-done.5 = bf16[64,2048]{1,0:T(8,128)(2,1)S(1)} collective-permute-done((bf16[64,2048]{1,0:T(8,128)(2,1)S(1)}, bf16[64,2048]{1,0:T(8,128)(2,1)S(1)}, u32[]{:S(2)}, u32[]{:S(2)}) %collective-permute-start.5) | collective-permute-done | bytes 262176 | tf_op jit(solution)/shard_map/ppermute | solution.py:863
  45.5 28.3 %all-gather.3.cloned.1.call-done.x_ref = bf16[2048,2048]{1,0:T(8,128)(2,1)} async-done(((bf16[256,2048]{1,0:T(8,128)(2,1)}), bf16[2048,2048]{1,0:T(8,128)(2,1)}) %all-gather.3.cloned.1.call-update) | async-done | bytes 8388624 | tf_op jit(solution)/shard_map/all_gather | solution.py:900
  78.5 10.6 %qkv_rows.1 = (bf16[2048,2048]{1,0:T(8,128)(2,1)}, bf16[2048,384]{1,0:T(8,128)(2,1)}) custom-call(bf16[2048,2048]{1,0:T(8,128)(2,1)} %all-gather.3.cloned.1.call-done.x_ref, f32[1,2048]{1,0:T(1,128)} %bitcast.52, bf16[2048,384]{1,0:T(8,128)(2,1)} %copy-done.3), custom_call_target="tpu_custom_call" | custom-call | flops 1 | bytes 1 | tf_op jit(solution)/shard_map/qkv_rows/pallas_call | solution.py:88
  89.1 5.8 head_forward.1
  96.5 16.8 %collective-permute-done.9.refs_2_ = bf16[2048,128]{1,0:T(8,128)(2,1)S(1)} collective-permute-done((bf16[2048,128]{1,0:T(8,128)(2,1)}, bf16[2048,128]{1,0:T(8,128)(2,1)S(1)}, u32[]{:S(2)}, u32[]{:S(2)}) %collective-permute-start.9) | collective-permute-done | bytes 524320 | tf_op jit(solution)/shard_map/ppermute | solution.py:863
  117.1 10.4 %collective-permute-done.13 = bf16[1024,128]{1,0:T(8,128)(2,1)S(1)} collective-permute-done((bf16[1024,128]{1,0:T(8,128)(2,1)S(1)}, bf16[1024,128]{1,0:T(8,128)(2,1)S(1)}, u32[]{:S(2)}, u32[]{:S(2)}) %collective-permute-start.13) | collective-permute-done | bytes 262176 | tf_op jit(solution)/shard_map/ppermute | solution.py:863
  132.8 18.2 %mid_rows.1 = (bf16[2048,2048]{1,0:T(8,128)(2,1)}, f32[256,2048]{1,0:T(8,128)}, bf16[256,1024]{1,0:T(8,128)(2,1)}) custom-call(s32[3]{0:T(128)} %copy-done.2, bf16[2048,2048]{1,0:T(8,128)(2,1)} %all-gather.3.cloned.1.call-done.x_ref, bf16[2048,128]{1,0:T(8,128)(2,1)} %bitcast.42, bf16[2048,128]{1,0:T(8,128)(2,1)} %copy-done.20, ...), custom_call_target="tpu_custom_call" | custom-call | flops 1 | bytes 1 | tf_op jit(solution)/shard_map/mid_rows/pallas_call | solution.py:300
  151.1 23.4 %ffn_first.2 = (bf16[2048,256]{1,0:T(8,128)(2,1)}, bf16[2048,256]{1,0:T(8,128)(2,1)}, bf16[2048,256]{1,0:T(8,128)(2,1)}, bf16[384,2048]{1,0:T(8,128)(2,1)}, bf16[384,2048]{1,0:T(8,128)(2,1)}) custom-call(bf16[2048,2048]{1,0:T(8,128)(2,1)} %get-tuple-element.87.h2_ref.h2_col_ref, bf16[2048,2048]{1,0:T(8,128)(2,1)} %all-gather.5.cloned.1.call-done.cot_ref.cot_col_ref, ...), custom_call_target="tpu_custom_call" | custom-call | flops 1 | bytes 1 | tf_op jit(solution)/shard_map/ffn_first/pallas_call | solution.py:384
  174.5 3.8 collective-permute-start.16
  178.3 23.4 %ffn_first.3 = (bf16[2048,256]{1,0:T(8,128)(2,1)}, bf16[2048,256]{1,0:T(8,128)(2,1)}, bf16[2048,256]{1,0:T(8,128)(2,1)}, bf16[384,2048]{1,0:T(8,128)(2,1)}, bf16[384,2048]{1,0:T(8,128)(2,1)}) custom-call(bf16[2048,2048]{1,0:T(8,128)(2,1)} %get-tuple-element.87.h2_ref.h2_col_ref, bf16[2048,2048]{1,0:T(8,128)(2,1)} %all-gather.5.cloned.1.call-done.cot_ref.cot_col_ref, ...), custom_call_target="tpu_custom_call" | custom-call | flops 1 | bytes 1 | tf_op jit(solution)/shard_map/ffn_first/pallas_call | solution.py:384
  201.7 12.2 %ffn_rest.2 = (bf16[2048,256]{1,0:T(8,128)(2,1)}, bf16[2048,256]{1,0:T(8,128)(2,1)}, bf16[2048,256]{1,0:T(8,128)(2,1)}) custom-call(bf16[2048,2048]{1,0:T(8,128)(2,1)} %get-tuple-element.87.h2_ref.h2_col_ref, bf16[2048,2048]{1,0:T(8,128)(2,1)} %all-gather.5.cloned.1.call-done.cot_ref.cot_col_ref, bf16[2048,1024]{1,0:T(8,128)(2,1)} %wg_ref.9, ...), custom_call_target="tpu_custom_call" | custom-call | flops 1 | bytes 1 | tf_op jit(solution)/shard_map/ffn_rest/pallas_call | solution.py:410
  221.1 12.2 %ffn_rest.3 = (bf16[2048,256]{1,0:T(8,128)(2,1)}, bf16[2048,256]{1,0:T(8,128)(2,1)}, bf16[2048,256]{1,0:T(8,128)(2,1)}) custom-call(bf16[2048,2048]{1,0:T(8,128)(2,1)} %get-tuple-element.87.h2_ref.h2_col_ref, bf16[2048,2048]{1,0:T(8,128)(2,1)} %all-gather.5.cloned.1.call-done.cot_ref.cot_col_ref, bf16[2048,1024]{1,0:T(8,128)(2,1)} %wg_ref.9, ...), custom_call_target="tpu_custom_call" | custom-call | flops 1 | bytes 1 | tf_op jit(solution)/shard_map/ffn_rest/pallas_call | solution.py:410
  233.4 12.8 %ffn_weights.2 = (bf16[384,2048]{1,0:T(8,128)(2,1)}, bf16[384,2048]{1,0:T(8,128)(2,1)}) custom-call(bf16[2048,2048]{1,0:T(8,128)(2,1)} %get-tuple-element.87.h2_ref.h2_col_ref, bf16[2048,2048]{1,0:T(8,128)(2,1)} %all-gather.5.cloned.1.call-done.cot_ref.cot_col_ref, bf16[2048,256]{1,0:T(8,128)(2,1)} %get-tuple-element.96.__1_.hid_ref.refs_2_, ...), custom_call_target="tpu_custom_call" | custom-call | flops 1 | bytes 1 | tf_op jit(solution)/shard_map/ffn_weights/pallas_call | solution.py:440
  246.1 2.8 collective-permute-start.22
  251.0 2.8 join.21._.array_ref
  255.6 2.8 join.22.refs_8_.array_ref
  259.8 24.0 %ffn_back.1.__1_ = bf16[2048,2048]{1,0:T(8,128)(2,1)} custom-call(bf16[2048,1024]{1,0:T(8,128)(2,1)} %wg_ref.9, bf16[2048,1024]{1,0:T(8,128)(2,1)} %wu_ref.9, bf16[2048,256]{1,0:T(8,128)(2,1)} %get-tuple-element.89.refs_0_, bf16[2048,256]{1,0:T(8,128)(2,1)} %get-tuple-element.92.refs_1_, bf16[2048,256]{1,0:T(8,128)(2,1)} %get-tuple-element.94.dg_ref.refs_2_, ...), custom_call_target="tpu_custom_call" | custom-call | flops 1 | bytes 1 | tf_op jit(solution)/shard_map/ffn_back/pallas_call | solution.py:620
  283.8 7.6 %collective-permute-start.19 = (bf16[384,2048]{1,0:T(8,128)(2,1)}, bf16[384,2048]{1,0:T(8,128)(2,1)}, u32[]{:S(2)}, u32[]{:S(2)}) collective-permute-start(bf16[384,2048]{1,0:T(8,128)(2,1)} %hold.15._.array_ref), channel_id=1, source_target_pairs={{0,1},{3,2},{4,5},{7,6},{8,9},{11,10},{12,13},{15,14},{16,17},{19,... | collective-permute-start | bytes 4718600 | tf_op jit(solution)/shard_map/ppermute | solution.py:792
  292.7 3.3 join.23._.array_ref
  298.2 3.4 join.24.refs_0_.array_ref
  304.1 3.8 finish_ffn.8
  307.9 13.6 %ffn_out.1.__1_.refs_1_ = bf16[8,384,2048]{2,1,0:T(8,128)(2,1)} custom-call(bf16[1024,2048]{1,0:T(8,128)(2,1)} %w_ref.1, bf16[2048,256]{1,0:T(8,128)(2,1)} %get-tuple-element.91.__1_.refs_0_, bf16[2048,256]{1,0:T(8,128)(2,1)} %get-tuple-element.93._.refs_1_, bf16[2048,256]{1,0:T(8,128)(2,1)} %get-tuple-element.96.__1_.hid_ref.refs_2_, ...), custom_call_target="tpu_custom_call" | custom-call | flops 1 | bytes 1 | tf_op jit(solution)/shard_map/ffn_out/pallas_call | solution.py:644
  321.5 5.8 collective-permute-start.24
  327.2 2.9 join.25._.array_ref
  332.0 2.8 join.26.refs_0_.array_ref
  339.1 4.0 finish_ffn.9
  343.0 13.5 %ffn_weights.3 = (bf16[384,2048]{1,0:T(8,128)(2,1)}, bf16[384,2048]{1,0:T(8,128)(2,1)}) custom-call(bf16[2048,2048]{1,0:T(8,128)(2,1)} %get-tuple-element.87.h2_ref.h2_col_ref, bf16[2048,2048]{1,0:T(8,128)(2,1)} %all-gather.5.cloned.1.call-done.cot_ref.cot_col_ref, bf16[2048,256]{1,0:T(8,128)(2,1)} %get-tuple-element.103._.refs_3_.hid_ref, ...), custom_call_target="tpu_custom_call" | custom-call | flops 1 | bytes 1 | tf_op jit(solution)/shard_map/ffn_weights/pallas_call | solution.py:440
  358.9 2.9 join.27._.array_ref
  363.6 2.9 join.28.refs_0_.array_ref
  368.4 8.9 %own_rows_back.1 = (f32[256,2048]{1,0:T(8,128)}, bf16[256,1024]{1,0:T(8,128)(2,1)}, bf16[8,384,2048]{2,1,0:T(8,128)(2,1)}, f32[1,2048]{1,0:T(1,128)}) custom-call(bf16[256,2048]{1,0:T(8,128)(2,1)} %reduce-scatter.4.cloned.1.call-done.d_h2_ref, f32[256,2048]{1,0:T(8,128)} %get-tuple-element.105.y1_ref, ...), custom_call_target="tpu_custom_call", output_to_operand_aliasing={{2}: (7, {})} | custom-call | flops 1 | bytes 1 | tf_op jit(solution)/shard_map/own_rows_back/pallas_call | solution.py:675
  378.4 3.7 finish_ffn.10
  382.1 7.5 %collective-permute-start.33 = (bf16[384,2048]{1,0:T(8,128)(2,1)}, bf16[384,2048]{1,0:T(8,128)(2,1)}, u32[]{:S(2)}, u32[]{:S(2)}) collective-permute-start(bf16[384,2048]{1,0:T(8,128)(2,1)} %hold.18._.array_ref), channel_id=1, source_target_pairs={{0,1},{3,2},{4,5},{7,6},{8,9},{11,10},{12,13},{15,14},{16,17},{19,... | collective-permute-start | bytes 4718600 | tf_op jit(solution)/shard_map/ppermute | solution.py:792
  391.5 3.5 all-to-all-start
  396.2 3.7 join.29._.array_ref
  401.8 3.5 join.30.refs_0_.array_ref
  406.8 4.1 finish_ffn.11
  412.2 10.6 %head_backward.1 = (bf16[8,2,128,384]{3,2,1,0:T(8,128)(2,1)}, f32[2,8,128]{2,1,0:T(8,128)}) custom-call(f32[1]{0:T(128)S(6)} %div.3.share_ref, bf16[8,2,128,384]{3,2,1,0:T(8,128)(2,1)} %bitcast.34, bf16[8,2,128,128]{3,2,1,0:T(8,128)(2,1)} %bitcast.43, s32[2,1024,1]{2,1,0:T(8,128)} %copy.64.doc_rows_ref, s32[2,1,1024]{2,1,0:T(1,128)} %compare_select_fusion.doc_cols_ref, ...), custom_call_target="tpu_custom_call" | custom-call | flops 1 | bytes 1 | tf_op jit(solution)/shard_map/head_backward/pallas_call | solution.py:240
  422.8 5.8 collective-permute-start.35
  428.7 3.1 join.31._.array_ref
  433.6 2.9 join.32.refs_0_.array_ref
  437.8 6.9 %collective-permute-done.31.arrived_ref = bf16[384,2048]{1,0:T(8,128)(2,1)S(1)} collective-permute-done((bf16[384,2048]{1,0:T(8,128)(2,1)}, bf16[384,2048]{1,0:T(8,128)(2,1)S(1)}, u32[]{:S(2)}, u32[]{:S(2)}) %collective-permute-start.31) | collective-permute-done | bytes 1572896 | tf_op jit(solution)/shard_map/ppermute | solution.py:792
  445.8 3.7 finish_ffn.12
  449.5 14.9 %qkv_back.1 = (bf16[2048,2048]{1,0:T(8,128)(2,1)}, bf16[2048,384]{1,0:T(8,128)(2,1)}) custom-call(bf16[2048,384]{1,0:T(8,128)(2,1)} %bitcast.44, bf16[2048,2048]{1,0:T(8,128)(2,1)} %get-tuple-element.125.h1_ref, bf16[2048,384]{1,0:T(8,128)(2,1)} %copy-done.3, f32[8,128]{1,0:T(8,128)} %get-tuple-element.130._), custom_call_target="tpu_custom_call" | custom-call | flops 1 | bytes 1 | tf_op jit(solution)/shard_map/qkv_back/pallas_call | solution.py:723
  464.4 2.9 collective-permute-start.37
  467.3 2.9 join.33._.array_ref
  472.0 2.8 join.34.refs_0_.array_ref
  475.4 5.0 reduce-scatter.6.cloned.1.call-done.refs_1_.mlp_ref
  483.7 3.9 finish_ffn.13
  489.5 9.9 %collective-permute-done.37.arrived_ref = bf16[2048,384]{1,0:T(8,128)(2,1)} collective-permute-done((bf16[2048,384]{1,0:T(8,128)(2,1)}, bf16[2048,384]{1,0:T(8,128)(2,1)}, u32[]{:S(2)}, u32[]{:S(2)}) %collective-permute-start.37) | collective-permute-done | bytes 1572896 | tf_op jit(solution)/shard_map/ppermute | solution.py:792
  499.4 3.0 join.35._.array_ref
  504.3 2.8 join.36.refs_0_.array_ref
  508.4 7.6 %collective-permute-start.41 = (bf16[128,2048]{1,0:T(8,128)(2,1)S(1)}, bf16[128,2048]{1,0:T(8,128)(2,1)}, u32[]{:S(2)}, u32[]{:S(2)}) collective-permute-start(bf16[128,2048]{1,0:T(8,128)(2,1)S(1)} %copy-done.4), channel_id=1, source_target_pairs={{0,1},{3,2},{4,5},{7,6},{8,9},{11,10},{12,13},{15,14},{16,17},{19,... | collective-permute-start | bytes 1572872 | tf_op jit(solution)/shard_map/ppermute | solution.py:792
  518.0 3.6 collective-permute-done.42.arrived_ref
  522.7 3.8 finish_ffn.14
  529.3 2.9 join.38.refs_0_.array_ref
  533.7 21.7 %collective-permute-done.39.arrived_ref = bf16[384,2048]{1,0:T(8,128)(2,1)} collective-permute-done((bf16[384,2048]{1,0:T(8,128)(2,1)}, bf16[384,2048]{1,0:T(8,128)(2,1)}, u32[]{:S(2)}, u32[]{:S(2)}) %collective-permute-start.39) | collective-permute-done | bytes 1572896 | tf_op jit(solution)/shard_map/ppermute | solution.py:792
  555.4 3.9 finish_ffn.15
  559.9 6.7 %last_rows.1 = (f32[256,2048]{1,0:T(8,128)}, f32[1,2048]{1,0:T(1,128)}, bf16[256,2048]{1,0:T(8,128)(2,1)}) custom-call(bf16[256,2048]{1,0:T(8,128)(2,1)} %reduce-scatter.8.cloned.1.call-done.d_h1_ref, bf16[256,2048]{1,0:T(8,128)(2,1)} %bitcast.38, f32[256,2048]{1,0:T(8,128)} %get-tuple-element.116.refs_0_.d_y1_ref, f32[1,2048]{1,0:T(1,128)} %bitcast.53, ...), custom_call_target="tpu_custom_call" | custom-call | flops 1 | bytes 1 | tf_op jit(solution)/shard_map/last_rows/pallas_call | solution.py:582
  581.8 7.2 %collective-permute-done.43.arrived_ref = bf16[2048,384]{1,0:T(8,128)(2,1)S(1)} collective-permute-done((bf16[2048,384]{1,0:T(8,128)(2,1)}, bf16[2048,384]{1,0:T(8,128)(2,1)S(1)}, u32[]{:S(2)}, u32[]{:S(2)}) %collective-permute-start.43) | collective-permute-done | bytes 1572896 | tf_op jit(solution)/shard_map/ppermute | solution.py:792
  590.2 3.2 finish_cut.2
  593.3 6.2 %collective-permute-done.49 = f32[4104]{0:T(1024)S(1)} collective-permute-done((f32[4104]{0:T(1024)S(1)}, f32[4104]{0:T(1024)S(1)}, u32[]{:S(2)}, u32[]{:S(2)}) %collective-permute-start.49) | collective-permute-done | bytes 16448 | tf_op jit(solution)/shard_map/ppermute | solution.py:1036
  601.6 3.5 collective-permute-done.50
  (214 shorter events, 113.0 us)
Async XLA Ops:
  7.2 21.6 %copy-start.1 = (bf16[128,2048]{1,0:T(8,128)(2,1)S(1)}, bf16[128,2048]{1,0:T(8,128)(2,1)}, u32[]{:S(2)}) copy-start(bf16[128,2048]{1,0:T(8,128)(2,1)} %refs_0_.1) | copy-start | bytes 1572868
  7.2 66.7 %all-gather.3.cloned.1.call-start = ((), (), s32[]{:S(2)}) async-start(), calls=%async_computation.4 | async-start | bytes 9437184 | tf_op jit(solution)/shard_map/all_gather | solution.py:900
  7.9 143.2 %all-gather.5.cloned.1.call-start = ((), (), s32[]{:S(2)}) async-start(), calls=%async_computation.5 | async-start | bytes 9437184 | tf_op jit(solution)/shard_map/all_gather | solution.py:900
  8.0 16.9 %collective-permute-start.1 = (bf16[128,2048]{1,0:T(8,128)(2,1)}, bf16[128,2048]{1,0:T(8,128)(2,1)S(1)}, u32[]{:S(2)}, u32[]{:S(2)}) collective-permute-start(bf16[128,2048]{1,0:T(8,128)(2,1)} %refs_0_.1), channel_id=1, source_target_pairs={{0,8},{4,12},{8,0},{12,4},{16,24},{20,28},{24,16},{28,20},{1,9},{5... | collective-permute-start | bytes 1572872 | tf_op jit(solution)/shard_map/ppermute | solution.py:863
  11.0 17.2 %collective-permute-start.3 = (bf16[128,2048]{1,0:T(8,128)(2,1)}, bf16[128,2048]{1,0:T(8,128)(2,1)S(1)}, u32[]{:S(2)}, u32[]{:S(2)}) collective-permute-start(bf16[128,2048]{1,0:T(8,128)(2,1)} %refs_0_.1), channel_id=1, source_target_pairs={{0,16},{4,20},{8,24},{12,28},{16,0},{20,4},{24,8},{28,12},{1,17},{... | collective-permute-start | bytes 1572872 | tf_op jit(solution)/shard_map/ppermute | solution.py:863
  24.9 13.7 %collective-permute-start.5 = (bf16[64,2048]{1,0:T(8,128)(2,1)S(1)}, bf16[64,2048]{1,0:T(8,128)(2,1)S(1)}, u32[]{:S(2)}, u32[]{:S(2)}) collective-permute-start(bf16[64,2048]{1,0:T(8,128)(2,1)S(1)} %slice.32), channel_id=1, source_target_pairs={{0,16},{4,20},{8,24},{12,28},{16,0},{20,4},{24,8},{28,12},{1,17},{... | collective-permute-start | bytes 786440 | tf_op jit(solution)/shard_map/ppermute | solution.py:863
  28.2 11.8 %collective-permute-start.6 = (bf16[64,2048]{1,0:T(8,128)(2,1)S(1)}, bf16[64,2048]{1,0:T(8,128)(2,1)S(1)}, u32[]{:S(2)}, u32[]{:S(2)}) collective-permute-start(bf16[64,2048]{1,0:T(8,128)(2,1)S(1)} %slice.33), channel_id=1, source_target_pairs={{0,8},{4,12},{8,0},{12,4},{16,24},{20,28},{24,16},{28,20},{1,9},{5... | collective-permute-start | bytes 786440 | tf_op jit(solution)/shard_map/ppermute | solution.py:863
  28.8 11.4 %collective-permute-start = (bf16[128,2048]{1,0:T(8,128)(2,1)S(1)}, bf16[128,2048]{1,0:T(8,128)(2,1)S(1)}, u32[]{:S(2)}, u32[]{:S(2)}) collective-permute-start(bf16[128,2048]{1,0:T(8,128)(2,1)S(1)} %copy-done.1), channel_id=1, source_target_pairs={{0,4},{4,0},{8,12},{12,8},{16,20},{20,16},{24,28},{28,24},{1,5},{5... | collective-permute-start | bytes 1572872 | tf_op jit(solution)/shard_map/ppermute | solution.py:863
  28.8 11.4 %collective-permute-start.2 = (bf16[128,2048]{1,0:T(8,128)(2,1)S(1)}, bf16[128,2048]{1,0:T(8,128)(2,1)S(1)}, u32[]{:S(2)}, u32[]{:S(2)}) collective-permute-start(bf16[128,2048]{1,0:T(8,128)(2,1)S(1)} %collective-permute-done.1.refs_2_), channel_id=1, source_target_pairs={{0,4},{4,0},{8,12},{12,8},{16,20},{20,16},{24,28},{28,24},{1,5},{5... | collective-permute-start | bytes 1572872 | tf_op jit(solution)/shard_map/ppermute | solution.py:863
  29.3 10.9 %collective-permute-start.4 = (bf16[128,2048]{1,0:T(8,128)(2,1)S(1)}, bf16[128,2048]{1,0:T(8,128)(2,1)}, u32[]{:S(2)}, u32[]{:S(2)}) collective-permute-start(bf16[128,2048]{1,0:T(8,128)(2,1)S(1)} %collective-permute-done.3.refs_4_), channel_id=1, source_target_pairs={{0,4},{4,0},{8,12},{12,8},{16,20},{20,16},{24,28},{28,24},{1,5},{5... | collective-permute-start | bytes 1572872 | tf_op jit(solution)/shard_map/ppermute | solution.py:863
  40.0 2.1 collective-permute-start.7
  40.2 34.6 %copy-start.33 = (s32[2,1,4]{2,1,0:T(1,128)S(1)}, s32[2,1,4]{2,1,0:T(1,128)}, u32[]{:S(2)}) copy-start(s32[2,1,4]{2,1,0:T(1,128)} %param.16) | copy-start | bytes 100
  45.5 30.8 %copy-start.32 = (s32[2,1,1024]{2,1,0:T(1,128)S(1)}, s32[2,1,1024]{2,1,0:T(1,128)}, u32[]{:S(2)}) copy-start(s32[2,1,1024]{2,1,0:T(1,128)} %param.17) | copy-start | bytes 24580
  45.5 31.4 %copy-start.24 = (bf16[2048,128]{1,0:T(8,128)(2,1)S(1)}, bf16[2048,128]{1,0:T(8,128)(2,1)}, u32[]{:S(2)}) copy-start(bf16[2048,128]{1,0:T(8,128)(2,1)} %param.18) | copy-start | bytes 1572868
  73.9 294.5 %reduce-scatter.4.cloned.1.call-start = ((), (), s32[]{:S(2)}) async-start(), calls=%async_computation.6 | async-start | bytes 9437184 | tf_op jit(solution)/shard_map/reduce_scatter | solution.py:903
  94.9 18.4 %collective-permute-start.9 = (bf16[2048,128]{1,0:T(8,128)(2,1)}, bf16[2048,128]{1,0:T(8,128)(2,1)S(1)}, u32[]{:S(2)}, u32[]{:S(2)}) collective-permute-start(bf16[2048,128]{1,0:T(8,128)(2,1)} %bitcast.39), channel_id=1, source_target_pairs={{0,8},{4,12},{8,0},{12,4},{16,24},{20,28},{24,16},{28,20},{1,9},{5... | collective-permute-start | bytes 1572872 | tf_op jit(solution)/shard_map/ppermute | solution.py:863
  96.3 20.0 %collective-permute-start.11 = (bf16[2048,128]{1,0:T(8,128)(2,1)}, bf16[2048,128]{1,0:T(8,128)(2,1)S(1)}, u32[]{:S(2)}, u32[]{:S(2)}) collective-permute-start(bf16[2048,128]{1,0:T(8,128)(2,1)} %bitcast.40), channel_id=1, source_target_pairs={{0,16},{4,20},{8,24},{12,28},{16,0},{20,4},{24,8},{28,12},{1,17},{... | collective-permute-start | bytes 1572872 | tf_op jit(solution)/shard_map/ppermute | solution.py:863
  113.3 18.7 %copy-start.17 = (bf16[2048,128]{1,0:T(8,128)(2,1)}, bf16[2048,128]{1,0:T(8,128)(2,1)S(1)}, u32[]{:S(2)}) copy-start(bf16[2048,128]{1,0:T(8,128)(2,1)S(1)} %collective-permute-done.9.refs_2_) | copy-start | bytes 1572868
  113.4 14.1 %collective-permute-start.13 = (bf16[1024,128]{1,0:T(8,128)(2,1)S(1)}, bf16[1024,128]{1,0:T(8,128)(2,1)S(1)}, u32[]{:S(2)}, u32[]{:S(2)}) collective-permute-start(bf16[1024,128]{1,0:T(8,128)(2,1)S(1)} %slice.34), channel_id=1, source_target_pairs={{0,16},{4,20},{8,24},{12,28},{16,0},{20,4},{24,8},{28,12},{1,17},{... | collective-permute-start | bytes 786440 | tf_op jit(solution)/shard_map/ppermute | solution.py:863
  116.3 15.7 %copy-start.18 = (bf16[2048,128]{1,0:T(8,128)(2,1)}, bf16[2048,128]{1,0:T(8,128)(2,1)S(1)}, u32[]{:S(2)}) copy-start(bf16[2048,128]{1,0:T(8,128)(2,1)S(1)} %collective-permute-done.11.refs_4_) | copy-start | bytes 1572868
  116.3 13.5 %collective-permute-start.14 = (bf16[1024,128]{1,0:T(8,128)(2,1)S(1)}, bf16[1024,128]{1,0:T(8,128)(2,1)S(1)}, u32[]{:S(2)}, u32[]{:S(2)}) collective-permute-start(bf16[1024,128]{1,0:T(8,128)(2,1)S(1)} %slice.35), channel_id=1, source_target_pairs={{0,8},{4,12},{8,0},{12,4},{16,24},{20,28},{24,16},{28,20},{1,9},{5... | collective-permute-start | bytes 786440 | tf_op jit(solution)/shard_map/ppermute | solution.py:863
  116.4 13.5 %collective-permute-start.8 = (bf16[2048,128]{1,0:T(8,128)(2,1)}, bf16[2048,128]{1,0:T(8,128)(2,1)S(1)}, u32[]{:S(2)}, u32[]{:S(2)}) collective-permute-start(bf16[2048,128]{1,0:T(8,128)(2,1)} %bitcast.41), channel_id=1, source_target_pairs={{0,4},{4,0},{8,12},{12,8},{16,20},{20,16},{24,28},{28,24},{1,5},{5... | collective-permute-start | bytes 1572872 | tf_op jit(solution)/shard_map/ppermute | solution.py:863
  116.5 13.5 %collective-permute-start.12 = (bf16[2048,128]{1,0:T(8,128)(2,1)S(1)}, bf16[2048,128]{1,0:T(8,128)(2,1)S(1)}, u32[]{:S(2)}, u32[]{:S(2)}) collective-permute-start(bf16[2048,128]{1,0:T(8,128)(2,1)S(1)} %collective-permute-done.11.refs_4_), channel_id=1, source_target_pairs={{0,4},{4,0},{8,12},{12,8},{16,20},{20,16},{24,28},{28,24},{1,5},{5... | collective-permute-start | bytes 1572872 | tf_op jit(solution)/shard_map/ppermute | solution.py:863
  117.0 13.0 %collective-permute-start.10 = (bf16[2048,128]{1,0:T(8,128)(2,1)S(1)}, bf16[2048,128]{1,0:T(8,128)(2,1)S(1)}, u32[]{:S(2)}, u32[]{:S(2)}) collective-permute-start(bf16[2048,128]{1,0:T(8,128)(2,1)S(1)} %collective-permute-done.9.refs_2_), channel_id=1, source_target_pairs={{0,4},{4,0},{8,12},{12,8},{16,20},{20,16},{24,28},{28,24},{1,5},{5... | collective-permute-start | bytes 1572872 | tf_op jit(solution)/shard_map/ppermute | solution.py:863
  129.9 2.2 collective-permute-start.15
  174.5 40.8 %collective-permute-start.16 = (bf16[384,2048]{1,0:T(8,128)(2,1)}, bf16[384,2048]{1,0:T(8,128)(2,1)S(1)}, u32[]{:S(2)}, u32[]{:S(2)}) collective-permute-start(bf16[384,2048]{1,0:T(8,128)(2,1)} %hold.12._.array_ref), channel_id=1, source_target_pairs={{0,1},{3,2},{4,5},{7,6},{8,9},{11,10},{12,13},{15,14},{16,17},{19,... | collective-permute-start | bytes 4718600 | tf_op jit(solution)/shard_map/ppermute | solution.py:792
  214.0 35.9 %collective-permute-start.18 = (bf16[384,2048]{1,0:T(8,128)(2,1)}, bf16[384,2048]{1,0:T(8,128)(2,1)S(1)}, u32[]{:S(2)}, u32[]{:S(2)}) collective-permute-start(bf16[384,2048]{1,0:T(8,128)(2,1)} %hold.13._.array_ref), channel_id=1, source_target_pairs={{0,1},{3,2},{4,5},{7,6},{8,9},{11,10},{12,13},{15,14},{16,17},{19,... | collective-permute-start | bytes 4718600 | tf_op jit(solution)/shard_map/ppermute | solution.py:792
  219.3 36.3 %collective-permute-start.17 = (bf16[384,2048]{1,0:T(8,128)(2,1)}, bf16[384,2048]{1,0:T(8,128)(2,1)}, u32[]{:S(2)}, u32[]{:S(2)}) collective-permute-start(bf16[384,2048]{1,0:T(8,128)(2,1)} %join.20._.array_ref), channel_id=1, source_target_pairs={{1,2},{2,1},{5,6},{6,5},{9,10},{10,9},{13,14},{14,13},{17,18},{18,... | collective-permute-start | bytes 4718600 | tf_op jit(solution)/shard_map/ppermute | solution.py:792
  246.1 45.4 %collective-permute-start.22 = (bf16[384,2048]{1,0:T(8,128)(2,1)}, bf16[384,2048]{1,0:T(8,128)(2,1)S(1)}, u32[]{:S(2)}, u32[]{:S(2)}) collective-permute-start(bf16[384,2048]{1,0:T(8,128)(2,1)} %hold.14._.array_ref), channel_id=1, source_target_pairs={{0,1},{3,2},{4,5},{7,6},{8,9},{11,10},{12,13},{15,14},{16,17},{19,... | collective-permute-start | bytes 4718600 | tf_op jit(solution)/shard_map/ppermute | solution.py:792
  253.8 44.3 %collective-permute-start.21 = (bf16[384,2048]{1,0:T(8,128)(2,1)}, bf16[384,2048]{1,0:T(8,128)(2,1)}, u32[]{:S(2)}, u32[]{:S(2)}) collective-permute-start(bf16[384,2048]{1,0:T(8,128)(2,1)} %join.21._.array_ref), channel_id=1, source_target_pairs={{1,2},{2,1},{5,6},{6,5},{9,10},{10,9},{13,14},{14,13},{17,18},{18,... | collective-permute-start | bytes 4718600 | tf_op jit(solution)/shard_map/ppermute | solution.py:792
  258.5 44.4 %collective-permute-start.20 = (bf16[384,2048]{1,0:T(8,128)(2,1)}, bf16[384,2048]{1,0:T(8,128)(2,1)S(1)}, u32[]{:S(2)}, u32[]{:S(2)}) collective-permute-start(bf16[384,2048]{1,0:T(8,128)(2,1)} %join.22.refs_8_.array_ref), channel_id=1, source_target_pairs={{1,0},{2,3},{5,4},{6,7},{9,8},{10,11},{13,12},{14,15},{17,16},{18,... | collective-permute-start | bytes 4718600 | tf_op jit(solution)/shard_map/ppermute | solution.py:792
  283.8 43.4 %collective-permute-start.19 = (bf16[384,2048]{1,0:T(8,128)(2,1)}, bf16[384,2048]{1,0:T(8,128)(2,1)}, u32[]{:S(2)}, u32[]{:S(2)}) collective-permute-start(bf16[384,2048]{1,0:T(8,128)(2,1)} %hold.15._.array_ref), channel_id=1, source_target_pairs={{0,1},{3,2},{4,5},{7,6},{8,9},{11,10},{12,13},{15,14},{16,17},{19,... | collective-permute-start | bytes 4718600 | tf_op jit(solution)/shard_map/ppermute | solution.py:792
  291.5 189.0 %reduce-scatter.6.cloned.1.call-start = ((), (), s32[]{:S(2)}) async-start(), calls=%async_computation.7 | async-start | bytes 14155776 | tf_op jit(solution)/shard_map/reduce_scatter | solution.py:903
  296.0 36.0 %collective-permute-start.26 = (bf16[384,2048]{1,0:T(8,128)(2,1)}, bf16[384,2048]{1,0:T(8,128)(2,1)}, u32[]{:S(2)}, u32[]{:S(2)}) collective-permute-start(bf16[384,2048]{1,0:T(8,128)(2,1)} %join.23._.array_ref), channel_id=1, source_target_pairs={{1,2},{2,1},{5,6},{6,5},{9,10},{10,9},{13,14},{14,13},{17,18},{18,... | collective-permute-start | bytes 4718600 | tf_op jit(solution)/shard_map/ppermute | solution.py:792
  301.6 36.3 %collective-permute-start.25 = (bf16[384,2048]{1,0:T(8,128)(2,1)}, bf16[384,2048]{1,0:T(8,128)(2,1)S(1)}, u32[]{:S(2)}, u32[]{:S(2)}) collective-permute-start(bf16[384,2048]{1,0:T(8,128)(2,1)} %join.24.refs_0_.array_ref), channel_id=1, source_target_pairs={{1,0},{2,3},{5,4},{6,7},{9,8},{10,11},{13,12},{14,15},{17,16},{18,... | collective-permute-start | bytes 4718600 | tf_op jit(solution)/shard_map/ppermute | solution.py:792
  321.5 37.5 %collective-permute-start.24 = (bf16[384,2048]{1,0:T(8,128)(2,1)}, bf16[384,2048]{1,0:T(8,128)(2,1)}, u32[]{:S(2)}, u32[]{:S(2)}) collective-permute-start(bf16[384,2048]{1,0:T(8,128)(2,1)} %hold.16._.array_ref), channel_id=1, source_target_pairs={{0,1},{3,2},{4,5},{7,6},{8,9},{11,10},{12,13},{15,14},{16,17},{19,... | collective-permute-start | bytes 4718600 | tf_op jit(solution)/shard_map/ppermute | solution.py:792
  330.2 33.5 %collective-permute-start.23 = (bf16[384,2048]{1,0:T(8,128)(2,1)}, bf16[384,2048]{1,0:T(8,128)(2,1)}, u32[]{:S(2)}, u32[]{:S(2)}) collective-permute-start(bf16[384,2048]{1,0:T(8,128)(2,1)} %join.25._.array_ref), channel_id=1, source_target_pairs={{1,2},{2,1},{5,6},{6,5},{9,10},{10,9},{13,14},{14,13},{17,18},{18,... | collective-permute-start | bytes 4718600 | tf_op jit(solution)/shard_map/ppermute | solution.py:792
  334.8 42.4 %collective-permute-start.30 = (bf16[384,2048]{1,0:T(8,128)(2,1)}, bf16[384,2048]{1,0:T(8,128)(2,1)S(1)}, u32[]{:S(2)}, u32[]{:S(2)}) collective-permute-start(bf16[384,2048]{1,0:T(8,128)(2,1)} %join.26.refs_0_.array_ref), channel_id=1, source_target_pairs={{1,0},{2,3},{5,4},{6,7},{9,8},{10,11},{13,12},{14,15},{17,16},{18,... | collective-permute-start | bytes 4718600 | tf_op jit(solution)/shard_map/ppermute | solution.py:792
  356.6 38.5 %collective-permute-start.29 = (bf16[384,2048]{1,0:T(8,128)(2,1)}, bf16[384,2048]{1,0:T(8,128)(2,1)S(1)}, u32[]{:S(2)}, u32[]{:S(2)}) collective-permute-start(bf16[384,2048]{1,0:T(8,128)(2,1)} %hold.17._.array_ref), channel_id=1, source_target_pairs={{0,1},{3,2},{4,5},{7,6},{8,9},{11,10},{12,13},{15,14},{16,17},{19,... | collective-permute-start | bytes 4718600 | tf_op jit(solution)/shard_map/ppermute | solution.py:792
  361.8 40.0 %collective-permute-start.28 = (bf16[384,2048]{1,0:T(8,128)(2,1)}, bf16[384,2048]{1,0:T(8,128)(2,1)}, u32[]{:S(2)}, u32[]{:S(2)}) collective-permute-start(bf16[384,2048]{1,0:T(8,128)(2,1)} %join.27._.array_ref), channel_id=1, source_target_pairs={{1,2},{2,1},{5,6},{6,5},{9,10},{10,9},{13,14},{14,13},{17,18},{18,... | collective-permute-start | bytes 4718600 | tf_op jit(solution)/shard_map/ppermute | solution.py:792
  366.5 40.2 %collective-permute-start.27 = (bf16[384,2048]{1,0:T(8,128)(2,1)}, bf16[384,2048]{1,0:T(8,128)(2,1)}, u32[]{:S(2)}, u32[]{:S(2)}) collective-permute-start(bf16[384,2048]{1,0:T(8,128)(2,1)} %join.28.refs_0_.array_ref), channel_id=1, source_target_pairs={{1,0},{2,3},{5,4},{6,7},{9,8},{10,11},{13,12},{14,15},{17,16},{18,... | collective-permute-start | bytes 4718600 | tf_op jit(solution)/shard_map/ppermute | solution.py:792
  382.1 46.6 %collective-permute-start.33 = (bf16[384,2048]{1,0:T(8,128)(2,1)}, bf16[384,2048]{1,0:T(8,128)(2,1)}, u32[]{:S(2)}, u32[]{:S(2)}) collective-permute-start(bf16[384,2048]{1,0:T(8,128)(2,1)} %hold.18._.array_ref), channel_id=1, source_target_pairs={{0,1},{3,2},{4,5},{7,6},{8,9},{11,10},{12,13},{15,14},{16,17},{19,... | collective-permute-start | bytes 4718600 | tf_op jit(solution)/shard_map/ppermute | solution.py:792
  391.5 19.9 %all-to-all-start = ((bf16[256,8,128]{2,0,1:T(8,128)(2,1)}), bf16[256,8,128]{2,0,1:T(8,128)(2,1)S(1)}, u32[]{:S(2)}, u32[]{:S(2)}) async-start(bf16[256,8,128]{2,0,1:T(8,128)(2,1)} %copy_bitcast_fusion), calls=%async_computation.1 | async-start | bytes 1048576 | tf_op jit(solution)/shard_map/all_to_all | solution.py:1002
  395.0 164.9 %reduce-scatter.8.cloned.1.call-start = ((), (), s32[]{:S(2)}) async-start(), calls=%async_computation.8 | async-start | bytes 9437184 | tf_op jit(solution)/shard_map/reduce_scatter | solution.py:903
  399.9 33.7 %collective-permute-start.32 = (bf16[384,2048]{1,0:T(8,128)(2,1)}, bf16[384,2048]{1,0:T(8,128)(2,1)}, u32[]{:S(2)}, u32[]{:S(2)}) collective-permute-start(bf16[384,2048]{1,0:T(8,128)(2,1)} %join.29._.array_ref), channel_id=1, source_target_pairs={{1,2},{2,1},{5,6},{6,5},{9,10},{10,9},{13,14},{14,13},{17,18},{18,... | collective-permute-start | bytes 4718600 | tf_op jit(solution)/shard_map/ppermute | solution.py:792
  405.3 39.3 %collective-permute-start.31 = (bf16[384,2048]{1,0:T(8,128)(2,1)}, bf16[384,2048]{1,0:T(8,128)(2,1)S(1)}, u32[]{:S(2)}, u32[]{:S(2)}) collective-permute-start(bf16[384,2048]{1,0:T(8,128)(2,1)} %join.30.refs_0_.array_ref), channel_id=1, source_target_pairs={{1,0},{2,3},{5,4},{6,7},{9,8},{10,11},{13,12},{14,15},{17,16},{18,... | collective-permute-start | bytes 4718600 | tf_op jit(solution)/shard_map/ppermute | solution.py:792
  422.8 44.5 %collective-permute-start.35 = (bf16[384,2048]{1,0:T(8,128)(2,1)}, bf16[384,2048]{1,0:T(8,128)(2,1)}, u32[]{:S(2)}, u32[]{:S(2)}) collective-permute-start(bf16[384,2048]{1,0:T(8,128)(2,1)} %hold.19._.array_ref), channel_id=1, source_target_pairs={{0,1},{3,2},{4,5},{7,6},{8,9},{11,10},{12,13},{15,14},{16,17},{19,... | collective-permute-start | bytes 4718600 | tf_op jit(solution)/shard_map/ppermute | solution.py:792
  431.8 40.2 %collective-permute-start.34 = (bf16[384,2048]{1,0:T(8,128)(2,1)}, bf16[384,2048]{1,0:T(8,128)(2,1)}, u32[]{:S(2)}, u32[]{:S(2)}) collective-permute-start(bf16[384,2048]{1,0:T(8,128)(2,1)} %join.31._.array_ref), channel_id=1, source_target_pairs={{1,2},{2,1},{5,6},{6,5},{9,10},{10,9},{13,14},{14,13},{17,18},{18,... | collective-permute-start | bytes 4718600 | tf_op jit(solution)/shard_map/ppermute | solution.py:792
  436.5 47.3 %collective-permute-start.38 = (bf16[384,2048]{1,0:T(8,128)(2,1)}, bf16[384,2048]{1,0:T(8,128)(2,1)}, u32[]{:S(2)}, u32[]{:S(2)}) collective-permute-start(bf16[384,2048]{1,0:T(8,128)(2,1)} %join.32.refs_0_.array_ref), channel_id=1, source_target_pairs={{1,0},{2,3},{5,4},{6,7},{9,8},{10,11},{13,12},{14,15},{17,16},{18,... | collective-permute-start | bytes 4718600 | tf_op jit(solution)/shard_map/ppermute | solution.py:792
  464.4 34.9 %collective-permute-start.37 = (bf16[2048,384]{1,0:T(8,128)(2,1)}, bf16[2048,384]{1,0:T(8,128)(2,1)}, u32[]{:S(2)}, u32[]{:S(2)}) collective-permute-start(bf16[2048,384]{1,0:T(8,128)(2,1)} %hold.20._.array_ref), channel_id=1, source_target_pairs={{0,1},{3,2},{4,5},{7,6},{8,9},{11,10},{12,13},{15,14},{16,17},{19,... | collective-permute-start | bytes 4718600 | tf_op jit(solution)/shard_map/ppermute | solution.py:792
  470.2 34.2 %collective-permute-start.36 = (bf16[384,2048]{1,0:T(8,128)(2,1)}, bf16[384,2048]{1,0:T(8,128)(2,1)}, u32[]{:S(2)}, u32[]{:S(2)}) collective-permute-start(bf16[384,2048]{1,0:T(8,128)(2,1)} %join.33._.array_ref), channel_id=1, source_target_pairs={{1,2},{2,1},{5,6},{6,5},{9,10},{10,9},{13,14},{14,13},{17,18},{18,... | collective-permute-start | bytes 4718600 | tf_op jit(solution)/shard_map/ppermute | solution.py:792
  482.4 39.2 %collective-permute-start.42 = (bf16[384,2048]{1,0:T(8,128)(2,1)S(1)}, bf16[384,2048]{1,0:T(8,128)(2,1)S(1)}, u32[]{:S(2)}, u32[]{:S(2)}) collective-permute-start(bf16[384,2048]{1,0:T(8,128)(2,1)S(1)} %copy-done.5), channel_id=1, source_target_pairs={{1,0},{2,3},{5,4},{6,7},{9,8},{10,11},{13,12},{14,15},{17,16},{18,... | collective-permute-start | bytes 4718600 | tf_op jit(solution)/shard_map/ppermute | solution.py:792
  502.4 26.9 %collective-permute-start.40 = (bf16[2048,384]{1,0:T(8,128)(2,1)}, bf16[2048,384]{1,0:T(8,128)(2,1)}, u32[]{:S(2)}, u32[]{:S(2)}) collective-permute-start(bf16[2048,384]{1,0:T(8,128)(2,1)} %join.35._.array_ref), channel_id=1, source_target_pairs={{1,2},{2,1},{5,6},{6,5},{9,10},{10,9},{13,14},{14,13},{17,18},{18,... | collective-permute-start | bytes 4718600 | tf_op jit(solution)/shard_map/ppermute | solution.py:792
  507.1 48.3 %collective-permute-start.39 = (bf16[384,2048]{1,0:T(8,128)(2,1)}, bf16[384,2048]{1,0:T(8,128)(2,1)}, u32[]{:S(2)}, u32[]{:S(2)}) collective-permute-start(bf16[384,2048]{1,0:T(8,128)(2,1)} %join.36.refs_0_.array_ref), channel_id=1, source_target_pairs={{1,0},{2,3},{5,4},{6,7},{9,8},{10,11},{13,12},{14,15},{17,16},{18,... | collective-permute-start | bytes 4718600 | tf_op jit(solution)/shard_map/ppermute | solution.py:792
  508.4 18.1 %collective-permute-start.41 = (bf16[128,2048]{1,0:T(8,128)(2,1)S(1)}, bf16[128,2048]{1,0:T(8,128)(2,1)}, u32[]{:S(2)}, u32[]{:S(2)}) collective-permute-start(bf16[128,2048]{1,0:T(8,128)(2,1)S(1)} %copy-done.4), channel_id=1, source_target_pairs={{0,1},{3,2},{4,5},{7,6},{8,9},{11,10},{12,13},{15,14},{16,17},{19,... | collective-permute-start | bytes 1572872 | tf_op jit(solution)/shard_map/ppermute | solution.py:792
  528.6 38.9 %collective-permute-start.44 = (bf16[128,2048]{1,0:T(8,128)(2,1)}, bf16[128,2048]{1,0:T(8,128)(2,1)S(1)}, u32[]{:S(2)}, u32[]{:S(2)}) collective-permute-start(bf16[128,2048]{1,0:T(8,128)(2,1)} %join.37._.array_ref), channel_id=1, source_target_pairs={{1,2},{2,1},{5,6},{6,5},{9,10},{10,9},{13,14},{14,13},{17,18},{18,... | collective-permute-start | bytes 1572872 | tf_op jit(solution)/shard_map/ppermute | solution.py:792
  532.2 56.8 %collective-permute-start.43 = (bf16[2048,384]{1,0:T(8,128)(2,1)}, bf16[2048,384]{1,0:T(8,128)(2,1)S(1)}, u32[]{:S(2)}, u32[]{:S(2)}) collective-permute-start(bf16[2048,384]{1,0:T(8,128)(2,1)} %join.38.refs_0_.array_ref), channel_id=1, source_target_pairs={{1,0},{2,3},{5,4},{6,7},{9,8},{10,11},{13,12},{14,15},{17,16},{18,... | collective-permute-start | bytes 4718600 | tf_op jit(solution)/shard_map/ppermute | solution.py:792
  559.9 6.8 %copy-start.31 = (f32[1,2048]{1,0:T(1,128)S(1)}, f32[1,2048]{1,0:T(1,128)}, u32[]{:S(2)}) copy-start(f32[1,2048]{1,0:T(1,128)} %get-tuple-element.150) | copy-start | bytes 24580
  567.4 4.0 collective-permute-start.46
  570.2 36.8 %collective-permute-start.45 = (bf16[128,2048]{1,0:T(8,128)(2,1)}, bf16[128,2048]{1,0:T(8,128)(2,1)S(1)}, u32[]{:S(2)}, u32[]{:S(2)}) collective-permute-start(bf16[128,2048]{1,0:T(8,128)(2,1)} %join.39._.array_ref), channel_id=1, source_target_pairs={{1,0},{2,3},{5,4},{6,7},{9,8},{10,11},{13,12},{14,15},{17,16},{18,... | collective-permute-start | bytes 1572872 | tf_op jit(solution)/shard_map/ppermute | solution.py:792
  571.5 3.8 collective-permute-start.47
  575.3 3.8 collective-permute-start.48
  579.1 20.4 %collective-permute-start.49 = (f32[4104]{0:T(1024)S(1)}, f32[4104]{0:T(1024)S(1)}, u32[]{:S(2)}, u32[]{:S(2)}) collective-permute-start(f32[4104]{0:T(1024)S(1)} %add.32), channel_id=1, source_target_pairs={{0,1},{1,0},{2,3},{3,2},{4,5},{5,4},{6,7},{7,6},{8,9},{9,8},{10,11... | collective-permute-start | bytes 49256 | tf_op jit(solution)/shard_map/ppermute | solution.py:1036
  600.1 4.9 collective-permute-start.50
  (27 other events, 48.4 us)
Sparse Core Ops, SparseCore 0:
  9.9 63.9 all-gather.2
  75.8 64.6 all-gather.4
  291.6 68.3 reduce-scatter.3
  389.7 90.6 reduce-scatter.5
  484.1 71.2 reduce-scatter.7

commit v6 on v5

--- a/solution.py
+++ b/solution.py
@@ -806,7 +806,7 @@
         else:
             self.send(stage + 1, land, array)
 
-    def tick(self, between=None):
+    def tick(self, between=None, turn=0):
         if self.size == 1 or self.size % 2:
             for land, array in self.waiting:
                 array = lax.psum(array, self.axis)
@@ -822,7 +822,7 @@
         for stage, can_move in enumerate(ready):
             if can_move:
                 self.move(stage)
-            if stage == max(len(ready) - 2, 0) and between:
+            if stage == turn and between:
                 result = between()
         return result
 
@@ -998,7 +998,7 @@
         chain.token = results[0]
         return results
 
-    d_y1, d_mixed_own, parts, gain_mlp_part = chain.tick(own_part)
+    d_y1, d_mixed_own, parts, gain_mlp_part = chain.tick(own_part, max(len(chain.stages) - 2, 0))
     d_mixed = lax.all_to_all(d_mixed_own, "heads", split_axis=1, concat_axis=0, tiled=True)
     parts = scatter(parts.reshape(-1, width))
     chain.tick()

time: 627 us -> 620 us (0.989)
  waiting for transfers between devices: 162 us -> 154 us
    unnamed x72 -> x68, local copies, waits for them, and re-layouts: 20.4 us -> 18 us
  transfers between devices with their start and end apart: 57 -> 57, of which waited for: 24 -> 21; matrix products, arithmetic and copies ran while one was open for 2% -> 2% of each run, Pallas kernels for 46% -> 46%
where the time goes in v6:
time: 620 us; the launch traced here: 609 us
  Pallas kernels  309 us (50%)
  waiting for transfers between devices  154 us (25%)
  starting transfers between devices  103 us (17%)
  local copies, waits for them, and re-layouts  23.5 us (4%)
  between operations  15.5 us (2%)
    ppermute x30, starting transfers between devices, send(): arrived = lax.ppermute(array, self.axis, self.stages[stage][1])  83.8 us
    ppermute x16, waiting for transfers between devices, flip(): return lax.ppermute(value, axis, [(i, i ^ bits) for i in range(size)])  61.1 us
    pallas_call x20, Pallas kernels, join(): pl.pallas_call(functools.partial(join_kernel, takers), name='join', grid=...  56.8 us
    ppermute x30, waiting for transfers between devices, send(): arrived = lax.ppermute(array, self.axis, self.stages[stage][1])  49.5 us
    pallas_call x2, Pallas kernels, ffn_first(): pl.pallas_call(functools.partial(first_kernel, blocks), name='ffn_first',...  46.9 us
    pallas_call x8, Pallas kernels, finish_ffn(): pl.pallas_call(functools.partial(finish_kernel, cols, is_top, takers), na...  31.8 us
    all_gather x2, waiting for transfers between devices, gather(): return lax.all_gather(array, 'heads', axis=0, tiled=True)  28.4 us
    pallas_call x2, Pallas kernels, ffn_weights(): pl.pallas_call(grads_kernel, name='ffn_weights', grid=(width // side,), i...  25.5 us
  transfers between devices with their start and end apart: 57, of which 21 were waited for; matrix products, arithmetic and copies ran while one was open for 2% of the time, Pallas kernels for 46%

profile of v6, /device:TPU:0, one launch (start us, length us, event | category | flops | bytes accessed | tf_op | source)
XLA Modules:
  0.0 609.4 jit_solution(10617678762379382532)
XLA Ops:
  8.0 3.0 collective-permute-start.1
  12.5 12.4 %collective-permute-done.1.refs_2_ = bf16[128,2048]{1,0:T(8,128)(2,1)S(1)} collective-permute-done((bf16[128,2048]{1,0:T(8,128)(2,1)}, bf16[128,2048]{1,0:T(8,128)(2,1)S(1)}, u32[]{:S(2)}, u32[]{:S(2)}) %collective-permute-start.1) | collective-permute-done | bytes 524320 | tf_op jit(solution)/shard_map/ppermute | solution.py:863
  29.3 9.3 %collective-permute-done.5 = bf16[64,2048]{1,0:T(8,128)(2,1)S(1)} collective-permute-done((bf16[64,2048]{1,0:T(8,128)(2,1)S(1)}, bf16[64,2048]{1,0:T(8,128)(2,1)S(1)}, u32[]{:S(2)}, u32[]{:S(2)}) %collective-permute-start.5) | collective-permute-done | bytes 262176 | tf_op jit(solution)/shard_map/ppermute | solution.py:863
  45.5 28.3 %all-gather.3.cloned.1.call-done.x_ref = bf16[2048,2048]{1,0:T(8,128)(2,1)} async-done(((bf16[256,2048]{1,0:T(8,128)(2,1)}), bf16[2048,2048]{1,0:T(8,128)(2,1)}) %all-gather.3.cloned.1.call-update) | async-done | bytes 8388624 | tf_op jit(solution)/shard_map/all_gather | solution.py:900
  78.5 10.6 %qkv_rows.1 = (bf16[2048,2048]{1,0:T(8,128)(2,1)}, bf16[2048,384]{1,0:T(8,128)(2,1)}) custom-call(bf16[2048,2048]{1,0:T(8,128)(2,1)} %all-gather.3.cloned.1.call-done.x_ref, f32[1,2048]{1,0:T(1,128)} %bitcast.52, bf16[2048,384]{1,0:T(8,128)(2,1)} %copy-done.3), custom_call_target="tpu_custom_call" | custom-call | flops 1 | bytes 1 | tf_op jit(solution)/shard_map/qkv_rows/pallas_call | solution.py:88
  89.1 5.8 head_forward.1
  96.5 16.9 %collective-permute-done.9.refs_2_ = bf16[2048,128]{1,0:T(8,128)(2,1)S(1)} collective-permute-done((bf16[2048,128]{1,0:T(8,128)(2,1)}, bf16[2048,128]{1,0:T(8,128)(2,1)S(1)}, u32[]{:S(2)}, u32[]{:S(2)}) %collective-permute-start.9) | collective-permute-done | bytes 524320 | tf_op jit(solution)/shard_map/ppermute | solution.py:863
  117.1 10.4 %collective-permute-done.13 = bf16[1024,128]{1,0:T(8,128)(2,1)S(1)} collective-permute-done((bf16[1024,128]{1,0:T(8,128)(2,1)S(1)}, bf16[1024,128]{1,0:T(8,128)(2,1)S(1)}, u32[]{:S(2)}, u32[]{:S(2)}) %collective-permute-start.13) | collective-permute-done | bytes 262176 | tf_op jit(solution)/shard_map/ppermute | solution.py:863
  132.8 18.2 %mid_rows.1 = (bf16[2048,2048]{1,0:T(8,128)(2,1)}, f32[256,2048]{1,0:T(8,128)}, bf16[256,1024]{1,0:T(8,128)(2,1)}) custom-call(s32[3]{0:T(128)} %copy-done.1, bf16[2048,2048]{1,0:T(8,128)(2,1)} %all-gather.3.cloned.1.call-done.x_ref, bf16[2048,128]{1,0:T(8,128)(2,1)} %bitcast.42, bf16[2048,128]{1,0:T(8,128)(2,1)} %copy-done.18, ...), custom_call_target="tpu_custom_call" | custom-call | flops 1 | bytes 1 | tf_op jit(solution)/shard_map/mid_rows/pallas_call | solution.py:300
  151.1 23.4 %ffn_first.2 = (bf16[2048,256]{1,0:T(8,128)(2,1)}, bf16[2048,256]{1,0:T(8,128)(2,1)}, bf16[2048,256]{1,0:T(8,128)(2,1)}, bf16[384,2048]{1,0:T(8,128)(2,1)}, bf16[384,2048]{1,0:T(8,128)(2,1)}) custom-call(bf16[2048,2048]{1,0:T(8,128)(2,1)} %get-tuple-element.87.h2_ref.h2_col_ref, bf16[2048,2048]{1,0:T(8,128)(2,1)} %all-gather.5.cloned.1.call-done.cot_ref.cot_col_ref, ...), custom_call_target="tpu_custom_call" | custom-call | flops 1 | bytes 1 | tf_op jit(solution)/shard_map/ffn_first/pallas_call | solution.py:384
  174.5 3.7 collective-permute-start.16
  178.3 23.5 %ffn_first.3 = (bf16[2048,256]{1,0:T(8,128)(2,1)}, bf16[2048,256]{1,0:T(8,128)(2,1)}, bf16[2048,256]{1,0:T(8,128)(2,1)}, bf16[384,2048]{1,0:T(8,128)(2,1)}, bf16[384,2048]{1,0:T(8,128)(2,1)}) custom-call(bf16[2048,2048]{1,0:T(8,128)(2,1)} %get-tuple-element.87.h2_ref.h2_col_ref, bf16[2048,2048]{1,0:T(8,128)(2,1)} %all-gather.5.cloned.1.call-done.cot_ref.cot_col_ref, ...), custom_call_target="tpu_custom_call" | custom-call | flops 1 | bytes 1 | tf_op jit(solution)/shard_map/ffn_first/pallas_call | solution.py:384
  201.7 12.2 %ffn_rest.2 = (bf16[2048,256]{1,0:T(8,128)(2,1)}, bf16[2048,256]{1,0:T(8,128)(2,1)}, bf16[2048,256]{1,0:T(8,128)(2,1)}) custom-call(bf16[2048,2048]{1,0:T(8,128)(2,1)} %get-tuple-element.87.h2_ref.h2_col_ref, bf16[2048,2048]{1,0:T(8,128)(2,1)} %all-gather.5.cloned.1.call-done.cot_ref.cot_col_ref, bf16[2048,1024]{1,0:T(8,128)(2,1)} %wg_ref.9, ...), custom_call_target="tpu_custom_call" | custom-call | flops 1 | bytes 1 | tf_op jit(solution)/shard_map/ffn_rest/pallas_call | solution.py:410
  220.1 12.3 %ffn_rest.3 = (bf16[2048,256]{1,0:T(8,128)(2,1)}, bf16[2048,256]{1,0:T(8,128)(2,1)}, bf16[2048,256]{1,0:T(8,128)(2,1)}) custom-call(bf16[2048,2048]{1,0:T(8,128)(2,1)} %get-tuple-element.87.h2_ref.h2_col_ref, bf16[2048,2048]{1,0:T(8,128)(2,1)} %all-gather.5.cloned.1.call-done.cot_ref.cot_col_ref, bf16[2048,1024]{1,0:T(8,128)(2,1)} %wg_ref.9, ...), custom_call_target="tpu_custom_call" | custom-call | flops 1 | bytes 1 | tf_op jit(solution)/shard_map/ffn_rest/pallas_call | solution.py:410
  232.4 12.7 %ffn_weights.2 = (bf16[384,2048]{1,0:T(8,128)(2,1)}, bf16[384,2048]{1,0:T(8,128)(2,1)}) custom-call(bf16[2048,2048]{1,0:T(8,128)(2,1)} %get-tuple-element.87.h2_ref.h2_col_ref, bf16[2048,2048]{1,0:T(8,128)(2,1)} %all-gather.5.cloned.1.call-done.cot_ref.cot_col_ref, bf16[2048,256]{1,0:T(8,128)(2,1)} %get-tuple-element.96.__1_.hid_ref.refs_2_, ...), custom_call_target="tpu_custom_call" | custom-call | flops 1 | bytes 1 | tf_op jit(solution)/shard_map/ffn_weights/pallas_call | solution.py:440
  245.1 4.9 collective-permute-start.22
  251.2 2.8 join.21._.array_ref
  256.9 2.8 join.22.refs_8_.array_ref
  261.1 24.0 %ffn_back.1.__1_ = bf16[2048,2048]{1,0:T(8,128)(2,1)} custom-call(bf16[2048,1024]{1,0:T(8,128)(2,1)} %wg_ref.9, bf16[2048,1024]{1,0:T(8,128)(2,1)} %wu_ref.9, bf16[2048,256]{1,0:T(8,128)(2,1)} %get-tuple-element.89.refs_0_, bf16[2048,256]{1,0:T(8,128)(2,1)} %get-tuple-element.92.refs_1_, bf16[2048,256]{1,0:T(8,128)(2,1)} %get-tuple-element.94.dg_ref.refs_2_, ...), custom_call_target="tpu_custom_call" | custom-call | flops 1 | bytes 1 | tf_op jit(solution)/shard_map/ffn_back/pallas_call | solution.py:620
  285.1 6.4 %collective-permute-start.19 = (bf16[384,2048]{1,0:T(8,128)(2,1)}, bf16[384,2048]{1,0:T(8,128)(2,1)S(1)}, u32[]{:S(2)}, u32[]{:S(2)}) collective-permute-start(bf16[384,2048]{1,0:T(8,128)(2,1)} %hold.15._.array_ref), channel_id=1, source_target_pairs={{0,1},{3,2},{4,5},{7,6},{8,9},{11,10},{12,13},{15,14},{16,17},{19,... | collective-permute-start | bytes 4718600 | tf_op jit(solution)/shard_map/ppermute | solution.py:792
  291.6 2.8 join.23._.array_ref
  296.6 3.5 join.24.refs_0_.array_ref
  302.6 4.1 finish_ffn.8
  306.8 13.5 %ffn_out.1.__1_.refs_1_ = bf16[8,384,2048]{2,1,0:T(8,128)(2,1)} custom-call(bf16[1024,2048]{1,0:T(8,128)(2,1)} %w_ref.1, bf16[2048,256]{1,0:T(8,128)(2,1)} %get-tuple-element.91.__1_.refs_0_, bf16[2048,256]{1,0:T(8,128)(2,1)} %get-tuple-element.93._.refs_1_, bf16[2048,256]{1,0:T(8,128)(2,1)} %get-tuple-element.96.__1_.hid_ref.refs_2_, ...), custom_call_target="tpu_custom_call" | custom-call | flops 1 | bytes 1 | tf_op jit(solution)/shard_map/ffn_out/pallas_call | solution.py:644
  320.3 6.6 %collective-permute-start.24 = (bf16[384,2048]{1,0:T(8,128)(2,1)}, bf16[384,2048]{1,0:T(8,128)(2,1)}, u32[]{:S(2)}, u32[]{:S(2)}) collective-permute-start(bf16[384,2048]{1,0:T(8,128)(2,1)} %hold.16._.array_ref), channel_id=1, source_target_pairs={{0,1},{3,2},{4,5},{7,6},{8,9},{11,10},{12,13},{15,14},{16,17},{19,... | collective-permute-start | bytes 4718600 | tf_op jit(solution)/shard_map/ppermute | solution.py:792
  328.0 3.1 join.25._.array_ref
  332.9 2.9 join.26.refs_0_.array_ref
  337.1 3.9 finish_ffn.9
  341.0 12.7 %ffn_weights.3 = (bf16[384,2048]{1,0:T(8,128)(2,1)}, bf16[384,2048]{1,0:T(8,128)(2,1)}) custom-call(bf16[2048,2048]{1,0:T(8,128)(2,1)} %get-tuple-element.87.h2_ref.h2_col_ref, bf16[2048,2048]{1,0:T(8,128)(2,1)} %all-gather.5.cloned.1.call-done.cot_ref.cot_col_ref, bf16[2048,256]{1,0:T(8,128)(2,1)} %get-tuple-element.103._.refs_3_.hid_ref, ...), custom_call_target="tpu_custom_call" | custom-call | flops 1 | bytes 1 | tf_op jit(solution)/shard_map/ffn_weights/pallas_call | solution.py:440
  353.7 5.8 collective-permute-start.29
  359.6 2.9 join.27._.array_ref
  364.2 2.9 join.28.refs_0_.array_ref
  369.0 8.8 %own_rows_back.1 = (f32[256,2048]{1,0:T(8,128)}, bf16[256,1024]{1,0:T(8,128)(2,1)}, bf16[8,384,2048]{2,1,0:T(8,128)(2,1)}, f32[1,2048]{1,0:T(1,128)}) custom-call(bf16[256,2048]{1,0:T(8,128)(2,1)} %reduce-scatter.4.cloned.1.call-done.d_h2_ref, f32[256,2048]{1,0:T(8,128)} %get-tuple-element.105.y1_ref, ...), custom_call_target="tpu_custom_call", output_to_operand_aliasing={{2}: (7, {})} | custom-call | flops 1 | bytes 1 | tf_op jit(solution)/shard_map/own_rows_back/pallas_call | solution.py:675
  379.8 3.5 all-to-all-start
  384.5 4.4 finish_ffn.10
  388.9 8.2 %collective-permute-start.33 = (bf16[384,2048]{1,0:T(8,128)(2,1)}, bf16[384,2048]{1,0:T(8,128)(2,1)}, u32[]{:S(2)}, u32[]{:S(2)}) collective-permute-start(bf16[384,2048]{1,0:T(8,128)(2,1)} %hold.18._.array_ref), channel_id=1, source_target_pairs={{0,1},{3,2},{4,5},{7,6},{8,9},{11,10},{12,13},{15,14},{16,17},{19,... | collective-permute-start | bytes 4718600 | tf_op jit(solution)/shard_map/ppermute | solution.py:792
  397.1 3.0 join.29._.array_ref
  401.8 2.8 join.30.refs_0_.array_ref
  406.1 4.0 finish_ffn.11
  411.6 10.6 %head_backward.1 = (bf16[8,2,128,384]{3,2,1,0:T(8,128)(2,1)}, f32[2,8,128]{2,1,0:T(8,128)}) custom-call(f32[1]{0:T(128)S(6)} %div.3.share_ref, bf16[8,2,128,384]{3,2,1,0:T(8,128)(2,1)} %bitcast.34, bf16[8,2,128,128]{3,2,1,0:T(8,128)(2,1)} %bitcast.43, s32[2,1024,1]{2,1,0:T(8,128)} %copy.64.doc_rows_ref, s32[2,1,1024]{2,1,0:T(1,128)} %compare_select_fusion.doc_cols_ref, ...), custom_call_target="tpu_custom_call" | custom-call | flops 1 | bytes 1 | tf_op jit(solution)/shard_map/head_backward/pallas_call | solution.py:240
  422.2 6.6 %collective-permute-start.34 = (bf16[384,2048]{1,0:T(8,128)(2,1)}, bf16[384,2048]{1,0:T(8,128)(2,1)}, u32[]{:S(2)}, u32[]{:S(2)}) collective-permute-start(bf16[384,2048]{1,0:T(8,128)(2,1)} %hold.19._.array_ref), channel_id=1, source_target_pairs={{0,1},{3,2},{4,5},{7,6},{8,9},{11,10},{12,13},{15,14},{16,17},{19,... | collective-permute-start | bytes 4718600 | tf_op jit(solution)/shard_map/ppermute | solution.py:792
  430.9 2.8 join.31._.array_ref
  435.5 2.9 join.32.refs_0_.array_ref
  439.7 3.4 collective-permute-done.31.arrived_ref
  444.4 3.8 finish_ffn.12
  448.2 14.9 %qkv_back.1 = (bf16[2048,2048]{1,0:T(8,128)(2,1)}, bf16[2048,384]{1,0:T(8,128)(2,1)}) custom-call(bf16[2048,384]{1,0:T(8,128)(2,1)} %bitcast.44, bf16[2048,2048]{1,0:T(8,128)(2,1)} %get-tuple-element.125.h1_ref, bf16[2048,384]{1,0:T(8,128)(2,1)} %copy-done.3, f32[8,128]{1,0:T(8,128)} %get-tuple-element.130._), custom_call_target="tpu_custom_call" | custom-call | flops 1 | bytes 1 | tf_op jit(solution)/shard_map/qkv_back/pallas_call | solution.py:723
  463.1 4.0 collective-permute-start.36
  467.1 2.9 join.33.refs_0_.array_ref
  473.0 2.8 join.34.refs_0_.array_ref
  477.2 4.0 finish_ffn.13
  483.0 16.0 %collective-permute-done.36.arrived_ref = bf16[2048,384]{1,0:T(8,128)(2,1)} collective-permute-done((bf16[2048,384]{1,0:T(8,128)(2,1)}, bf16[2048,384]{1,0:T(8,128)(2,1)}, u32[]{:S(2)}, u32[]{:S(2)}) %collective-permute-start.36) | collective-permute-done | bytes 1572896 | tf_op jit(solution)/shard_map/ppermute | solution.py:792
  499.1 3.4 join.35._.array_ref
  504.4 2.9 join.36.refs_0_.array_ref
  508.6 6.6 %collective-permute-start.41 = (bf16[128,2048]{1,0:T(8,128)(2,1)S(1)}, bf16[128,2048]{1,0:T(8,128)(2,1)}, u32[]{:S(2)}, u32[]{:S(2)}) collective-permute-start(bf16[128,2048]{1,0:T(8,128)(2,1)S(1)} %copy-done.4), channel_id=1, source_target_pairs={{0,1},{3,2},{4,5},{7,6},{8,9},{11,10},{12,13},{15,14},{16,17},{19,... | collective-permute-start | bytes 1572872 | tf_op jit(solution)/shard_map/ppermute | solution.py:792
  518.3 3.7 finish_ffn.14
  526.1 2.9 join.38.refs_0_.array_ref
  530.5 18.5 %collective-permute-done.39.arrived_ref = bf16[384,2048]{1,0:T(8,128)(2,1)S(1)} collective-permute-done((bf16[384,2048]{1,0:T(8,128)(2,1)}, bf16[384,2048]{1,0:T(8,128)(2,1)S(1)}, u32[]{:S(2)}, u32[]{:S(2)}) %collective-permute-start.39) | collective-permute-done | bytes 1572896 | tf_op jit(solution)/shard_map/ppermute | solution.py:792
  550.1 3.9 finish_ffn.15
  554.6 6.7 %last_rows.1 = (f32[256,2048]{1,0:T(8,128)}, f32[1,2048]{1,0:T(1,128)}, bf16[256,2048]{1,0:T(8,128)(2,1)}) custom-call(bf16[256,2048]{1,0:T(8,128)(2,1)} %reduce-scatter.8.cloned.1.call-done.d_h1_ref, bf16[256,2048]{1,0:T(8,128)(2,1)} %bitcast.38, f32[256,2048]{1,0:T(8,128)} %get-tuple-element.116.refs_0_.d_y1_ref, f32[1,2048]{1,0:T(1,128)} %bitcast.53, ...), custom_call_target="tpu_custom_call" | custom-call | flops 1 | bytes 1 | tf_op jit(solution)/shard_map/last_rows/pallas_call | solution.py:582
  567.2 2.8 collective-permute-done.47
  576.5 8.0 %collective-permute-done.43.arrived_ref = bf16[2048,384]{1,0:T(8,128)(2,1)} collective-permute-done((bf16[2048,384]{1,0:T(8,128)(2,1)}, bf16[2048,384]{1,0:T(8,128)(2,1)}, u32[]{:S(2)}, u32[]{:S(2)}) %collective-permute-start.43) | collective-permute-done | bytes 1572896 | tf_op jit(solution)/shard_map/ppermute | solution.py:792
  584.5 3.2 finish_cut.2
  587.7 4.7 collective-permute-done.49
  594.4 3.5 collective-permute-done.50
  (210 shorter events, 104.9 us)
Async XLA Ops:
  7.2 21.6 %copy-start.2 = (bf16[128,2048]{1,0:T(8,128)(2,1)S(1)}, bf16[128,2048]{1,0:T(8,128)(2,1)}, u32[]{:S(2)}) copy-start(bf16[128,2048]{1,0:T(8,128)(2,1)} %refs_0_.1) | copy-start | bytes 1572868
  7.2 66.7 %all-gather.3.cloned.1.call-start = ((), (), s32[]{:S(2)}) async-start(), calls=%async_computation.4 | async-start | bytes 9437184 | tf_op jit(solution)/shard_map/all_gather | solution.py:900
  7.9 143.1 %all-gather.5.cloned.1.call-start = ((), (), s32[]{:S(2)}) async-start(), calls=%async_computation.5 | async-start | bytes 9437184 | tf_op jit(solution)/shard_map/all_gather | solution.py:900
  8.0 16.9 %collective-permute-start.1 = (bf16[128,2048]{1,0:T(8,128)(2,1)}, bf16[128,2048]{1,0:T(8,128)(2,1)S(1)}, u32[]{:S(2)}, u32[]{:S(2)}) collective-permute-start(bf16[128,2048]{1,0:T(8,128)(2,1)} %refs_0_.1), channel_id=1, source_target_pairs={{0,8},{4,12},{8,0},{12,4},{16,24},{20,28},{24,16},{28,20},{1,9},{5... | collective-permute-start | bytes 1572872 | tf_op jit(solution)/shard_map/ppermute | solution.py:863
  11.0 17.2 %collective-permute-start.3 = (bf16[128,2048]{1,0:T(8,128)(2,1)}, bf16[128,2048]{1,0:T(8,128)(2,1)S(1)}, u32[]{:S(2)}, u32[]{:S(2)}) collective-permute-start(bf16[128,2048]{1,0:T(8,128)(2,1)} %refs_0_.1), channel_id=1, source_target_pairs={{0,16},{4,20},{8,24},{12,28},{16,0},{20,4},{24,8},{28,12},{1,17},{... | collective-permute-start | bytes 1572872 | tf_op jit(solution)/shard_map/ppermute | solution.py:863
  24.9 13.7 %collective-permute-start.5 = (bf16[64,2048]{1,0:T(8,128)(2,1)S(1)}, bf16[64,2048]{1,0:T(8,128)(2,1)S(1)}, u32[]{:S(2)}, u32[]{:S(2)}) collective-permute-start(bf16[64,2048]{1,0:T(8,128)(2,1)S(1)} %slice.32), channel_id=1, source_target_pairs={{0,16},{4,20},{8,24},{12,28},{16,0},{20,4},{24,8},{28,12},{1,17},{... | collective-permute-start | bytes 786440 | tf_op jit(solution)/shard_map/ppermute | solution.py:863
  28.2 11.8 %collective-permute-start.6 = (bf16[64,2048]{1,0:T(8,128)(2,1)S(1)}, bf16[64,2048]{1,0:T(8,128)(2,1)S(1)}, u32[]{:S(2)}, u32[]{:S(2)}) collective-permute-start(bf16[64,2048]{1,0:T(8,128)(2,1)S(1)} %slice.33), channel_id=1, source_target_pairs={{0,8},{4,12},{8,0},{12,4},{16,24},{20,28},{24,16},{28,20},{1,9},{5... | collective-permute-start | bytes 786440 | tf_op jit(solution)/shard_map/ppermute | solution.py:863
  28.8 11.4 %collective-permute-start = (bf16[128,2048]{1,0:T(8,128)(2,1)S(1)}, bf16[128,2048]{1,0:T(8,128)(2,1)S(1)}, u32[]{:S(2)}, u32[]{:S(2)}) collective-permute-start(bf16[128,2048]{1,0:T(8,128)(2,1)S(1)} %copy-done.2), channel_id=1, source_target_pairs={{0,4},{4,0},{8,12},{12,8},{16,20},{20,16},{24,28},{28,24},{1,5},{5... | collective-permute-start | bytes 1572872 | tf_op jit(solution)/shard_map/ppermute | solution.py:863
  28.8 11.4 %collective-permute-start.2 = (bf16[128,2048]{1,0:T(8,128)(2,1)S(1)}, bf16[128,2048]{1,0:T(8,128)(2,1)S(1)}, u32[]{:S(2)}, u32[]{:S(2)}) collective-permute-start(bf16[128,2048]{1,0:T(8,128)(2,1)S(1)} %collective-permute-done.1.refs_2_), channel_id=1, source_target_pairs={{0,4},{4,0},{8,12},{12,8},{16,20},{20,16},{24,28},{28,24},{1,5},{5... | collective-permute-start | bytes 1572872 | tf_op jit(solution)/shard_map/ppermute | solution.py:863
  29.3 10.9 %collective-permute-start.4 = (bf16[128,2048]{1,0:T(8,128)(2,1)S(1)}, bf16[128,2048]{1,0:T(8,128)(2,1)}, u32[]{:S(2)}, u32[]{:S(2)}) collective-permute-start(bf16[128,2048]{1,0:T(8,128)(2,1)S(1)} %collective-permute-done.3.refs_4_), channel_id=1, source_target_pairs={{0,4},{4,0},{8,12},{12,8},{16,20},{20,16},{24,28},{28,24},{1,5},{5... | collective-permute-start | bytes 1572872 | tf_op jit(solution)/shard_map/ppermute | solution.py:863
  40.0 2.1 collective-permute-start.7
  40.2 34.6 %copy-start.31 = (s32[2,1,4]{2,1,0:T(1,128)S(1)}, s32[2,1,4]{2,1,0:T(1,128)}, u32[]{:S(2)}) copy-start(s32[2,1,4]{2,1,0:T(1,128)} %param.16) | copy-start | bytes 100
  45.5 30.8 %copy-start.30 = (s32[2,1,1024]{2,1,0:T(1,128)S(1)}, s32[2,1,1024]{2,1,0:T(1,128)}, u32[]{:S(2)}) copy-start(s32[2,1,1024]{2,1,0:T(1,128)} %param.17) | copy-start | bytes 24580
  45.5 31.5 %copy-start.22 = (bf16[2048,128]{1,0:T(8,128)(2,1)S(1)}, bf16[2048,128]{1,0:T(8,128)(2,1)}, u32[]{:S(2)}) copy-start(bf16[2048,128]{1,0:T(8,128)(2,1)} %param.18) | copy-start | bytes 1572868
  73.9 295.1 %reduce-scatter.4.cloned.1.call-start = ((), (), s32[]{:S(2)}) async-start(), calls=%async_computation.6 | async-start | bytes 9437184 | tf_op jit(solution)/shard_map/reduce_scatter | solution.py:903
  94.9 18.4 %collective-permute-start.9 = (bf16[2048,128]{1,0:T(8,128)(2,1)}, bf16[2048,128]{1,0:T(8,128)(2,1)S(1)}, u32[]{:S(2)}, u32[]{:S(2)}) collective-permute-start(bf16[2048,128]{1,0:T(8,128)(2,1)} %bitcast.39), channel_id=1, source_target_pairs={{0,8},{4,12},{8,0},{12,4},{16,24},{20,28},{24,16},{28,20},{1,9},{5... | collective-permute-start | bytes 1572872 | tf_op jit(solution)/shard_map/ppermute | solution.py:863
  96.3 20.0 %collective-permute-start.11 = (bf16[2048,128]{1,0:T(8,128)(2,1)}, bf16[2048,128]{1,0:T(8,128)(2,1)S(1)}, u32[]{:S(2)}, u32[]{:S(2)}) collective-permute-start(bf16[2048,128]{1,0:T(8,128)(2,1)} %bitcast.40), channel_id=1, source_target_pairs={{0,16},{4,20},{8,24},{12,28},{16,0},{20,4},{24,8},{28,12},{1,17},{... | collective-permute-start | bytes 1572872 | tf_op jit(solution)/shard_map/ppermute | solution.py:863
  113.4 18.7 %copy-start.15 = (bf16[2048,128]{1,0:T(8,128)(2,1)}, bf16[2048,128]{1,0:T(8,128)(2,1)S(1)}, u32[]{:S(2)}) copy-start(bf16[2048,128]{1,0:T(8,128)(2,1)S(1)} %collective-permute-done.9.refs_2_) | copy-start | bytes 1572868
  113.4 14.1 %collective-permute-start.13 = (bf16[1024,128]{1,0:T(8,128)(2,1)S(1)}, bf16[1024,128]{1,0:T(8,128)(2,1)S(1)}, u32[]{:S(2)}, u32[]{:S(2)}) collective-permute-start(bf16[1024,128]{1,0:T(8,128)(2,1)S(1)} %slice.34), channel_id=1, source_target_pairs={{0,16},{4,20},{8,24},{12,28},{16,0},{20,4},{24,8},{28,12},{1,17},{... | collective-permute-start | bytes 786440 | tf_op jit(solution)/shard_map/ppermute | solution.py:863
  116.3 15.7 %copy-start.16 = (bf16[2048,128]{1,0:T(8,128)(2,1)}, bf16[2048,128]{1,0:T(8,128)(2,1)S(1)}, u32[]{:S(2)}) copy-start(bf16[2048,128]{1,0:T(8,128)(2,1)S(1)} %collective-permute-done.11.refs_4_) | copy-start | bytes 1572868
  116.4 13.5 %collective-permute-start.14 = (bf16[1024,128]{1,0:T(8,128)(2,1)S(1)}, bf16[1024,128]{1,0:T(8,128)(2,1)S(1)}, u32[]{:S(2)}, u32[]{:S(2)}) collective-permute-start(bf16[1024,128]{1,0:T(8,128)(2,1)S(1)} %slice.35), channel_id=1, source_target_pairs={{0,8},{4,12},{8,0},{12,4},{16,24},{20,28},{24,16},{28,20},{1,9},{5... | collective-permute-start | bytes 786440 | tf_op jit(solution)/shard_map/ppermute | solution.py:863
  116.4 13.5 %collective-permute-start.8 = (bf16[2048,128]{1,0:T(8,128)(2,1)}, bf16[2048,128]{1,0:T(8,128)(2,1)S(1)}, u32[]{:S(2)}, u32[]{:S(2)}) collective-permute-start(bf16[2048,128]{1,0:T(8,128)(2,1)} %bitcast.41), channel_id=1, source_target_pairs={{0,4},{4,0},{8,12},{12,8},{16,20},{20,16},{24,28},{28,24},{1,5},{5... | collective-permute-start | bytes 1572872 | tf_op jit(solution)/shard_map/ppermute | solution.py:863
  116.5 13.5 %collective-permute-start.12 = (bf16[2048,128]{1,0:T(8,128)(2,1)S(1)}, bf16[2048,128]{1,0:T(8,128)(2,1)S(1)}, u32[]{:S(2)}, u32[]{:S(2)}) collective-permute-start(bf16[2048,128]{1,0:T(8,128)(2,1)S(1)} %collective-permute-done.11.refs_4_), channel_id=1, source_target_pairs={{0,4},{4,0},{8,12},{12,8},{16,20},{20,16},{24,28},{28,24},{1,5},{5... | collective-permute-start | bytes 1572872 | tf_op jit(solution)/shard_map/ppermute | solution.py:863
  117.0 13.0 %collective-permute-start.10 = (bf16[2048,128]{1,0:T(8,128)(2,1)S(1)}, bf16[2048,128]{1,0:T(8,128)(2,1)S(1)}, u32[]{:S(2)}, u32[]{:S(2)}) collective-permute-start(bf16[2048,128]{1,0:T(8,128)(2,1)S(1)} %collective-permute-done.9.refs_2_), channel_id=1, source_target_pairs={{0,4},{4,0},{8,12},{12,8},{16,20},{20,16},{24,28},{28,24},{1,5},{5... | collective-permute-start | bytes 1572872 | tf_op jit(solution)/shard_map/ppermute | solution.py:863
  129.9 2.2 collective-permute-start.15
  174.5 40.8 %collective-permute-start.16 = (bf16[384,2048]{1,0:T(8,128)(2,1)}, bf16[384,2048]{1,0:T(8,128)(2,1)S(1)}, u32[]{:S(2)}, u32[]{:S(2)}) collective-permute-start(bf16[384,2048]{1,0:T(8,128)(2,1)} %hold.12._.array_ref), channel_id=1, source_target_pairs={{0,1},{3,2},{4,5},{7,6},{8,9},{11,10},{12,13},{15,14},{16,17},{19,... | collective-permute-start | bytes 4718600 | tf_op jit(solution)/shard_map/ppermute | solution.py:792
  214.0 36.1 %collective-permute-start.18 = (bf16[384,2048]{1,0:T(8,128)(2,1)}, bf16[384,2048]{1,0:T(8,128)(2,1)S(1)}, u32[]{:S(2)}, u32[]{:S(2)}) collective-permute-start(bf16[384,2048]{1,0:T(8,128)(2,1)} %hold.13._.array_ref), channel_id=1, source_target_pairs={{0,1},{3,2},{4,5},{7,6},{8,9},{11,10},{12,13},{15,14},{16,17},{19,... | collective-permute-start | bytes 4718600 | tf_op jit(solution)/shard_map/ppermute | solution.py:792
  219.3 36.5 %collective-permute-start.17 = (bf16[384,2048]{1,0:T(8,128)(2,1)}, bf16[384,2048]{1,0:T(8,128)(2,1)S(1)}, u32[]{:S(2)}, u32[]{:S(2)}) collective-permute-start(bf16[384,2048]{1,0:T(8,128)(2,1)} %join.20._.array_ref), channel_id=1, source_target_pairs={{1,2},{2,1},{5,6},{6,5},{9,10},{10,9},{13,14},{14,13},{17,18},{18,... | collective-permute-start | bytes 4718600 | tf_op jit(solution)/shard_map/ppermute | solution.py:792
  245.1 46.4 %collective-permute-start.22 = (bf16[384,2048]{1,0:T(8,128)(2,1)}, bf16[384,2048]{1,0:T(8,128)(2,1)}, u32[]{:S(2)}, u32[]{:S(2)}) collective-permute-start(bf16[384,2048]{1,0:T(8,128)(2,1)} %hold.14._.array_ref), channel_id=1, source_target_pairs={{0,1},{3,2},{4,5},{7,6},{8,9},{11,10},{12,13},{15,14},{16,17},{19,... | collective-permute-start | bytes 4718600 | tf_op jit(solution)/shard_map/ppermute | solution.py:792
  254.0 42.6 %collective-permute-start.21 = (bf16[384,2048]{1,0:T(8,128)(2,1)}, bf16[384,2048]{1,0:T(8,128)(2,1)}, u32[]{:S(2)}, u32[]{:S(2)}) collective-permute-start(bf16[384,2048]{1,0:T(8,128)(2,1)} %join.21._.array_ref), channel_id=1, source_target_pairs={{1,2},{2,1},{5,6},{6,5},{9,10},{10,9},{13,14},{14,13},{17,18},{18,... | collective-permute-start | bytes 4718600 | tf_op jit(solution)/shard_map/ppermute | solution.py:792
  259.8 41.6 %collective-permute-start.20 = (bf16[384,2048]{1,0:T(8,128)(2,1)}, bf16[384,2048]{1,0:T(8,128)(2,1)S(1)}, u32[]{:S(2)}, u32[]{:S(2)}) collective-permute-start(bf16[384,2048]{1,0:T(8,128)(2,1)} %join.22.refs_8_.array_ref), channel_id=1, source_target_pairs={{1,0},{2,3},{5,4},{6,7},{9,8},{10,11},{13,12},{14,15},{17,16},{18,... | collective-permute-start | bytes 4718600 | tf_op jit(solution)/shard_map/ppermute | solution.py:792
  285.1 41.8 %collective-permute-start.19 = (bf16[384,2048]{1,0:T(8,128)(2,1)}, bf16[384,2048]{1,0:T(8,128)(2,1)S(1)}, u32[]{:S(2)}, u32[]{:S(2)}) collective-permute-start(bf16[384,2048]{1,0:T(8,128)(2,1)} %hold.15._.array_ref), channel_id=1, source_target_pairs={{0,1},{3,2},{4,5},{7,6},{8,9},{11,10},{12,13},{15,14},{16,17},{19,... | collective-permute-start | bytes 4718600 | tf_op jit(solution)/shard_map/ppermute | solution.py:792
  291.5 180.9 %reduce-scatter.6.cloned.1.call-start = ((), (), s32[]{:S(2)}) async-start(), calls=%async_computation.7 | async-start | bytes 14155776 | tf_op jit(solution)/shard_map/reduce_scatter | solution.py:903
  294.4 38.5 %collective-permute-start.26 = (bf16[384,2048]{1,0:T(8,128)(2,1)}, bf16[384,2048]{1,0:T(8,128)(2,1)}, u32[]{:S(2)}, u32[]{:S(2)}) collective-permute-start(bf16[384,2048]{1,0:T(8,128)(2,1)} %join.23._.array_ref), channel_id=1, source_target_pairs={{1,2},{2,1},{5,6},{6,5},{9,10},{10,9},{13,14},{14,13},{17,18},{18,... | collective-permute-start | bytes 4718600 | tf_op jit(solution)/shard_map/ppermute | solution.py:792
  300.1 36.9 %collective-permute-start.25 = (bf16[384,2048]{1,0:T(8,128)(2,1)}, bf16[384,2048]{1,0:T(8,128)(2,1)}, u32[]{:S(2)}, u32[]{:S(2)}) collective-permute-start(bf16[384,2048]{1,0:T(8,128)(2,1)} %join.24.refs_0_.array_ref), channel_id=1, source_target_pairs={{1,0},{2,3},{5,4},{6,7},{9,8},{10,11},{13,12},{14,15},{17,16},{18,... | collective-permute-start | bytes 4718600 | tf_op jit(solution)/shard_map/ppermute | solution.py:792
  320.3 39.3 %collective-permute-start.24 = (bf16[384,2048]{1,0:T(8,128)(2,1)}, bf16[384,2048]{1,0:T(8,128)(2,1)}, u32[]{:S(2)}, u32[]{:S(2)}) collective-permute-start(bf16[384,2048]{1,0:T(8,128)(2,1)} %hold.16._.array_ref), channel_id=1, source_target_pairs={{0,1},{3,2},{4,5},{7,6},{8,9},{11,10},{12,13},{15,14},{16,17},{19,... | collective-permute-start | bytes 4718600 | tf_op jit(solution)/shard_map/ppermute | solution.py:792
  331.1 33.1 %collective-permute-start.23 = (bf16[384,2048]{1,0:T(8,128)(2,1)}, bf16[384,2048]{1,0:T(8,128)(2,1)}, u32[]{:S(2)}, u32[]{:S(2)}) collective-permute-start(bf16[384,2048]{1,0:T(8,128)(2,1)} %join.25._.array_ref), channel_id=1, source_target_pairs={{1,2},{2,1},{5,6},{6,5},{9,10},{10,9},{13,14},{14,13},{17,18},{18,... | collective-permute-start | bytes 4718600 | tf_op jit(solution)/shard_map/ppermute | solution.py:792
  335.8 47.5 %collective-permute-start.30 = (bf16[384,2048]{1,0:T(8,128)(2,1)}, bf16[384,2048]{1,0:T(8,128)(2,1)S(1)}, u32[]{:S(2)}, u32[]{:S(2)}) collective-permute-start(bf16[384,2048]{1,0:T(8,128)(2,1)} %join.26.refs_0_.array_ref), channel_id=1, source_target_pairs={{1,0},{2,3},{5,4},{6,7},{9,8},{10,11},{13,12},{14,15},{17,16},{18,... | collective-permute-start | bytes 4718600 | tf_op jit(solution)/shard_map/ppermute | solution.py:792
  353.7 43.3 %collective-permute-start.29 = (bf16[384,2048]{1,0:T(8,128)(2,1)}, bf16[384,2048]{1,0:T(8,128)(2,1)}, u32[]{:S(2)}, u32[]{:S(2)}) collective-permute-start(bf16[384,2048]{1,0:T(8,128)(2,1)} %hold.17._.array_ref), channel_id=1, source_target_pairs={{0,1},{3,2},{4,5},{7,6},{8,9},{11,10},{12,13},{15,14},{16,17},{19,... | collective-permute-start | bytes 4718600 | tf_op jit(solution)/shard_map/ppermute | solution.py:792
  362.4 39.4 %collective-permute-start.28 = (bf16[384,2048]{1,0:T(8,128)(2,1)}, bf16[384,2048]{1,0:T(8,128)(2,1)}, u32[]{:S(2)}, u32[]{:S(2)}) collective-permute-start(bf16[384,2048]{1,0:T(8,128)(2,1)} %join.27._.array_ref), channel_id=1, source_target_pairs={{1,2},{2,1},{5,6},{6,5},{9,10},{10,9},{13,14},{14,13},{17,18},{18,... | collective-permute-start | bytes 4718600 | tf_op jit(solution)/shard_map/ppermute | solution.py:792
  367.1 39.0 %collective-permute-start.27 = (bf16[384,2048]{1,0:T(8,128)(2,1)}, bf16[384,2048]{1,0:T(8,128)(2,1)}, u32[]{:S(2)}, u32[]{:S(2)}) collective-permute-start(bf16[384,2048]{1,0:T(8,128)(2,1)} %join.28.refs_0_.array_ref), channel_id=1, source_target_pairs={{1,0},{2,3},{5,4},{6,7},{9,8},{10,11},{13,12},{14,15},{17,16},{18,... | collective-permute-start | bytes 4718600 | tf_op jit(solution)/shard_map/ppermute | solution.py:792
  379.8 31.0 %all-to-all-start = ((bf16[256,8,128]{2,0,1:T(8,128)(2,1)}), bf16[256,8,128]{2,0,1:T(8,128)(2,1)S(1)}, u32[]{:S(2)}, u32[]{:S(2)}) async-start(bf16[256,8,128]{2,0,1:T(8,128)(2,1)} %copy_bitcast_fusion), calls=%async_computation.1 | async-start | bytes 1048576 | tf_op jit(solution)/shard_map/all_to_all | solution.py:1002
  383.3 171.4 %reduce-scatter.8.cloned.1.call-start = ((), (), s32[]{:S(2)}) async-start(), calls=%async_computation.8 | async-start | bytes 9437184 | tf_op jit(solution)/shard_map/reduce_scatter | solution.py:903
  388.9 42.0 %collective-permute-start.33 = (bf16[384,2048]{1,0:T(8,128)(2,1)}, bf16[384,2048]{1,0:T(8,128)(2,1)}, u32[]{:S(2)}, u32[]{:S(2)}) collective-permute-start(bf16[384,2048]{1,0:T(8,128)(2,1)} %hold.18._.array_ref), channel_id=1, source_target_pairs={{0,1},{3,2},{4,5},{7,6},{8,9},{11,10},{12,13},{15,14},{16,17},{19,... | collective-permute-start | bytes 4718600 | tf_op jit(solution)/shard_map/ppermute | solution.py:792
  400.0 35.5 %collective-permute-start.32 = (bf16[384,2048]{1,0:T(8,128)(2,1)}, bf16[384,2048]{1,0:T(8,128)(2,1)}, u32[]{:S(2)}, u32[]{:S(2)}) collective-permute-start(bf16[384,2048]{1,0:T(8,128)(2,1)} %join.29._.array_ref), channel_id=1, source_target_pairs={{1,2},{2,1},{5,6},{6,5},{9,10},{10,9},{13,14},{14,13},{17,18},{18,... | collective-permute-start | bytes 4718600 | tf_op jit(solution)/shard_map/ppermute | solution.py:792
  404.7 38.4 %collective-permute-start.31 = (bf16[384,2048]{1,0:T(8,128)(2,1)}, bf16[384,2048]{1,0:T(8,128)(2,1)S(1)}, u32[]{:S(2)}, u32[]{:S(2)}) collective-permute-start(bf16[384,2048]{1,0:T(8,128)(2,1)} %join.30.refs_0_.array_ref), channel_id=1, source_target_pairs={{1,0},{2,3},{5,4},{6,7},{9,8},{10,11},{13,12},{14,15},{17,16},{18,... | collective-permute-start | bytes 4718600 | tf_op jit(solution)/shard_map/ppermute | solution.py:792
  422.2 44.9 %collective-permute-start.34 = (bf16[384,2048]{1,0:T(8,128)(2,1)}, bf16[384,2048]{1,0:T(8,128)(2,1)}, u32[]{:S(2)}, u32[]{:S(2)}) collective-permute-start(bf16[384,2048]{1,0:T(8,128)(2,1)} %hold.19._.array_ref), channel_id=1, source_target_pairs={{0,1},{3,2},{4,5},{7,6},{8,9},{11,10},{12,13},{15,14},{16,17},{19,... | collective-permute-start | bytes 4718600 | tf_op jit(solution)/shard_map/ppermute | solution.py:792
  433.7 39.3 %collective-permute-start.38 = (bf16[384,2048]{1,0:T(8,128)(2,1)}, bf16[384,2048]{1,0:T(8,128)(2,1)}, u32[]{:S(2)}, u32[]{:S(2)}) collective-permute-start(bf16[384,2048]{1,0:T(8,128)(2,1)} %join.31._.array_ref), channel_id=1, source_target_pairs={{1,2},{2,1},{5,6},{6,5},{9,10},{10,9},{13,14},{14,13},{17,18},{18,... | collective-permute-start | bytes 4718600 | tf_op jit(solution)/shard_map/ppermute | solution.py:792
  438.4 38.7 %collective-permute-start.37 = (bf16[384,2048]{1,0:T(8,128)(2,1)}, bf16[384,2048]{1,0:T(8,128)(2,1)}, u32[]{:S(2)}, u32[]{:S(2)}) collective-permute-start(bf16[384,2048]{1,0:T(8,128)(2,1)} %join.32.refs_0_.array_ref), channel_id=1, source_target_pairs={{1,0},{2,3},{5,4},{6,7},{9,8},{10,11},{13,12},{14,15},{17,16},{18,... | collective-permute-start | bytes 4718600 | tf_op jit(solution)/shard_map/ppermute | solution.py:792
  463.1 36.0 %collective-permute-start.36 = (bf16[2048,384]{1,0:T(8,128)(2,1)}, bf16[2048,384]{1,0:T(8,128)(2,1)}, u32[]{:S(2)}, u32[]{:S(2)}) collective-permute-start(bf16[2048,384]{1,0:T(8,128)(2,1)} %hold.20._.array_ref), channel_id=1, source_target_pairs={{0,1},{3,2},{4,5},{7,6},{8,9},{11,10},{12,13},{15,14},{16,17},{19,... | collective-permute-start | bytes 4718600 | tf_op jit(solution)/shard_map/ppermute | solution.py:792
  470.0 34.5 %collective-permute-start.35 = (bf16[384,2048]{1,0:T(8,128)(2,1)}, bf16[384,2048]{1,0:T(8,128)(2,1)}, u32[]{:S(2)}, u32[]{:S(2)}) collective-permute-start(bf16[384,2048]{1,0:T(8,128)(2,1)} %join.33.refs_0_.array_ref), channel_id=1, source_target_pairs={{1,2},{2,1},{5,6},{6,5},{9,10},{10,9},{13,14},{14,13},{17,18},{18,... | collective-permute-start | bytes 4718600 | tf_op jit(solution)/shard_map/ppermute | solution.py:792
  475.9 41.3 %collective-permute-start.42 = (bf16[384,2048]{1,0:T(8,128)(2,1)}, bf16[384,2048]{1,0:T(8,128)(2,1)S(1)}, u32[]{:S(2)}, u32[]{:S(2)}) collective-permute-start(bf16[384,2048]{1,0:T(8,128)(2,1)} %join.34.refs_0_.array_ref), channel_id=1, source_target_pairs={{1,0},{2,3},{5,4},{6,7},{9,8},{10,11},{13,12},{14,15},{17,16},{18,... | collective-permute-start | bytes 4718600 | tf_op jit(solution)/shard_map/ppermute | solution.py:792
  502.5 23.6 %collective-permute-start.40 = (bf16[2048,384]{1,0:T(8,128)(2,1)}, bf16[2048,384]{1,0:T(8,128)(2,1)}, u32[]{:S(2)}, u32[]{:S(2)}) collective-permute-start(bf16[2048,384]{1,0:T(8,128)(2,1)} %join.35._.array_ref), channel_id=1, source_target_pairs={{1,2},{2,1},{5,6},{6,5},{9,10},{10,9},{13,14},{14,13},{17,18},{18,... | collective-permute-start | bytes 4718600 | tf_op jit(solution)/shard_map/ppermute | solution.py:792
  507.3 41.7 %collective-permute-start.39 = (bf16[384,2048]{1,0:T(8,128)(2,1)}, bf16[384,2048]{1,0:T(8,128)(2,1)S(1)}, u32[]{:S(2)}, u32[]{:S(2)}) collective-permute-start(bf16[384,2048]{1,0:T(8,128)(2,1)} %join.36.refs_0_.array_ref), channel_id=1, source_target_pairs={{1,0},{2,3},{5,4},{6,7},{9,8},{10,11},{13,12},{14,15},{17,16},{18,... | collective-permute-start | bytes 4718600 | tf_op jit(solution)/shard_map/ppermute | solution.py:792
  508.6 14.8 %collective-permute-start.41 = (bf16[128,2048]{1,0:T(8,128)(2,1)S(1)}, bf16[128,2048]{1,0:T(8,128)(2,1)}, u32[]{:S(2)}, u32[]{:S(2)}) collective-permute-start(bf16[128,2048]{1,0:T(8,128)(2,1)S(1)} %copy-done.4), channel_id=1, source_target_pairs={{0,1},{3,2},{4,5},{7,6},{8,9},{11,10},{12,13},{15,14},{16,17},{19,... | collective-permute-start | bytes 1572872 | tf_op jit(solution)/shard_map/ppermute | solution.py:792
  525.4 36.8 %collective-permute-start.44 = (bf16[128,2048]{1,0:T(8,128)(2,1)}, bf16[128,2048]{1,0:T(8,128)(2,1)S(1)}, u32[]{:S(2)}, u32[]{:S(2)}) collective-permute-start(bf16[128,2048]{1,0:T(8,128)(2,1)} %join.37._.array_ref), channel_id=1, source_target_pairs={{1,2},{2,1},{5,6},{6,5},{9,10},{10,9},{13,14},{14,13},{17,18},{18,... | collective-permute-start | bytes 1572872 | tf_op jit(solution)/shard_map/ppermute | solution.py:792
  529.0 55.5 %collective-permute-start.43 = (bf16[2048,384]{1,0:T(8,128)(2,1)}, bf16[2048,384]{1,0:T(8,128)(2,1)}, u32[]{:S(2)}, u32[]{:S(2)}) collective-permute-start(bf16[2048,384]{1,0:T(8,128)(2,1)} %join.38.refs_0_.array_ref), channel_id=1, source_target_pairs={{1,0},{2,3},{5,4},{6,7},{9,8},{10,11},{13,12},{14,15},{17,16},{18,... | collective-permute-start | bytes 4718600 | tf_op jit(solution)/shard_map/ppermute | solution.py:792
  554.6 6.8 %copy-start.29 = (f32[1,2048]{1,0:T(1,128)S(1)}, f32[1,2048]{1,0:T(1,128)}, u32[]{:S(2)}) copy-start(f32[1,2048]{1,0:T(1,128)} %get-tuple-element.150) | copy-start | bytes 24580
  562.1 4.0 collective-permute-start.46
  564.8 35.0 %collective-permute-start.45 = (bf16[128,2048]{1,0:T(8,128)(2,1)}, bf16[128,2048]{1,0:T(8,128)(2,1)S(1)}, u32[]{:S(2)}, u32[]{:S(2)}) collective-permute-start(bf16[128,2048]{1,0:T(8,128)(2,1)} %join.39._.array_ref), channel_id=1, source_target_pairs={{1,0},{2,3},{5,4},{6,7},{9,8},{10,11},{13,12},{14,15},{17,16},{18,... | collective-permute-start | bytes 1572872 | tf_op jit(solution)/shard_map/ppermute | solution.py:792
  566.2 3.8 collective-permute-start.47
  570.0 3.8 collective-permute-start.48
  573.8 18.6 %collective-permute-start.49 = (f32[4104]{0:T(1024)S(1)}, f32[4104]{0:T(1024)S(1)}, u32[]{:S(2)}, u32[]{:S(2)}) collective-permute-start(f32[4104]{0:T(1024)S(1)} %add.32), channel_id=1, source_target_pairs={{0,1},{1,0},{2,3},{3,2},{4,5},{5,4},{6,7},{7,6},{8,9},{9,8},{10,11... | collective-permute-start | bytes 49256 | tf_op jit(solution)/shard_map/ppermute | solution.py:1036
  593.0 4.9 collective-permute-start.50
  (25 other events, 46.0 us)
Sparse Core Ops, SparseCore 0:
  9.9 63.9 all-gather.2
  75.8 64.6 all-gather.4
  291.6 68.4 reduce-scatter.3
  378.0 93.5 reduce-scatter.5
  475.3 71.2 reduce-scatter.7
